TPU v7x, 32 devices: a whole 2x2x4 slice. The times are simulated.
32 devices in a mesh: ctx: 4 (over y, x), exp: 8 (over z, core).
Axes of the slice: x: 2, y: 2, z: 4, core: 2. Of those that a mesh axis runs over, the one named last changes fastest.
Arguments:
- tokens: bfloat16 [12288, 2048], P(('ctx', 'exp')), may hold values from -6 to 6
- cotangent: bfloat16 [12288, 2048], P(('ctx', 'exp')), may hold values from -6 to 6
- routes: int32 [12288, 8], P(('ctx', 'exp')), may hold values from 0 to 15, all different within a row; in each aligned block of 384 rows (0 to 383, 384 to 767, ...) at most 240 rows name the same one
- block_of_slot: int32 [8, 8], P('exp'), may hold values from 0 to 7, as said below
- cont_seg: int32 [8, 512], P('exp'), may hold values from 0 to 1, never falling along the last dimension, each value on 1 to 384 neighbouring positions
- w_query: bfloat16 [2048, 2048], P(('ctx', 'exp')), may hold values from -0.125 to 0.125
- w_key: bfloat16 [2048, 2048], P(('ctx', 'exp')), may hold values from -0.125 to 0.125
- w_value: bfloat16 [2048, 2048], P(('ctx', 'exp')), may hold values from -0.125 to 0.125
- w_out: bfloat16 [2048, 2048], P(('ctx', 'exp')), may hold values from -0.75 to 0.75
- w_router: bfloat16 [2048, 16], P(('ctx', 'exp')), may hold values from -0.0625 to 0.0625
- attn_gain: bfloat16 [2048], P(('ctx', 'exp')), may hold values from 0.099609375 to 1.8984375
- query_gain: bfloat16 [2048], P(('ctx', 'exp')), may hold values from 0.099609375 to 1.8984375
- key_gain: bfloat16 [2048], P(('ctx', 'exp')), may hold values from 0.099609375 to 1.8984375
- ffn_gain: bfloat16 [2048], P(('ctx', 'exp')), may hold values from 0.099609375 to 1.8984375
- w_gate: bfloat16 [16, 2048, 1024], P('exp', 'ctx'), may hold values from -0.125 to 0.125
- w_up: bfloat16 [16, 2048, 1024], P('exp', 'ctx'), may hold values from -0.125 to 0.125
- w_down: bfloat16 [16, 1024, 2048], P('exp', 'ctx'), may hold values from -3 to 3
Outputs:
- activations: bfloat16 [12288, 2048], P(('ctx', 'exp'))
- input_grad: float32 [12288, 2048], P(('ctx', 'exp'))
- query_grad: float32 [2048, 2048], P(('ctx', 'exp'))
- key_grad: float32 [2048, 2048], P(('ctx', 'exp'))
- value_grad: float32 [2048, 2048], P(('ctx', 'exp'))
- out_grad: float32 [2048, 2048], P(('ctx', 'exp'))
- router_grad: float32 [2048, 16], P(('ctx', 'exp'))
- attn_gain_grad: float32 [2048], P(('ctx', 'exp'))
- query_gain_grad: float32 [2048], P(('ctx', 'exp'))
- key_gain_grad: float32 [2048], P(('ctx', 'exp'))
- ffn_gain_grad: float32 [2048], P(('ctx', 'exp'))
- gate_grad: float32 [16, 2048, 1024], P('exp', 'ctx')
- up_grad: float32 [16, 2048, 1024], P('exp', 'ctx')
- down_grad: float32 [16, 1024, 2048], P('exp', 'ctx')
Inputs may be any that keep to these rules, and one draw needn't show every extreme that they name: `block_of_slot`: each row is a permutation of the group's 8 blocks, and slots 2c and 2c + 1 hold blocks b and 7 - b for some b. `cont_seg`: numbers never fall along a row; every continuation has 128 to 384 positions. `routes`: A row names 8 different experts; in the rows of one device no expert is named more than 240 times, a bound that some block reaches.
All inputs are finite; a program needn't handle non-finite values.
Results may differ from a plain program's by a relative error of at most 0.019.
Values may be sent and summed in bfloat16 or wider, within the bound.
No kernel may reach another device: no remote copies, remote signals or barrier semaphores. Data moves between devices by JAX's collectives and lax.ppermute only.
A program may use at most 512 MiB of HBM per device.

v0:
```python
import math

import jax
import jax.numpy as jnp
from jax import lax
from jax.sharding import PartitionSpec as P

D = 2048
HEADS = 16
HD = 128
TOP = 8
PROMPT = 1024
CONT = 2
CTOK = 512


epsilon = 1e-05
rope_base = 10000.0


def inverse_root(values):
    return lax.rsqrt(jnp.mean(values * values, axis=-1, keepdims=True) + epsilon)


def norm_back(gradient, normed, root_part):
    return root_part * (gradient - normed * jnp.mean(gradient * normed, axis=-1, keepdims=True))


def angles(position):
    half_dim = HD // 2
    inverse = rope_base ** (-2.0 * jnp.arange(half_dim, dtype=jnp.float32) / HD)
    phases = position.astype(jnp.float32)[:, None] * inverse[None, :]
    return (jnp.cos(phases)[:, None, :], jnp.sin(phases)[:, None, :])


def rotate(values, cos_part, sin_part):
    half_dim = HD // 2
    former = values[..., :half_dim]
    latter = values[..., half_dim:]
    return jnp.concatenate(
        [former * cos_part - latter * sin_part, latter * cos_part + former * sin_part], axis=-1
    )


def rotate_back(gradient, cos_part, sin_part):
    half_dim = HD // 2
    former = gradient[..., :half_dim]
    latter = gradient[..., half_dim:]
    return jnp.concatenate(
        [former * cos_part + latter * sin_part, latter * cos_part - former * sin_part], axis=-1
    )


def token_meta(place, seg_row):
    in_cont = place >= PROMPT
    cont_index = jnp.clip(place - PROMPT, 0, CTOK - 1)
    seg_ids = jnp.where(in_cont, jnp.take(seg_row, cont_index), -1)
    starts = jnp.sum(
        (seg_row[None, :] < jnp.arange(CONT, dtype=jnp.int32)[:, None]).astype(jnp.int32), axis=1
    )
    first_pos = jnp.take(starts, jnp.clip(seg_ids, 0, CONT - 1))
    position = jnp.where(in_cont, PROMPT + cont_index - first_pos, place)
    return (seg_ids, position)


def visible(query_place, query_seg, key_place, key_seg):
    causal = key_place[None, :] <= query_place[:, None]
    shared = (key_seg[None, :] < 0) | (key_seg[None, :] == query_seg[:, None])
    return causal & shared


def local(
    tokens,
    cotangent,
    routes,
    block_of_slot,
    cont_seg,
    w_query,
    w_key,
    w_value,
    w_out,
    w_router,
    attn_gain,
    query_gain,
    key_gain,
    ffn_gain,
    w_gate,
    w_up,
    w_down,
):
    tok_rows = tokens.shape[0]
    block_rows = tok_rows // 2
    slot_table = block_of_slot[0]
    seg_row = cont_seg[0]
    group_rows = slot_table.shape[0] * block_rows
    ctx_index = lax.axis_index("ctx")
    local_ids = jnp.arange(tok_rows, dtype=jnp.int32)
    own_place = (
        jnp.take(slot_table, 2 * ctx_index + local_ids // block_rows) * block_rows
        + local_ids % block_rows
    )
    every_ids = jnp.arange(group_rows, dtype=jnp.int32)
    all_place = jnp.take(slot_table, every_ids // block_rows) * block_rows + every_ids % block_rows
    own_seg, own_pos = token_meta(own_place, seg_row)
    all_seg, unused_pos = token_meta(all_place, seg_row)
    allowed = visible(own_place, own_seg, all_place, all_seg)
    cos_part, sin_part = angles(own_pos)
    factor = 1.0 / math.sqrt(HD)
    gathered = (
        lax.all_gather(w_query, ("ctx", "exp"), axis=0, tiled=True),
        lax.all_gather(w_key, ("ctx", "exp"), axis=0, tiled=True),
        lax.all_gather(w_value, ("ctx", "exp"), axis=0, tiled=True),
        lax.all_gather(w_out, ("ctx", "exp"), axis=0, tiled=True),
        lax.all_gather(w_router, ("ctx", "exp"), axis=0, tiled=True),
        lax.all_gather(attn_gain, ("ctx", "exp"), axis=0, tiled=True),
        lax.all_gather(query_gain, ("ctx", "exp"), axis=0, tiled=True),
        lax.all_gather(key_gain, ("ctx", "exp"), axis=0, tiled=True),
        lax.all_gather(ffn_gain, ("ctx", "exp"), axis=0, tiled=True),
    )
    query_full, key_full, value_full, out_full, router_full = (
        gathered[0],
        gathered[1],
        gathered[2],
        gathered[3],
        gathered[4],
    )
    gain_attn = gathered[5].astype(jnp.float32)
    gain_query = gathered[6].astype(jnp.float32)
    gain_key = gathered[7].astype(jnp.float32)
    gain_ffn = gathered[8].astype(jnp.float32)
    gate_full, up_full, down_full = (
        lax.all_gather(w_gate, "ctx", axis=1, tiled=True),
        lax.all_gather(w_up, "ctx", axis=1, tiled=True),
        lax.all_gather(w_down, "ctx", axis=1, tiled=True),
    )
    inputs = tokens.astype(jnp.float32)
    root_one = inverse_root(inputs)
    normed_one = inputs * root_one
    hidden_one = (normed_one * gain_attn).astype(jnp.bfloat16)
    query_pre = jnp.dot(hidden_one, query_full, preferred_element_type=jnp.float32)
    key_pre = jnp.dot(hidden_one, key_full, preferred_element_type=jnp.float32)
    value_pre = jnp.dot(hidden_one, value_full, preferred_element_type=jnp.float32)
    root_query = inverse_root(query_pre)
    normed_query = query_pre * root_query
    root_key = inverse_root(key_pre)
    normed_key = key_pre * root_key
    query_rot = rotate(
        (normed_query * gain_query).reshape(tok_rows, HEADS, HD), cos_part, sin_part
    ).astype(jnp.bfloat16)
    key_rot = rotate(
        (normed_key * gain_key).reshape(tok_rows, HEADS, HD), cos_part, sin_part
    ).astype(jnp.bfloat16)
    value_low = value_pre.astype(jnp.bfloat16).reshape(tok_rows, HEADS, HD)
    keys_all, values_all = (
        lax.all_gather(key_rot, "ctx", axis=0, tiled=True),
        lax.all_gather(value_low, "ctx", axis=0, tiled=True),
    )

    def masked_scores(keys_given):
        raw_scores = (
            jnp.einsum("qhd,khd->hqk", query_rot, keys_given, preferred_element_type=jnp.float32)
            * factor
        )
        return jnp.where(allowed[None], raw_scores, -1e30)

    masked = masked_scores(keys_all)
    row_max = jnp.max(masked, axis=-1, keepdims=True)
    exponent = jnp.exp(masked - row_max)
    row_total = jnp.sum(exponent, axis=-1, keepdims=True)
    weights = exponent / row_total
    log_total = row_max + jnp.log(row_total)
    context = jnp.einsum(
        "hqk,khd->qhd", weights.astype(jnp.bfloat16), values_all, preferred_element_type=jnp.float32
    )
    context_low = context.reshape(tok_rows, D).astype(jnp.bfloat16)
    middle = inputs + jnp.dot(context_low, out_full, preferred_element_type=jnp.float32)
    root_two = inverse_root(middle)
    normed_two = middle * root_two
    hidden_two = (normed_two * gain_ffn).astype(jnp.bfloat16)
    logits = jnp.dot(hidden_two, router_full, preferred_element_type=jnp.float32)
    router_prob = jax.nn.softmax(logits, axis=-1)
    expert_count = logits.shape[1]
    member = routes[:, :, None] == jnp.arange(expert_count, dtype=jnp.int32)[None, None, :]
    gate_share = jnp.sum(jnp.where(member, router_prob[:, None, :], 0.0), axis=-1)
    flat_routes = routes.reshape(-1)
    route_hits = (
        flat_routes[:, None] == jnp.arange(expert_count, dtype=jnp.int32)[None, :]
    ).astype(jnp.int32)
    slot_index = jnp.sum((jnp.cumsum(route_hits, axis=0) - route_hits) * route_hits, axis=1)
    capacity = 8 * ((5 * tok_rows * TOP // (4 * expert_count) + 7) // 8)
    dest_row = flat_routes * capacity + slot_index
    route_count = tok_rows * TOP
    source_row = (
        jnp.full((expert_count * capacity,), route_count, jnp.int32)
        .at[dest_row]
        .set(jnp.arange(route_count, dtype=jnp.int32))
    )
    padded_two = jnp.concatenate([hidden_two, jnp.zeros((1, D), jnp.bfloat16)], axis=0)
    outgoing = padded_two[source_row // TOP].reshape(expert_count, capacity, D)
    arrived = lax.all_to_all(outgoing, "exp", split_axis=0, concat_axis=1, tiled=True)
    gate_pre = jnp.einsum("erd,edf->erf", arrived, gate_full, preferred_element_type=jnp.float32)
    up_pre = jnp.einsum("erd,edf->erf", arrived, up_full, preferred_element_type=jnp.float32)
    silu_gate = jax.nn.silu(gate_pre)
    hidden = (silu_gate * up_pre).astype(jnp.bfloat16)
    result = jnp.einsum(
        "erf,efd->erd", hidden, down_full, preferred_element_type=jnp.float32
    ).astype(jnp.bfloat16)
    returned = lax.all_to_all(result, "exp", split_axis=1, concat_axis=0, tiled=True)
    picked = (
        returned.reshape(expert_count * capacity, D)[dest_row]
        .reshape(tok_rows, TOP, D)
        .astype(jnp.float32)
    )
    mixture = jnp.einsum("tk,tkd->td", gate_share, picked)
    output = (middle + mixture).astype(jnp.bfloat16)
    upstream = cotangent.astype(jnp.float32)
    grad_share = jnp.einsum("td,tkd->tk", upstream, picked)
    grad_result = (
        (gate_share[:, :, None] * upstream[:, None, :]).astype(jnp.bfloat16).reshape(route_count, D)
    )
    grad_padded = jnp.concatenate([grad_result, jnp.zeros((1, D), jnp.bfloat16)], axis=0)
    grad_outgoing = grad_padded[source_row].reshape(expert_count, capacity, D)
    grad_arrived = lax.all_to_all(grad_outgoing, "exp", split_axis=0, concat_axis=1, tiled=True)
    grad_hidden = jnp.einsum(
        "erd,efd->erf", grad_arrived, down_full, preferred_element_type=jnp.float32
    )
    grad_down = jnp.einsum("erf,erd->efd", hidden, grad_arrived, preferred_element_type=jnp.float32)
    sigmoid_gate = jax.nn.sigmoid(gate_pre)
    grad_gate_pre = (
        grad_hidden * up_pre * (sigmoid_gate * (1.0 + gate_pre * (1.0 - sigmoid_gate)))
    ).astype(jnp.bfloat16)
    grad_up_pre = (grad_hidden * silu_gate).astype(jnp.bfloat16)
    grad_gate = jnp.einsum(
        "erd,erf->edf", arrived, grad_gate_pre, preferred_element_type=jnp.float32
    )
    grad_up = jnp.einsum("erd,erf->edf", arrived, grad_up_pre, preferred_element_type=jnp.float32)
    grad_rows = jnp.einsum(
        "erf,edf->erd", grad_gate_pre, gate_full, preferred_element_type=jnp.float32
    ) + jnp.einsum("erf,edf->erd", grad_up_pre, up_full, preferred_element_type=jnp.float32)
    grad_back = lax.all_to_all(grad_rows, "exp", split_axis=1, concat_axis=0, tiled=True)
    grad_two = jnp.sum(
        grad_back.reshape(expert_count * capacity, D)[dest_row].reshape(tok_rows, TOP, D), axis=1
    )
    grad_prob = jnp.sum(jnp.where(member, grad_share[:, :, None], 0.0), axis=1)
    grad_logits = (
        router_prob * (grad_prob - jnp.sum(router_prob * grad_prob, axis=-1, keepdims=True))
    ).astype(jnp.bfloat16)
    grad_router = jnp.einsum(
        "td,te->de", hidden_two, grad_logits, preferred_element_type=jnp.float32
    )
    grad_two = grad_two + jnp.einsum(
        "te,de->td", grad_logits, router_full, preferred_element_type=jnp.float32
    )
    grad_ffn_gain = jnp.sum(grad_two * normed_two, axis=0)
    grad_middle = upstream + norm_back(grad_two * gain_ffn, normed_two, root_two)
    grad_branch = grad_middle.astype(jnp.bfloat16)
    grad_context = (
        jnp.einsum("te,de->td", grad_branch, out_full, preferred_element_type=jnp.float32)
        .astype(jnp.bfloat16)
        .reshape(tok_rows, HEADS, HD)
    )
    keys_use, values_use = (keys_all, values_all)
    prob_again = jnp.exp(masked_scores(keys_use) - log_total)
    grad_weights = jnp.einsum(
        "qhd,khd->hqk", grad_context, values_use, preferred_element_type=jnp.float32
    )
    row_delta = jnp.sum(prob_again * grad_weights, axis=-1, keepdims=True)
    grad_scores = (prob_again * (grad_weights - row_delta)).astype(jnp.bfloat16)
    grad_query_rot = (
        jnp.einsum("hqk,khd->qhd", grad_scores, keys_use, preferred_element_type=jnp.float32)
        * factor
    )
    prob_low = prob_again.astype(jnp.bfloat16)
    key_term = (
        jnp.einsum("hqk,qhd->khd", grad_scores, query_rot, preferred_element_type=jnp.float32)
        * factor
    )
    value_term = jnp.einsum(
        "hqk,qhd->khd", prob_low, grad_context, preferred_element_type=jnp.float32
    )
    both_grads = lax.psum_scatter(
        jnp.concatenate(
            [
                key_term.reshape(tok_rows * lax.axis_size("ctx"), D),
                value_term.reshape(tok_rows * lax.axis_size("ctx"), D),
            ],
            axis=1,
        ),
        "ctx",
        scatter_dimension=0,
        tiled=True,
    )
    grad_key_flat = both_grads[:, :D]
    grad_value_flat = both_grads[:, D:]
    grad_key_norm = rotate_back(
        grad_key_flat.reshape(tok_rows, HEADS, HD), cos_part, sin_part
    ).reshape(tok_rows, D)
    grad_key_gain = jnp.sum(grad_key_norm * normed_key, axis=0)
    grad_key_pre = norm_back(grad_key_norm * gain_key, normed_key, root_key).astype(jnp.bfloat16)
    grad_query_norm = rotate_back(grad_query_rot, cos_part, sin_part).reshape(tok_rows, D)
    grad_query_gain = jnp.sum(grad_query_norm * normed_query, axis=0)
    grad_query_pre = norm_back(grad_query_norm * gain_query, normed_query, root_query).astype(
        jnp.bfloat16
    )
    grad_value_pre = grad_value_flat.astype(jnp.bfloat16)
    grad_one = jnp.einsum(
        "te,de->td", grad_query_pre, query_full, preferred_element_type=jnp.float32
    )
    grad_one = grad_one + jnp.einsum(
        "te,de->td", grad_key_pre, key_full, preferred_element_type=jnp.float32
    )
    grad_one = grad_one + jnp.einsum(
        "te,de->td", grad_value_pre, value_full, preferred_element_type=jnp.float32
    )
    grad_attn_gain = jnp.sum(grad_one * normed_one, axis=0)
    grad_input = grad_middle + norm_back(grad_one * gain_attn, normed_one, root_one)
    grad_query = jnp.einsum(
        "td,te->de", hidden_one, grad_query_pre, preferred_element_type=jnp.float32
    )
    grad_key = jnp.einsum("td,te->de", hidden_one, grad_key_pre, preferred_element_type=jnp.float32)
    grad_value = jnp.einsum(
        "td,te->de", hidden_one, grad_value_pre, preferred_element_type=jnp.float32
    )
    grad_output = jnp.einsum(
        "td,te->de", context_low, grad_branch, preferred_element_type=jnp.float32
    )
    small_terms = (
        grad_query,
        grad_key,
        grad_value,
        grad_output,
        grad_router,
        grad_attn_gain,
        grad_query_gain,
        grad_key_gain,
        grad_ffn_gain,
    )
    summed = (
        lax.psum_scatter(small_terms[0], ("ctx", "exp"), scatter_dimension=0, tiled=True),
        lax.psum_scatter(small_terms[1], ("ctx", "exp"), scatter_dimension=0, tiled=True),
        lax.psum_scatter(small_terms[2], ("ctx", "exp"), scatter_dimension=0, tiled=True),
        lax.psum_scatter(small_terms[3], ("ctx", "exp"), scatter_dimension=0, tiled=True),
        lax.psum_scatter(small_terms[4], ("ctx", "exp"), scatter_dimension=0, tiled=True),
        lax.psum_scatter(small_terms[5], ("ctx", "exp"), scatter_dimension=0, tiled=True),
        lax.psum_scatter(small_terms[6], ("ctx", "exp"), scatter_dimension=0, tiled=True),
        lax.psum_scatter(small_terms[7], ("ctx", "exp"), scatter_dimension=0, tiled=True),
        lax.psum_scatter(small_terms[8], ("ctx", "exp"), scatter_dimension=0, tiled=True),
    )
    projection_grads = (summed[0], summed[1], summed[2], summed[3])
    remaining = (summed[4], summed[5], summed[6], summed[7], summed[8])
    expert_sums = (
        lax.psum_scatter(
            grad_gate.astype(jnp.bfloat16), "ctx", scatter_dimension=1, tiled=True
        ).astype(jnp.float32),
        lax.psum_scatter(
            grad_up.astype(jnp.bfloat16), "ctx", scatter_dimension=1, tiled=True
        ).astype(jnp.float32),
        lax.psum_scatter(
            grad_down.astype(jnp.bfloat16), "ctx", scatter_dimension=1, tiled=True
        ).astype(jnp.float32),
    )
    return (
        output,
        grad_input,
        projection_grads[0],
        projection_grads[1],
        projection_grads[2],
        projection_grads[3],
        remaining[0],
        remaining[1],
        remaining[2],
        remaining[3],
        remaining[4],
        expert_sums[0],
        expert_sums[1],
        expert_sums[2],
    )


def solution(mesh):
    in_specs = (
        P(("ctx", "exp"), None),
        P(("ctx", "exp"), None),
        P(("ctx", "exp"), None),
        P("exp", None),
        P("exp", None),
        P(("ctx", "exp"), None),
        P(("ctx", "exp"), None),
        P(("ctx", "exp"), None),
        P(("ctx", "exp"), None),
        P(("ctx", "exp"), None),
        P(("ctx", "exp")),
        P(("ctx", "exp")),
        P(("ctx", "exp")),
        P(("ctx", "exp")),
        P("exp", "ctx", None),
        P("exp", "ctx", None),
        P("exp", "ctx", None),
    )
    out_specs = (
        P(("ctx", "exp"), None),
        P(("ctx", "exp"), None),
        P(("ctx", "exp"), None),
        P(("ctx", "exp"), None),
        P(("ctx", "exp"), None),
        P(("ctx", "exp"), None),
        P(("ctx", "exp"), None),
        P(("ctx", "exp")),
        P(("ctx", "exp")),
        P(("ctx", "exp")),
        P(("ctx", "exp")),
        P("exp", "ctx", None),
        P("exp", "ctx", None),
        P("exp", "ctx", None),
    )
    return jax.shard_map(local, mesh=mesh, in_specs=in_specs, out_specs=out_specs, check_vma=False)
```

profile of v0, /device:TPU:0, one launch (start us, length us, event | category | flops | bytes accessed | tf_op | source)
XLA Modules:
  0.0 4219.8 jit_solution(1194981778887134118)
XLA Ops:
  12.9 42.7 %all-reduce.11 = (bf16[2048]{0:T(1024)(128)(2,1)S(1)}, bf16[2048]{0:T(1024)(128)(2,1)S(1)}, bf16[2048]{0:T(1024)(128)(2,1)S(1)}, bf16[2048]{0:T(1024)(128)(2,1)}) all-reduce(bf16[2048]{0:T(1024)(128)(2,1)S(1)} %dynamic-update-slice, bf16[2048]{0:T(1024)(128)(2,1)S(1)} %dynamic-update-slice.2, ...), channel_id=1, replica_groups=mesh['ctx'=4,'exp'=8] {'ctx','exp'}, use_global_device_ids=true, to_apply=%add.2 | all-reduce | flops 8192 | bytes 32768
  70.7 21.0 all-gather.15.cloned.1.call-done
  101.7 68.9 %all-gather.17.cloned.1.call-done = bf16[2048,2048]{1,0:T(8,128)(2,1)} async-done(((bf16[64,2048]{1,0:T(8,128)(2,1)}), bf16[2048,2048]{1,0:T(8,128)(2,1)}) %all-gather.17.cloned.1.call-update) | async-done | bytes 8388624 | tf_op jit(solution)/shard_map/all_gather | solution.py:111
  181.2 9.2 fusion.87
  190.5 11.0 subtract_convert_fusion.1
  203.5 46.0 %all-gather.11.cloned.1.call-done = bf16[2048,2048]{1,0:T(8,128)(2,1)} async-done(((bf16[64,2048]{1,0:T(8,128)(2,1)}), bf16[2048,2048]{1,0:T(8,128)(2,1)}) %all-gather.11.cloned.1.call-update) | async-done | bytes 8388624 | tf_op jit(solution)/shard_map/all_gather | solution.py:112
  249.5 8.0 convolution_convert_fusion.5
  269.3 9.5 gather_fusion
  288.5 11.8 scatter_custom_fusion
  303.2 17.5 all-gather.19.cloned.1.call-done
  320.7 20.6 fusion.91
  341.2 16.5 fusion
  357.8 35.1 all-gather.13.cloned.1.call-done
  392.9 16.4 fusion.27
  409.3 63.8 %all-gather.21.cloned.1.call-done = bf16[2048,2048]{1,0:T(8,128)(2,1)} async-done(((bf16[64,2048]{1,0:T(8,128)(2,1)}), bf16[2048,2048]{1,0:T(8,128)(2,1)}) %all-gather.21.cloned.1.call-update) | async-done | bytes 8388624 | tf_op jit(solution)/shard_map/all_gather | solution.py:113
  481.7 15.5 gather_fusion.2
  504.3 339.7 %all-to-all-done = bf16[16,240,2048]{2,1,0:T(8,128)(2,1)} async-done(((bf16[16,240,2048]{2,1,0:T(8,128)(2,1)}), bf16[16,240,2048]{2,1,0:T(8,128)(2,1)}, u32[]{:S(2)}, u32[]{:S(2)}) %all-to-all-start) | async-done | bytes 15728672 | tf_op jit(solution)/shard_map/all_to_all | solution.py:200
  844.0 13.6 copy.118
  857.6 23.4 fusion.93
  881.0 28.0 multiply_convert_fusion.3
  909.0 21.2 convolution_convert_fusion
  930.3 45.9 %copy.119 = bf16[2,1920,2048]{2,0,1:T(2,128)(2,1)} copy(bf16[2,1920,2048]{2,1,0:T(8,128)(2,1)S(1)} %convolution_convert_fusion) | data formatting | bytes 31457280 | tf_op jit(solution)/shard_map/convert_element_type | solution.py:207
  982.0 370.8 %all-gather = bf16[32,64,16]{1,2,0:T(8,128)(2,1)S(1)} all-gather(bf16[1,64,16]{1,2,0:T(8,128)(2,1)S(1)} %bitcast.201), channel_id=1, replica_groups=mesh['ctx'=4,'exp'=8] {'ctx','exp'}, dimensions={0}, use_global_device_ids=true | all-gather | bytes 67584 | tf_op jit(solution)/shard_map/all_gather | solution.py:114
  1356.2 16.8 copy.120
  1373.0 31.3 gather_fusion.3
  1404.4 9.8 fusion.8
  1423.5 35.7 gather_fusion.4
  1459.2 346.4 %all_to_all.66 = bf16[16,240,2048]{2,1,0:T(8,128)(2,1)S(1)} all-to-all(bf16[16,240,2048]{2,1,0:T(8,128)(2,1)} %bitcast.173), channel_id=1, replica_groups=mesh['ctx'=4,'exp'=8] {'exp'}, dimensions={0} | all-to-all | bytes 31457280 | tf_op jit(solution)/shard_map/all_to_all | solution.py:223
  1805.7 6.3 copy.122
  1812.0 31.1 multiply_convert_fusion.1
  1843.0 25.0 fusion.94
  1868.0 32.0 convolution_add_fusion
  1900.0 51.8 %copy.123 = f32[2,1920,2048]{2,0,1:T(2,128)} copy(f32[2,1920,2048]{2,1,0:T(8,128)} %convolution_add_fusion) | data formatting | bytes 62914560 | tf_op jit(solution)/shard_map/add | solution.py:237
  1951.8 7.1 all-to-all-start.3
  1959.3 6.4 fusion.10
  1965.7 671.4 %all-to-all-done.3 = f32[2,1920,2048]{2,0,1:T(2,128)} async-done(((f32[2,1920,2048]{2,0,1:T(2,128)}), f32[2,1920,2048]{2,0,1:T(2,128)}, u32[]{:S(2)}, u32[]{:S(2)}) %all-to-all-start.3) | async-done | bytes 31457312 | tf_op jit(solution)/shard_map/all_to_all | solution.py:240
  2637.2 30.1 copy.124
  2667.3 34.0 gather_fusion.5
  2701.3 12.0 bitcast_reduce_fusion
  2725.1 19.9 fusion.3
  2745.0 29.9 multiply_reduce_fusion
  2774.9 32.0 multiply_convert_fusion
  2806.9 14.6 broadcast_multiply_fusion
  2821.5 17.1 pad_maximum_fusion
  2841.8 25.0 convolution_convert_fusion.1
  2866.9 24.4 convolution_convert_fusion.2
  2891.4 24.3 convolution_convert_fusion.3
  2917.6 10.1 fusion.28
  2927.8 130.7 %reduce-scatter.12.cloned.1.call-done = f32[384,4096]{0,1:T(8,128)} async-done(((f32[1536,4096]{0,1:T(8,128)}), f32[384,4096]{0,1:T(8,128)}) %reduce-scatter.12.cloned.1.call-update) | async-done | bytes 6291472 | tf_op jit(solution)/shard_map/reduce_scatter | solution.py:281
  3058.5 10.7 fusion.31
  3069.3 12.0 multiply_bitcast_fusion
  3090.1 7.6 multiply_add_fusion
  3100.8 8.3 fusion.77
  3119.1 8.4 fusion.75
  3127.5 68.2 %reduce-scatter.28.cloned.1.call-done = f32[64,16]{1,0:T(8,128)} async-done(((f32[2048,16]{1,0:T(8,128)}), f32[64,16]{1,0:T(8,128)}) %reduce-scatter.28.cloned.1.call-update) | async-done | bytes 4112
  3197.1 84.3 %reduce-scatter.26.cloned.1.call-done = bf16[2,256,2048]{2,1,0:T(8,128)(2,1)} async-done(((bf16[2,1024,2048]{2,1,0:T(8,128)(2,1)}), bf16[2,256,2048]{2,1,0:T(8,128)(2,1)}) %reduce-scatter.26.cloned.1.call-update) | async-done | bytes 2097168 | tf_op jit(solution)/shard_map/reduce_scatter | solution.py:358
  3285.6 85.7 %reduce-scatter.24.cloned.1.call-done = bf16[2,512,1024]{2,1,0:T(8,128)(2,1)} async-done(((bf16[2,2048,1024]{2,1,0:T(8,128)(2,1)}), bf16[2,512,1024]{2,1,0:T(8,128)(2,1)}) %reduce-scatter.24.cloned.1.call-update) | async-done | bytes 2097168 | tf_op jit(solution)/shard_map/reduce_scatter | solution.py:355
  3375.3 85.3 %reduce-scatter.22.cloned.1.call-done = bf16[2,512,1024]{2,1,0:T(8,128)(2,1)} async-done(((bf16[2,2048,1024]{2,1,0:T(8,128)(2,1)}), bf16[2,512,1024]{2,1,0:T(8,128)(2,1)}) %reduce-scatter.22.cloned.1.call-update) | async-done | bytes 2097168 | tf_op jit(solution)/shard_map/reduce_scatter | solution.py:352
  3475.9 10.2 fusion.21
  3486.1 42.4 %all-reduce.10 = (f32[2048]{0:T(1024)S(1)}, f32[2048]{0:T(1024)S(1)}, f32[2048]{0:T(1024)S(1)}, f32[2048]{0:T(1024)S(1)}) all-reduce(f32[2048]{0:T(1024)S(1)} %get-tuple-element.20, f32[2048]{0:T(1024)S(1)} %get-tuple-element.18, f32[2048]{0:T(1024)S(1)} %get-tuple-element.16, ...), channel_id=8, replica_groups=mesh['ctx'=4,'exp'=8] {'ctx','exp'}, use_global_device_ids=true, to_apply=%region_29.30.clone | all-reduce | flops 8192 | bytes 65536
  3536.2 114.8 %reduce-scatter.20.cloned.1.call-done = f32[64,2048]{1,0:T(8,128)} async-done(((f32[2048,2048]{1,0:T(8,128)}), f32[64,2048]{1,0:T(8,128)}) %reduce-scatter.20.cloned.1.call-update) | async-done | bytes 524304 | tf_op jit(solution)/shard_map/reduce_scatter | solution.py:342
  3651.1 187.3 %reduce-scatter.18.cloned.1.call-done = f32[64,2048]{1,0:T(8,128)} async-done(((f32[2048,2048]{1,0:T(8,128)}), f32[64,2048]{1,0:T(8,128)}) %reduce-scatter.18.cloned.1.call-update) | async-done | bytes 524304 | tf_op jit(solution)/shard_map/reduce_scatter | solution.py:341
  3838.3 187.2 %reduce-scatter.14.cloned.1.call-done = f32[64,2048]{1,0:T(8,128)} async-done(((f32[2048,2048]{1,0:T(8,128)}), f32[64,2048]{1,0:T(8,128)}) %reduce-scatter.14.cloned.1.call-update) | async-done | bytes 524304 | tf_op jit(solution)/shard_map/reduce_scatter | solution.py:339
  4025.6 187.2 %reduce-scatter.16.cloned.1.call-done = f32[64,2048]{1,0:T(8,128)} async-done(((f32[2048,2048]{1,0:T(8,128)}), f32[64,2048]{1,0:T(8,128)}) %reduce-scatter.16.cloned.1.call-update) | async-done | bytes 524304 | tf_op jit(solution)/shard_map/reduce_scatter | solution.py:340
  (314 shorter events, 173.6 us)
Async XLA Ops:
  7.2 61.7 %copy-start.1 = (bf16[384,2048]{1,0:T(8,128)(2,1)S(1)}, bf16[384,2048]{1,0:T(8,128)(2,1)}, u32[]{:S(2)}) copy-start(bf16[384,2048]{1,0:T(8,128)(2,1)} %param.17) | copy-start | bytes 4718596
  7.2 84.4 %all-gather.15.cloned.1.call-start = ((), (), s32[]{:S(2)}) async-start(), calls=%async_computation.15 | async-start | bytes 8650752 | tf_op jit(solution)/shard_map/all_gather | solution.py:110
  7.9 162.7 %all-gather.17.cloned.1.call-start = ((), (), s32[]{:S(2)}) async-start(), calls=%async_computation.16 | async-start | bytes 8650752 | tf_op jit(solution)/shard_map/all_gather | solution.py:111
  8.7 240.8 %all-gather.11.cloned.1.call-start = ((), (), s32[]{:S(2)}) async-start(), calls=%async_computation.13 | async-start | bytes 8650752 | tf_op jit(solution)/shard_map/all_gather | solution.py:112
  9.4 311.2 %all-gather.19.cloned.1.call-start = ((), (), s32[]{:S(2)}) async-start(), calls=%async_computation.17 | async-start | bytes 7864320 | tf_op jit(solution)/shard_map/all_gather | solution.py:155
  55.6 193.9 %copy-start.30 = (f32[2048]{0:T(1024)}, f32[2048]{0:T(1024)S(1)}, u32[]{:S(2)}) copy-start(f32[2048]{0:T(1024)S(1)} %convert_element_type.119) | copy-start | bytes 24580
  55.6 121.2 %copy-start.43 = (f32[2048]{0:T(1024)}, f32[2048]{0:T(1024)S(1)}, u32[]{:S(2)}) copy-start(f32[2048]{0:T(1024)S(1)} %convert_element_type.125) | copy-start | bytes 24580
  55.6 42.2 copy-start.45
  69.3 180.3 %copy-start.39 = (f32[384]{0:T(512)}, f32[384]{0:T(512)S(1)}, u32[]{:S(2)}) copy-start(f32[384]{0:T(512)S(1)} %add_rsqrt_fusion.3) | copy-start | bytes 4612
  70.6 119.8 %copy-start.26 = (f32[384,64]{1,0:T(8,128)}, f32[384,64]{1,0:T(8,128)S(1)}, u32[]{:S(2)}) copy-start(f32[384,64]{1,0:T(8,128)S(1)} %get-tuple-element.61) | copy-start | bytes 294916
  70.6 119.8 %copy-start.28 = (f32[384,64]{1,0:T(8,128)}, f32[384,64]{1,0:T(8,128)S(1)}, u32[]{:S(2)}) copy-start(f32[384,64]{1,0:T(8,128)S(1)} %get-tuple-element.62) | copy-start | bytes 294916
  201.4 119.2 %copy-start.17 = (bf16[384,16,64]{2,0,1:T(8,128)(2,1)}, bf16[384,16,64]{2,0,1:T(8,128)(2,1)S(1)}, u32[]{:S(2)}) copy-start(bf16[384,16,64]{2,0,1:T(8,128)(2,1)S(1)} %get-tuple-element.41) | copy-start | bytes 2359300
  203.5 189.4 %all-gather.13.cloned.1.call-start = ((), (), s32[]{:S(2)}) async-start(), calls=%async_computation.14 | async-start | bytes 7864320 | tf_op jit(solution)/shard_map/all_gather | solution.py:156
  257.5 8.8 copy-start.51
  257.5 10.5 copy-start.69
  257.5 11.0 copy-start.72
  257.5 11.8 copy-start
  260.4 212.6 %all-gather.21.cloned.1.call-start = ((), (), s32[]{:S(2)}) async-start(), calls=%async_computation.18 | async-start | bytes 8650752 | tf_op jit(solution)/shard_map/all_gather | solution.py:113
  261.0 596.6 %all-gather.23.cloned.1.call-start = ((), (), s32[]{:S(2)}) async-start(), calls=%async_computation.19 | async-start | bytes 10485760 | tf_op jit(solution)/shard_map/all_gather | solution.py:132
  268.6 210.7 %copy-start.41 = (f32[2048]{0:T(1024)}, f32[2048]{0:T(1024)S(1)}, u32[]{:S(2)}) copy-start(f32[2048]{0:T(1024)S(1)} %convert_element_type.130) | copy-start | bytes 24580
  269.3 31.6 copy-start.70
  341.2 51.6 %copy-start.36 = (f32[16,384]{1,0:T(8,128)}, f32[16,384]{1,0:T(8,128)S(1)}, u32[]{:S(2)}) copy-start(f32[16,384]{1,0:T(8,128)S(1)} %get-tuple-element.77) | copy-start | bytes 73732
  357.8 51.5 %copy-start.53 = (f32[16,384]{1,0:T(8,128)}, f32[16,384]{1,0:T(8,128)S(1)}, u32[]{:S(2)}) copy-start(f32[16,384]{1,0:T(8,128)S(1)} %fusion) | copy-start | bytes 73732
  409.3 69.9 %copy-start.21 = (bf16[16,128,384]{2,1,0:T(8,128)(2,1)}, bf16[16,128,384]{2,1,0:T(8,128)(2,1)S(1)}, u32[]{:S(2)}) copy-start(bf16[16,128,384]{2,1,0:T(8,128)(2,1)S(1)} %fusion.27) | copy-start | bytes 4718596
  497.2 346.8 %all-to-all-start = ((bf16[16,240,2048]{2,1,0:T(8,128)(2,1)}), bf16[16,240,2048]{2,1,0:T(8,128)(2,1)}, u32[]{:S(2)}, u32[]{:S(2)}) async-start(bf16[16,240,2048]{2,1,0:T(8,128)(2,1)} %bitcast.172), calls=%async_computation | async-start | bytes 31457280 | tf_op jit(solution)/shard_map/all_to_all | solution.py:200
  502.8 378.2 %all-gather.25.cloned.1.call-start = ((), (), s32[]{:S(2)}) async-start(), calls=%async_computation.20 | async-start | bytes 10485760 | tf_op jit(solution)/shard_map/all_gather | solution.py:133
  503.6 405.5 %all-gather.27.cloned.1.call-start = ((), (), s32[]{:S(2)}) async-start(), calls=%async_computation.21 | async-start | bytes 10485760 | tf_op jit(solution)/shard_map/all_gather | solution.py:134
  976.2 376.8 %copy-start.24 = (bf16[384,2048]{1,0:T(8,128)(2,1)S(1)}, bf16[384,2048]{1,0:T(8,128)(2,1)}, u32[]{:S(2)}) copy-start(bf16[384,2048]{1,0:T(8,128)(2,1)} %param.18) | copy-start | bytes 4718596
  976.2 380.1 %all-to-all-start.1 = ((bf16[2,1920,2048]{2,0,1:T(2,128)(2,1)}), bf16[2,1920,2048]{2,0,1:T(2,128)(2,1)}, u32[]{:S(2)}, u32[]{:S(2)}) async-start(bf16[2,1920,2048]{2,0,1:T(2,128)(2,1)} %copy.119), calls=%async_computation.1 | async-start | bytes 31457280 | tf_op jit(solution)/shard_map/all_to_all | solution.py:208
  981.9 373.1 %copy-start.59 = (s32[3072,1]{0,1:T(1,128)S(1)}, s32[3072,1]{0,1:T(1,128)}, u32[]{:S(2)}) copy-start(s32[3072,1]{0,1:T(1,128)} %copy-done.58) | copy-start | bytes 36868
  981.9 373.1 %copy-start.15 = (bf16[384,2048]{1,0:T(8,128)(2,1)S(1)}, bf16[384,2048]{1,0:T(8,128)(2,1)}, u32[]{:S(2)}) copy-start(bf16[384,2048]{1,0:T(8,128)(2,1)} %copy-done.14) | copy-start | bytes 4718596
  1355.0 18.0 copy-start.47
  1355.6 17.4 copy-start.56
  1356.2 16.8 copy-start.67
  1404.4 9.8 copy-start.52
  1404.4 10.8 copy-start.20
  1951.8 7.5 copy-start.33
  1951.8 7.5 copy-start.38
  1951.8 685.4 %all-to-all-start.3 = ((f32[2,1920,2048]{2,0,1:T(2,128)}), f32[2,1920,2048]{2,0,1:T(2,128)}, u32[]{:S(2)}, u32[]{:S(2)}) async-start(f32[2,1920,2048]{2,0,1:T(2,128)} %copy.123), calls=%async_computation.3 | async-start | bytes 62914560 | tf_op jit(solution)/shard_map/all_to_all | solution.py:240
  1958.9 1099.6 %reduce-scatter.12.cloned.1.call-start = ((), (), s32[]{:S(2)}) async-start(), calls=%async_computation.22 | async-start | bytes 31457280 | tf_op jit(solution)/shard_map/reduce_scatter | solution.py:281
  2637.2 30.1 copy-start.48
  2701.3 12.0 copy-start.4
  2701.3 12.1 copy-start.35
  2701.3 12.1 copy-start.42
  2701.3 12.1 copy-start.65
  2774.9 32.0 copy-start.18
  2774.9 32.0 copy-start.19
  2838.6 357.1 %reduce-scatter.28.cloned.1.call-start = ((), (), s32[]{:S(2)}) async-start(), calls=%async_computation.30 | async-start | bytes 1081344
  2841.8 439.7 %reduce-scatter.26.cloned.1.call-start = ((), (), s32[]{:S(2)}) async-start(), calls=%async_computation.29 | async-start | bytes 10485760 | tf_op jit(solution)/shard_map/reduce_scatter | solution.py:358
  2866.8 504.4 %reduce-scatter.24.cloned.1.call-start = ((), (), s32[]{:S(2)}) async-start(), calls=%async_computation.28 | async-start | bytes 10485760 | tf_op jit(solution)/shard_map/reduce_scatter | solution.py:355
  2891.3 569.2 %reduce-scatter.22.cloned.1.call-start = ((), (), s32[]{:S(2)}) async-start(), calls=%async_computation.27 | async-start | bytes 10485760 | tf_op jit(solution)/shard_map/reduce_scatter | solution.py:352
  2915.8 735.3 %reduce-scatter.20.cloned.1.call-start = ((), (), s32[]{:S(2)}) async-start(), calls=%async_computation.26 | async-start | bytes 17301504 | tf_op jit(solution)/shard_map/reduce_scatter | solution.py:342
  2927.7 130.8 %copy-start.2 = (bf16[384,2048]{1,0:T(8,128)(2,1)S(1)}, bf16[384,2048]{1,0:T(8,128)(2,1)}, u32[]{:S(2)}) copy-start(bf16[384,2048]{1,0:T(8,128)(2,1)} %param.17) | copy-start | bytes 4718596
  2927.7 130.8 %copy-start.31 = (f32[2048]{0:T(1024)S(1)}, f32[2048]{0:T(1024)}, u32[]{:S(2)}) copy-start(f32[2048]{0:T(1024)} %copy-done.30) | copy-start | bytes 24580
  2927.7 130.8 %copy-start.40 = (f32[384]{0:T(512)S(1)}, f32[384]{0:T(512)}, u32[]{:S(2)}) copy-start(f32[384]{0:T(512)} %copy-done.39) | copy-start | bytes 4612
  2927.8 910.6 %reduce-scatter.18.cloned.1.call-start = ((), (), s32[]{:S(2)}) async-start(), calls=%async_computation.25 | async-start | bytes 17301504 | tf_op jit(solution)/shard_map/reduce_scatter | solution.py:341
  3069.3 956.3 %reduce-scatter.14.cloned.1.call-start = ((), (), s32[]{:S(2)}) async-start(), calls=%async_computation.23 | async-start | bytes 17301504 | tf_op jit(solution)/shard_map/reduce_scatter | solution.py:339
  3090.1 7.6 copy-start.10
  3090.1 7.6 copy-start.46
  3090.1 7.6 copy-start.63
  3109.1 1103.7 %reduce-scatter.16.cloned.1.call-start = ((), (), s32[]{:S(2)}) async-start(), calls=%async_computation.24 | async-start | bytes 17301504 | tf_op jit(solution)/shard_map/reduce_scatter | solution.py:340
  3460.6 10.3 slice-start.5
  3464.8 11.1 slice-start
  3475.9 10.2 copy-start.66
  (37 other events, 132.3 us)
Sparse Core Ops, SparseCore 0:
  11.0 80.5 all-gather.14
  94.6 75.9 all-gather.16
  173.6 75.8 all-gather.10
  251.8 68.8 all-gather.18
  322.9 69.9 all-gather.12
  395.7 77.3 all-gather.20
  474.9 86.1 all-gather.22
  563.0 87.5 all-gather.24
  652.5 87.5 all-gather.26
  2838.7 219.6 reduce-scatter.11
  3060.8 134.8 reduce-scatter.27
  3198.6 82.7 reduce-scatter.25
  3284.8 86.3 reduce-scatter.23
  3374.1 86.3 reduce-scatter.21
  3463.4 187.6 reduce-scatter.19
  3653.9 184.3 reduce-scatter.17
  3841.2 184.3 reduce-scatter.13
  4028.4 184.3 reduce-scatter.15
where the time goes:
time: 4230 us; the launch traced here: 4220 us
  waiting for transfers between devices  2400 us (57%)
  blocking collectives  802 us (19%)
  matrix products  456 us (11%)
  local copies, waits for them, and re-layouts  365 us (9%)
  other arithmetic  162 us (4%)
    all_to_all x1, waiting for transfers between devices, local(): lax.all_to_all(grad_rows, 'exp', split_axis=1, concat_axis=0, tiled=True)  671 us
    all_gather x1, blocking collectives, local(): lax.all_gather(w_router, ('ctx', 'exp'), axis=0, tiled=True)  371 us
    all_to_all x1, blocking collectives, local(): lax.all_to_all(grad_outgoing, 'exp', split_axis=0, concat_axis=1, tiled=T...  346 us
    all_to_all x1, waiting for transfers between devices, local(): lax.all_to_all(outgoing, 'exp', split_axis=0, concat_axis=1, tiled=True)  340 us
    reduce_scatter x1, waiting for transfers between devices, local(): lax.psum_scatter(small_terms[2], ('ctx', 'exp'), scatter_dimension=0, til...  187 us
    reduce_scatter x1, waiting for transfers between devices, local(): lax.psum_scatter(small_terms[0], ('ctx', 'exp'), scatter_dimension=0, til...  187 us
    reduce_scatter x1, waiting for transfers between devices, local(): lax.psum_scatter(small_terms[1], ('ctx', 'exp'), scatter_dimension=0, til...  187 us
    reduce_scatter x1, waiting for transfers between devices, local(): lax.psum_scatter(jnp.concatenate([key_term.reshape(tok_rows * lax.axis_si...  131 us
  transfers between devices with their start and end apart: 21, of which 17 were waited for; matrix products, arithmetic and copies ran while one was open for 11% of the time, Pallas kernels for 0%

commit v1 on v0

v1 whole, which is shorter than its diff:
```python
import math

import jax
import jax.numpy as jnp
from jax import lax
from jax.sharding import PartitionSpec as P

D = 2048
HEADS = 16
HD = 128
TOP = 8
PROMPT = 1024
CONT = 2
CTOK = 512

epsilon = 1e-05
rope_base = 10000.0
BF = jnp.bfloat16
F32 = jnp.float32
BOTH = ("ctx", "exp")
X_PAIRS = [(i, i ^ 1) for i in range(4)]
Y_PAIRS = [(i, i ^ 2) for i in range(4)]


def inverse_root(values):
    return lax.rsqrt(jnp.mean(values * values, axis=-1, keepdims=True) + epsilon)


def norm_back(gradient, normed, root_part):
    return root_part * (gradient - normed * jnp.mean(gradient * normed, axis=-1, keepdims=True))


def angles(position):
    half_dim = HD // 2
    inverse = rope_base ** (-2.0 * jnp.arange(half_dim, dtype=F32) / HD)
    phases = position.astype(F32)[:, None] * inverse[None, :]
    return (jnp.cos(phases)[:, None, :], jnp.sin(phases)[:, None, :])


def rotate(values, cos_part, sin_part):
    half_dim = HD // 2
    former = values[..., :half_dim]
    latter = values[..., half_dim:]
    return jnp.concatenate(
        [former * cos_part - latter * sin_part, latter * cos_part + former * sin_part], axis=-1
    )


def rotate_back(gradient, cos_part, sin_part):
    half_dim = HD // 2
    former = gradient[..., :half_dim]
    latter = gradient[..., half_dim:]
    return jnp.concatenate(
        [former * cos_part + latter * sin_part, latter * cos_part - former * sin_part], axis=-1
    )


def send_x(value):
    return lax.ppermute(value, "ctx", X_PAIRS)


def send_y(value):
    return lax.ppermute(value, "ctx", Y_PAIRS)


def after(value, *others):
    return lax.optimization_barrier((value,) + others)[0]


def gather_pieces(value, half):
    from_x = send_x(value)
    from_y = send_y(value)
    far_low = send_y(from_x[:half])
    far_high = send_x(from_y[half:])
    return from_x, from_y, far_low, far_high


def scatter_sum(take, me):
    low = send_x(jnp.stack([take(me ^ 1, 0), take(me ^ 3, 0)]).astype(BF))
    high = send_y(jnp.stack([take(me ^ 2, 1), take(me ^ 3, 1)]).astype(BF))
    low_next = send_y((take(me ^ 2, 0).astype(F32) + low[1].astype(F32)).astype(BF))
    high_next = send_x((take(me ^ 1, 1).astype(F32) + high[1].astype(F32)).astype(BF))
    first = take(me, 0).astype(F32) + low[0].astype(F32) + low_next.astype(F32)
    second = take(me, 1).astype(F32) + high[0].astype(F32) + high_next.astype(F32)
    return first, second


def gather_rows(weight, me):
    if lax.axis_size("ctx") != 4:
        return lax.all_gather(weight, "ctx", axis=1, tiled=True), weight
    count, rows, columns = weight.shape
    from_x, from_y, far_low, far_high = gather_pieces(weight, count // 2)
    whole = jnp.zeros((count, 4 * rows, columns), weight.dtype)
    whole = lax.dynamic_update_slice(whole, weight, (0, me * rows, 0))
    whole = lax.dynamic_update_slice(whole, from_x, (0, (me ^ 1) * rows, 0))
    whole = lax.dynamic_update_slice(whole, from_y, (0, (me ^ 2) * rows, 0))
    whole = lax.dynamic_update_slice(whole, far_low, (0, (me ^ 3) * rows, 0))
    whole = lax.dynamic_update_slice(whole, far_high, (count // 2, (me ^ 3) * rows, 0))
    return whole, far_low


def scatter_rows(gradient, me):
    if lax.axis_size("ctx") != 4:
        return lax.psum_scatter(gradient, "ctx", scatter_dimension=1, tiled=True).astype(F32)
    count, rows, columns = gradient.shape
    rows, half = rows // 4, count // 2

    def take(owner, part):
        return lax.dynamic_slice(gradient, (part * half, owner * rows, 0), (half, rows, columns))

    return jnp.concatenate(scatter_sum(take, me), axis=0)


def pick_blocks(blocks, order):
    return jnp.concatenate(
        [
            lax.dynamic_index_in_dim(blocks, order[i], 0, keepdims=False)
            for i in range(order.shape[0])
        ],
        axis=0,
    )


def gather_group(rows, slot_table, me):
    block = rows.shape[0] // 2
    if lax.axis_size("ctx") != 4:
        blocks = slot_table.shape[0]
        whole = lax.all_gather(rows, "ctx", axis=0, tiled=True).reshape(blocks, block, -1)
        match = slot_table[None, :] == jnp.arange(blocks, dtype=jnp.int32)[:, None]
        order = jnp.sum(jnp.where(match, jnp.arange(blocks, dtype=jnp.int32)[None, :], 0), axis=1)
        return pick_blocks(whole, order), rows
    from_x, from_y, far_low, far_high = gather_pieces(rows, block)
    parts = (
        (rows[:block], me, 0),
        (rows[block:], me, 1),
        (from_x[:block], me ^ 1, 0),
        (from_x[block:], me ^ 1, 1),
        (from_y[:block], me ^ 2, 0),
        (from_y[block:], me ^ 2, 1),
        (far_low, me ^ 3, 0),
        (far_high, me ^ 3, 1),
    )
    whole = jnp.zeros((8 * block, rows.shape[1]), rows.dtype)
    for part, owner, slot in parts:
        start = slot_table[2 * owner + slot] * block
        whole = lax.dynamic_update_slice(whole, part, (start, 0))
    return whole, far_low


def scatter_group(partial, slot_table, me):
    blocks = slot_table.shape[0]
    block = partial.shape[0] // blocks
    if lax.axis_size("ctx") != 4:
        ordered = pick_blocks(partial.reshape(blocks, block, -1), slot_table)
        return lax.psum_scatter(
            ordered.astype(BF), "ctx", scatter_dimension=0, tiled=True
        ).astype(F32)

    def take(owner, part):
        start = slot_table[2 * owner + part] * block
        return lax.dynamic_slice(partial, (start, 0), (block, partial.shape[1]))

    return jnp.concatenate(scatter_sum(take, me), axis=0)


def prefix_count(member):
    rows, columns = member.shape
    width = 128
    blocks = rows // width
    ones = member.astype(BF).reshape(blocks, width, columns)
    lower = (
        jnp.arange(width)[:, None] > jnp.arange(width)[None, :]
    ).astype(BF)
    inner = jnp.einsum("pq,bqc->bpc", lower, ones, preferred_element_type=F32)
    totals = jnp.sum(ones.astype(F32), axis=1)
    before = (jnp.arange(blocks)[:, None] > jnp.arange(blocks)[None, :]).astype(F32)
    outer = jnp.sum(before[:, :, None] * totals[None, :, :], axis=1)
    return (inner + outer[:, None, :]).reshape(rows, columns).astype(jnp.int32)


def local(
    tokens,
    cotangent,
    routes,
    block_of_slot,
    cont_seg,
    w_query,
    w_key,
    w_value,
    w_out,
    w_router,
    attn_gain,
    query_gain,
    key_gain,
    ffn_gain,
    w_gate,
    w_up,
    w_down,
):
    ctx_size = lax.axis_size("ctx")
    exp_size = lax.axis_size("exp")
    me = lax.axis_index("ctx")
    exp_index = lax.axis_index("exp")
    tok_rows = tokens.shape[0]
    part_rows = w_query.shape[0]
    own_width = D // ctx_size
    own_heads = HEADS // ctx_size
    experts = w_router.shape[1]
    own_experts = w_gate.shape[0]
    slot_table = block_of_slot[0]
    seg_row = cont_seg[0]
    group_rows = ctx_size * tok_rows
    factor = 1.0 / math.sqrt(HD)

    tokens_group, tokens_there = gather_group(tokens, slot_table, me)
    small = jnp.concatenate(
        [w_router] + [g[:, None] for g in (attn_gain, query_gain, key_gain, ffn_gain)], axis=1
    )
    small_full = lax.all_gather(small, BOTH, axis=0, tiled=True)
    router_full = small_full[:, :experts]
    gains = small_full[:, experts:].astype(F32)
    gain_attn, gain_ffn = gains[:, 0], gains[:, 3]
    own_gains = lax.dynamic_slice(gains, (me * own_width, 0), (own_width, 4))
    gain_query, gain_key = own_gains[:, 1], own_gains[:, 2]
    by_owner = jnp.stack(
        [w.reshape(part_rows, ctx_size, own_width) for w in (w_query, w_key, w_value)], axis=2
    )
    by_owner = jnp.swapaxes(by_owner, 0, 1).reshape(ctx_size, part_rows, 3 * own_width)
    own_columns = lax.all_to_all(by_owner, "ctx", split_axis=0, concat_axis=0, tiled=True)
    qkv_full = lax.all_gather(own_columns, "exp", axis=1, tiled=True).reshape(D, 3 * own_width)
    out_full = lax.all_gather(w_out, "exp", axis=0, tiled=True)
    routes_all = lax.all_gather(routes, "exp", axis=0, tiled=True)
    upstream_all = lax.all_gather(cotangent, "exp", axis=0, tiled=True)
    gate_full, gate_there = gather_rows(after(w_gate, tokens_there), me)
    up_full, up_there = gather_rows(after(w_up, gate_there), me)

    own_ids = exp_index * own_experts + jnp.arange(own_experts, dtype=jnp.int32)
    member = jnp.any(routes_all[:, :, None] == own_ids[None, None, :], axis=1)
    place_of = prefix_count(member)
    capacity = exp_size * 8 * ((5 * tok_rows * TOP // (4 * experts) + 7) // 8)
    all_rows = exp_size * tok_rows
    row_ids = jnp.arange(capacity, dtype=jnp.int32)
    hit = (place_of.T[:, None, :] == row_ids[None, :, None]) & member.T[:, None, :]
    token_ids = jnp.arange(all_rows, dtype=jnp.int32)
    token_of_row = jnp.sum(jnp.where(hit, token_ids[None, None, :], 0), axis=2)
    counts = jnp.sum(member.astype(jnp.int32), axis=0)
    real_row = row_ids[None, :] < counts[:, None]
    row_of = jnp.where(
        member, place_of + capacity * jnp.arange(own_experts, dtype=jnp.int32)[None, :], 0
    )

    seg_ids = jnp.concatenate([jnp.full((PROMPT,), -1, jnp.int32), seg_row])
    starts = jnp.sum(
        (seg_row[None, :] < jnp.arange(CONT, dtype=jnp.int32)[:, None]).astype(jnp.int32), axis=1
    )
    first_pos = jnp.sum(
        jnp.where(
            seg_row[:, None] == jnp.arange(CONT, dtype=jnp.int32)[None, :], starts[None, :], 0
        ),
        axis=1,
    )
    cont_pos = PROMPT + jnp.arange(CTOK, dtype=jnp.int32) - first_pos
    position = jnp.concatenate([jnp.arange(PROMPT, dtype=jnp.int32), cont_pos])
    place = jnp.arange(group_rows, dtype=jnp.int32)
    allowed = (place[None, :] <= place[:, None]) & (
        (seg_ids[None, :] < 0) | (seg_ids[None, :] == seg_ids[:, None])
    )
    cos_part, sin_part = angles(position)
    group_inputs = tokens_group.astype(F32)
    hidden_one = (group_inputs * inverse_root(group_inputs) * gain_attn).astype(BF)
    projected = jnp.dot(hidden_one, qkv_full, preferred_element_type=F32)
    query_pre = projected[:, :own_width]
    key_pre = projected[:, own_width : 2 * own_width]
    value_low = projected[:, 2 * own_width :].astype(BF).reshape(group_rows, own_heads, HD)
    squares = jnp.stack([jnp.sum(query_pre * query_pre, axis=1), jnp.sum(key_pre * key_pre, axis=1)])
    roots = lax.rsqrt(lax.psum(squares, "ctx") / D + epsilon)
    root_query, root_key = roots[0][:, None], roots[1][:, None]
    normed_query = query_pre * root_query
    normed_key = key_pre * root_key
    query_rot = rotate(
        (normed_query * gain_query).reshape(group_rows, own_heads, HD), cos_part, sin_part
    ).astype(BF)
    key_rot = rotate(
        (normed_key * gain_key).reshape(group_rows, own_heads, HD), cos_part, sin_part
    ).astype(BF)

    def masked_scores():
        raw = jnp.einsum("qhd,khd->hqk", query_rot, key_rot, preferred_element_type=F32) * factor
        return jnp.where(allowed[None], raw, -1e30)

    masked = masked_scores()
    row_max = jnp.max(masked, axis=-1, keepdims=True)
    exponent = jnp.exp(masked - row_max)
    row_total = jnp.sum(exponent, axis=-1, keepdims=True)
    log_total = row_max + jnp.log(row_total)
    context = jnp.einsum(
        "hqk,khd->qhd", (exponent / row_total).astype(BF), value_low, preferred_element_type=F32
    )
    context_low = context.reshape(group_rows, own_width).astype(BF)
    branch_part = jnp.dot(context_low, out_full, preferred_element_type=F32)
    branch = scatter_group(branch_part, slot_table, me)
    down_full, unused = gather_rows(after(w_down, up_there, branch), me)

    inputs = tokens.astype(F32)
    middle = inputs + branch
    root_two = inverse_root(middle)
    normed_two = middle * root_two
    hidden_two = (normed_two * gain_ffn).astype(BF)
    hidden_all = lax.all_gather(hidden_two, "exp", axis=0, tiled=True)
    logits = jnp.dot(hidden_two, router_full, preferred_element_type=F32)
    router_prob = jax.nn.softmax(logits, axis=-1)

    arrived = hidden_all[token_of_row]
    upstream_rows = upstream_all[token_of_row]
    row_logits = jnp.einsum("erd,dx->erx", arrived, router_full, preferred_element_type=F32)
    row_prob = jax.nn.softmax(row_logits, axis=-1)
    own_column = own_ids[:, None, None] == jnp.arange(experts, dtype=jnp.int32)[None, None, :]
    gate_row = jnp.sum(jnp.where(own_column, row_prob, 0.0), axis=-1)
    gate_row = jnp.where(real_row, gate_row, 0.0)[:, :, None]
    gate_pre = jnp.einsum("erd,edf->erf", arrived, gate_full, preferred_element_type=F32)
    up_pre = jnp.einsum("erd,edf->erf", arrived, up_full, preferred_element_type=F32)
    grad_raw = jnp.einsum("erd,efd->erf", upstream_rows, down_full, preferred_element_type=F32)
    sigmoid_gate = jax.nn.sigmoid(gate_pre)
    silu_gate = gate_pre * sigmoid_gate
    hidden = silu_gate * up_pre
    hidden_gated = (hidden * gate_row).astype(BF)
    share_row = jnp.sum(hidden * grad_raw, axis=-1)
    grad_hidden = grad_raw * gate_row
    grad_gate_pre = (
        grad_hidden * up_pre * (sigmoid_gate * (1.0 + gate_pre * (1.0 - sigmoid_gate)))
    ).astype(BF)
    grad_up_pre = (grad_hidden * silu_gate).astype(BF)
    grad_rows = (
        jnp.einsum("erf,edf->erd", grad_gate_pre, gate_full, preferred_element_type=F32)
        + jnp.einsum("erf,edf->erd", grad_up_pre, up_full, preferred_element_type=F32)
    ).astype(BF)

    def combine(rows_given):
        flat = rows_given.reshape(own_experts * capacity, -1)
        total = 0.0
        for own in range(own_experts):
            total = total + jnp.where(member[:, own : own + 1], flat[row_of[:, own]], 0).astype(F32)
        return total

    grad_two = lax.psum_scatter(
        combine(grad_rows).astype(BF), "exp", scatter_dimension=0, tiled=True
    ).astype(F32)
    share_token = jnp.sum(jnp.where(hit, share_row[:, :, None], 0.0), axis=1)
    share_token = jnp.swapaxes(share_token.reshape(own_experts, exp_size, tok_rows), 0, 1)
    share_back = lax.all_to_all(share_token, "exp", split_axis=0, concat_axis=0, tiled=True)
    grad_prob = share_back.reshape(experts, tok_rows).T
    result = jnp.einsum(
        "erf,efd->erd", hidden_gated, down_full, preferred_element_type=F32
    ).astype(BF)
    mixture = lax.psum_scatter(
        combine(result).astype(BF), "exp", scatter_dimension=0, tiled=True
    ).astype(F32)
    output = (middle + mixture).astype(BF)

    def weight_grad(left, right):
        return jnp.einsum("era,erb->eab", left, right, preferred_element_type=F32).astype(BF)

    gate_grad = scatter_rows(weight_grad(arrived, grad_gate_pre), me)
    up_grad = scatter_rows(weight_grad(arrived, grad_up_pre), me)
    down_grad = scatter_rows(weight_grad(hidden_gated, upstream_rows), me)

    grad_logits = (
        router_prob * (grad_prob - jnp.sum(router_prob * grad_prob, axis=-1, keepdims=True))
    ).astype(BF)
    grad_router = jnp.einsum("td,te->de", hidden_two, grad_logits, preferred_element_type=F32)
    grad_two = grad_two + jnp.einsum(
        "te,de->td", grad_logits, router_full, preferred_element_type=F32
    )
    grad_ffn_gain = jnp.sum(grad_two * normed_two, axis=0)
    grad_middle = cotangent.astype(F32) + norm_back(grad_two * gain_ffn, normed_two, root_two)

    branch_grad, unused = gather_group(grad_middle.astype(BF), slot_table, me)
    grad_context = (
        jnp.einsum("te,de->td", branch_grad, out_full, preferred_element_type=F32)
        .astype(BF)
        .reshape(group_rows, own_heads, HD)
    )
    out_grad = jnp.einsum("td,te->de", context_low, branch_grad, preferred_element_type=F32)
    prob_again = jnp.exp(masked_scores() - log_total)
    grad_weights = jnp.einsum("qhd,khd->hqk", grad_context, value_low, preferred_element_type=F32)
    row_delta = jnp.sum(prob_again * grad_weights, axis=-1, keepdims=True)
    grad_scores = (prob_again * (grad_weights - row_delta)).astype(BF)
    grad_query_rot = (
        jnp.einsum("hqk,khd->qhd", grad_scores, key_rot, preferred_element_type=F32) * factor
    )
    grad_key_rot = (
        jnp.einsum("hqk,qhd->khd", grad_scores, query_rot, preferred_element_type=F32) * factor
    )
    grad_value = jnp.einsum(
        "hqk,qhd->khd", prob_again.astype(BF), grad_context, preferred_element_type=F32
    ).reshape(group_rows, own_width)
    grad_query_norm = rotate_back(grad_query_rot, cos_part, sin_part).reshape(group_rows, own_width)
    grad_key_norm = rotate_back(grad_key_rot, cos_part, sin_part).reshape(group_rows, own_width)
    grad_query_gain = jnp.sum(grad_query_norm * normed_query, axis=0)
    grad_key_gain = jnp.sum(grad_key_norm * normed_key, axis=0)
    scaled_query = grad_query_norm * gain_query
    scaled_key = grad_key_norm * gain_key
    means = (
        lax.psum(
            jnp.stack(
                [
                    jnp.sum(scaled_query * normed_query, axis=1),
                    jnp.sum(scaled_key * normed_key, axis=1),
                ]
            ),
            "ctx",
        )
        / D
    )
    grad_projected = jnp.concatenate(
        [
            root_query * (scaled_query - normed_query * means[0][:, None]),
            root_key * (scaled_key - normed_key * means[1][:, None]),
            grad_value,
        ],
        axis=1,
    ).astype(BF)
    grad_one_part = jnp.einsum("te,de->td", grad_projected, qkv_full, preferred_element_type=F32)
    grad_one = scatter_group(grad_one_part, slot_table, me)
    qkv_grad = jnp.einsum("td,te->de", hidden_one, grad_projected, preferred_element_type=F32)
    out_sum = lax.psum_scatter(
        out_grad.astype(BF), "exp", scatter_dimension=0, tiled=True
    ).astype(F32)
    qkv_sum = lax.psum_scatter(
        qkv_grad.astype(BF).reshape(ctx_size, exp_size * part_rows, 3 * own_width),
        "exp",
        scatter_dimension=1,
        tiled=True,
    )
    qkv_own = lax.all_to_all(qkv_sum, "ctx", split_axis=0, concat_axis=0, tiled=True).astype(F32)
    projection_grads = [
        jnp.swapaxes(qkv_own[:, :, i * own_width : (i + 1) * own_width], 0, 1).reshape(part_rows, D)
        for i in range(3)
    ]
    root_one = inverse_root(inputs)
    normed_one = inputs * root_one
    grad_attn_gain = jnp.sum(grad_one * normed_one, axis=0)
    grad_input = grad_middle + norm_back(grad_one * gain_attn, normed_one, root_one)
    head_gains = lax.psum_scatter(
        jnp.stack([grad_query_gain, grad_key_gain], axis=1), "exp", scatter_dimension=0, tiled=True
    )
    whole_sums = lax.psum_scatter(
        jnp.concatenate([grad_router, grad_ffn_gain[:, None], grad_attn_gain[:, None]], axis=1),
        BOTH,
        scatter_dimension=0,
        tiled=True,
    )
    return (
        output,
        grad_input,
        projection_grads[0],
        projection_grads[1],
        projection_grads[2],
        out_sum,
        whole_sums[:, :experts],
        whole_sums[:, experts + 1],
        head_gains[:, 0],
        head_gains[:, 1],
        whole_sums[:, experts],
        gate_grad,
        up_grad,
        down_grad,
    )


def solution(mesh):
    rows = P(BOTH, None)
    weights = P("exp", "ctx", None)
    in_specs = (
        (rows, rows, rows, P("exp", None), P("exp", None))
        + (rows,) * 5
        + (P(BOTH),) * 4
        + (weights,) * 3
    )
    out_specs = (rows,) * 7 + (P(BOTH),) * 4 + (weights,) * 3
    return jax.shard_map(local, mesh=mesh, in_specs=in_specs, out_specs=out_specs, check_vma=False)
```

time: 4230 us -> 1880 us (0.44)
  waiting for transfers between devices: 2400 us -> 735 us
  blocking collectives: 802 us -> 105 us
  local copies, waits for them, and re-layouts: 365 us -> 312 us
  other arithmetic: 162 us -> 214 us
    all_to_all x3 -> x2, waiting for transfers between devices: 1010 us -> 5.88 us  [the longest x1 5.88 us: local(): lax.all_to_all(share_token, 'exp', split_axis=0, concat_axis=0, tiled=True)]
    reduce_scatter x8 -> x4, waiting for transfers between devices: 1060 us -> 133 us  [the longest x1 102 us: local(): lax.psum_scatter(combine(grad_rows).astype(BF), 'exp', scatter_dimension=...]
    ppermute x0 -> x40, waiting for transfers between devices: none -> 544 us  [the longest x20 274 us: send_y(): return lax.ppermute(value, 'ctx', Y_PAIRS)]
    all_to_all x1, blocking collectives: 346 us -> 16.4 us  [local(): lax.all_to_all(by_owner, 'ctx', split_axis=0, concat_axis=0, tiled=True)]
    all_gather x1 -> x2, blocking collectives: 371 us -> 59.4 us  [the longest x1 43.9 us: local(): small_full = lax.all_gather(small, BOTH, axis=0, tiled=True)]
    all_gather x9 -> x4, waiting for transfers between devices: 252 us -> 0.05 us  [the longest x1 0.02 us: local(): lax.all_gather(own_columns, 'exp', axis=1, tiled=True)]
    unnamed x2 -> x0, blocking collectives: 85.1 us -> none
    all_to_all x4 -> x0, local copies, waits for them, and re-layouts: 66.8 us -> none  [the longest x1 30.1 us: local(): lax.all_to_all(grad_rows, 'exp', split_axis=1, concat_axis=0, tiled=True)]
  transfers between devices with their start and end apart: 21 -> 52, of which waited for: 17 -> 29; matrix products, arithmetic and copies ran while one was open for 11% -> 23% of each run, Pallas kernels for 0% -> 0%
where the time goes in v1:
time: 1880 us
  waiting for transfers between devices  735 us (39%)
  matrix products  432 us (23%)
  local copies, waits for them, and re-layouts  312 us (17%)
  other arithmetic  214 us (11%)
  blocking collectives  105 us (6%)
  starting transfers between devices  57.1 us (3%)
  between operations  21.7 us (1%)
    ppermute x20, waiting for transfers between devices, send_y(): return lax.ppermute(value, 'ctx', Y_PAIRS)  274 us
    ppermute x20, waiting for transfers between devices, send_x(): return lax.ppermute(value, 'ctx', X_PAIRS)  270 us
    gather x4, local copies, waits for them, and re-layouts, combine(): flat[row_of[:, own]]  125 us
    reduce_scatter x1, waiting for transfers between devices, local(): lax.psum_scatter(combine(grad_rows).astype(BF), 'exp', scatter_dimension=...  102 us
    dot_general x3, matrix products, weight_grad(): jnp.einsum('era,erb->eab', left, right, preferred_element_type=F32)  75.2 us
    unnamed x12, waiting for transfers between devices  51.8 us
    all_gather x1, blocking collectives, local(): small_full = lax.all_gather(small, BOTH, axis=0, tiled=True)  43.9 us
    dot_general x1, matrix products, local(): jnp.einsum('erd,efd->erf', upstream_rows, down_full, preferred_element_ty...  39 us
  transfers between devices with their start and end apart: 52, of which 29 were waited for; matrix products, arithmetic and copies ran while one was open for 23% of the time, Pallas kernels for 0%

profile of v1, /device:TPU:0, one launch (start us, length us, event | category | flops | bytes accessed | tf_op | source)
XLA Modules:
  0.0 1876.6 jit_solution(12617949288056509935)
XLA Ops:
  16.8 16.4 all_to_all.15
  40.5 43.9 %all-gather = bf16[32,64,20]{1,2,0:T(8,128)(2,1)S(1)} all-gather(bf16[1,64,20]{1,2,0:T(8,128)(2,1)S(1)} %bitcast.364), channel_id=1, replica_groups=mesh['ctx'=4,'exp'=8] {'ctx','exp'}, dimensions={0}, use_global_device_ids=true | all-gather | bytes 84480 | tf_op jit(solution)/shard_map/all_gather | solution.py:219
  106.7 10.6 collective-permute-done.2
  128.7 15.8 fusion.52
  148.6 14.3 psum.14
  187.0 7.6 subtract_convert_fusion.1
  194.6 19.9 %fusion.108 = (f32[4,1536]{1,0:T(4,128)S(1)}, f32[4,1536,1536]{1,2,0:T(8,128)}) fusion(bf16[1536,4,64]{2,0,1:T(8,128)(2,1)} %get-tuple-element.102, bf16[1536,4,64]{2,0,1:T(8,128)(2,1)} %get-tuple-element.103, bf16[1536,4,64]{2,0,1:T(8,128)(2,1)} %get-tuple-element.79, bf16[1536,4,64]{2,0,1:T(8,128)(2,1)} %get-tuple-element.78, pred[1536,1536]{0,1:T(8,128)(4,1)} %fusion.14), kind=kOutput, calls=%fused_computation.341 | convolution fusion | flops 2450515968 | bytes 43278336 | tf_op jit(solution)/shard_map/qhd,khd->hqk/dot_general | solution.py:288
  214.6 15.0 fusion.4
  229.7 16.2 fusion.28
  254.3 31.3 %collective-permute-done.4 = bf16[2,192,2048]{2,1,0:T(8,128)(2,1)S(1)} collective-permute-done((bf16[2,192,2048]{2,1,0:T(8,128)(2,1)S(1)}, bf16[2,192,2048]{2,1,0:T(8,128)(2,1)S(1)}, u32[]{:S(2)}, u32[]{:S(2)}) %collective-permute-start.4) | collective-permute-done | bytes 1572896 | tf_op jit(solution)/shard_map/ppermute | solution.py:59
  287.1 15.6 collective-permute-done.5
  305.1 14.7 collective-permute-done.7
  327.0 41.8 %collective-permute-done.8 = bf16[2,512,1024]{2,1,0:T(8,128)(2,1)S(1)} collective-permute-done((bf16[2,512,1024]{2,1,0:T(8,128)(2,1)S(1)}, bf16[2,512,1024]{2,1,0:T(8,128)(2,1)S(1)}, u32[]{:S(2)}, u32[]{:S(2)}) %collective-permute-start.8) | collective-permute-done | bytes 2097184 | tf_op jit(solution)/shard_map/ppermute | solution.py:59
  371.9 18.7 collective-permute-done.10
  392.4 15.5 all_gather.21
  410.0 13.8 select_reduce_fusion.1
  423.8 9.1 collective-permute-done.12
  435.8 44.0 %collective-permute-done.14 = bf16[1,512,1024]{2,1,0:T(8,128)(2,1)} collective-permute-done((bf16[1,512,1024]{2,1,0:T(8,128)(2,1)S(1)}, bf16[1,512,1024]{2,1,0:T(8,128)(2,1)}, u32[]{:S(2)}, u32[]{:S(2)}) %collective-permute-start.14) | collective-permute-done | bytes 1048608 | tf_op jit(solution)/shard_map/ppermute | solution.py:63
  490.6 34.0 %collective-permute-done.13 = bf16[2,512,1024]{2,1,0:T(8,128)(2,1)} collective-permute-done((bf16[2,512,1024]{2,1,0:T(8,128)(2,1)}, bf16[2,512,1024]{2,1,0:T(8,128)(2,1)}, u32[]{:S(2)}, u32[]{:S(2)}) %collective-permute-start.13) | collective-permute-done | bytes 2097184 | tf_op jit(solution)/shard_map/ppermute | solution.py:63
  530.4 20.6 %collective-permute-done.11 = bf16[1,512,1024]{2,1,0:T(8,128)(2,1)S(1)} collective-permute-done((bf16[1,512,1024]{2,1,0:T(8,128)(2,1)S(1)}, bf16[1,512,1024]{2,1,0:T(8,128)(2,1)S(1)}, u32[]{:S(2)}, u32[]{:S(2)}) %collective-permute-start.11) | collective-permute-done | bytes 1048608 | tf_op jit(solution)/shard_map/ppermute | solution.py:59
  562.7 8.8 collective-permute-done.15
  585.2 6.2 collective-permute-done.18
  597.2 35.9 %gather_fusion.3 = bf16[3840,2048]{1,0:T(8,128)(2,1)} fusion(bf16[3072,2048]{1,0:T(8,128)(2,1)} %all-gather.12.cloned.1.call-done, s32[4096]{0:T(1024)S(1)} %pad_clamp_fusion), kind=kCustom, calls=%fused_computation.3 | custom fusion | bytes 31472640 | tf_op jit(solution)/shard_map/gather | solution.py:314
  633.0 35.7 %gather_fusion = bf16[3840,2048]{1,0:T(8,128)(2,1)} fusion(bf16[3072,2048]{1,0:T(8,128)(2,1)} %all-gather.10.cloned.1.call-done, s32[4096]{0:T(1024)S(1)} %pad_clamp_fusion), kind=kCustom, calls=%fused_computation | custom fusion | bytes 31472640 | tf_op jit(solution)/shard_map/gather | solution.py:313
  668.7 24.6 %fusion.116 = f32[2,1920,1024]{1,2,0:T(8,128)} fusion(bf16[2,1920,2048]{2,1,0:T(8,128)(2,1)} %bitcast.316, bf16[2,2048,1024]{2,1,0:T(8,128)(2,1)} %copy-done.12), kind=kOutput, calls=%fused_computation.345 | convolution fusion | flops 16106127360 | bytes 39845888 | tf_op jit(solution)/shard_map/erd,edf->erf/dot_general | solution.py:320
  693.3 24.8 %fusion.117 = f32[2,1920,1024]{1,2,0:T(8,128)} fusion(bf16[2,1920,2048]{2,1,0:T(8,128)(2,1)} %bitcast.317, bf16[2,2048,1024]{2,1,0:T(8,128)(2,1)} %copy-done.13), kind=kOutput, calls=%fused_computation.346 | convolution fusion | flops 16106127360 | bytes 39845888 | tf_op jit(solution)/shard_map/erd,edf->erf/dot_general | solution.py:321
  718.2 9.7 fusion.109
  728.0 39.0 %multiply_reduce_fusion.1 = (f32[2,1920]{1,0:T(2,128)}, bf16[2,1920,1024]{1,2,0:T(8,128)(2,1)}, bf16[2,1920,1024]{1,2,0:T(8,128)(2,1)}, bf16[2,1920,1024]{1,2,0:T(8,128)(2,1)}) fusion(f32[2,1920,1024]{1,2,0:T(8,128)} %fusion.117, f32[2,1920,1024]{1,2,0:T(8,128)} %fusion.116, f32[2,1920]{1,0:T(2,128)S(1)} %compare_select_fusion.3, ...), kind=kOutput, calls=%fused_computation.27 | convolution fusion | flops 16180834304 | bytes 79198208 | tf_op jit(solution)/shard_map/erd,efd->erf/dot_general | solution.py:322
  767.0 24.0 %convolution_convert_fusion = bf16[2,1920,2048]{2,1,0:T(8,128)(2,1)} fusion(bf16[2,1920,1024]{1,2,0:T(8,128)(2,1)} %get-tuple-element.42, bf16[2,1024,2048]{2,1,0:T(8,128)(2,1)} %constant_dynamic-update-slice_fusion.4), kind=kOutput, calls=%fused_computation.38 | convolution fusion | flops 16113991680 | bytes 31981568 | tf_op jit(solution)/shard_map/erf,efd->erd/dot_general | solution.py:352
  791.0 31.3 %gather_fusion.1 = bf16[3072,2048]{1,0:T(8,128)(2,1)} fusion(bf16[3840,2048]{1,0:T(8,128)(2,1)} %bitcast.314, s32[3072]{0:T(1024)S(1)} %copy-done.50), kind=kCustom, calls=%fused_computation.1 | custom fusion | bytes 25178112 | tf_op jit(solution)/shard_map/gather | solution.py:342
  822.3 31.3 %gather_fusion.2 = bf16[3072,2048]{1,0:T(8,128)(2,1)} fusion(bf16[3840,2048]{1,0:T(8,128)(2,1)} %bitcast.315, s32[3072]{0:T(1024)S(1)} %copy-done.51), kind=kCustom, calls=%fused_computation.2 | custom fusion | bytes 25178112 | tf_op jit(solution)/shard_map/gather | solution.py:342
  853.7 26.2 %fusion.118 = f32[2,1920,2048]{2,1,0:T(8,128)} fusion(bf16[2,1920,1024]{1,2,0:T(8,128)(2,1)} %get-tuple-element.43, bf16[2,2048,1024]{2,1,0:T(8,128)(2,1)} %copy-done.13), kind=kOutput, calls=%fused_computation.347 | convolution fusion | flops 16106127360 | bytes 47710208 | tf_op jit(solution)/shard_map/erf,edf->erd/dot_general | solution.py:335
  879.9 30.2 %add_convert_fusion = bf16[2,1920,2048]{2,1,0:T(8,128)(2,1)} fusion(f32[2,1920,2048]{2,1,0:T(8,128)} %fusion.118, bf16[2,1920,1024]{1,2,0:T(8,128)(2,1)} %get-tuple-element.41, bf16[2,2048,1024]{2,1,0:T(8,128)(2,1)} %copy-done.12), kind=kOutput, calls=%fused_computation.20 | convolution fusion | flops 16121856000 | bytes 63438848 | tf_op jit(solution)/shard_map/erf,edf->erd/dot_general | solution.py:334
  910.1 31.3 %gather_fusion.4 = bf16[3072,2048]{1,0:T(8,128)(2,1)} fusion(bf16[3840,2048]{1,0:T(8,128)(2,1)} %bitcast.312, s32[3072]{0:T(1024)S(1)} %copy-done.50), kind=kCustom, calls=%fused_computation.4 | custom fusion | bytes 25178112 | tf_op jit(solution)/shard_map/gather | solution.py:342
  941.4 31.3 %gather_fusion.5 = bf16[3072,2048]{1,0:T(8,128)(2,1)} fusion(bf16[3840,2048]{1,0:T(8,128)(2,1)} %bitcast.313, s32[3072]{0:T(1024)S(1)} %copy-done.51), kind=kCustom, calls=%fused_computation.5 | custom fusion | bytes 25178112 | tf_op jit(solution)/shard_map/gather | solution.py:342
  972.8 32.0 %add_convert_fusion.1 = (bf16[3072,2048]{1,0:T(8,128)(2,1)}, bf16[3072,2048]{1,0:T(8,128)(2,1)}) fusion(bf16[3072,2048]{1,0:T(8,128)(2,1)} %gather_fusion.5, bf16[3072,2048]{1,0:T(8,128)(2,1)} %gather_fusion.4, pred[3072]{0:T(1024)(128)(4,1)S(1)} %copy-done.76, pred[3072]{0:T(1024)(128)(4,1)S(1)} %copy-done.75, bf16[3072,2048]{1,0:T(8,128)(2,1)} %gather_fusion.2, ...), kind=kLoop, calls=%fused_computation.22 | loop fusion | flops 75497472 | bytes 75503616 | tf_op jit(solution)/shard_map/convert_element_type | solution.py:346
  1007.8 15.2 select_reduce_fusion
  1027.6 5.9 all-to-all-done.1
  1033.6 102.1 %reduce-scatter.13.cloned.1.call-done = bf16[384,2048]{1,0:T(8,128)(2,1)} async-done(((bf16[3072,2048]{1,0:T(8,128)(2,1)}), bf16[384,2048]{1,0:T(8,128)(2,1)}) %reduce-scatter.13.cloned.1.call-update) | async-done | bytes 1572880 | tf_op jit(solution)/shard_map/reduce_scatter | solution.py:345
  1144.5 30.1 %collective-permute-done.20 = bf16[384,2048]{1,0:T(8,128)(2,1)S(1)} collective-permute-done((bf16[384,2048]{1,0:T(8,128)(2,1)S(1)}, bf16[384,2048]{1,0:T(8,128)(2,1)S(1)}, u32[]{:S(2)}, u32[]{:S(2)}) %collective-permute-start.20) | collective-permute-done | bytes 1572896 | tf_op jit(solution)/shard_map/ppermute | solution.py:59
  1178.2 14.5 collective-permute-done.22
  1196.4 28.5 %multiply_reduce_fusion = (f32[4,1536]{1,0:T(4,128)S(1)}, f32[4,1536,1536]{1,2,0:T(8,128)}) fusion(f32[4,1536,1536]{1,2,0:T(8,128)} %get-tuple-element.133, f32[4,1536]{1,0:T(4,128)S(1)} %log_add_fusion, bf16[1536,4,128]{0,2,1:T(8,128)(2,1)S(1)} %bitcast.327, bf16[1536,4,128]{0,2,1:T(8,128)(2,1)S(1)} %bitcast.331), kind=kOutput, calls=%fused_computation.15 | convolution fusion | flops 2444224512 | bytes 78692352 | tf_op jit(solution)/shard_map/qhd,khd->hqk/dot_general | solution.py:385
  1224.9 31.7 %multiply_convert_fusion = bf16[4,1536,1536]{1,2,0:T(8,128)(2,1)} fusion(f32[4,1536,1536]{1,2,0:T(8,128)} %get-tuple-element.138, f32[4,1536,1536]{1,2,0:T(8,128)} %get-tuple-element.133, f32[4,1536]{1,0:T(4,128)S(1)} %get-tuple-element.137, f32[4,1536]{1,0:T(4,128)S(1)} %log_add_fusion), kind=kLoop, calls=%fused_computation.14 | loop fusion | flops 37748736 | bytes 94420992 | tf_op jit(solution)/shard_map/convert_element_type | solution.py:387
  1256.6 10.1 fusion.18
  1266.8 12.7 fusion.19
  1279.5 17.1 fusion.29
  1317.1 15.1 psum.15
  1337.0 15.5 convolution_convert_fusion.1
  1353.3 26.3 %convolution_convert_fusion.3 = bf16[2,2048,1024]{2,1,0:T(8,128)(2,1)} fusion(bf16[2,1920,2048]{2,1,0:T(8,128)(2,1)} %bitcast.319, bf16[2,1920,1024]{1,2,0:T(8,128)(2,1)} %get-tuple-element.43), kind=kOutput, calls=%fused_computation.43 | convolution fusion | flops 16110321664 | bytes 31981568 | tf_op jit(solution)/shard_map/era,erb->eab/dot_general | solution.py:361
  1384.2 26.3 %convolution_convert_fusion.4 = bf16[2,2048,1024]{2,1,0:T(8,128)(2,1)} fusion(bf16[2,1920,2048]{2,1,0:T(8,128)(2,1)} %bitcast.320, bf16[2,1920,1024]{1,2,0:T(8,128)(2,1)} %get-tuple-element.41), kind=kOutput, calls=%fused_computation.44 | convolution fusion | flops 16110321664 | bytes 31981568 | tf_op jit(solution)/shard_map/era,erb->eab/dot_general | solution.py:361
  1414.4 22.6 %convolution_convert_fusion.2 = bf16[2,1024,2048]{2,1,0:T(8,128)(2,1)S(1)} fusion(bf16[2,1920,1024]{1,2,0:T(8,128)(2,1)} %get-tuple-element.42, bf16[2,1920,2048]{2,1,0:T(8,128)(2,1)} %bitcast.322), kind=kOutput, calls=%fused_computation.42 | convolution fusion | flops 16110321664 | bytes 31981568 | tf_op jit(solution)/shard_map/era,erb->eab/dot_general | solution.py:361
  1437.1 19.7 %fusion.50 = f32[1536,2048]{1,0:T(8,128)} fusion(bf16[2048,1536]{1,0:T(8,128)(2,1)} %bitcast.378, bf16[1536,512]{0,1:T(8,128)(2,1)} %bitcast.332, bf16[1536,512]{0,1:T(8,128)(2,1)} %copy-done.38, bf16[1536,512]{0,1:T(8,128)(2,1)} %copy-done.37), kind=kOutput, calls=%fused_computation.139 | convolution fusion | flops 9677832192 | bytes 23592960 | tf_op jit(solution)/shard_map/te,de->td/dot_general | solution.py:423
  1472.1 27.1 %collective-permute-done.24 = bf16[2,192,2048]{2,1,0:T(8,128)(2,1)} collective-permute-done((bf16[2,192,2048]{2,1,0:T(8,128)(2,1)}, bf16[2,192,2048]{2,1,0:T(8,128)(2,1)}, u32[]{:S(2)}, u32[]{:S(2)}) %collective-permute-start.24) | collective-permute-done | bytes 1572896 | tf_op jit(solution)/shard_map/ppermute | solution.py:59
  1505.0 39.0 %collective-permute-done.28 = bf16[2,1,512,1024]{3,2,1,0:T(8,128)(2,1)S(1)} collective-permute-done((bf16[2,1,512,1024]{3,2,1,0:T(8,128)(2,1)S(1)}, bf16[2,1,512,1024]{3,2,1,0:T(8,128)(2,1)S(1)}, u32[]{:S(2)}, u32[]{:S(2)}) %collective-permute-start.28) | collective-permute-done | bytes 2097184 | tf_op jit(solution)/shard_map/ppermute | solution.py:59
  1548.7 19.7 %collective-permute-done.25 = bf16[192,2048]{1,0:T(8,128)(2,1)S(1)} collective-permute-done((bf16[192,2048]{1,0:T(8,128)(2,1)S(1)}, bf16[192,2048]{1,0:T(8,128)(2,1)S(1)}, u32[]{:S(2)}, u32[]{:S(2)}) %collective-permute-start.25) | collective-permute-done | bytes 786464 | tf_op jit(solution)/shard_map/ppermute | solution.py:63
  1571.7 14.4 collective-permute-done.36
  1590.4 90.3 %collective-permute-done.33 = bf16[1,512,1024]{2,1,0:T(8,128)(2,1)S(1)} collective-permute-done((bf16[1,512,1024]{2,1,0:T(8,128)(2,1)S(1)}, bf16[1,512,1024]{2,1,0:T(8,128)(2,1)S(1)}, u32[]{:S(2)}, u32[]{:S(2)}) %collective-permute-start.33) | collective-permute-done | bytes 1048608 | tf_op jit(solution)/shard_map/ppermute | solution.py:63
  1690.2 8.1 convolution_convert_fusion.5
  1698.4 19.1 %collective-permute-done.29 = bf16[1,512,1024]{2,1,0:T(8,128)(2,1)} collective-permute-done((bf16[1,512,1024]{2,1,0:T(8,128)(2,1)}, bf16[1,512,1024]{2,1,0:T(8,128)(2,1)}, u32[]{:S(2)}, u32[]{:S(2)}) %collective-permute-start.29) | collective-permute-done | bytes 1048608 | tf_op jit(solution)/shard_map/ppermute | solution.py:63
  1730.5 17.8 collective-permute-done.31
  1752.8 8.6 collective-permute-done.39
  1772.2 6.5 fusion.23
  1778.8 50.3 %reduce-scatter.19.cloned.1.call-done = f32[64,18]{1,0:T(8,128)} async-done(((f32[2048,18]{1,0:T(8,128)}), f32[64,18]{1,0:T(8,128)}) %reduce-scatter.19.cloned.1.call-update) | async-done | bytes 4624
  1832.6 30.9 %reduce-scatter.17.cloned.1.call-done = bf16[64,2048]{1,0:T(8,128)(2,1)} async-done(((bf16[512,2048]{1,0:T(8,128)(2,1)}), bf16[64,2048]{1,0:T(8,128)(2,1)}) %reduce-scatter.17.cloned.1.call-update) | async-done | bytes 262160 | tf_op jit(solution)/shard_map/reduce_scatter | solution.py:426
  (455 shorter events, 288.1 us)
Async XLA Ops:
  7.2 121.5 %all-gather.6.cloned.1.call-start = ((), (), s32[]{:S(2)}) async-start(), calls=%async_computation.9 | async-start | bytes 7077888 | tf_op jit(solution)/shard_map/all_gather | solution.py:230
  33.3 212.7 %all-gather.8.cloned.1.call-start = ((), (), s32[]{:S(2)}) async-start(), calls=%async_computation.10 | async-start | bytes 2359296 | tf_op jit(solution)/shard_map/all_gather | solution.py:231
  34.0 563.1 %all-gather.12.cloned.1.call-start = ((), (), s32[]{:S(2)}) async-start(), calls=%async_computation.13 | async-start | bytes 14155776 | tf_op jit(solution)/shard_map/all_gather | solution.py:233
  34.1 60.7 %collective-permute-start = (bf16[384,2048]{1,0:T(8,128)(2,1)S(1)}, bf16[384,2048]{1,0:T(8,128)(2,1)}, u32[]{:S(2)}, u32[]{:S(2)}) collective-permute-start(bf16[384,2048]{1,0:T(8,128)(2,1)S(1)} %copy-done.5), channel_id=1, source_target_pairs={{0,8},{8,0},{16,24},{24,16},{1,9},{9,1},{17,25},{25,17},{2,10},{10... | collective-permute-start | bytes 4718600 | tf_op jit(solution)/shard_map/ppermute | solution.py:59
  35.0 65.1 %collective-permute-start.1 = (bf16[384,2048]{1,0:T(8,128)(2,1)S(1)}, bf16[384,2048]{1,0:T(8,128)(2,1)S(1)}, u32[]{:S(2)}, u32[]{:S(2)}) collective-permute-start(bf16[384,2048]{1,0:T(8,128)(2,1)S(1)} %copy-done.5), channel_id=1, source_target_pairs={{0,16},{8,24},{16,0},{24,8},{1,17},{9,25},{17,1},{25,9},{2,18},{10... | collective-permute-start | bytes 4718600 | tf_op jit(solution)/shard_map/ppermute | solution.py:63
  35.6 597.4 %all-gather.10.cloned.1.call-start = ((), (), s32[]{:S(2)}) async-start(), calls=%async_computation.11 | async-start | bytes 14155776 | tf_op jit(solution)/shard_map/all_gather | solution.py:309
  84.7 236.7 %copy-start.43 = (f32[2048,1]{0,1:T(1,128)}, f32[2048,1]{0,1:T(1,128)S(1)}, u32[]{:S(2)}) copy-start(f32[2048,1]{0,1:T(1,128)S(1)} %get-tuple-element.112) | copy-start | bytes 24580
  97.2 20.1 %collective-permute-start.2 = (bf16[192,2048]{1,0:T(8,128)(2,1)}, bf16[192,2048]{1,0:T(8,128)(2,1)}, u32[]{:S(2)}, u32[]{:S(2)}) collective-permute-start(bf16[192,2048]{1,0:T(8,128)(2,1)} %get-tuple-element.106), channel_id=1, source_target_pairs={{0,16},{8,24},{16,0},{24,8},{1,17},{9,25},{17,1},{25,9},{2,18},{10... | collective-permute-start | bytes 2359304 | tf_op jit(solution)/shard_map/ppermute | solution.py:63
  102.5 19.9 %collective-permute-start.3 = (bf16[192,2048]{1,0:T(8,128)(2,1)}, bf16[192,2048]{1,0:T(8,128)(2,1)}, u32[]{:S(2)}, u32[]{:S(2)}) collective-permute-start(bf16[192,2048]{1,0:T(8,128)(2,1)} %get-tuple-element.104), channel_id=1, source_target_pairs={{0,8},{8,0},{16,24},{24,16},{1,9},{9,1},{17,25},{25,17},{2,10},{10... | collective-permute-start | bytes 2359304 | tf_op jit(solution)/shard_map/ppermute | solution.py:59
  106.6 80.4 %copy-start.14 = (f32[1536,64]{1,0:T(8,128)}, f32[1536,64]{1,0:T(8,128)S(1)}, u32[]{:S(2)}) copy-start(f32[1536,64]{1,0:T(8,128)S(1)} %get-tuple-element.120) | copy-start | bytes 1179652
  106.7 80.4 %copy-start.15 = (f32[1536,64]{1,0:T(8,128)}, f32[1536,64]{1,0:T(8,128)S(1)}, u32[]{:S(2)}) copy-start(f32[1536,64]{1,0:T(8,128)S(1)} %get-tuple-element.121) | copy-start | bytes 1179652
  252.1 33.4 %collective-permute-start.4 = (bf16[2,192,2048]{2,1,0:T(8,128)(2,1)S(1)}, bf16[2,192,2048]{2,1,0:T(8,128)(2,1)S(1)}, u32[]{:S(2)}, u32[]{:S(2)}) collective-permute-start(bf16[2,192,2048]{2,1,0:T(8,128)(2,1)S(1)} %pad_maximum_fusion.18), channel_id=1, source_target_pairs={{0,8},{8,0},{16,24},{24,16},{1,9},{9,1},{17,25},{25,17},{2,10},{10... | collective-permute-start | bytes 4718600 | tf_op jit(solution)/shard_map/ppermute | solution.py:59
  253.2 33.9 %collective-permute-start.6 = (bf16[2,192,2048]{2,1,0:T(8,128)(2,1)S(1)}, bf16[2,192,2048]{2,1,0:T(8,128)(2,1)S(1)}, u32[]{:S(2)}, u32[]{:S(2)}) collective-permute-start(bf16[2,192,2048]{2,1,0:T(8,128)(2,1)S(1)} %pad_maximum_fusion.19), channel_id=1, source_target_pairs={{0,16},{8,24},{16,0},{24,8},{1,17},{9,25},{17,1},{25,9},{2,18},{10... | collective-permute-start | bytes 4718600 | tf_op jit(solution)/shard_map/ppermute | solution.py:63
  285.8 16.9 collective-permute-start.5
  303.3 16.5 collective-permute-start.7
  324.6 811.1 %reduce-scatter.13.cloned.1.call-start = ((), (), s32[]{:S(2)}) async-start(), calls=%async_computation.14 | async-start | bytes 14155776 | tf_op jit(solution)/shard_map/reduce_scatter | solution.py:345
  325.3 43.6 %collective-permute-start.8 = (bf16[2,512,1024]{2,1,0:T(8,128)(2,1)S(1)}, bf16[2,512,1024]{2,1,0:T(8,128)(2,1)S(1)}, u32[]{:S(2)}, u32[]{:S(2)}) collective-permute-start(bf16[2,512,1024]{2,1,0:T(8,128)(2,1)S(1)} %copy-done.29), channel_id=1, source_target_pairs={{0,8},{8,0},{16,24},{24,16},{1,9},{9,1},{17,25},{25,17},{2,10},{10... | collective-permute-start | bytes 6291464 | tf_op jit(solution)/shard_map/ppermute | solution.py:59
  370.3 20.4 %collective-permute-start.10 = (bf16[1,512,1024]{2,1,0:T(8,128)(2,1)S(1)}, bf16[1,512,1024]{2,1,0:T(8,128)(2,1)S(1)}, u32[]{:S(2)}, u32[]{:S(2)}) collective-permute-start(bf16[1,512,1024]{2,1,0:T(8,128)(2,1)S(1)} %slice.326), channel_id=1, source_target_pairs={{0,16},{8,24},{16,0},{24,8},{1,17},{9,25},{17,1},{25,9},{2,18},{10... | collective-permute-start | bytes 3145736 | tf_op jit(solution)/shard_map/ppermute | solution.py:63
  390.6 42.2 %collective-permute-start.12 = (bf16[2,512,1024]{2,1,0:T(8,128)(2,1)}, bf16[2,512,1024]{2,1,0:T(8,128)(2,1)S(1)}, u32[]{:S(2)}, u32[]{:S(2)}) collective-permute-start(bf16[2,512,1024]{2,1,0:T(8,128)(2,1)} %param.32), channel_id=1, source_target_pairs={{0,8},{8,0},{16,24},{24,16},{1,9},{9,1},{17,25},{25,17},{2,10},{10... | collective-permute-start | bytes 6291464 | tf_op jit(solution)/shard_map/ppermute | solution.py:59
  408.4 75.6 %collective-permute-start.9 = (bf16[2,512,1024]{2,1,0:T(8,128)(2,1)}, bf16[2,512,1024]{2,1,0:T(8,128)(2,1)}, u32[]{:S(2)}, u32[]{:S(2)}) collective-permute-start(bf16[2,512,1024]{2,1,0:T(8,128)(2,1)} %param.31), channel_id=1, source_target_pairs={{0,16},{8,24},{16,0},{24,8},{1,17},{9,25},{17,1},{25,9},{2,18},{10... | collective-permute-start | bytes 6291464 | tf_op jit(solution)/shard_map/ppermute | solution.py:63
  432.9 46.8 %collective-permute-start.14 = (bf16[1,512,1024]{2,1,0:T(8,128)(2,1)S(1)}, bf16[1,512,1024]{2,1,0:T(8,128)(2,1)}, u32[]{:S(2)}, u32[]{:S(2)}) collective-permute-start(bf16[1,512,1024]{2,1,0:T(8,128)(2,1)S(1)} %slice.328), channel_id=1, source_target_pairs={{0,16},{8,24},{16,0},{24,8},{1,17},{9,25},{17,1},{25,9},{2,18},{10... | collective-permute-start | bytes 3145736 | tf_op jit(solution)/shard_map/ppermute | solution.py:63
  434.9 89.8 %collective-permute-start.13 = (bf16[2,512,1024]{2,1,0:T(8,128)(2,1)}, bf16[2,512,1024]{2,1,0:T(8,128)(2,1)}, u32[]{:S(2)}, u32[]{:S(2)}) collective-permute-start(bf16[2,512,1024]{2,1,0:T(8,128)(2,1)} %param.32), channel_id=1, source_target_pairs={{0,16},{8,24},{16,0},{24,8},{1,17},{9,25},{17,1},{25,9},{2,18},{10... | collective-permute-start | bytes 6291464 | tf_op jit(solution)/shard_map/ppermute | solution.py:63
  479.7 78.7 %collective-permute-start.16 = (bf16[2,256,2048]{2,1,0:T(8,128)(2,1)}, bf16[2,256,2048]{2,1,0:T(8,128)(2,1)}, u32[]{:S(2)}, u32[]{:S(2)}) collective-permute-start(bf16[2,256,2048]{2,1,0:T(8,128)(2,1)} %param.33), channel_id=1, source_target_pairs={{0,8},{8,0},{16,24},{24,16},{1,9},{9,1},{17,25},{25,17},{2,10},{10... | collective-permute-start | bytes 6291464 | tf_op jit(solution)/shard_map/ppermute | solution.py:59
  482.5 90.3 %collective-permute-start.17 = (bf16[2,256,2048]{2,1,0:T(8,128)(2,1)}, bf16[2,256,2048]{2,1,0:T(8,128)(2,1)S(1)}, u32[]{:S(2)}, u32[]{:S(2)}) collective-permute-start(bf16[2,256,2048]{2,1,0:T(8,128)(2,1)} %param.33), channel_id=1, source_target_pairs={{0,16},{8,24},{16,0},{24,8},{1,17},{9,25},{17,1},{25,9},{2,18},{10... | collective-permute-start | bytes 6291464 | tf_op jit(solution)/shard_map/ppermute | solution.py:63
  485.3 65.7 %collective-permute-start.11 = (bf16[1,512,1024]{2,1,0:T(8,128)(2,1)S(1)}, bf16[1,512,1024]{2,1,0:T(8,128)(2,1)S(1)}, u32[]{:S(2)}, u32[]{:S(2)}) collective-permute-start(bf16[1,512,1024]{2,1,0:T(8,128)(2,1)S(1)} %slice.327), channel_id=1, source_target_pairs={{0,8},{8,0},{16,24},{24,16},{1,9},{9,1},{17,25},{25,17},{2,10},{10... | collective-permute-start | bytes 3145736 | tf_op jit(solution)/shard_map/ppermute | solution.py:59
  526.9 44.5 %collective-permute-start.15 = (bf16[1,512,1024]{2,1,0:T(8,128)(2,1)}, bf16[1,512,1024]{2,1,0:T(8,128)(2,1)}, u32[]{:S(2)}, u32[]{:S(2)}) collective-permute-start(bf16[1,512,1024]{2,1,0:T(8,128)(2,1)} %slice.329), channel_id=1, source_target_pairs={{0,8},{8,0},{16,24},{24,16},{1,9},{9,1},{17,25},{25,17},{2,10},{10... | collective-permute-start | bytes 3145736 | tf_op jit(solution)/shard_map/ppermute | solution.py:59
  559.7 31.7 %collective-permute-start.18 = (bf16[1,256,2048]{2,1,0:T(8,128)(2,1)S(1)}, bf16[1,256,2048]{2,1,0:T(8,128)(2,1)S(1)}, u32[]{:S(2)}, u32[]{:S(2)}) collective-permute-start(bf16[1,256,2048]{2,1,0:T(8,128)(2,1)S(1)} %slice.331), channel_id=1, source_target_pairs={{0,16},{8,24},{16,0},{24,8},{1,17},{9,25},{17,1},{25,9},{2,18},{10... | collective-permute-start | bytes 3145736 | tf_op jit(solution)/shard_map/ppermute | solution.py:63
  572.9 23.2 %collective-permute-start.19 = (bf16[1,256,2048]{2,1,0:T(8,128)(2,1)S(1)}, bf16[1,256,2048]{2,1,0:T(8,128)(2,1)S(1)}, u32[]{:S(2)}, u32[]{:S(2)}) collective-permute-start(bf16[1,256,2048]{2,1,0:T(8,128)(2,1)S(1)} %slice.332), channel_id=1, source_target_pairs={{0,8},{8,0},{16,24},{24,16},{1,9},{9,1},{17,25},{25,17},{2,10},{10... | collective-permute-start | bytes 3145736 | tf_op jit(solution)/shard_map/ppermute | solution.py:59
  1004.8 130.9 %copy-start.1 = (f32[384,2048]{1,0:T(8,128)S(1)}, f32[384,2048]{1,0:T(8,128)}, u32[]{:S(2)}) copy-start(f32[384,2048]{1,0:T(8,128)} %copy-done) | copy-start | bytes 9437188
  1004.8 130.9 %copy-start.44 = (f32[2048,1]{0,1:T(1,128)S(1)}, f32[2048,1]{0,1:T(1,128)}, u32[]{:S(2)}) copy-start(f32[2048,1]{0,1:T(1,128)} %copy-done.43) | copy-start | bytes 24580
  1004.8 130.9 %copy-start.62 = (f32[384]{0:T(512)S(1)}, f32[384]{0:T(512)}, u32[]{:S(2)}) copy-start(f32[384]{0:T(512)} %copy-done.61) | copy-start | bytes 4612
  1023.0 10.5 all-to-all-start.1
  1027.5 738.3 %reduce-scatter.21.cloned.1.call-start = ((), (), s32[]{:S(2)}) async-start(), calls=%async_computation.18 | async-start | bytes 294912
  1033.6 105.4 %copy-start.52 = (bf16[384,16]{0,1:T(8,128)(2,1)}, bf16[384,16]{0,1:T(8,128)(2,1)S(1)}, u32[]{:S(2)}) copy-start(bf16[384,16]{0,1:T(8,128)(2,1)S(1)} %fusion.83) | copy-start | bytes 36868
  1140.7 34.0 %collective-permute-start.20 = (bf16[384,2048]{1,0:T(8,128)(2,1)S(1)}, bf16[384,2048]{1,0:T(8,128)(2,1)S(1)}, u32[]{:S(2)}, u32[]{:S(2)}) collective-permute-start(bf16[384,2048]{1,0:T(8,128)(2,1)S(1)} %fusion.97), channel_id=1, source_target_pairs={{0,8},{8,0},{16,24},{24,16},{1,9},{9,1},{17,25},{25,17},{2,10},{10... | collective-permute-start | bytes 4718600 | tf_op jit(solution)/shard_map/ppermute | solution.py:59
  1142.1 35.2 %collective-permute-start.21 = (bf16[384,2048]{1,0:T(8,128)(2,1)S(1)}, bf16[384,2048]{1,0:T(8,128)(2,1)S(1)}, u32[]{:S(2)}, u32[]{:S(2)}) collective-permute-start(bf16[384,2048]{1,0:T(8,128)(2,1)S(1)} %fusion.97), channel_id=1, source_target_pairs={{0,16},{8,24},{16,0},{24,8},{1,17},{9,25},{17,1},{25,9},{2,18},{10... | collective-permute-start | bytes 4718600 | tf_op jit(solution)/shard_map/ppermute | solution.py:63
  1174.8 17.9 collective-permute-start.22
  1177.6 15.2 collective-permute-start.23
  1317.0 450.9 %reduce-scatter.15.cloned.1.call-start = ((), (), s32[]{:S(2)}) async-start(), calls=%async_computation.15 | async-start | bytes 7077888 | tf_op jit(solution)/shard_map/reduce_scatter | solution.py:429
  1352.5 419.7 %reduce-scatter.11.cloned.1.call-start = ((), (), s32[]{:S(2)}) async-start(), calls=%async_computation.12 | async-start | bytes 14155776 | tf_op jit(solution)/shard_map/reduce_scatter | solution.py:355
  1353.3 475.8 %reduce-scatter.19.cloned.1.call-start = ((), (), s32[]{:S(2)}) async-start(), calls=%async_computation.17 | async-start | bytes 1081344
  1383.8 117.7 %collective-permute-start.32 = (bf16[2,1,512,1024]{3,2,1,0:T(8,128)(2,1)}, bf16[2,1,512,1024]{3,2,1,0:T(8,128)(2,1)}, u32[]{:S(2)}, u32[]{:S(2)}) collective-permute-start(bf16[2,1,512,1024]{3,2,1,0:T(8,128)(2,1)} %pad_maximum_fusion.10), channel_id=1, source_target_pairs={{0,8},{8,0},{16,24},{24,16},{1,9},{9,1},{17,25},{25,17},{2,10},{10... | collective-permute-start | bytes 6291464 | tf_op jit(solution)/shard_map/ppermute | solution.py:59
  1437.1 150.6 %copy-start.11 = (bf16[2,1024,2048]{2,1,0:T(8,128)(2,1)}, bf16[2,1024,2048]{2,1,0:T(8,128)(2,1)S(1)}, u32[]{:S(2)}) copy-start(bf16[2,1024,2048]{2,1,0:T(8,128)(2,1)S(1)} %convolution_convert_fusion.2) | copy-start | bytes 25165828
  1461.6 37.6 %collective-permute-start.24 = (bf16[2,192,2048]{2,1,0:T(8,128)(2,1)}, bf16[2,192,2048]{2,1,0:T(8,128)(2,1)}, u32[]{:S(2)}, u32[]{:S(2)}) collective-permute-start(bf16[2,192,2048]{2,1,0:T(8,128)(2,1)} %pad_maximum_fusion.20), channel_id=1, source_target_pairs={{0,8},{8,0},{16,24},{24,16},{1,9},{9,1},{17,25},{25,17},{2,10},{10... | collective-permute-start | bytes 4718600 | tf_op jit(solution)/shard_map/ppermute | solution.py:59
  1463.4 80.7 %collective-permute-start.28 = (bf16[2,1,512,1024]{3,2,1,0:T(8,128)(2,1)S(1)}, bf16[2,1,512,1024]{3,2,1,0:T(8,128)(2,1)S(1)}, u32[]{:S(2)}, u32[]{:S(2)}) collective-permute-start(bf16[2,1,512,1024]{3,2,1,0:T(8,128)(2,1)S(1)} %pad_maximum_fusion.8), channel_id=1, source_target_pairs={{0,8},{8,0},{16,24},{24,16},{1,9},{9,1},{17,25},{25,17},{2,10},{10... | collective-permute-start | bytes 6291464 | tf_op jit(solution)/shard_map/ppermute | solution.py:59
  1464.9 121.2 %collective-permute-start.36 = (bf16[2,1,256,2048]{3,2,1,0:T(8,128)(2,1)S(1)}, bf16[2,1,256,2048]{3,2,1,0:T(8,128)(2,1)S(1)}, u32[]{:S(2)}, u32[]{:S(2)}) collective-permute-start(bf16[2,1,256,2048]{3,2,1,0:T(8,128)(2,1)S(1)} %pad_maximum_fusion.12), channel_id=1, source_target_pairs={{0,8},{8,0},{16,24},{24,16},{1,9},{9,1},{17,25},{25,17},{2,10},{10... | collective-permute-start | bytes 6291464 | tf_op jit(solution)/shard_map/ppermute | solution.py:59
  1469.0 78.6 %collective-permute-start.26 = (bf16[2,192,2048]{2,1,0:T(8,128)(2,1)}, bf16[2,192,2048]{2,1,0:T(8,128)(2,1)S(1)}, u32[]{:S(2)}, u32[]{:S(2)}) collective-permute-start(bf16[2,192,2048]{2,1,0:T(8,128)(2,1)} %pad_maximum_fusion.21), channel_id=1, source_target_pairs={{0,16},{8,24},{16,0},{24,8},{1,17},{9,25},{17,1},{25,9},{2,18},{10... | collective-permute-start | bytes 4718600 | tf_op jit(solution)/shard_map/ppermute | solution.py:63
  1499.2 89.9 %collective-permute-start.34 = (bf16[2,1,512,1024]{3,2,1,0:T(8,128)(2,1)S(1)}, bf16[2,1,512,1024]{3,2,1,0:T(8,128)(2,1)S(1)}, u32[]{:S(2)}, u32[]{:S(2)}) collective-permute-start(bf16[2,1,512,1024]{3,2,1,0:T(8,128)(2,1)S(1)} %pad_maximum_fusion.11), channel_id=1, source_target_pairs={{0,16},{8,24},{16,0},{24,8},{1,17},{9,25},{17,1},{25,9},{2,18},{10... | collective-permute-start | bytes 6291464 | tf_op jit(solution)/shard_map/ppermute | solution.py:63
  1501.5 66.9 %collective-permute-start.25 = (bf16[192,2048]{1,0:T(8,128)(2,1)S(1)}, bf16[192,2048]{1,0:T(8,128)(2,1)S(1)}, u32[]{:S(2)}, u32[]{:S(2)}) collective-permute-start(bf16[192,2048]{1,0:T(8,128)(2,1)S(1)} %fusion.56), channel_id=1, source_target_pairs={{0,16},{8,24},{16,0},{24,8},{1,17},{9,25},{17,1},{25,9},{2,18},{10... | collective-permute-start | bytes 2359304 | tf_op jit(solution)/shard_map/ppermute | solution.py:63
  1544.0 177.5 %collective-permute-start.38 = (bf16[2,1,256,2048]{3,2,1,0:T(8,128)(2,1)}, bf16[2,1,256,2048]{3,2,1,0:T(8,128)(2,1)}, u32[]{:S(2)}, u32[]{:S(2)}) collective-permute-start(bf16[2,1,256,2048]{3,2,1,0:T(8,128)(2,1)} %pad_maximum_fusion.13), channel_id=1, source_target_pairs={{0,16},{8,24},{16,0},{24,8},{1,17},{9,25},{17,1},{25,9},{2,18},{10... | collective-permute-start | bytes 6291464 | tf_op jit(solution)/shard_map/ppermute | solution.py:63
  1547.6 150.7 %collective-permute-start.30 = (bf16[2,1,512,1024]{3,2,1,0:T(8,128)(2,1)}, bf16[2,1,512,1024]{3,2,1,0:T(8,128)(2,1)}, u32[]{:S(2)}, u32[]{:S(2)}) collective-permute-start(bf16[2,1,512,1024]{3,2,1,0:T(8,128)(2,1)} %pad_maximum_fusion.9), channel_id=1, source_target_pairs={{0,16},{8,24},{16,0},{24,8},{1,17},{9,25},{17,1},{25,9},{2,18},{10... | collective-permute-start | bytes 6291464 | tf_op jit(solution)/shard_map/ppermute | solution.py:63
  1568.4 112.4 %collective-permute-start.33 = (bf16[1,512,1024]{2,1,0:T(8,128)(2,1)S(1)}, bf16[1,512,1024]{2,1,0:T(8,128)(2,1)S(1)}, u32[]{:S(2)}, u32[]{:S(2)}) collective-permute-start(bf16[1,512,1024]{2,1,0:T(8,128)(2,1)S(1)} %fusion.42), channel_id=1, source_target_pairs={{0,16},{8,24},{16,0},{24,8},{1,17},{9,25},{17,1},{25,9},{2,18},{10... | collective-permute-start | bytes 3145736 | tf_op jit(solution)/shard_map/ppermute | solution.py:63
  1571.7 115.6 %copy-start.10 = (f32[192,2048]{1,0:T(8,128)}, f32[192,2048]{1,0:T(8,128)S(1)}, u32[]{:S(2)}) copy-start(f32[192,2048]{1,0:T(8,128)S(1)} %get-tuple-element.44) | copy-start | bytes 4718596
  1586.1 94.6 %copy-start.26 = (bf16[2,1,256,2048]{3,2,1,0:T(8,128)(2,1)}, bf16[2,1,256,2048]{3,2,1,0:T(8,128)(2,1)S(1)}, u32[]{:S(2)}) copy-start(bf16[2,1,256,2048]{3,2,1,0:T(8,128)(2,1)S(1)} %collective-permute-done.36) | copy-start | bytes 6291460
  1586.1 99.9 %collective-permute-start.27 = (bf16[192,2048]{1,0:T(8,128)(2,1)S(1)}, bf16[192,2048]{1,0:T(8,128)(2,1)S(1)}, u32[]{:S(2)}, u32[]{:S(2)}) collective-permute-start(bf16[192,2048]{1,0:T(8,128)(2,1)S(1)} %get-tuple-element.45), channel_id=1, source_target_pairs={{0,8},{8,0},{16,24},{24,16},{1,9},{9,1},{17,25},{25,17},{2,10},{10... | collective-permute-start | bytes 2359304 | tf_op jit(solution)/shard_map/ppermute | solution.py:59
  1589.1 97.9 %copy-start.36 = (bf16[2,192,2048]{2,1,0:T(8,128)(2,1)S(1)}, bf16[2,192,2048]{2,1,0:T(8,128)(2,1)}, u32[]{:S(2)}) copy-start(bf16[2,192,2048]{2,1,0:T(8,128)(2,1)} %copy-done.35) | copy-start | bytes 4718596
  1589.1 93.0 %copy-start.32 = (bf16[2,1,512,1024]{3,2,1,0:T(8,128)(2,1)}, bf16[2,1,512,1024]{3,2,1,0:T(8,128)(2,1)S(1)}, u32[]{:S(2)}) copy-start(bf16[2,1,512,1024]{3,2,1,0:T(8,128)(2,1)S(1)} %collective-permute-done.34) | copy-start | bytes 6291460
  1589.1 132.5 %collective-permute-start.37 = (bf16[1,256,2048]{2,1,0:T(8,128)(2,1)}, bf16[1,256,2048]{2,1,0:T(8,128)(2,1)S(1)}, u32[]{:S(2)}, u32[]{:S(2)}) collective-permute-start(bf16[1,256,2048]{2,1,0:T(8,128)(2,1)} %fusion.38), channel_id=1, source_target_pairs={{0,16},{8,24},{16,0},{24,8},{1,17},{9,25},{17,1},{25,9},{2,18},{10... | collective-permute-start | bytes 3145736 | tf_op jit(solution)/shard_map/ppermute | solution.py:63
  1680.7 36.7 %collective-permute-start.29 = (bf16[1,512,1024]{2,1,0:T(8,128)(2,1)}, bf16[1,512,1024]{2,1,0:T(8,128)(2,1)}, u32[]{:S(2)}, u32[]{:S(2)}) collective-permute-start(bf16[1,512,1024]{2,1,0:T(8,128)(2,1)} %fusion.46), channel_id=1, source_target_pairs={{0,16},{8,24},{16,0},{24,8},{1,17},{9,25},{17,1},{25,9},{2,18},{10... | collective-permute-start | bytes 3145736 | tf_op jit(solution)/shard_map/ppermute | solution.py:63
  1686.1 40.0 %collective-permute-start.35 = (bf16[1,512,1024]{2,1,0:T(8,128)(2,1)}, bf16[1,512,1024]{2,1,0:T(8,128)(2,1)}, u32[]{:S(2)}, u32[]{:S(2)}) collective-permute-start(bf16[1,512,1024]{2,1,0:T(8,128)(2,1)} %get-tuple-element.67), channel_id=1, source_target_pairs={{0,8},{8,0},{16,24},{24,16},{1,9},{9,1},{17,25},{25,17},{2,10},{10... | collective-permute-start | bytes 3145736 | tf_op jit(solution)/shard_map/ppermute | solution.py:59
  1689.8 173.6 %reduce-scatter.17.cloned.1.call-start = ((), (), s32[]{:S(2)}) async-start(), calls=%async_computation.16 | async-start | bytes 2359296 | tf_op jit(solution)/shard_map/reduce_scatter | solution.py:426
  1721.1 27.2 %collective-permute-start.31 = (bf16[1,512,1024]{2,1,0:T(8,128)(2,1)S(1)}, bf16[1,512,1024]{2,1,0:T(8,128)(2,1)S(1)}, u32[]{:S(2)}, u32[]{:S(2)}) collective-permute-start(bf16[1,512,1024]{2,1,0:T(8,128)(2,1)S(1)} %get-tuple-element.73), channel_id=1, source_target_pairs={{0,8},{8,0},{16,24},{24,16},{1,9},{9,1},{17,25},{25,17},{2,10},{10... | collective-permute-start | bytes 3145736 | tf_op jit(solution)/shard_map/ppermute | solution.py:59
  1724.5 36.9 %collective-permute-start.39 = (bf16[1,256,2048]{2,1,0:T(8,128)(2,1)S(1)}, bf16[1,256,2048]{2,1,0:T(8,128)(2,1)S(1)}, u32[]{:S(2)}, u32[]{:S(2)}) collective-permute-start(bf16[1,256,2048]{2,1,0:T(8,128)(2,1)S(1)} %get-tuple-element.61), channel_id=1, source_target_pairs={{0,8},{8,0},{16,24},{24,16},{1,9},{9,1},{17,25},{25,17},{2,10},{10... | collective-permute-start | bytes 3145736 | tf_op jit(solution)/shard_map/ppermute | solution.py:59
  1767.9 97.3 %all-to-all-start.2 = ((bf16[4,64,1536]{2,1,0:T(8,128)(2,1)}), bf16[4,64,1536]{2,1,0:T(8,128)(2,1)}, u32[]{:S(2)}, u32[]{:S(2)}) async-start(bf16[4,64,1536]{2,1,0:T(8,128)(2,1)} %reduce-scatter.15.cloned.1.call-done), calls=%async_computation.5 | async-start | bytes 1572864 | tf_op jit(solution)/shard_map/all_to_all | solution.py:435
  (81 other events, 1246.6 us)
Sparse Core Ops, SparseCore 0:
  33.4 66.0 all-gather.5
  101.1 27.9 all-gather.7
  130.8 116.2 all-gather.11
  324.7 115.8 all-gather.9
  1005.0 130.6 reduce-scatter.12
  1317.1 32.8 reduce-scatter.20
  1352.6 72.2 reduce-scatter.14
  1427.3 127.5 reduce-scatter.10
  1690.0 139.0 reduce-scatter.18
  1831.2 32.1 reduce-scatter.16

commit v2 on v1

v2 whole, which is shorter than its diff:
```python
import functools
import math

import jax
import jax.numpy as jnp
from jax import lax
from jax.experimental import pallas as pl
from jax.experimental.pallas import tpu as pltpu
from jax.sharding import PartitionSpec as P

D = 2048
HEADS = 16
HD = 128
TOP = 8
PROMPT = 1024
CONT = 2
CTOK = 512

epsilon = 1e-05
rope_base = 10000.0
BF = jnp.bfloat16
F32 = jnp.float32
BOTH = ("ctx", "exp")
X_PAIRS = [(i, i ^ 1) for i in range(4)]
Y_PAIRS = [(i, i ^ 2) for i in range(4)]
XY_PAIRS = [(i, i ^ 3) for i in range(4)]
NT = (((1,), (1,)), ((), ()))
TN = (((0,), (0,)), ((), ()))
TILE = 256
WIN = 512
NOWHERE = -(1 << 20)


def inverse_root(values):
    return lax.rsqrt(jnp.mean(values * values, axis=-1, keepdims=True) + epsilon)


def norm_back(gradient, normed, root_part):
    return root_part * (gradient - normed * jnp.mean(gradient * normed, axis=-1, keepdims=True))


def angles(position):
    half_dim = HD // 2
    inverse = rope_base ** (-2.0 * jnp.arange(half_dim, dtype=F32) / HD)
    phases = position.astype(F32)[:, None] * inverse[None, :]
    return (jnp.cos(phases)[:, None, :], jnp.sin(phases)[:, None, :])


def rotate(values, cos_part, sin_part):
    half_dim = HD // 2
    former = values[..., :half_dim]
    latter = values[..., half_dim:]
    return jnp.concatenate(
        [former * cos_part - latter * sin_part, latter * cos_part + former * sin_part], axis=-1
    )


def rotate_back(gradient, cos_part, sin_part):
    half_dim = HD // 2
    former = gradient[..., :half_dim]
    latter = gradient[..., half_dim:]
    return jnp.concatenate(
        [former * cos_part + latter * sin_part, latter * cos_part - former * sin_part], axis=-1
    )


def send_x(value):
    return lax.ppermute(value, "ctx", X_PAIRS)


def send_y(value):
    return lax.ppermute(value, "ctx", Y_PAIRS)


def send_xy(value):
    return lax.ppermute(value, "ctx", XY_PAIRS)


def after(value, *others):
    return lax.optimization_barrier((value,) + others)[0]


def gather_pieces(value, half):
    from_x = send_x(value)
    from_y = send_y(value)
    far_low = send_y(from_x[:half])
    far_high = send_x(from_y[half:])
    return from_x, from_y, far_low, far_high


def scatter_sum(take, me):
    low = send_x(jnp.stack([take(me ^ 1, 0), take(me ^ 3, 0)]).astype(BF))
    high = send_y(jnp.stack([take(me ^ 2, 1), take(me ^ 3, 1)]).astype(BF))
    low_next = send_y((take(me ^ 2, 0).astype(F32) + low[1].astype(F32)).astype(BF))
    high_next = send_x((take(me ^ 1, 1).astype(F32) + high[1].astype(F32)).astype(BF))
    first = take(me, 0).astype(F32) + low[0].astype(F32) + low_next.astype(F32)
    second = take(me, 1).astype(F32) + high[0].astype(F32) + high_next.astype(F32)
    return first, second


def gather_rows(weight, me):
    if lax.axis_size("ctx") != 4:
        return lax.all_gather(weight, "ctx", axis=1, tiled=True)
    count, rows, columns = weight.shape
    whole = jnp.zeros((count, 4 * rows, columns), weight.dtype)
    parts = (weight, send_x(weight), send_y(weight), send_xy(weight))
    for away, part in enumerate(parts):
        whole = lax.dynamic_update_slice(whole, part, (0, (me ^ away) * rows, 0))
    return whole


def scatter_rows(gradient, me):
    if lax.axis_size("ctx") != 4:
        return lax.psum_scatter(gradient, "ctx", scatter_dimension=1, tiled=True).astype(F32)
    count, rows, columns = gradient.shape
    rows = rows // 4

    def take(away):
        return lax.dynamic_slice(gradient, (0, (me ^ away) * rows, 0), (count, rows, columns))

    parts = (take(0), send_x(take(1)), send_y(take(2)), send_xy(take(3)))
    return sum(part.astype(F32) for part in parts)


def exchange(blocks, me):
    if lax.axis_size("ctx") != 4:
        return lax.all_to_all(blocks, "ctx", split_axis=0, concat_axis=0, tiled=True)
    sends = (lambda part: part, send_x, send_y, send_xy)
    whole = jnp.zeros_like(blocks)
    for away, send in enumerate(sends):
        part = send(lax.dynamic_slice_in_dim(blocks, me ^ away, 1, 0))
        whole = lax.dynamic_update_slice_in_dim(whole, part, me ^ away, 0)
    return whole


def sum_over_ctx(value):
    if lax.axis_size("ctx") != 4:
        return lax.psum(value, "ctx")
    return (value + send_x(value)) + (send_y(value) + send_xy(value))


def pick_blocks(blocks, order):
    return jnp.concatenate(
        [
            lax.dynamic_index_in_dim(blocks, order[i], 0, keepdims=False)
            for i in range(order.shape[0])
        ],
        axis=0,
    )


def gather_group(rows, slot_table, me):
    block = rows.shape[0] // 2
    if lax.axis_size("ctx") != 4:
        blocks = slot_table.shape[0]
        whole = lax.all_gather(rows, "ctx", axis=0, tiled=True).reshape(blocks, block, -1)
        match = slot_table[None, :] == jnp.arange(blocks, dtype=jnp.int32)[:, None]
        order = jnp.sum(jnp.where(match, jnp.arange(blocks, dtype=jnp.int32)[None, :], 0), axis=1)
        return pick_blocks(whole, order), rows
    from_x, from_y, far_low, far_high = gather_pieces(rows, block)
    parts = (
        (rows[:block], me, 0),
        (rows[block:], me, 1),
        (from_x[:block], me ^ 1, 0),
        (from_x[block:], me ^ 1, 1),
        (from_y[:block], me ^ 2, 0),
        (from_y[block:], me ^ 2, 1),
        (far_low, me ^ 3, 0),
        (far_high, me ^ 3, 1),
    )
    whole = jnp.zeros((8 * block, rows.shape[1]), rows.dtype)
    for part, owner, slot in parts:
        start = slot_table[2 * owner + slot] * block
        whole = lax.dynamic_update_slice(whole, part, (start, 0))
    return whole, far_low


def scatter_group(partial, slot_table, me):
    blocks = slot_table.shape[0]
    block = partial.shape[0] // blocks
    if lax.axis_size("ctx") != 4:
        ordered = pick_blocks(partial.reshape(blocks, block, -1), slot_table)
        return lax.psum_scatter(
            ordered.astype(BF), "ctx", scatter_dimension=0, tiled=True
        ).astype(F32)

    def take(owner, part):
        start = slot_table[2 * owner + part] * block
        return lax.dynamic_slice(partial, (start, 0), (block, partial.shape[1]))

    return jnp.concatenate(scatter_sum(take, me), axis=0)


def prefix_count(member):
    rows, columns = member.shape
    width = 128
    blocks = rows // width
    ones = member.astype(BF).reshape(blocks, width, columns)
    lower = (
        jnp.arange(width)[:, None] > jnp.arange(width)[None, :]
    ).astype(BF)
    inner = jnp.einsum("pq,bqc->bpc", lower, ones, preferred_element_type=F32)
    totals = jnp.sum(ones.astype(F32), axis=1)
    before = (jnp.arange(blocks)[:, None] > jnp.arange(blocks)[None, :]).astype(F32)
    outer = jnp.sum(before[:, :, None] * totals[None, :, :], axis=1)
    return (inner + outer[:, None, :]).reshape(rows, columns).astype(jnp.int32)


def dot(a,b,dims=(((1,),(0,)),((),()))):
    return lax.dot_general(a,b,dims,preferred_element_type=F32)

def tile_scores(query, key, seg_q, seg_k, first, width, factor):
    scores = dot(query, key, NT) * factor
    rows = query.shape[0]
    q_place = first + lax.broadcasted_iota(jnp.int32, (rows, width), 0)
    k_place = lax.broadcasted_iota(jnp.int32, (rows, width), 1)
    allowed = k_place <= q_place
    if first >= PROMPT:
        allowed = allowed & ((seg_k < 0) | (seg_k == seg_q))
    return jnp.where(allowed, scores, -1e30)

def attend_kernel(tile, tiles, factor, q_ref, k_ref, v_ref, sq_ref, sk_ref, o_ref):
    at = pl.program_id(1)
    for i in range(tiles):
        @pl.when(at == i)
        def _():
            width = (i + 1) * tile
            scores = tile_scores(q_ref[...], k_ref[:width], sq_ref[...], sk_ref[:, :width], i * tile, width, factor)
            weight = jnp.exp(scores - jnp.max(scores, axis=1, keepdims=True))
            total = jnp.sum(weight, axis=1, keepdims=True)
            o_ref[...] = (dot(weight.astype(BF), v_ref[:width]) / total).astype(BF)

def attend(q, k, v, seg, tile=512):
    rows, width = q.shape
    heads, tiles = width // HD, rows // tile
    return pl.pallas_call(
        functools.partial(attend_kernel, tile, tiles, 1.0 / math.sqrt(HD)),
        out_shape=jax.ShapeDtypeStruct((rows, width), BF),
        grid=(heads, tiles),
        in_specs=[
            pl.BlockSpec((tile, HD), lambda h, i: (i, h)),
            pl.BlockSpec((rows, HD), lambda h, i: (0, h)),
            pl.BlockSpec((rows, HD), lambda h, i: (0, h)),
            pl.BlockSpec((tile, 1), lambda h, i: (i, 0)),
            pl.BlockSpec((1, rows), lambda h, i: (0, 0)),
        ],
        out_specs=pl.BlockSpec((tile, HD), lambda h, i: (i, h)),
        compiler_params=pltpu.CompilerParams(vmem_limit_bytes=40 << 20),
        cost_estimate=pl.CostEstimate(flops=2*2*heads*rows*rows*HD*6//10, bytes_accessed=8*rows*width, transcendentals=heads*rows*rows*6//10),
    )(q, k, v, seg[:, None], seg[None, :])

def attend_back_kernel(tile, tiles, factor, q_ref, k_ref, v_ref, d_ref, sq_ref, sk_ref, dq_ref, dk_ref, dv_ref):
    at = pl.program_id(1)
    @pl.when(at == 0)
    def _():
        dk_ref[...] = jnp.zeros_like(dk_ref)
        dv_ref[...] = jnp.zeros_like(dv_ref)
    for i in range(tiles):
        @pl.when(at == i)
        def _():
            width = (i + 1) * tile
            query, grad = q_ref[...], d_ref[...]
            scores = tile_scores(query, k_ref[:width], sq_ref[...], sk_ref[:, :width], i * tile, width, factor)
            weight = jnp.exp(scores - jnp.max(scores, axis=1, keepdims=True))
            weight = weight / jnp.sum(weight, axis=1, keepdims=True)
            grad_weight = dot(grad, v_ref[:width], NT)
            delta = jnp.sum(weight * grad_weight, axis=1, keepdims=True)
            grad_score = (weight * (grad_weight - delta)).astype(BF)
            dq_ref[...] = dot(grad_score, k_ref[:width]) * factor
            dk_ref[:width] += dot(grad_score, query, TN) * factor
            dv_ref[:width] += dot(weight.astype(BF), grad, TN)

def attend_back(q, k, v, d, seg, tile=512):
    rows, width = q.shape
    heads, tiles = width // HD, rows // tile
    own = pl.BlockSpec((tile, HD), lambda h, i: (i, h))
    whole = pl.BlockSpec((rows, HD), lambda h, i: (0, h))
    return pl.pallas_call(
        functools.partial(attend_back_kernel, tile, tiles, 1.0 / math.sqrt(HD)),
        out_shape=[jax.ShapeDtypeStruct((rows, width), F32)] * 3,
        grid=(heads, tiles),
        in_specs=[own, whole, whole, own,
            pl.BlockSpec((tile, 1), lambda h, i: (i, 0)),
            pl.BlockSpec((1, rows), lambda h, i: (0, 0)),
        ],
        out_specs=[own, whole, whole],
        compiler_params=pltpu.CompilerParams(vmem_limit_bytes=40 << 20),
        cost_estimate=pl.CostEstimate(flops=5*2*heads*rows*rows*HD*6//10, bytes_accessed=20*rows*width, transcendentals=heads*rows*rows*6//10),
    )(q, k, v, d, seg[:, None], seg[None, :])


def pick_rows(tok, lo, windows, source_ref, acc_ref, total):
    span = lax.broadcasted_iota(jnp.int32, (TILE, WIN), 1)
    def window(j):
        base = lo + j * WIN
        start = pl.multiple_of(jnp.minimum(base, total - WIN), 128)
        match = (tok - start == span) & (tok >= base)
        return dot(match.astype(F32).astype(BF), source_ref[pl.ds(start, WIN), :])
    acc_ref[...] = window(0)
    @pl.loop(1, windows)
    def _(j):
        acc_ref[...] += window(j)
    return acc_ref[...].astype(BF)

def back_rows_kernel(total, tiles_ref, lo_ref, win_ref, tok_ref, dy_ref, wd_ref, rows_ref, raw_ref, acc_ref):
    e, i = pl.program_id(0), pl.program_id(1)
    at = e * pl.num_programs(1) + i
    @pl.when(i < tiles_ref[e])
    def _():
        rows = pick_rows(tok_ref[...], lo_ref[at], win_ref[at], dy_ref, acc_ref, total)
        rows_ref[...] = rows
        raw_ref[...] = dot(rows, wd_ref[...], NT)
    @pl.when(i >= tiles_ref[e])
    def _():
        rows_ref[...] = jnp.zeros_like(rows_ref)

def back_rows(tiles, lo, win, tok, dy, wd):
    total, width = dy.shape
    experts, ff, _ = wd.shape
    nt = tok.shape[0] // (experts * TILE)
    last = lambda e, i, t: jnp.minimum(i, jnp.maximum(t[e] - 1, 0))
    spec = lambda n: pl.BlockSpec((None, TILE, n), lambda e, i, t, a, b: (e, i, 0))
    return pl.pallas_call(
        functools.partial(back_rows_kernel, total),
        out_shape=[jax.ShapeDtypeStruct((experts, nt * TILE, width), BF), jax.ShapeDtypeStruct((experts, nt * TILE, ff), F32)],
        grid_spec=pltpu.PrefetchScalarGridSpec(
            num_scalar_prefetch=3, grid=(experts, nt),
            in_specs=[
                pl.BlockSpec((TILE, 1), lambda e, i, t, a, b: (e * nt + i, 0)),
                pl.BlockSpec((total, width), lambda e, i, t, a, b: (0, 0), pipeline_mode=pl.Buffered(1)),
                pl.BlockSpec((None, ff, width), lambda e, i, t, a, b: (e, 0, 0)),
            ],
            out_specs=[spec(width), pl.BlockSpec((None, TILE, ff), lambda e, i, t, a, b: (e, last(e, i, t), 0))],
            scratch_shapes=[pltpu.VMEM((TILE, width), F32)],
        ),
        compiler_params=pltpu.CompilerParams(vmem_limit_bytes=56 << 20),
        cost_estimate=pl.CostEstimate(flops=experts*total*(width*ff+WIN*width), bytes_accessed=4*total*width+2*experts*ff*width+4*experts*total*(width+ff)//2, transcendentals=0),
    )(tiles, lo, win, tok, dy, wd)

def expert_kernel(total, own, tiles_ref, lo_ref, win_ref, id_ref, tok_ref, h_ref, wr_ref, wg_ref, wu_ref, raw_ref,
                  rows_ref, hid_ref, da_ref, db_ref, dh_ref, share_ref, acc_ref):
    e, i = pl.program_id(0), pl.program_id(1)
    at = e * pl.num_programs(1) + i
    @pl.when(i < tiles_ref[e])
    def _():
        rows = pick_rows(tok_ref[...], lo_ref[at], win_ref[at], h_ref, acc_ref, total)
        rows_ref[...] = rows
        logits = dot(rows, wr_ref[...])
        probs = jnp.exp(logits - jnp.max(logits, axis=1, keepdims=True))
        column = lax.broadcasted_iota(jnp.int32, probs.shape, 1)
        gate = jnp.sum(jnp.where(column == id_ref[0] + e, probs, 0.0), axis=1, keepdims=True) / jnp.sum(probs, axis=1, keepdims=True)
        part = wg_ref.shape[1] // 4
        share = 0.0
        for c in range(4):
            cols = slice(c * part, (c + 1) * part)
            a = dot(rows, wg_ref[:, cols])
            b = dot(rows, wu_ref[:, cols])
            raw = raw_ref[:, cols]
            sig = 1.0 / (1.0 + jnp.exp(-a))
            silu = a * sig
            hid = silu * b
            share += jnp.sum(hid * raw, axis=1, keepdims=True)
            raw = raw * gate
            hid_ref[:, cols] = (hid * gate).astype(BF)
            da_ref[:, cols] = (raw * b * (sig * (1.0 + a * (1.0 - sig)))).astype(BF)
            db_ref[:, cols] = (raw * silu).astype(BF)
        share_ref[...] = share
        dh_ref[...] = (dot(da_ref[...], wg_ref[...], NT) + dot(db_ref[...], wu_ref[...], NT)).astype(BF)
    @pl.when(i >= tiles_ref[e])
    def _():
        for ref in (rows_ref, hid_ref, da_ref, db_ref, dh_ref, share_ref):
            ref[...] = jnp.zeros_like(ref)

def expert_rows(tiles, lo, win, first_id, tok, h, wr, wg, wu, raw):
    total, width = h.shape
    experts, _, ff = wg.shape
    nt = tok.shape[0] // (experts * TILE)
    spec = lambda n: pl.BlockSpec((None, TILE, n), lambda e, i, t, a, b, d: (e, i, 0))
    shp = lambda n, dt=BF: jax.ShapeDtypeStruct((experts, nt * TILE, n), dt)
    return pl.pallas_call(
        functools.partial(expert_kernel, total, experts),
        out_shape=[shp(width), shp(ff), shp(ff), shp(ff), shp(width), shp(1, F32)],
        grid_spec=pltpu.PrefetchScalarGridSpec(
            num_scalar_prefetch=4, grid=(experts, nt),
            in_specs=[
                pl.BlockSpec((TILE, 1), lambda e, i, t, a, b, d: (e * nt + i, 0)),
                pl.BlockSpec((total, width), lambda e, i, t, a, b, d: (0, 0), pipeline_mode=pl.Buffered(1)),
                pl.BlockSpec(wr.shape, lambda e, i, t, a, b, d: (0, 0), pipeline_mode=pl.Buffered(1)),
                pl.BlockSpec((None, width, ff), lambda e, i, t, a, b, d: (e, 0, 0)),
                pl.BlockSpec((None, width, ff), lambda e, i, t, a, b, d: (e, 0, 0)),
                pl.BlockSpec((None, TILE, ff), lambda e, i, t, a, b, d: (e, jnp.minimum(i, jnp.maximum(t[e] - 1, 0)), 0)),
            ],
            out_specs=[spec(width), spec(ff), spec(ff), spec(ff), spec(width), spec(1)],
            scratch_shapes=[pltpu.VMEM((TILE, width), F32)],
        ),
        compiler_params=pltpu.CompilerParams(vmem_limit_bytes=60 << 20),
        cost_estimate=pl.CostEstimate(flops=experts*total*(4*width*ff+WIN*width), bytes_accessed=4*total*width+4*experts*ff*width+experts*total*(4*width+10*ff)//2, transcendentals=experts*total*ff//2),
    )(tiles, lo, win, first_id, tok, h, wr, wg, wu, raw)

def combine_kernel(
    experts, start_ref, more_ref, wide_ref, pos_ref, rows_ref, share_ref, out_ref, own_ref, acc_ref
):
    i = pl.program_id(0)
    span = lax.broadcasted_iota(jnp.int32, (TILE, TILE), 1)
    wide_span = lax.broadcasted_iota(jnp.int32, (TILE, 384), 1)
    last = rows_ref.shape[1] - TILE

    def window(e, j):
        base = start_ref[e, i] + j * TILE
        start = pl.multiple_of(jnp.minimum(base, last), 16)
        pos = pos_ref[:, e : e + 1]
        match = (pos - start == span) & (pos >= base)
        return dot(match.astype(F32).astype(BF), rows_ref[e, pl.ds(start, TILE), :])

    acc_ref[...] = sum(window(e, 0) for e in range(experts))
    for e in range(experts):
        wide = pl.multiple_of(wide_ref[e, i], 128)
        match = pos_ref[:, e : e + 1] - wide == wide_span
        share = share_ref[e, :, pl.ds(wide, 384)]
        own_ref[:, e : e + 1] = jnp.sum(jnp.where(match, share, 0.0), axis=1, keepdims=True)

        @pl.when(more_ref[e, i] > 0)
        def _():
            acc_ref[...] += window(e, 1)

    out_ref[...] = acc_ref[...].astype(BF)


def combine_rows(start, more, wide, pos, rows, share):
    experts, capacity, width = rows.shape
    total = pos.shape[0]
    return pl.pallas_call(
        functools.partial(combine_kernel, experts),
        out_shape=[
            jax.ShapeDtypeStruct((total, width), BF),
            jax.ShapeDtypeStruct((total, experts), F32),
        ],
        grid_spec=pltpu.PrefetchScalarGridSpec(
            num_scalar_prefetch=3,
            grid=(total // TILE,),
            in_specs=[
                pl.BlockSpec((TILE, experts), lambda i, *_: (i, 0)),
                pl.BlockSpec(rows.shape, lambda i, *_: (0, 0, 0), pipeline_mode=pl.Buffered(1)),
                pl.BlockSpec(share.shape, lambda i, *_: (0, 0, 0), pipeline_mode=pl.Buffered(1)),
            ],
            out_specs=[
                pl.BlockSpec((TILE, width), lambda i, *_: (i, 0)),
                pl.BlockSpec((TILE, experts), lambda i, *_: (i, 0)),
            ],
            scratch_shapes=[pltpu.VMEM((TILE, width), F32)],
        ),
        compiler_params=pltpu.CompilerParams(vmem_limit_bytes=48 << 20),
        cost_estimate=pl.CostEstimate(
            flops=2 * experts * total * TILE * width,
            bytes_accessed=2 * (experts * capacity + total) * width,
            transcendentals=0,
        ),
    )(start, more, wide, pos, rows, share)


def local(
    tokens,
    cotangent,
    routes,
    block_of_slot,
    cont_seg,
    w_query,
    w_key,
    w_value,
    w_out,
    w_router,
    attn_gain,
    query_gain,
    key_gain,
    ffn_gain,
    w_gate,
    w_up,
    w_down,
):
    ctx_size = lax.axis_size("ctx")
    exp_size = lax.axis_size("exp")
    me = lax.axis_index("ctx")
    exp_index = lax.axis_index("exp")
    tok_rows = tokens.shape[0]
    part_rows = w_query.shape[0]
    own_width = D // ctx_size
    own_heads = HEADS // ctx_size
    experts = w_router.shape[1]
    own_experts = w_gate.shape[0]
    slot_table = block_of_slot[0]
    seg_row = cont_seg[0]
    group_rows = ctx_size * tok_rows
    factor = 1.0 / math.sqrt(HD)

    tokens_group, tokens_there = gather_group(tokens, slot_table, me)
    small = jnp.concatenate(
        [w_router] + [g[:, None] for g in (attn_gain, query_gain, key_gain, ffn_gain)], axis=1
    )
    small = jnp.pad(small, ((0, 0), (0, 128 - small.shape[1])))
    by_owner = jnp.stack(
        [w.reshape(part_rows, ctx_size, own_width) for w in (w_query, w_key, w_value)], axis=2
    )
    by_owner = jnp.swapaxes(by_owner, 0, 1).reshape(ctx_size, part_rows, 3 * own_width)
    by_owner = jnp.concatenate(
        [by_owner, jnp.broadcast_to(small, (ctx_size,) + small.shape)], axis=2
    )
    own_columns = exchange(by_owner, me)
    packed = lax.all_gather(own_columns, "exp", axis=1, tiled=True).reshape(D, 3 * own_width + 128)
    small_full = packed[:, 3 * own_width :]
    router_full = small_full[:, :experts]
    gains = small_full[:, experts : experts + 4].astype(F32)
    gain_attn, gain_ffn = gains[:, 0], gains[:, 3]
    own_gains = lax.dynamic_slice(gains, (me * own_width, 0), (own_width, 4))
    gain_query, gain_key = own_gains[:, 1], own_gains[:, 2]
    out_full = lax.all_gather(w_out, "exp", axis=0, tiled=True)
    routes_all = lax.all_to_all(
        jnp.broadcast_to(routes[None], (exp_size,) + routes.shape),
        "exp",
        split_axis=0,
        concat_axis=0,
        tiled=True,
    ).reshape(exp_size * tok_rows, TOP)
    upstream_all = lax.all_gather(cotangent, "exp", axis=0, tiled=True)
    gate_full = gather_rows(after(w_gate, tokens_there), me)
    up_full = gather_rows(after(w_up, tokens_there), me)
    down_full = gather_rows(after(w_down, tokens_there), me)

    own_ids = exp_index * own_experts + jnp.arange(own_experts, dtype=jnp.int32)
    member = jnp.any(routes_all[:, :, None] == own_ids[None, None, :], axis=1)
    place_of = prefix_count(member)
    capacity = exp_size * 8 * ((5 * tok_rows * TOP // (4 * experts) + 7) // 8)
    row_tiles = (capacity + TILE - 1) // TILE
    capacity = row_tiles * TILE
    all_rows = exp_size * tok_rows
    row_ids = jnp.arange(capacity, dtype=jnp.int32)
    hit = (place_of.T[:, None, :] == row_ids[None, :, None]) & member.T[:, None, :]
    token_ids = jnp.arange(all_rows, dtype=jnp.int32)
    token_of_row = jnp.max(jnp.where(hit, token_ids[None, None, :], -1), axis=2)
    counts = jnp.sum(member.astype(jnp.int32), axis=0)
    used_tiles = (counts + TILE - 1) // TILE
    by_tile = token_of_row.reshape(own_experts * row_tiles, TILE)
    low_token = jnp.maximum(by_tile[:, 0], 0) // 128 * 128
    windows = jnp.maximum((jnp.max(by_tile, axis=1) - low_token) // WIN + 1, 1)
    token_column = token_of_row.reshape(-1, 1)
    place_column = jnp.where(member, place_of, NOWHERE)
    first_place = place_of[::TILE].T
    in_tile = jnp.sum(member.reshape(-1, TILE, own_experts).astype(jnp.int32), axis=1).T
    first_row = first_place // 16 * 16
    more_rows = (first_place + in_tile - first_row > TILE).astype(jnp.int32)
    share_row_start = jnp.minimum(first_place // 128 * 128, capacity - 384)

    seg_ids = jnp.concatenate([jnp.full((PROMPT,), -1, jnp.int32), seg_row])
    starts = jnp.sum(
        (seg_row[None, :] < jnp.arange(CONT, dtype=jnp.int32)[:, None]).astype(jnp.int32), axis=1
    )
    first_pos = jnp.sum(
        jnp.where(
            seg_row[:, None] == jnp.arange(CONT, dtype=jnp.int32)[None, :], starts[None, :], 0
        ),
        axis=1,
    )
    cont_pos = PROMPT + jnp.arange(CTOK, dtype=jnp.int32) - first_pos
    position = jnp.concatenate([jnp.arange(PROMPT, dtype=jnp.int32), cont_pos])
    cos_part, sin_part = angles(position)
    group_inputs = tokens_group.astype(F32)
    hidden_one = (group_inputs * inverse_root(group_inputs) * gain_attn).astype(BF)
    projected = jnp.dot(hidden_one, packed, preferred_element_type=F32)
    query_pre = projected[:, :own_width]
    key_pre = projected[:, own_width : 2 * own_width]
    value_low = projected[:, 2 * own_width : 3 * own_width].astype(BF)
    squares = jnp.stack([jnp.sum(query_pre * query_pre, axis=1), jnp.sum(key_pre * key_pre, axis=1)])
    roots = lax.rsqrt(sum_over_ctx(squares) / D + epsilon)
    root_query, root_key = roots[0][:, None], roots[1][:, None]
    normed_query = query_pre * root_query
    normed_key = key_pre * root_key

    def turn(values, turning):
        heads = values.reshape(group_rows, own_heads, HD)
        return turning(heads, cos_part, sin_part).reshape(group_rows, own_width)

    query_rot = turn(normed_query * gain_query, rotate).astype(BF)
    key_rot = turn(normed_key * gain_key, rotate).astype(BF)
    context_low = attend(query_rot, key_rot, value_low, seg_ids)
    branch_part = jnp.dot(context_low, out_full, preferred_element_type=F32)
    branch = scatter_group(branch_part, slot_table, me)
    inputs = tokens.astype(F32)
    middle = inputs + branch
    root_two = inverse_root(middle)
    normed_two = middle * root_two
    hidden_two = (normed_two * gain_ffn).astype(BF)
    hidden_all = lax.all_gather(hidden_two, "exp", axis=0, tiled=True)
    logits = jnp.dot(hidden_two, router_full, preferred_element_type=F32)
    router_prob = jax.nn.softmax(logits, axis=-1)

    upstream_rows, grad_raw = back_rows(
        used_tiles, low_token, windows, token_column, upstream_all, down_full
    )
    arrived, hidden_gated, grad_gate_pre, grad_up_pre, grad_rows, share_row = expert_rows(
        used_tiles,
        low_token,
        windows,
        own_ids[:1],
        token_column,
        hidden_all,
        router_full,
        gate_full,
        up_full,
        grad_raw,
    )
    grad_two_part, share_token = combine_rows(
        first_row,
        more_rows,
        share_row_start,
        place_column,
        grad_rows,
        share_row.reshape(own_experts, 1, capacity),
    )
    grad_two = lax.psum_scatter(
        grad_two_part, "exp", scatter_dimension=0, tiled=True
    ).astype(F32)
    share_back = lax.all_to_all(
        share_token.reshape(exp_size, tok_rows, own_experts),
        "exp",
        split_axis=0,
        concat_axis=0,
        tiled=True,
    )
    grad_prob = jnp.swapaxes(share_back, 0, 1).reshape(tok_rows, experts)
    result = jnp.einsum(
        "erf,efd->erd", hidden_gated, down_full, preferred_element_type=F32
    ).astype(BF)
    mixture_part, unused = combine_rows(
        first_row,
        more_rows,
        share_row_start,
        place_column,
        result,
        share_row.reshape(own_experts, 1, capacity),
    )
    mixture = lax.psum_scatter(mixture_part, "exp", scatter_dimension=0, tiled=True).astype(F32)
    output = (middle + mixture).astype(BF)

    def weight_grad(left, right):
        return jnp.einsum("era,erb->eab", left, right, preferred_element_type=F32).astype(BF)

    gate_grad = scatter_rows(weight_grad(arrived, grad_gate_pre), me)
    up_grad = scatter_rows(weight_grad(arrived, grad_up_pre), me)
    down_grad = scatter_rows(weight_grad(hidden_gated, upstream_rows), me)

    grad_logits = (
        router_prob * (grad_prob - jnp.sum(router_prob * grad_prob, axis=-1, keepdims=True))
    ).astype(BF)
    grad_router = jnp.einsum("td,te->de", hidden_two, grad_logits, preferred_element_type=F32)
    grad_two = grad_two + jnp.einsum(
        "te,de->td", grad_logits, router_full, preferred_element_type=F32
    )
    grad_ffn_gain = jnp.sum(grad_two * normed_two, axis=0)
    grad_middle = cotangent.astype(F32) + norm_back(grad_two * gain_ffn, normed_two, root_two)

    branch_grad, unused = gather_group(grad_middle.astype(BF), slot_table, me)
    grad_context = lax.dot_general(branch_grad, out_full, NT, preferred_element_type=F32).astype(BF)
    out_grad = jnp.einsum("td,te->de", context_low, branch_grad, preferred_element_type=F32)
    grad_query_rot, grad_key_rot, grad_value = attend_back(
        query_rot, key_rot, value_low, grad_context, seg_ids
    )
    grad_query_norm = turn(grad_query_rot, rotate_back)
    grad_key_norm = turn(grad_key_rot, rotate_back)
    grad_query_gain = jnp.sum(grad_query_norm * normed_query, axis=0)
    grad_key_gain = jnp.sum(grad_key_norm * normed_key, axis=0)
    scaled_query = grad_query_norm * gain_query
    scaled_key = grad_key_norm * gain_key
    means = (
        sum_over_ctx(
            jnp.stack(
                [
                    jnp.sum(scaled_query * normed_query, axis=1),
                    jnp.sum(scaled_key * normed_key, axis=1),
                ]
            )
        )
        / D
    )
    grad_projected = jnp.concatenate(
        [
            root_query * (scaled_query - normed_query * means[0][:, None]),
            root_key * (scaled_key - normed_key * means[1][:, None]),
            grad_value,
        ],
        axis=1,
    ).astype(BF)
    grad_packed = jnp.pad(grad_projected, ((0, 0), (0, 128)))
    grad_one_part = lax.dot_general(grad_packed, packed, NT, preferred_element_type=F32)
    grad_one = scatter_group(grad_one_part, slot_table, me)
    qkv_grad = jnp.einsum("td,te->de", hidden_one, grad_projected, preferred_element_type=F32)
    out_sum = lax.psum_scatter(
        out_grad.astype(BF), "exp", scatter_dimension=0, tiled=True
    ).astype(F32)
    qkv_sum = lax.psum_scatter(
        qkv_grad.astype(BF).reshape(ctx_size, exp_size * part_rows, 3 * own_width),
        "exp",
        scatter_dimension=1,
        tiled=True,
    )
    qkv_own = exchange(qkv_sum, me).astype(F32)
    projection_grads = [
        jnp.swapaxes(qkv_own[:, :, i * own_width : (i + 1) * own_width], 0, 1).reshape(part_rows, D)
        for i in range(3)
    ]
    root_one = inverse_root(inputs)
    normed_one = inputs * root_one
    grad_attn_gain = jnp.sum(grad_one * normed_one, axis=0)
    grad_input = grad_middle + norm_back(grad_one * gain_attn, normed_one, root_one)
    early_sums = lax.psum_scatter(
        jnp.concatenate([grad_router, grad_ffn_gain[:, None]], axis=1),
        BOTH,
        scatter_dimension=0,
        tiled=True,
    )
    head_gains = lax.dynamic_update_slice(
        jnp.zeros((2, D), F32), jnp.stack([grad_query_gain, grad_key_gain]), (0, me * own_width)
    )
    late_sums = lax.dynamic_slice(
        lax.psum(jnp.concatenate([grad_attn_gain[None], head_gains]), BOTH),
        (0, (me * exp_size + exp_index) * part_rows),
        (3, part_rows),
    )
    return (
        output,
        grad_input,
        projection_grads[0],
        projection_grads[1],
        projection_grads[2],
        out_sum,
        early_sums[:, :experts],
        late_sums[0],
        late_sums[1],
        late_sums[2],
        early_sums[:, experts],
        gate_grad,
        up_grad,
        down_grad,
    )


def solution(mesh):
    rows = P(BOTH, None)
    weights = P("exp", "ctx", None)
    in_specs = (
        (rows, rows, rows, P("exp", None), P("exp", None))
        + (rows,) * 5
        + (P(BOTH),) * 4
        + (weights,) * 3
    )
    out_specs = (rows,) * 7 + (P(BOTH),) * 4 + (weights,) * 3
    return jax.shard_map(local, mesh=mesh, in_specs=in_specs, out_specs=out_specs, check_vma=False)
```

time: 1880 us -> 1480 us (0.79)
  matrix products: 432 us -> 163 us
  Pallas kernels: 0 us -> 247 us
  local copies, waits for them, and re-layouts: 312 us -> 153 us
  waiting for transfers between devices: 735 us -> 634 us
  other arithmetic: 214 us -> 119 us
  blocking collectives: 105 us -> 42.5 us
  starting transfers between devices: 57.1 us -> 96 us
    dot_general x14 -> x3, matrix products: 288 us -> 33.6 us  [the longest x1 16.1 us: local(): projected = jnp.dot(hidden_one, packed, preferred_element_type=F32)]
    pallas_call x0 -> x6, Pallas kernels: none -> 247 us  [the longest x1 109 us: expert_rows(): pl.pallas_call(functools.partial(expert_kernel, total, experts), out_shap...]
    gather x6 -> x0, local copies, waits for them, and re-layouts: 197 us -> none  [the longest x4 125 us: combine(): flat[row_of[:, own]]]
    convert_element_type x4 -> x3, other arithmetic: 65 us -> 1.27 us  [the longest x1 1.24 us: local(): gains = small_full[:, experts:experts + 4].astype(F32)]
    all_gather x2 -> x0, blocking collectives: 59.4 us -> none  [the longest x1 43.9 us: local(): small_full = lax.all_gather(small, BOTH, axis=0, tiled=True)]
    unnamed x12 -> x10, waiting for transfers between devices: 51.8 us -> 1.49 us
    ppermute x0 -> x10, starting transfers between devices: none -> 47.7 us  [send_xy(): return lax.ppermute(value, 'ctx', XY_PAIRS)]
    reduce_sum x3 -> x2, other arithmetic: 44 us -> 0.25 us  [the longest x1 0.14 us: local(): counts = jnp.sum(member.astype(jnp.int32), axis=0)]
  transfers between devices with their start and end apart: 52 -> 57, of which waited for: 29 -> 24; matrix products, arithmetic and copies ran while one was open for 23% -> 26% of each run, Pallas kernels for 0% -> 8%
where the time goes in v2:
time: 1480 us
  waiting for transfers between devices  634 us (43%)
  Pallas kernels  247 us (17%)
  matrix products  163 us (11%)
  local copies, waits for them, and re-layouts  153 us (10%)
  other arithmetic  119 us (8%)
  starting transfers between devices  96 us (6%)
  blocking collectives  42.5 us (3%)
  between operations  21.3 us (1%)
    ppermute x18, waiting for transfers between devices, send_y(): return lax.ppermute(value, 'ctx', Y_PAIRS)  281 us
    ppermute x18, waiting for transfers between devices, send_x(): return lax.ppermute(value, 'ctx', X_PAIRS)  238 us
    pallas_call x1, Pallas kernels, expert_rows(): pl.pallas_call(functools.partial(expert_kernel, total, experts), out_shap...  109 us
    reduce_scatter x1, waiting for transfers between devices, local(): lax.psum_scatter(grad_two_part, 'exp', scatter_dimension=0, tiled=True)  97.1 us
    dot_general x3, matrix products, weight_grad(): jnp.einsum('era,erb->eab', left, right, preferred_element_type=F32)  71.8 us
    ppermute x10, starting transfers between devices, send_xy(): return lax.ppermute(value, 'ctx', XY_PAIRS)  47.7 us
    pallas_call x1, Pallas kernels, back_rows(): pl.pallas_call(functools.partial(back_rows_kernel, total), out_shape=[jax...  47.6 us
    psum x1, blocking collectives, local(): lax.psum(jnp.concatenate([grad_attn_gain[None], head_gains]), BOTH)  42.5 us
  transfers between devices with their start and end apart: 57, of which 24 were waited for; matrix products, arithmetic and copies ran while one was open for 26% of the time, Pallas kernels for 8%

profile of v2, /device:TPU:0, one launch (start us, length us, event | category | flops | bytes accessed | tf_op | source)
XLA Modules:
  0.0 1475.4 jit_solution(10975434713332215730)
XLA Ops:
  21.1 4.5 collective-permute-done.4
  25.7 5.2 collective-permute-done.5
  42.5 26.1 %collective-permute-done = bf16[384,2048]{1,0:T(8,128)(2,1)} collective-permute-done((bf16[384,2048]{1,0:T(8,128)(2,1)S(1)}, bf16[384,2048]{1,0:T(8,128)(2,1)}, u32[]{:S(2)}, u32[]{:S(2)}) %collective-permute-start) | collective-permute-done | bytes 1572896 | tf_op jit(solution)/shard_map/ppermute | solution.py:68
  73.6 13.6 collective-permute-done.2
  91.4 10.0 all-gather.5.cloned.1.call-done
  103.6 16.1 %fusion.20 = f32[1536,1664]{1,0:T(8,128)S(1)} fusion(bf16[2048,1664]{1,0:T(8,128)(2,1)} %bitcast.231, bf16[1536,2048]{1,0:T(8,128)(2,1)} %copy-done.17, f32[2048]{0:T(1024)S(1)} %get-tuple-element.61, f32[1536]{0:T(1024)S(1)} %add_rsqrt_fusion.1), kind=kOutput, calls=%fused_computation.72 | convolution fusion | flops 10481565696 | bytes 23345152 | tf_op jit(solution)/shard_map/dot_general | solution.py:567
  123.8 4.3 multiply_cosine_fusion
  131.4 5.0 fusion.18
  136.5 4.9 reshape.288
  141.4 5.0 reshape.287
  146.4 8.4 subtract_convert_fusion
  154.8 4.3 pad_maximum_fusion.4
  160.5 19.8 %shard_map.272 = bf16[1536,512]{1,0:T(8,128)(2,1)S(1)} custom-call(bf16[1536,512]{1,0:T(8,128)(2,1)S(1)} %bitcast.205, bf16[1536,512]{1,0:T(8,128)(2,1)S(1)} %bitcast.207, bf16[1536,512]{1,0:T(8,128)(2,1)S(1)} %slice.351.v_ref, s32[1536,1]{1,0:T(8,128)S(1)} %broadcast_in_dim.122.sq_ref, s32[1,1536]{1,0:T(1,128)S(1)} %broadcast_in_dim.112.sk_ref), custom_call_target="tpu_custom_call" | custom-call | flops 2899102976 | bytes 6291456 | tf_op jit(solution)/shard_map/pallas_call | solution.py:236
  182.6 5.6 fusion.80
  192.2 32.5 %collective-permute-done.10 = bf16[2,192,2048]{2,1,0:T(8,128)(2,1)S(1)} collective-permute-done((bf16[2,192,2048]{2,1,0:T(8,128)(2,1)S(1)}, bf16[2,192,2048]{2,1,0:T(8,128)(2,1)S(1)}, u32[]{:S(2)}, u32[]{:S(2)}) %collective-permute-start.10) | collective-permute-done | bytes 1572896 | tf_op jit(solution)/shard_map/ppermute | solution.py:68
  226.5 16.6 %collective-permute-done.11 = bf16[192,2048]{1,0:T(8,128)(2,1)S(1)} collective-permute-done((bf16[192,2048]{1,0:T(8,128)(2,1)S(1)}, bf16[192,2048]{1,0:T(8,128)(2,1)S(1)}, u32[]{:S(2)}, u32[]{:S(2)}) %collective-permute-start.11) | collective-permute-done | bytes 786464 | tf_op jit(solution)/shard_map/ppermute | solution.py:72
  245.2 15.8 %collective-permute-done.13 = bf16[192,2048]{1,0:T(8,128)(2,1)S(1)} collective-permute-done((bf16[192,2048]{1,0:T(8,128)(2,1)S(1)}, bf16[192,2048]{1,0:T(8,128)(2,1)S(1)}, u32[]{:S(2)}, u32[]{:S(2)}) %collective-permute-start.13) | collective-permute-done | bytes 786464 | tf_op jit(solution)/shard_map/ppermute | solution.py:68
  270.5 5.7 all-to-all-done
  281.8 15.3 %select_reduce_fusion = s32[2,2048]{1,0:T(2,128)} fusion(s32[2,3072]{1,0:T(2,128)S(1)} %copy.259, pred[2,3072]{1,0:T(4,128)(4,1)S(1)} %bitcast.242), kind=kLoop, calls=%fused_computation | loop fusion | flops 50327552 | bytes 47104 | tf_op jit(solution)/shard_map/reduce_max | solution.py:538
  302.7 23.9 %collective-permute-done.14 = bf16[2,512,1024]{2,1,0:T(8,128)(2,1)} collective-permute-done((bf16[2,512,1024]{2,1,0:T(8,128)(2,1)}, bf16[2,512,1024]{2,1,0:T(8,128)(2,1)}, u32[]{:S(2)}, u32[]{:S(2)}) %collective-permute-start.14) | collective-permute-done | bytes 2097184 | tf_op jit(solution)/shard_map/ppermute | solution.py:68
  334.9 36.7 %collective-permute-done.17 = bf16[2,512,1024]{2,1,0:T(8,128)(2,1)} collective-permute-done((bf16[2,512,1024]{2,1,0:T(8,128)(2,1)}, bf16[2,512,1024]{2,1,0:T(8,128)(2,1)}, u32[]{:S(2)}, u32[]{:S(2)}) %collective-permute-start.17) | collective-permute-done | bytes 2097184 | tf_op jit(solution)/shard_map/ppermute | solution.py:68
  373.5 87.7 %collective-permute-done.18 = bf16[2,512,1024]{2,1,0:T(8,128)(2,1)} collective-permute-done((bf16[2,512,1024]{2,1,0:T(8,128)(2,1)}, bf16[2,512,1024]{2,1,0:T(8,128)(2,1)}, u32[]{:S(2)}, u32[]{:S(2)}) %collective-permute-start.18) | collective-permute-done | bytes 2097184 | tf_op jit(solution)/shard_map/ppermute | solution.py:72
  466.6 4.4 broadcast_in_dim.117
  485.3 21.1 %collective-permute-done.20 = bf16[2,256,2048]{2,1,0:T(8,128)(2,1)} collective-permute-done((bf16[2,256,2048]{2,1,0:T(8,128)(2,1)}, bf16[2,256,2048]{2,1,0:T(8,128)(2,1)}, u32[]{:S(2)}, u32[]{:S(2)}) %collective-permute-start.20) | collective-permute-done | bytes 2097184 | tf_op jit(solution)/shard_map/ppermute | solution.py:68
  509.6 41.6 %collective-permute-done.21 = bf16[2,256,2048]{2,1,0:T(8,128)(2,1)} collective-permute-done((bf16[2,256,2048]{2,1,0:T(8,128)(2,1)}, bf16[2,256,2048]{2,1,0:T(8,128)(2,1)}, u32[]{:S(2)}, u32[]{:S(2)}) %collective-permute-start.21) | collective-permute-done | bytes 2097184 | tf_op jit(solution)/shard_map/ppermute | solution.py:72
  559.3 47.6 %shard_map.273 = (bf16[2,2048,2048]{2,1,0:T(8,128)(2,1)}, f32[2,2048,1024]{2,1,0:T(8,128)}) custom-call(s32[2]{0:T(128)} %and_select_fusion.1.tiles_ref, s32[16]{0:T(128)} %get-tuple-element.71.lo_ref, s32[16]{0:T(128)} %get-tuple-element.70.win_ref, s32[4096,1]{1,0:T(8,128)} %bitcast.225, bf16[3072,2048]{1,0:T(8,128)(2,1)} %all-gather.11.cloned.1.call-done.dy_ref, ...), custom_call_target="tpu_custom_call" | custom-call | flops 19327352832 | bytes 71303168 | tf_op jit(solution)/shard_map/pallas_call | solution.py:323
  607.0 109.0 %shard_map.274 = (bf16[2,2048,2048]{2,1,0:T(8,128)(2,1)}, bf16[2,2048,1024]{2,1,0:T(8,128)(2,1)}, bf16[2,2048,1024]{2,1,0:T(8,128)(2,1)}, bf16[2,2048,1024]{2,1,...) custom-call(s32[2]{0:T(128)} %and_select_fusion.1.tiles_ref, s32[16]{0:T(128)} %get-tuple-element.71.lo_ref, ...), custom_call_target="tpu_custom_call" | custom-call | flops 57982058496 | bytes 98566144 | tf_op jit(solution)/shard_map/pallas_call | solution.py:380
  718.2 20.4 %shard_map.276 = (bf16[3072,2048]{1,0:T(8,128)(2,1)}, f32[3072,2]{1,0:T(8,128)S(1)}) custom-call(s32[2,12]{1,0:T(2,128)S(1)} %copy.262.start_ref, s32[2,12]{1,0:T(2,128)S(1)} %copy.263.more_ref, s32[2,12]{1,0:T(2,128)S(1)} %copy.264.wide_ref, s32[3072,2]{1,0:T(8,128)S(1)} %broadcast_select_fusion.pos_ref, bf16[2,2048,2048]{2,1,0:T(8,128)(2,1)} %get-tuple-element.38.rows_ref, ...), custom_call_target="tpu_custom_call" | custom-call | flops 6442450944 | bytes 29360128 | tf_op jit(solution)/shard_map/pallas_call | solution.py:432
  745.2 25.2 %convolution_convert_fusion.rows_ref = bf16[2,2048,2048]{2,1,0:T(8,128)(2,1)} fusion(bf16[2,2048,1024]{2,1,0:T(8,128)(2,1)} %get-tuple-element.35, bf16[2,1024,2048]{2,1,0:T(8,128)(2,1)} %constant_dynamic-update-slice_fusion.5.wd_ref), kind=kOutput, calls=%fused_computation.8 | convolution fusion | flops 17188257792 | bytes 33554432 | tf_op jit(solution)/shard_map/erf,efd->erd/dot_general | solution.py:629
  770.8 97.1 %reduce-scatter.10.cloned.1.call-done = bf16[384,2048]{1,0:T(8,128)(2,1)} async-done(((bf16[3072,2048]{1,0:T(8,128)(2,1)}), bf16[384,2048]{1,0:T(8,128)(2,1)}) %reduce-scatter.10.cloned.1.call-update) | async-done | bytes 1572880 | tf_op jit(solution)/shard_map/reduce_scatter | solution.py:618
  867.9 5.3 multiply_reduce_fusion
  874.6 20.3 %shard_map.275 = (bf16[3072,2048]{1,0:T(8,128)(2,1)}, f32[3072,2]{1,0:T(8,128)}) custom-call(s32[2,12]{1,0:T(2,128)S(1)} %copy.262.start_ref, s32[2,12]{1,0:T(2,128)S(1)} %copy.263.more_ref, s32[2,12]{1,0:T(2,128)S(1)} %copy.264.wide_ref, s32[3072,2]{1,0:T(8,128)S(1)} %broadcast_select_fusion.pos_ref, ...), custom_call_target="tpu_custom_call" | custom-call | flops 6442450944 | bytes 29360128 | tf_op jit(solution)/shard_map/pallas_call | solution.py:432
  896.8 4.4 fusion.72
  908.1 29.0 %collective-permute-done.23 = bf16[384,2048]{1,0:T(8,128)(2,1)S(1)} collective-permute-done((bf16[384,2048]{1,0:T(8,128)(2,1)}, bf16[384,2048]{1,0:T(8,128)(2,1)S(1)}, u32[]{:S(2)}, u32[]{:S(2)}) %collective-permute-start.23) | collective-permute-done | bytes 1572896 | tf_op jit(solution)/shard_map/ppermute | solution.py:68
  940.7 24.3 %convolution_convert_fusion.4 = bf16[2,2048,1024]{2,1,0:T(8,128)(2,1)} fusion(bf16[2,2048,2048]{2,1,0:T(8,128)(2,1)} %get-tuple-element.44, bf16[2,2048,1024]{2,1,0:T(8,128)(2,1)} %get-tuple-element.45), kind=kOutput, calls=%fused_computation.12 | convolution fusion | flops 17184063488 | bytes 33554432 | tf_op jit(solution)/shard_map/era,erb->eab/dot_general | solution.py:644
  967.9 3.6 convolution_convert_fusion.6.d_ref
  971.5 30.0 %shard_map.277 = (f32[1536,512]{1,0:T(8,128)S(1)}, f32[1536,512]{1,0:T(8,128)S(1)}, f32[1536,512]{1,0:T(8,128)}) custom-call(bf16[1536,512]{1,0:T(8,128)(2,1)S(1)} %bitcast.206, bf16[1536,512]{1,0:T(8,128)(2,1)S(1)} %bitcast.208, bf16[1536,512]{1,0:T(8,128)(2,1)S(1)} %copy-done.2, bf16[1536,512]{1,0:T(8,128)(2,1)S(1)} %convolution_convert_fusion.6.d_ref, ...), custom_call_target="tpu_custom_call" | custom-call | flops 7247757312 | bytes 15728640 | tf_op jit(solution)/shard_map/pallas_call | solution.py:278
  1003.2 4.9 reshape.295
  1010.7 8.1 multiply_add_fusion.1
  1030.2 6.0 constant_dynamic-slice_fusion.8
  1043.0 13.9 convolution_convert_fusion.1
  1057.0 23.1 %convolution_convert_fusion.3 = bf16[2,2048,1024]{2,1,0:T(8,128)(2,1)S(1)} fusion(bf16[2,2048,2048]{2,1,0:T(8,128)(2,1)} %get-tuple-element.44, bf16[2,2048,1024]{2,1,0:T(8,128)(2,1)} %get-tuple-element.46), kind=kOutput, calls=%fused_computation.11 | convolution fusion | flops 17184063488 | bytes 33554432 | tf_op jit(solution)/shard_map/era,erb->eab/dot_general | solution.py:644
  1088.8 13.9 fusion.4
  1102.6 4.6 copy-done.26
  1110.4 20.6 %collective-permute-done.38 = bf16[2,512,1024]{2,1,0:T(8,128)(2,1)} collective-permute-done((bf16[2,512,1024]{2,1,0:T(8,128)(2,1)}, bf16[2,512,1024]{2,1,0:T(8,128)(2,1)}, u32[]{:S(2)}, u32[]{:S(2)}) %collective-permute-start.38) | collective-permute-done | bytes 2097184 | tf_op jit(solution)/shard_map/ppermute | solution.py:72
  1132.5 24.4 %convolution_convert_fusion.2 = bf16[2,1024,2048]{2,1,0:T(8,128)(2,1)} fusion(bf16[2,2048,1024]{2,1,0:T(8,128)(2,1)} %get-tuple-element.35, bf16[2,2048,2048]{2,1,0:T(8,128)(2,1)} %get-tuple-element.47), kind=kOutput, calls=%fused_computation.10 | convolution fusion | flops 17184063488 | bytes 33554432 | tf_op jit(solution)/shard_map/era,erb->eab/dot_general | solution.py:644
  1156.9 5.9 constant_dynamic-slice_fusion.2
  1162.8 32.3 %collective-permute-start.45 = (bf16[2,256,2048]{2,1,0:T(8,128)(2,1)}, bf16[2,256,2048]{2,1,0:T(8,128)(2,1)}, u32[]{:S(2)}, u32[]{:S(2)}) collective-permute-start(bf16[2,256,2048]{2,1,0:T(8,128)(2,1)} %get-tuple-element.89), channel_id=1, source_target_pairs={{0,24},{8,16},{16,8},{24,0},{1,25},{9,17},{17,9},{25,1},{2,26},{10... | collective-permute-start | bytes 6291464 | tf_op jit(solution)/shard_map/ppermute | solution.py:76
  1195.2 7.5 convert_add_fusion.3
  1204.7 10.0 collective-permute-done.41
  1215.7 38.8 %collective-permute-done.30 = bf16[2,192,2048]{2,1,0:T(8,128)(2,1)} collective-permute-done((bf16[2,192,2048]{2,1,0:T(8,128)(2,1)}, bf16[2,192,2048]{2,1,0:T(8,128)(2,1)}, u32[]{:S(2)}, u32[]{:S(2)}) %collective-permute-start.30) | collective-permute-done | bytes 1572896 | tf_op jit(solution)/shard_map/ppermute | solution.py:68
  1258.5 4.9 convolution_convert_fusion.5
  1263.4 7.4 convert_add_fusion.2
  1270.8 67.5 %collective-permute-done.32 = bf16[2,192,2048]{2,1,0:T(8,128)(2,1)} collective-permute-done((bf16[2,192,2048]{2,1,0:T(8,128)(2,1)}, bf16[2,192,2048]{2,1,0:T(8,128)(2,1)}, u32[]{:S(2)}, u32[]{:S(2)}) %collective-permute-start.32) | collective-permute-done | bytes 1572896 | tf_op jit(solution)/shard_map/ppermute | solution.py:72
  1338.3 16.7 %collective-permute-done.31 = bf16[192,2048]{1,0:T(8,128)(2,1)S(1)} collective-permute-done((bf16[192,2048]{1,0:T(8,128)(2,1)S(1)}, bf16[192,2048]{1,0:T(8,128)(2,1)S(1)}, u32[]{:S(2)}, u32[]{:S(2)}) %collective-permute-start.31) | collective-permute-done | bytes 786464 | tf_op jit(solution)/shard_map/ppermute | solution.py:72
  1355.0 4.1 fusion.25
  1360.1 7.2 convert_add_fusion.1
  1370.2 8.3 collective-permute-done.33
  1384.8 42.5 %psum.7 = f32[3,2048]{1,0:T(4,128)S(1)} all-reduce(f32[3,2048]{1,0:T(4,128)S(1)} %pad_maximum_fusion.11), channel_id=1, replica_groups=mesh['ctx'=4,'exp'=8] {'ctx','exp'}, use_global_device_ids=true, to_apply=%region_30.31 | all-reduce | flops 6144 | bytes 49152 | tf_op jit(solution)/shard_map/psum | solution.py:723
  1427.4 6.5 fusion.12
  1441.9 5.6 dynamic_update_slice.143
  1447.8 5.6 dynamic_update_slice.144
  1453.7 5.6 dynamic_update_slice.145
  1459.7 5.6 dynamic_update_slice.146
  (407 shorter events, 202.4 us)
Async XLA Ops:
  7.2 94.2 %all-gather.5.cloned.1.call-start = ((), (), s32[]{:S(2)}) async-start(), calls=%async_computation.7 | async-start | bytes 7667712 | tf_op jit(solution)/shard_map/all_gather | solution.py:508
  16.6 9.1 collective-permute-start.4
  19.6 11.3 collective-permute-start.5
  21.1 9.8 collective-permute-start.6
  31.9 150.7 %all-gather.7.cloned.1.call-start = ((), (), s32[]{:S(2)}) async-start(), calls=%async_computation.8 | async-start | bytes 2359296 | tf_op jit(solution)/shard_map/all_gather | solution.py:515
  32.6 526.7 %all-gather.11.cloned.1.call-start = ((), (), s32[]{:S(2)}) async-start(), calls=%async_computation.10 | async-start | bytes 14155776 | tf_op jit(solution)/shard_map/all_gather | solution.py:523
  33.4 573.6 %all-gather.9.cloned.1.call-start = ((), (), s32[]{:S(2)}) async-start(), calls=%async_computation.9 | async-start | bytes 14155776 | tf_op jit(solution)/shard_map/all_gather | solution.py:591
  33.4 35.2 %collective-permute-start = (bf16[384,2048]{1,0:T(8,128)(2,1)S(1)}, bf16[384,2048]{1,0:T(8,128)(2,1)}, u32[]{:S(2)}, u32[]{:S(2)}) collective-permute-start(bf16[384,2048]{1,0:T(8,128)(2,1)S(1)} %copy-done.18), channel_id=1, source_target_pairs={{0,8},{8,0},{16,24},{24,16},{1,9},{9,1},{17,25},{25,17},{2,10},{10... | collective-permute-start | bytes 4718600 | tf_op jit(solution)/shard_map/ppermute | solution.py:68
  34.7 37.0 %collective-permute-start.1 = (bf16[384,2048]{1,0:T(8,128)(2,1)S(1)}, bf16[384,2048]{1,0:T(8,128)(2,1)S(1)}, u32[]{:S(2)}, u32[]{:S(2)}) collective-permute-start(bf16[384,2048]{1,0:T(8,128)(2,1)S(1)} %copy-done.18), channel_id=1, source_target_pairs={{0,16},{8,24},{16,0},{24,8},{1,17},{9,25},{17,1},{25,9},{2,18},{10... | collective-permute-start | bytes 4718600 | tf_op jit(solution)/shard_map/ppermute | solution.py:72
  69.9 17.3 %collective-permute-start.2 = (bf16[192,2048]{1,0:T(8,128)(2,1)S(1)}, bf16[192,2048]{1,0:T(8,128)(2,1)S(1)}, u32[]{:S(2)}, u32[]{:S(2)}) collective-permute-start(bf16[192,2048]{1,0:T(8,128)(2,1)S(1)} %get-tuple-element.118), channel_id=1, source_target_pairs={{0,16},{8,24},{16,0},{24,8},{1,17},{9,25},{17,1},{25,9},{2,18},{10... | collective-permute-start | bytes 2359304 | tf_op jit(solution)/shard_map/ppermute | solution.py:72
  71.9 16.8 %collective-permute-start.3 = (bf16[192,2048]{1,0:T(8,128)(2,1)S(1)}, bf16[192,2048]{1,0:T(8,128)(2,1)S(1)}, u32[]{:S(2)}, u32[]{:S(2)}) collective-permute-start(bf16[192,2048]{1,0:T(8,128)(2,1)S(1)} %get-tuple-element.116), channel_id=1, source_target_pairs={{0,8},{8,0},{16,24},{24,16},{1,9},{9,1},{17,25},{25,17},{2,10},{10... | collective-permute-start | bytes 2359304 | tf_op jit(solution)/shard_map/ppermute | solution.py:68
  103.6 159.1 %copy-start.34 = (f32[2048]{0:T(1024)}, f32[2048]{0:T(1024)S(1)}, u32[]{:S(2)}) copy-start(f32[2048]{0:T(1024)S(1)} %get-tuple-element.60) | copy-start | bytes 24580
  120.3 11.0 collective-permute-start.8
  121.8 9.5 collective-permute-start.9
  123.3 8.0 collective-permute-start.7
  188.9 35.8 %collective-permute-start.10 = (bf16[2,192,2048]{2,1,0:T(8,128)(2,1)S(1)}, bf16[2,192,2048]{2,1,0:T(8,128)(2,1)S(1)}, u32[]{:S(2)}, u32[]{:S(2)}) collective-permute-start(bf16[2,192,2048]{2,1,0:T(8,128)(2,1)S(1)} %pad_maximum_fusion.6), channel_id=1, source_target_pairs={{0,8},{8,0},{16,24},{24,16},{1,9},{9,1},{17,25},{25,17},{2,10},{10... | collective-permute-start | bytes 4718600 | tf_op jit(solution)/shard_map/ppermute | solution.py:68
  190.6 35.8 %collective-permute-start.12 = (bf16[2,192,2048]{2,1,0:T(8,128)(2,1)S(1)}, bf16[2,192,2048]{2,1,0:T(8,128)(2,1)S(1)}, u32[]{:S(2)}, u32[]{:S(2)}) collective-permute-start(bf16[2,192,2048]{2,1,0:T(8,128)(2,1)S(1)} %pad_maximum_fusion.7), channel_id=1, source_target_pairs={{0,16},{8,24},{16,0},{24,8},{1,17},{9,25},{17,1},{25,9},{2,18},{10... | collective-permute-start | bytes 4718600 | tf_op jit(solution)/shard_map/ppermute | solution.py:72
  224.9 18.1 %collective-permute-start.11 = (bf16[192,2048]{1,0:T(8,128)(2,1)S(1)}, bf16[192,2048]{1,0:T(8,128)(2,1)S(1)}, u32[]{:S(2)}, u32[]{:S(2)}) collective-permute-start(bf16[192,2048]{1,0:T(8,128)(2,1)S(1)} %fusion.28), channel_id=1, source_target_pairs={{0,16},{8,24},{16,0},{24,8},{1,17},{9,25},{17,1},{25,9},{2,18},{10... | collective-permute-start | bytes 2359304 | tf_op jit(solution)/shard_map/ppermute | solution.py:72
  243.7 17.3 %collective-permute-start.13 = (bf16[192,2048]{1,0:T(8,128)(2,1)S(1)}, bf16[192,2048]{1,0:T(8,128)(2,1)S(1)}, u32[]{:S(2)}, u32[]{:S(2)}) collective-permute-start(bf16[192,2048]{1,0:T(8,128)(2,1)S(1)} %get-tuple-element.79), channel_id=1, source_target_pairs={{0,8},{8,0},{16,24},{24,16},{1,9},{9,1},{17,25},{25,17},{2,10},{10... | collective-permute-start | bytes 2359304 | tf_op jit(solution)/shard_map/ppermute | solution.py:68
  262.7 632.3 %copy-start.45 = (f32[384]{0:T(512)}, f32[384]{0:T(512)S(1)}, u32[]{:S(2)}) copy-start(f32[384]{0:T(512)S(1)} %add_rsqrt_fusion.3) | copy-start | bytes 4612
  266.6 9.6 all-to-all-start
  270.0 597.9 %reduce-scatter.10.cloned.1.call-start = ((), (), s32[]{:S(2)}) async-start(), calls=%async_computation.12 | async-start | bytes 14155776 | tf_op jit(solution)/shard_map/reduce_scatter | solution.py:618
  277.7 48.9 %collective-permute-start.14 = (bf16[2,512,1024]{2,1,0:T(8,128)(2,1)}, bf16[2,512,1024]{2,1,0:T(8,128)(2,1)}, u32[]{:S(2)}, u32[]{:S(2)}) collective-permute-start(bf16[2,512,1024]{2,1,0:T(8,128)(2,1)} %param.31), channel_id=1, source_target_pairs={{0,8},{8,0},{16,24},{24,16},{1,9},{9,1},{17,25},{25,17},{2,10},{10... | collective-permute-start | bytes 6291464 | tf_op jit(solution)/shard_map/ppermute | solution.py:68
  279.2 49.8 %collective-permute-start.15 = (bf16[2,512,1024]{2,1,0:T(8,128)(2,1)}, bf16[2,512,1024]{2,1,0:T(8,128)(2,1)}, u32[]{:S(2)}, u32[]{:S(2)}) collective-permute-start(bf16[2,512,1024]{2,1,0:T(8,128)(2,1)} %param.31), channel_id=1, source_target_pairs={{0,16},{8,24},{16,0},{24,8},{1,17},{9,25},{17,1},{25,9},{2,18},{10... | collective-permute-start | bytes 6291464 | tf_op jit(solution)/shard_map/ppermute | solution.py:72
  280.7 90.9 %collective-permute-start.17 = (bf16[2,512,1024]{2,1,0:T(8,128)(2,1)}, bf16[2,512,1024]{2,1,0:T(8,128)(2,1)}, u32[]{:S(2)}, u32[]{:S(2)}) collective-permute-start(bf16[2,512,1024]{2,1,0:T(8,128)(2,1)} %param.32), channel_id=1, source_target_pairs={{0,8},{8,0},{16,24},{24,16},{1,9},{9,1},{17,25},{25,17},{2,10},{10... | collective-permute-start | bytes 6291464 | tf_op jit(solution)/shard_map/ppermute | solution.py:68
  281.3 180.0 %collective-permute-start.18 = (bf16[2,512,1024]{2,1,0:T(8,128)(2,1)}, bf16[2,512,1024]{2,1,0:T(8,128)(2,1)}, u32[]{:S(2)}, u32[]{:S(2)}) collective-permute-start(bf16[2,512,1024]{2,1,0:T(8,128)(2,1)} %param.32), channel_id=1, source_target_pairs={{0,16},{8,24},{16,0},{24,8},{1,17},{9,25},{17,1},{25,9},{2,18},{10... | collective-permute-start | bytes 6291464 | tf_op jit(solution)/shard_map/ppermute | solution.py:72
  299.4 180.5 %collective-permute-start.16 = (bf16[2,512,1024]{2,1,0:T(8,128)(2,1)}, bf16[2,512,1024]{2,1,0:T(8,128)(2,1)}, u32[]{:S(2)}, u32[]{:S(2)}) collective-permute-start(bf16[2,512,1024]{2,1,0:T(8,128)(2,1)} %param.31), channel_id=1, source_target_pairs={{0,24},{8,16},{16,8},{24,0},{1,25},{9,17},{17,9},{25,1},{2,26},{10... | collective-permute-start | bytes 6291464 | tf_op jit(solution)/shard_map/ppermute | solution.py:76
  326.6 155.2 %collective-permute-start.19 = (bf16[2,512,1024]{2,1,0:T(8,128)(2,1)}, bf16[2,512,1024]{2,1,0:T(8,128)(2,1)}, u32[]{:S(2)}, u32[]{:S(2)}) collective-permute-start(bf16[2,512,1024]{2,1,0:T(8,128)(2,1)} %param.32), channel_id=1, source_target_pairs={{0,24},{8,16},{16,8},{24,0},{1,25},{9,17},{17,9},{25,1},{2,26},{10... | collective-permute-start | bytes 6291464 | tf_op jit(solution)/shard_map/ppermute | solution.py:76
  329.1 177.4 %collective-permute-start.20 = (bf16[2,256,2048]{2,1,0:T(8,128)(2,1)}, bf16[2,256,2048]{2,1,0:T(8,128)(2,1)}, u32[]{:S(2)}, u32[]{:S(2)}) collective-permute-start(bf16[2,256,2048]{2,1,0:T(8,128)(2,1)} %param.33), channel_id=1, source_target_pairs={{0,8},{8,0},{16,24},{24,16},{1,9},{9,1},{17,25},{25,17},{2,10},{10... | collective-permute-start | bytes 6291464 | tf_op jit(solution)/shard_map/ppermute | solution.py:68
  371.6 179.6 %collective-permute-start.21 = (bf16[2,256,2048]{2,1,0:T(8,128)(2,1)}, bf16[2,256,2048]{2,1,0:T(8,128)(2,1)}, u32[]{:S(2)}, u32[]{:S(2)}) collective-permute-start(bf16[2,256,2048]{2,1,0:T(8,128)(2,1)} %param.33), channel_id=1, source_target_pairs={{0,16},{8,24},{16,0},{24,8},{1,17},{9,25},{17,1},{25,9},{2,18},{10... | collective-permute-start | bytes 6291464 | tf_op jit(solution)/shard_map/ppermute | solution.py:72
  461.2 93.1 %collective-permute-start.22 = (bf16[2,256,2048]{2,1,0:T(8,128)(2,1)}, bf16[2,256,2048]{2,1,0:T(8,128)(2,1)}, u32[]{:S(2)}, u32[]{:S(2)}) collective-permute-start(bf16[2,256,2048]{2,1,0:T(8,128)(2,1)} %param.33), channel_id=1, source_target_pairs={{0,24},{8,16},{16,8},{24,0},{1,25},{9,17},{17,9},{25,1},{2,26},{10... | collective-permute-start | bytes 6291464 | tf_op jit(solution)/shard_map/ppermute | solution.py:76
  485.3 65.9 %copy-start.24 = (bf16[2,2048,1024]{2,1,0:T(8,128)(2,1)}, bf16[2,2048,1024]{2,1,0:T(8,128)(2,1)S(1)}, u32[]{:S(2)}) copy-start(bf16[2,2048,1024]{2,1,0:T(8,128)(2,1)S(1)} %constant_dynamic-update-slice_fusion.9.wu_ref) | copy-start | bytes 25165828
  741.8 28.6 %all-to-all-start.1 = ((f32[8,384,2]{1,2,0:T(2,128)}), f32[8,384,2]{1,2,0:T(2,128)S(1)}, u32[]{:S(2)}, u32[]{:S(2)}) async-start(f32[8,384,2]{1,2,0:T(2,128)} %copy.270), calls=%async_computation.3 | async-start | bytes 49152 | tf_op jit(solution)/shard_map/all_to_all | solution.py:621
  745.1 622.1 %reduce-scatter.16.cloned.1.call-start = ((), (), s32[]{:S(2)}) async-start(), calls=%async_computation.15 | async-start | bytes 1081344
  745.2 122.7 %copy-start.35 = (f32[2048]{0:T(1024)S(1)}, f32[2048]{0:T(1024)}, u32[]{:S(2)}) copy-start(f32[2048]{0:T(1024)} %copy-done.34) | copy-start | bytes 24580
  874.5 552.8 %reduce-scatter.8.cloned.1.call-start = ((), (), s32[]{:S(2)}) async-start(), calls=%async_computation.11 | async-start | bytes 14155776 | tf_op jit(solution)/shard_map/reduce_scatter | solution.py:640
  895.0 539.0 %reduce-scatter.12.cloned.1.call-start = ((), (), s32[]{:S(2)}) async-start(), calls=%async_computation.13 | async-start | bytes 7077888 | tf_op jit(solution)/shard_map/reduce_scatter | solution.py:698
  901.3 35.7 %collective-permute-start.23 = (bf16[384,2048]{1,0:T(8,128)(2,1)}, bf16[384,2048]{1,0:T(8,128)(2,1)S(1)}, u32[]{:S(2)}, u32[]{:S(2)}) collective-permute-start(bf16[384,2048]{1,0:T(8,128)(2,1)} %fusion.72), channel_id=1, source_target_pairs={{0,8},{8,0},{16,24},{24,16},{1,9},{9,1},{17,25},{25,17},{2,10},{10... | collective-permute-start | bytes 4718600 | tf_op jit(solution)/shard_map/ppermute | solution.py:68
  902.9 37.2 %collective-permute-start.24 = (bf16[384,2048]{1,0:T(8,128)(2,1)}, bf16[384,2048]{1,0:T(8,128)(2,1)S(1)}, u32[]{:S(2)}, u32[]{:S(2)}) collective-permute-start(bf16[384,2048]{1,0:T(8,128)(2,1)} %fusion.72), channel_id=1, source_target_pairs={{0,16},{8,24},{16,0},{24,8},{1,17},{9,25},{17,1},{25,9},{2,18},{10... | collective-permute-start | bytes 4718600 | tf_op jit(solution)/shard_map/ppermute | solution.py:72
  937.2 27.9 %collective-permute-start.25 = (bf16[192,2048]{1,0:T(8,128)(2,1)S(1)}, bf16[192,2048]{1,0:T(8,128)(2,1)S(1)}, u32[]{:S(2)}, u32[]{:S(2)}) collective-permute-start(bf16[192,2048]{1,0:T(8,128)(2,1)S(1)} %get-tuple-element.112), channel_id=1, source_target_pairs={{0,16},{8,24},{16,0},{24,8},{1,17},{9,25},{17,1},{25,9},{2,18},{10... | collective-permute-start | bytes 2359304 | tf_op jit(solution)/shard_map/ppermute | solution.py:72
  940.4 24.8 %collective-permute-start.26 = (bf16[192,2048]{1,0:T(8,128)(2,1)S(1)}, bf16[192,2048]{1,0:T(8,128)(2,1)S(1)}, u32[]{:S(2)}, u32[]{:S(2)}) collective-permute-start(bf16[192,2048]{1,0:T(8,128)(2,1)S(1)} %get-tuple-element.110), channel_id=1, source_target_pairs={{0,8},{8,0},{16,24},{24,16},{1,9},{9,1},{17,25},{25,17},{2,10},{10... | collective-permute-start | bytes 2359304 | tf_op jit(solution)/shard_map/ppermute | solution.py:68
  1025.9 14.7 collective-permute-start.28
  1028.1 12.9 collective-permute-start.29
  1029.7 11.4 collective-permute-start.27
  1036.2 72.8 %collective-permute-start.39 = (bf16[2,512,1024]{2,1,0:T(8,128)(2,1)}, bf16[2,512,1024]{2,1,0:T(8,128)(2,1)}, u32[]{:S(2)}, u32[]{:S(2)}) collective-permute-start(bf16[2,512,1024]{2,1,0:T(8,128)(2,1)} %get-tuple-element.95), channel_id=1, source_target_pairs={{0,24},{8,16},{16,8},{24,0},{1,25},{9,17},{17,9},{25,1},{2,26},{10... | collective-permute-start | bytes 6291464 | tf_op jit(solution)/shard_map/ppermute | solution.py:76
  1039.1 91.9 %collective-permute-start.38 = (bf16[2,512,1024]{2,1,0:T(8,128)(2,1)}, bf16[2,512,1024]{2,1,0:T(8,128)(2,1)}, u32[]{:S(2)}, u32[]{:S(2)}) collective-permute-start(bf16[2,512,1024]{2,1,0:T(8,128)(2,1)} %get-tuple-element.96), channel_id=1, source_target_pairs={{0,16},{8,24},{16,0},{24,8},{1,17},{9,25},{17,1},{25,9},{2,18},{10... | collective-permute-start | bytes 6291464 | tf_op jit(solution)/shard_map/ppermute | solution.py:72
  1040.5 122.3 %collective-permute-start.37 = (bf16[2,512,1024]{2,1,0:T(8,128)(2,1)}, bf16[2,512,1024]{2,1,0:T(8,128)(2,1)}, u32[]{:S(2)}, u32[]{:S(2)}) collective-permute-start(bf16[2,512,1024]{2,1,0:T(8,128)(2,1)} %get-tuple-element.94), channel_id=1, source_target_pairs={{0,8},{8,0},{16,24},{24,16},{1,9},{9,1},{17,25},{25,17},{2,10},{10... | collective-permute-start | bytes 6291464 | tf_op jit(solution)/shard_map/ppermute | solution.py:68
  1056.9 382.7 %reduce-scatter.14.cloned.1.call-start = ((), (), s32[]{:S(2)}) async-start(), calls=%async_computation.14 | async-start | bytes 2359296 | tf_op jit(solution)/shard_map/reduce_scatter | solution.py:695
  1085.4 118.5 %collective-permute-start.42 = (bf16[2,512,1024]{2,1,0:T(8,128)(2,1)}, bf16[2,512,1024]{2,1,0:T(8,128)(2,1)}, u32[]{:S(2)}, u32[]{:S(2)}) collective-permute-start(bf16[2,512,1024]{2,1,0:T(8,128)(2,1)} %get-tuple-element.92), channel_id=1, source_target_pairs={{0,24},{8,16},{16,8},{24,0},{1,25},{9,17},{17,9},{25,1},{2,26},{10... | collective-permute-start | bytes 6291464 | tf_op jit(solution)/shard_map/ppermute | solution.py:76
  1088.3 126.4 %collective-permute-start.41 = (bf16[2,512,1024]{2,1,0:T(8,128)(2,1)}, bf16[2,512,1024]{2,1,0:T(8,128)(2,1)}, u32[]{:S(2)}, u32[]{:S(2)}) collective-permute-start(bf16[2,512,1024]{2,1,0:T(8,128)(2,1)} %get-tuple-element.93), channel_id=1, source_target_pairs={{0,16},{8,24},{16,0},{24,8},{1,17},{9,25},{17,1},{25,9},{2,18},{10... | collective-permute-start | bytes 6291464 | tf_op jit(solution)/shard_map/ppermute | solution.py:72
  1109.8 147.1 %collective-permute-start.40 = (bf16[2,512,1024]{2,1,0:T(8,128)(2,1)S(1)}, bf16[2,512,1024]{2,1,0:T(8,128)(2,1)}, u32[]{:S(2)}, u32[]{:S(2)}) collective-permute-start(bf16[2,512,1024]{2,1,0:T(8,128)(2,1)S(1)} %copy-done.31), channel_id=1, source_target_pairs={{0,8},{8,0},{16,24},{24,16},{1,9},{9,1},{17,25},{25,17},{2,10},{10... | collective-permute-start | bytes 6291464 | tf_op jit(solution)/shard_map/ppermute | solution.py:68
  1131.0 123.6 %collective-permute-start.30 = (bf16[2,192,2048]{2,1,0:T(8,128)(2,1)}, bf16[2,192,2048]{2,1,0:T(8,128)(2,1)}, u32[]{:S(2)}, u32[]{:S(2)}) collective-permute-start(bf16[2,192,2048]{2,1,0:T(8,128)(2,1)} %pad_maximum_fusion.8), channel_id=1, source_target_pairs={{0,8},{8,0},{16,24},{24,16},{1,9},{9,1},{17,25},{25,17},{2,10},{10... | collective-permute-start | bytes 4718600 | tf_op jit(solution)/shard_map/ppermute | solution.py:68
  1162.8 95.6 %slice-start.5 = ((s8[6291456]{0:T(1024)(128)(4,1)}), s8[4194304]{0:T(1024)(128)(4,1)S(1)}, s32[]{:S(2)}) async-start(s8[6291456]{0:T(1024)(128)(4,1)} %bitcast.221), calls=%async_computation.21 | async-start | bytes 8388608
  1162.8 95.6 %slice-start.6 = ((s8[6291456]{0:T(1024)(128)(4,1)}), s8[2097152]{0:T(1024)(128)(4,1)S(1)}, s32[]{:S(2)}) async-start(s8[6291456]{0:T(1024)(128)(4,1)} %bitcast.221), calls=%async_computation.22 | async-start | bytes 4194304
  1162.8 197.2 %collective-permute-start.45 = (bf16[2,256,2048]{2,1,0:T(8,128)(2,1)}, bf16[2,256,2048]{2,1,0:T(8,128)(2,1)}, u32[]{:S(2)}, u32[]{:S(2)}) collective-permute-start(bf16[2,256,2048]{2,1,0:T(8,128)(2,1)} %get-tuple-element.89), channel_id=1, source_target_pairs={{0,24},{8,16},{16,8},{24,0},{1,25},{9,17},{17,9},{25,1},{2,26},{10... | collective-permute-start | bytes 6291464 | tf_op jit(solution)/shard_map/ppermute | solution.py:76
  1202.7 55.8 %copy-start.12 = (bf16[1536,512]{1,0:T(8,128)(2,1)S(1)}, bf16[1536,512]{1,0:T(8,128)(2,1)}, u32[]{:S(2)}) copy-start(bf16[1536,512]{1,0:T(8,128)(2,1)} %copy-done.11) | copy-start | bytes 4718596
  1203.9 156.1 %collective-permute-start.44 = (bf16[2,256,2048]{2,1,0:T(8,128)(2,1)}, bf16[2,256,2048]{2,1,0:T(8,128)(2,1)}, u32[]{:S(2)}, u32[]{:S(2)}) collective-permute-start(bf16[2,256,2048]{2,1,0:T(8,128)(2,1)} %get-tuple-element.90), channel_id=1, source_target_pairs={{0,16},{8,24},{16,0},{24,8},{1,17},{9,25},{17,1},{25,9},{2,18},{10... | collective-permute-start | bytes 6291464 | tf_op jit(solution)/shard_map/ppermute | solution.py:72
  1214.7 145.3 %collective-permute-start.43 = (bf16[2,256,2048]{2,1,0:T(8,128)(2,1)}, bf16[2,256,2048]{2,1,0:T(8,128)(2,1)}, u32[]{:S(2)}, u32[]{:S(2)}) collective-permute-start(bf16[2,256,2048]{2,1,0:T(8,128)(2,1)} %get-tuple-element.88), channel_id=1, source_target_pairs={{0,8},{8,0},{16,24},{24,16},{1,9},{9,1},{17,25},{25,17},{2,10},{10... | collective-permute-start | bytes 6291464 | tf_op jit(solution)/shard_map/ppermute | solution.py:68
  1254.5 83.8 %collective-permute-start.32 = (bf16[2,192,2048]{2,1,0:T(8,128)(2,1)}, bf16[2,192,2048]{2,1,0:T(8,128)(2,1)}, u32[]{:S(2)}, u32[]{:S(2)}) collective-permute-start(bf16[2,192,2048]{2,1,0:T(8,128)(2,1)} %pad_maximum_fusion.9), channel_id=1, source_target_pairs={{0,16},{8,24},{16,0},{24,8},{1,17},{9,25},{17,1},{25,9},{2,18},{10... | collective-permute-start | bytes 4718600 | tf_op jit(solution)/shard_map/ppermute | solution.py:72
  1256.9 98.0 %collective-permute-start.31 = (bf16[192,2048]{1,0:T(8,128)(2,1)S(1)}, bf16[192,2048]{1,0:T(8,128)(2,1)S(1)}, u32[]{:S(2)}, u32[]{:S(2)}) collective-permute-start(bf16[192,2048]{1,0:T(8,128)(2,1)S(1)} %fusion.24), channel_id=1, source_target_pairs={{0,16},{8,24},{16,0},{24,8},{1,17},{9,25},{17,1},{25,9},{2,18},{10... | collective-permute-start | bytes 2359304 | tf_op jit(solution)/shard_map/ppermute | solution.py:72
  1359.0 19.5 %collective-permute-start.33 = (bf16[192,2048]{1,0:T(8,128)(2,1)S(1)}, bf16[192,2048]{1,0:T(8,128)(2,1)S(1)}, u32[]{:S(2)}, u32[]{:S(2)}) collective-permute-start(bf16[192,2048]{1,0:T(8,128)(2,1)S(1)} %get-tuple-element.73), channel_id=1, source_target_pairs={{0,8},{8,0},{16,24},{24,16},{1,9},{9,1},{17,25},{25,17},{2,10},{10... | collective-permute-start | bytes 2359304 | tf_op jit(solution)/shard_map/ppermute | solution.py:68
  1435.2 12.3 collective-permute-start.34
  1437.5 15.9 %collective-permute-start.35 = (bf16[1,64,1536]{2,1,0:T(8,128)(2,1)S(1)}, bf16[1,64,1536]{2,1,0:T(8,128)(2,1)S(1)}, u32[]{:S(2)}, u32[]{:S(2)}) collective-permute-start(bf16[1,64,1536]{2,1,0:T(8,128)(2,1)S(1)} %get-tuple-element.128), channel_id=1, source_target_pairs={{0,16},{8,24},{16,0},{24,8},{1,17},{9,25},{17,1},{25,9},{2,18},{10... | collective-permute-start | bytes 589832 | tf_op jit(solution)/shard_map/ppermute | solution.py:72
  1437.9 21.4 %collective-permute-start.36 = (bf16[1,64,1536]{2,1,0:T(8,128)(2,1)S(1)}, bf16[1,64,1536]{2,1,0:T(8,128)(2,1)S(1)}, u32[]{:S(2)}, u32[]{:S(2)}) collective-permute-start(bf16[1,64,1536]{2,1,0:T(8,128)(2,1)S(1)} %get-tuple-element.127), channel_id=1, source_target_pairs={{0,24},{8,16},{16,8},{24,0},{1,25},{9,17},{17,9},{25,1},{2,26},{10... | collective-permute-start | bytes 589832 | tf_op jit(solution)/shard_map/ppermute | solution.py:76
  (63 other events, 621.5 us)
Sparse Core Ops, SparseCore 0:
  32.0 69.3 all-gather.4
  103.0 27.7 all-gather.6
  132.4 116.2 all-gather.10
  266.1 115.4 all-gather.8
  738.7 129.0 reduce-scatter.9
  874.7 134.5 reduce-scatter.15
  1011.6 125.5 reduce-scatter.7
  1139.7 68.1 reduce-scatter.11
  1263.5 34.1 reduce-scatter.13

commit v3 on v2

v3 whole, which is shorter than its diff:
```python
import functools
import math

import jax
import jax.numpy as jnp
from jax import lax
from jax.experimental import pallas as pl
from jax.experimental.pallas import tpu as pltpu
from jax.sharding import PartitionSpec as P

D = 2048
HEADS = 16
HD = 128
TOP = 8
PROMPT = 1024
CONT = 2
CTOK = 512

epsilon = 1e-05
rope_base = 10000.0
BF = jnp.bfloat16
F32 = jnp.float32
BOTH = ("ctx", "exp")
X_PAIRS = [(i, i ^ 1) for i in range(4)]
Y_PAIRS = [(i, i ^ 2) for i in range(4)]
XY_PAIRS = [(i, i ^ 3) for i in range(4)]
NT = (((1,), (1,)), ((), ()))
TN = (((0,), (0,)), ((), ()))
TILE = 256
WIN = 512
NOWHERE = -(1 << 20)


def inverse_root(values):
    return lax.rsqrt(jnp.mean(values * values, axis=-1, keepdims=True) + epsilon)


def norm_back(gradient, normed, root_part):
    return root_part * (gradient - normed * jnp.mean(gradient * normed, axis=-1, keepdims=True))


def angles(position):
    half_dim = HD // 2
    inverse = rope_base ** (-2.0 * jnp.arange(half_dim, dtype=F32) / HD)
    phases = position.astype(F32)[:, None] * inverse[None, :]
    cosine, sine = jnp.cos(phases), jnp.sin(phases)
    return jnp.concatenate([cosine, cosine], axis=1), jnp.concatenate([-sine, sine], axis=1)


def send_x(value):
    return lax.ppermute(value, "ctx", X_PAIRS)


def send_y(value):
    return lax.ppermute(value, "ctx", Y_PAIRS)


def send_xy(value):
    return lax.ppermute(value, "ctx", XY_PAIRS)


def after(value, *others):
    return lax.optimization_barrier((value,) + others)[0]


def after_all(values, *others):
    return lax.optimization_barrier(tuple(values) + others)[: len(values)]


def gather_pieces(value, half):
    from_x = send_x(value)
    from_y = send_y(value)
    far_low = send_y(from_x[:half])
    far_high = send_x(from_y[half:])
    return from_x, from_y, far_low, far_high


def scatter_payload(take, me):
    low = jnp.stack([take(me ^ 1, 0), take(me ^ 3, 0)]).astype(BF)
    high = jnp.stack([take(me ^ 2, 1), take(me ^ 3, 1)]).astype(BF)
    return low, high


def scatter_first(take, me):
    low, high = scatter_payload(take, me)
    return send_x(low), send_y(high)


def scatter_second(take, me, low, high):
    low_next = send_y((take(me ^ 2, 0).astype(F32) + low[1].astype(F32)).astype(BF))
    high_next = send_x((take(me ^ 1, 1).astype(F32) + high[1].astype(F32)).astype(BF))
    return low_next, high_next


def scatter_end(take, me, low, high, low_next, high_next):
    first = take(me, 0).astype(F32) + low[0].astype(F32) + low_next.astype(F32)
    second = take(me, 1).astype(F32) + high[0].astype(F32) + high_next.astype(F32)
    return first, second


def exchange(blocks, me):
    if lax.axis_size("ctx") != 4:
        return lax.all_to_all(blocks, "ctx", split_axis=0, concat_axis=0, tiled=True)
    sends = (lambda part: part, send_x, send_y, send_xy)
    whole = jnp.zeros_like(blocks)
    for away, send in enumerate(sends):
        part = send(lax.dynamic_slice_in_dim(blocks, me ^ away, 1, 0))
        whole = lax.dynamic_update_slice_in_dim(whole, part, me ^ away, 0)
    return whole


def sum_over_ctx(value):
    if lax.axis_size("ctx") != 4:
        return lax.psum(value, "ctx")
    value = value + send_x(value)
    return value + send_y(value)


def sum_to_rows(values, me):
    ctx_size, exp_size = lax.axis_size("ctx"), lax.axis_size("exp")
    count, width = values.shape
    parts = values.reshape(count, ctx_size, exp_size, width // (ctx_size * exp_size))
    parts = jnp.transpose(parts, (2, 1, 0, 3))
    parts = jnp.sum(lax.all_to_all(parts, "exp", split_axis=0, concat_axis=0, tiled=True), axis=0)
    return jnp.sum(exchange(parts, me), axis=0)


def gather_expert(w_gate, w_up, w_down, me):
    if lax.axis_size("ctx") != 4:
        return (
            lax.all_gather(jnp.stack([w_gate, w_up]), "ctx", axis=1, tiled=True),
            lax.all_gather(w_down, "ctx", axis=0, tiled=True),
        )
    width = w_gate.shape[1]
    packed = jnp.concatenate([w_gate, w_up, w_down[:, :width], w_down[:, width:]], axis=0)
    return packed, send_x(packed), send_y(packed)


def gather_expert_far(near):
    if lax.axis_size("ctx") != 4:
        return ()
    half = near[1].shape[0] // 2
    return send_y(near[1][:half]), send_x(near[2][half:])


def build_expert(w_gate, w_down, near, far, me):
    if lax.axis_size("ctx") != 4:
        return near
    rows, width = w_gate.shape
    half = rows // 2
    both = jnp.zeros((2, 4 * rows, width), BF)
    down = jnp.zeros((2 * rows, 2 * width), BF)

    def put_both(whole, part, owner, which, first):
        return lax.dynamic_update_slice(whole, part[None], (which, owner * rows + first, 0))

    def put_down(whole, part, owner, which):
        return lax.dynamic_update_slice(whole, part, (owner * half, which * width))

    for away, part in enumerate(near):
        both = put_both(both, part[:rows], me ^ away, 0, 0)
        both = put_both(both, part[rows : 2 * rows], me ^ away, 1, 0)
        down = put_down(down, part[2 * rows : 2 * rows + half], me ^ away, 0)
        down = put_down(down, part[2 * rows + half :], me ^ away, 1)
    low, high = far
    both = put_both(both, low[:rows], me ^ 3, 0, 0)
    both = put_both(both, low[rows:], me ^ 3, 1, 0)
    both = put_both(both, high[:half], me ^ 3, 1, half)
    down = put_down(down, high[half:rows], me ^ 3, 0)
    down = put_down(down, high[rows:], me ^ 3, 1)
    return both, down


def expert_take(grads):
    gate_up, down = grads
    rows, width = gate_up.shape[0] // 4, gate_up.shape[1] // 2
    half = down.shape[0] // 8

    def take(owner, part):
        first = (2 * owner + part) * half
        return jnp.concatenate(
            [
                lax.dynamic_slice(gate_up, (owner * rows, part * width), (rows, width)),
                lax.dynamic_slice(down, (first, 0), (half, width)),
                lax.dynamic_slice(down, (first, width), (half, width)),
            ],
            axis=0,
        )

    return take


def scatter_expert_first(grads, me):
    if lax.axis_size("ctx") != 4:
        return tuple(
            lax.psum_scatter(grad, "ctx", scatter_dimension=0, tiled=True) for grad in grads
        )
    return scatter_first(expert_take(grads), me)


def scatter_expert_second(grads, sums, me):
    if lax.axis_size("ctx") != 4:
        return ()
    return scatter_second(expert_take(grads), me, *sums)


def scatter_expert_end(grads, sums, more, me):
    if lax.axis_size("ctx") != 4:
        gate_up, down = (part.astype(F32) for part in sums)
        width = gate_up.shape[1] // 2
        return gate_up[:, :width], gate_up[:, width:], down
    first, second = scatter_end(expert_take(grads), me, *sums, *more)
    rows, half = grads[0].shape[0] // 4, grads[1].shape[0] // 8
    down = [
        jnp.concatenate([part[rows : rows + half], part[rows + half :]], axis=1)
        for part in (first, second)
    ]
    return first[:rows], second[:rows], jnp.concatenate(down, axis=0)


def pick_blocks(blocks, order):
    return jnp.concatenate(
        [
            lax.dynamic_index_in_dim(blocks, order[i], 0, keepdims=False)
            for i in range(order.shape[0])
        ],
        axis=0,
    )


def gather_group(rows, slot_table, me):
    block = rows.shape[0] // 2
    if lax.axis_size("ctx") != 4:
        blocks = slot_table.shape[0]
        whole = lax.all_gather(rows, "ctx", axis=0, tiled=True).reshape(blocks, block, -1)
        match = slot_table[None, :] == jnp.arange(blocks, dtype=jnp.int32)[:, None]
        order = jnp.sum(jnp.where(match, jnp.arange(blocks, dtype=jnp.int32)[None, :], 0), axis=1)
        return pick_blocks(whole, order), ()
    from_x, from_y, far_low, far_high = gather_pieces(rows, block)
    parts = (
        (rows[:block], me, 0),
        (rows[block:], me, 1),
        (from_x[:block], me ^ 1, 0),
        (from_x[block:], me ^ 1, 1),
        (from_y[:block], me ^ 2, 0),
        (from_y[block:], me ^ 2, 1),
        (far_low, me ^ 3, 0),
        (far_high, me ^ 3, 1),
    )
    whole = jnp.zeros((8 * block, rows.shape[1]), rows.dtype)
    for part, owner, slot in parts:
        start = slot_table[2 * owner + slot] * block
        whole = lax.dynamic_update_slice(whole, part, (start, 0))
    return whole, (far_low, far_high)


def scatter_group(partial, slot_table, me):
    blocks = slot_table.shape[0]
    block = partial.shape[0] // blocks
    if lax.axis_size("ctx") != 4:
        ordered = pick_blocks(partial.reshape(blocks, block, -1), slot_table).astype(BF)
        whole = lax.psum_scatter(ordered, "ctx", scatter_dimension=0, tiled=True)
        return whole.astype(F32), (ordered,), (whole,)

    def take(owner, part):
        start = slot_table[2 * owner + part] * block
        return lax.dynamic_slice(partial, (start, 0), (block, partial.shape[1]))

    sent = scatter_payload(take, me)
    near = send_x(sent[0]), send_y(sent[1])
    far = scatter_second(take, me, *near)
    return jnp.concatenate(scatter_end(take, me, *near, *far), axis=0), sent, far


def prefix_count(member):
    rows, columns = member.shape
    width = 128
    blocks = rows // width
    ones = member.astype(BF).reshape(blocks, width, columns)
    lower = (
        jnp.arange(width)[:, None] > jnp.arange(width)[None, :]
    ).astype(BF)
    inner = jnp.einsum("pq,bqc->bpc", lower, ones, preferred_element_type=F32)
    totals = jnp.sum(ones.astype(F32), axis=1)
    before = (jnp.arange(blocks)[:, None] > jnp.arange(blocks)[None, :]).astype(F32)
    outer = jnp.sum(before[:, :, None] * totals[None, :, :], axis=1)
    return (inner + outer[:, None, :]).reshape(rows, columns).astype(jnp.int32)


def dot(left, right, dims=(((1,), (0,)), ((), ()))):
    return lax.dot_general(left, right, dims, preferred_element_type=F32)


def turned(values, cosine, sine):
    return values * cosine + pltpu.roll(values, HD // 2, 1) * sine


def tile_weights(query, key, seg_q, seg_k, first, factor):
    rows, width = query.shape[0], key.shape[0]
    scores = dot(query, key, NT) * factor
    q_place = first + lax.broadcasted_iota(jnp.int32, (rows, width), 0)
    k_place = lax.broadcasted_iota(jnp.int32, (rows, width), 1)
    allowed = k_place <= q_place
    if first >= PROMPT:
        allowed = allowed & ((seg_k < 0) | (seg_k == seg_q))
    scores = jnp.where(allowed, scores, -1e30)
    weights = jnp.exp(scores - jnp.max(scores, axis=1, keepdims=True))
    return weights, jnp.sum(weights, axis=1, keepdims=True)


def attend_kernel(
    tiles,
    factor,
    qp_ref,
    kp_ref,
    vp_ref,
    root_ref,
    key_root_ref,
    gain_ref,
    cos_ref,
    sin_ref,
    sq_ref,
    sk_ref,
    q_ref,
    k_ref,
    v_ref,
    o_ref,
):
    at = pl.program_id(1)
    tile = qp_ref.shape[0]

    @pl.when(at == 0)
    def _():
        keys = kp_ref[...] * key_root_ref[:, 1:2] * gain_ref[1:2]
        k_ref[...] = turned(keys, cos_ref[...], sin_ref[...]).astype(BF)
        v_ref[...] = vp_ref[...].astype(BF)

    for i in range(tiles):

        @pl.when(at == i)
        def _():
            own = slice(i * tile, (i + 1) * tile)
            width = (i + 1) * tile
            queries = qp_ref[...] * root_ref[:, 0:1] * gain_ref[0:1]
            query = turned(queries, cos_ref[own], sin_ref[own]).astype(BF)
            q_ref[...] = query
            weights, total = tile_weights(
                query, k_ref[:width], sq_ref[...], sk_ref[:, :width], i * tile, factor
            )
            o_ref[...] = (dot(weights.astype(BF), v_ref[:width]) / total).astype(BF)


def attend(projected, roots, gains, cosine, sine, seg, width, tile=512):
    rows = projected.shape[0]
    heads, tiles = width // HD, rows // tile
    own = pl.BlockSpec((tile, HD), lambda h, i: (i, h))
    whole = pl.BlockSpec((rows, HD), lambda h, i: (0, h))
    pairs = heads * rows * rows * (tiles + 1) // (2 * tiles)
    return pl.pallas_call(
        functools.partial(attend_kernel, tiles, 1.0 / math.sqrt(HD)),
        out_shape=[jax.ShapeDtypeStruct((rows, width), BF)] * 4,
        grid=(heads, tiles),
        in_specs=[
            own,
            pl.BlockSpec((rows, HD), lambda h, i: (0, heads + h)),
            pl.BlockSpec((rows, HD), lambda h, i: (0, 2 * heads + h)),
            pl.BlockSpec((tile, 2), lambda h, i: (i, 0)),
            pl.BlockSpec((rows, 2), lambda h, i: (0, 0)),
            pl.BlockSpec((2, HD), lambda h, i: (0, h)),
            pl.BlockSpec((rows, HD), lambda h, i: (0, 0)),
            pl.BlockSpec((rows, HD), lambda h, i: (0, 0)),
            pl.BlockSpec((tile, 1), lambda h, i: (i, 0)),
            pl.BlockSpec((1, rows), lambda h, i: (0, 0)),
        ],
        out_specs=[own, whole, whole, own],
        compiler_params=pltpu.CompilerParams(vmem_limit_bytes=48 << 20),
        cost_estimate=pl.CostEstimate(
            flops=4 * pairs * HD, bytes_accessed=20 * rows * width, transcendentals=pairs
        ),
    )(
        projected,
        projected,
        projected,
        roots,
        roots,
        gains,
        cosine,
        sine,
        seg[:, None],
        seg[None, :],
    )


def attend_back_kernel(
    tiles,
    factor,
    q_ref,
    k_ref,
    v_ref,
    d_ref,
    cos_ref,
    sin_ref,
    sq_ref,
    sk_ref,
    dq_ref,
    dk_ref,
    dv_ref,
):
    at = pl.program_id(1)
    tile = q_ref.shape[0]

    @pl.when(at == 0)
    def _():
        dk_ref[...] = jnp.zeros_like(dk_ref)
        dv_ref[...] = jnp.zeros_like(dv_ref)

    for i in range(tiles):

        @pl.when(at == i)
        def _():
            own = slice(i * tile, (i + 1) * tile)
            width = (i + 1) * tile
            query, grad = q_ref[...], d_ref[...]
            weights, total = tile_weights(
                query, k_ref[:width], sq_ref[...], sk_ref[:, :width], i * tile, factor
            )
            weights = weights / total
            grad_weights = dot(grad, v_ref[:width], NT)
            delta = jnp.sum(weights * grad_weights, axis=1, keepdims=True)
            grad_scores = (weights * (grad_weights - delta)).astype(BF)
            grad_query = dot(grad_scores, k_ref[:width]) * factor
            dq_ref[...] = turned(grad_query, cos_ref[own], -sin_ref[own])
            dk_ref[:width] += dot(grad_scores, query, TN)
            dv_ref[:width] += dot(weights.astype(BF), grad, TN)

    @pl.when(at == tiles - 1)
    def _():
        dk_ref[...] = turned(dk_ref[...] * factor, cos_ref[...], -sin_ref[...])


def attend_back(q, k, v, grad, cosine, sine, seg, tile=512):
    rows, width = q.shape
    heads, tiles = width // HD, rows // tile
    own = pl.BlockSpec((tile, HD), lambda h, i: (i, h))
    whole = pl.BlockSpec((rows, HD), lambda h, i: (0, h))
    table = pl.BlockSpec((rows, HD), lambda h, i: (0, 0))
    pairs = heads * rows * rows * (tiles + 1) // (2 * tiles)
    return pl.pallas_call(
        functools.partial(attend_back_kernel, tiles, 1.0 / math.sqrt(HD)),
        out_shape=[jax.ShapeDtypeStruct((rows, width), F32)] * 3,
        grid=(heads, tiles),
        in_specs=[
            own,
            whole,
            whole,
            own,
            table,
            table,
            pl.BlockSpec((tile, 1), lambda h, i: (i, 0)),
            pl.BlockSpec((1, rows), lambda h, i: (0, 0)),
        ],
        out_specs=[own, whole, whole],
        compiler_params=pltpu.CompilerParams(vmem_limit_bytes=48 << 20),
        cost_estimate=pl.CostEstimate(
            flops=10 * pairs * HD, bytes_accessed=20 * rows * width, transcendentals=pairs
        ),
    )(q, k, v, grad, cosine, sine, seg[:, None], seg[None, :])


def pick_rows(tok, low, windows, source_ref, acc_ref):
    last = source_ref.shape[0] - WIN
    span = lax.broadcasted_iota(jnp.int32, (TILE, WIN), 1)

    def window(j):
        base = low + j * WIN
        start = pl.multiple_of(jnp.minimum(base, last), 128)
        match = (tok - start == span) & (tok >= base)
        return dot(match.astype(F32).astype(BF), source_ref[pl.ds(start, WIN), :])

    acc_ref[...] = window(0)

    @pl.loop(1, windows)
    def _(j):
        acc_ref[...] += window(j)

    return acc_ref[...].astype(BF)


def back_rows_kernel(
    tiles_ref, low_ref, windows_ref, tok_ref, dy_ref, wd_ref, rows_ref, raw_ref, acc_ref
):
    i = pl.program_id(0)

    @pl.when(i < tiles_ref[0])
    def _():
        rows = pick_rows(tok_ref[...], low_ref[i], windows_ref[i], dy_ref, acc_ref)
        rows_ref[...] = rows
        raw_ref[...] = dot(rows, wd_ref[...], NT)

    @pl.when(i >= tiles_ref[0])
    def _():
        rows_ref[...] = jnp.zeros_like(rows_ref)
        raw_ref[...] = jnp.zeros_like(raw_ref)


def back_rows(tables, upstream, w_down):
    total, width = upstream.shape
    ff = w_down.shape[0]
    capacity = tables[3].shape[0]
    tile = lambda n: pl.BlockSpec((TILE, n), lambda i, *_: (i, 0))
    once = lambda shape: pl.BlockSpec(shape, lambda i, *_: (0, 0), pipeline_mode=pl.Buffered(1))
    return pl.pallas_call(
        back_rows_kernel,
        out_shape=[
            jax.ShapeDtypeStruct((capacity, width), BF),
            jax.ShapeDtypeStruct((capacity, ff), F32),
        ],
        grid_spec=pltpu.PrefetchScalarGridSpec(
            num_scalar_prefetch=3,
            grid=(capacity // TILE,),
            in_specs=[tile(1), once((total, width)), once((ff, width))],
            out_specs=[tile(width), tile(ff)],
            scratch_shapes=[pltpu.VMEM((TILE, width), F32)],
        ),
        compiler_params=pltpu.CompilerParams(vmem_limit_bytes=48 << 20),
        cost_estimate=pl.CostEstimate(
            flops=total * (width * ff + WIN * width),
            bytes_accessed=2 * total * width + 2 * ff * width + capacity * (2 * width + 4 * ff),
            transcendentals=0,
        ),
    )(*tables, upstream, w_down)


def expert_kernel(
    own,
    tiles_ref,
    low_ref,
    windows_ref,
    id_ref,
    tok_ref,
    h_ref,
    router_ref,
    wg_ref,
    wu_ref,
    raw_ref,
    rows_ref,
    hid_ref,
    dab_ref,
    dh_ref,
    share_ref,
    acc_ref,
):
    i = pl.program_id(0)
    ff = wg_ref.shape[1]

    @pl.when(i < tiles_ref[0])
    def _():
        rows = pick_rows(tok_ref[...], low_ref[i], windows_ref[i], h_ref, acc_ref)
        rows_ref[...] = rows
        logits = dot(rows, router_ref[...])
        probs = jnp.exp(logits - jnp.max(logits, axis=1, keepdims=True))
        column = lax.broadcasted_iota(jnp.int32, probs.shape, 1)
        mine = jnp.sum(jnp.where(column == id_ref[0] + own, probs, 0.0), axis=1, keepdims=True)
        gate = mine / jnp.sum(probs, axis=1, keepdims=True)
        share = 0.0
        part = ff // 4
        for c in range(4):
            cols = slice(c * part, (c + 1) * part)
            a = dot(rows, wg_ref[:, cols])
            b = dot(rows, wu_ref[:, cols])
            raw = raw_ref[:, cols]
            sig = 1.0 / (1.0 + jnp.exp(-a))
            silu = a * sig
            hid = silu * b
            share += jnp.sum(hid * raw, axis=1, keepdims=True)
            raw = raw * gate
            hid_ref[:, cols] = (hid * gate).astype(BF)
            dab_ref[:, cols] = (raw * b * (sig * (1.0 + a * (1.0 - sig)))).astype(BF)
            dab_ref[:, ff + c * part : ff + (c + 1) * part] = (raw * silu).astype(BF)
        share_ref[...] = share
        dh = dot(dab_ref[:, :ff], wg_ref[...], NT) + dot(dab_ref[:, ff:], wu_ref[...], NT)
        dh_ref[...] = dh.astype(BF)

    @pl.when(i >= tiles_ref[0])
    def _():
        for ref in (rows_ref, hid_ref, dab_ref, dh_ref, share_ref):
            ref[...] = jnp.zeros_like(ref)


def expert_rows(tables, own, first_id, hidden, router, gate_up, raw):
    total, width = hidden.shape
    ff = gate_up.shape[2]
    capacity = tables[3].shape[0]
    tile = lambda n: pl.BlockSpec((TILE, n), lambda i, *_: (i, 0))
    once = lambda shape: pl.BlockSpec(shape, lambda i, *_: (0, 0), pipeline_mode=pl.Buffered(1))
    half = lambda k: pl.BlockSpec(
        (None, width, ff), lambda i, *_: (k, 0, 0), pipeline_mode=pl.Buffered(1)
    )
    made = lambda n, dtype=BF: jax.ShapeDtypeStruct((capacity, n), dtype)
    return pl.pallas_call(
        functools.partial(expert_kernel, own),
        out_shape=[made(width), made(ff), made(2 * ff), made(width), made(1, F32)],
        grid_spec=pltpu.PrefetchScalarGridSpec(
            num_scalar_prefetch=4,
            grid=(capacity // TILE,),
            in_specs=[
                tile(1),
                once((total, width)),
                once(router.shape),
                half(0),
                half(1),
                tile(ff),
            ],
            out_specs=[tile(width), tile(ff), tile(2 * ff), tile(width), tile(1)],
            scratch_shapes=[pltpu.VMEM((TILE, width), F32)],
        ),
        compiler_params=pltpu.CompilerParams(vmem_limit_bytes=56 << 20),
        cost_estimate=pl.CostEstimate(
            flops=total * (4 * width * ff + WIN * width),
            bytes_accessed=2 * total * width + 4 * ff * width + capacity * (4 * width + 10 * ff),
            transcendentals=total * ff,
        ),
    )(*tables[:3], first_id, tables[3], hidden, router, gate_up, gate_up, raw)


def combine_kernel(experts, start_ref, more_ref, wide_ref, pos_ref, *refs):
    rows_refs, share_refs = refs[:experts], refs[experts : 2 * experts]
    out_ref, own_ref, acc_ref = refs[2 * experts :]
    i = pl.program_id(0)
    span = lax.broadcasted_iota(jnp.int32, (TILE, TILE), 1)
    wide_span = lax.broadcasted_iota(jnp.int32, (TILE, 384), 1)
    last = rows_refs[0].shape[0] - TILE

    def window(e, j):
        base = start_ref[e, i] + j * TILE
        start = pl.multiple_of(jnp.minimum(base, last), 16)
        pos = pos_ref[:, e : e + 1]
        match = (pos - start == span) & (pos >= base)
        return dot(match.astype(F32).astype(BF), rows_refs[e][pl.ds(start, TILE), :])

    acc_ref[...] = sum(window(e, 0) for e in range(experts))
    for e in range(experts):
        wide = pl.multiple_of(wide_ref[e, i], 128)
        match = pos_ref[:, e : e + 1] - wide == wide_span
        share = share_refs[e][:, pl.ds(wide, 384)]
        own_ref[:, e : e + 1] = jnp.sum(jnp.where(match, share, 0.0), axis=1, keepdims=True)

        @pl.when(more_ref[e, i] > 0)
        def _():
            acc_ref[...] += window(e, 1)

    out_ref[...] = acc_ref[...].astype(BF)


def combine_rows(tables, rows, shares):
    experts, (capacity, width) = len(rows), rows[0].shape
    total = tables[3].shape[0]
    once = lambda shape: pl.BlockSpec(shape, lambda i, *_: (0, 0), pipeline_mode=pl.Buffered(1))
    tile = lambda n: pl.BlockSpec((TILE, n), lambda i, *_: (i, 0))
    return pl.pallas_call(
        functools.partial(combine_kernel, experts),
        out_shape=[
            jax.ShapeDtypeStruct((total, width), BF),
            jax.ShapeDtypeStruct((total, experts), F32),
        ],
        grid_spec=pltpu.PrefetchScalarGridSpec(
            num_scalar_prefetch=3,
            grid=(total // TILE,),
            in_specs=[tile(experts)]
            + [once((capacity, width))] * experts
            + [once((1, capacity))] * experts,
            out_specs=[tile(width), tile(experts)],
            scratch_shapes=[pltpu.VMEM((TILE, width), F32)],
        ),
        compiler_params=pltpu.CompilerParams(vmem_limit_bytes=48 << 20),
        cost_estimate=pl.CostEstimate(
            flops=2 * experts * total * TILE * width,
            bytes_accessed=2 * (experts * capacity + total) * width,
            transcendentals=0,
        ),
    )(*tables, *rows, *shares)


def local(
    tokens,
    cotangent,
    routes,
    block_of_slot,
    cont_seg,
    w_query,
    w_key,
    w_value,
    w_out,
    w_router,
    attn_gain,
    query_gain,
    key_gain,
    ffn_gain,
    w_gate,
    w_up,
    w_down,
):
    ctx_size = lax.axis_size("ctx")
    exp_size = lax.axis_size("exp")
    me = lax.axis_index("ctx")
    exp_index = lax.axis_index("exp")
    tok_rows = tokens.shape[0]
    part_rows = w_query.shape[0]
    own_width = D // ctx_size
    own_heads = HEADS // ctx_size
    experts = w_router.shape[1]
    own_experts = w_gate.shape[0]
    slot_table = block_of_slot[0]
    seg_row = cont_seg[0]
    group_rows = ctx_size * tok_rows
    factor = 1.0 / math.sqrt(HD)

    tokens_group, tokens_there = gather_group(tokens, slot_table, me)
    small = jnp.concatenate(
        [w_router] + [g[:, None] for g in (attn_gain, query_gain, key_gain, ffn_gain)], axis=1
    )
    small = jnp.pad(small, ((0, 0), (0, 128 - small.shape[1])))
    by_owner = jnp.stack(
        [w.reshape(part_rows, ctx_size, own_width) for w in (w_query, w_key, w_value)], axis=2
    )
    by_owner = jnp.swapaxes(by_owner, 0, 1).reshape(ctx_size, part_rows, 3 * own_width)
    by_owner = jnp.concatenate(
        [by_owner, jnp.broadcast_to(small, (ctx_size,) + small.shape)], axis=2
    )
    own_columns = exchange(by_owner, me)
    packed = lax.all_gather(own_columns, "exp", axis=1, tiled=True).reshape(D, 3 * own_width + 128)
    small_full = packed[:, 3 * own_width :]
    router_full = small_full[:, :experts]
    gains = small_full[:, experts : experts + 4].astype(F32)
    gain_attn, gain_ffn = gains[:, 0], gains[:, 3]
    own_gains = lax.dynamic_slice(gains, (me * own_width, 0), (own_width, 4))
    gain_query, gain_key = own_gains[:, 1], own_gains[:, 2]
    out_full = lax.all_gather(w_out, "exp", axis=0, tiled=True)
    routes_all = lax.all_to_all(
        jnp.broadcast_to(routes[None], (exp_size,) + routes.shape),
        "exp",
        split_axis=0,
        concat_axis=0,
        tiled=True,
    ).reshape(exp_size * tok_rows, TOP)
    upstream_all = lax.all_gather(cotangent, "exp", axis=0, tiled=True)
    first_near = gather_expert(*after_all((w_gate[0], w_up[0], w_down[0]), *tokens_there), me)

    own_ids = exp_index * own_experts + jnp.arange(own_experts, dtype=jnp.int32)
    member = jnp.any(routes_all[:, :, None] == own_ids[None, None, :], axis=1)
    place_of = prefix_count(member)
    capacity = exp_size * 8 * ((5 * tok_rows * TOP // (4 * experts) + 7) // 8)
    row_tiles = (capacity + TILE - 1) // TILE
    capacity = row_tiles * TILE
    all_rows = exp_size * tok_rows
    row_ids = jnp.arange(capacity, dtype=jnp.int32)
    hit = (place_of.T[:, None, :] == row_ids[None, :, None]) & member.T[:, None, :]
    token_ids = jnp.arange(all_rows, dtype=jnp.int32)
    token_of_row = jnp.max(jnp.where(hit, token_ids[None, None, :], -1), axis=2)
    counts = jnp.sum(member.astype(jnp.int32), axis=0)
    used_tiles = (counts + TILE - 1) // TILE
    by_tile = token_of_row.reshape(own_experts * row_tiles, TILE)
    low_token = jnp.maximum(by_tile[:, 0], 0) // 128 * 128
    windows = jnp.maximum((jnp.max(by_tile, axis=1) - low_token) // WIN + 1, 1)
    low_token = low_token.reshape(own_experts, row_tiles)
    windows = windows.reshape(own_experts, row_tiles)
    row_tables = [
        (used_tiles[e : e + 1], low_token[e], windows[e], token_of_row[e][:, None])
        for e in range(own_experts)
    ]
    place_column = jnp.where(member, place_of, NOWHERE)
    first_place = place_of[::TILE].T
    in_tile = jnp.sum(member.reshape(-1, TILE, own_experts).astype(jnp.int32), axis=1).T
    first_row = first_place // 16 * 16
    more_rows = (first_place + in_tile - first_row > TILE).astype(jnp.int32)
    share_row_start = jnp.minimum(first_place // 128 * 128, capacity - 384)
    token_tables = (first_row, more_rows, share_row_start, place_column)

    seg_ids = jnp.concatenate([jnp.full((PROMPT,), -1, jnp.int32), seg_row])
    starts = jnp.sum(
        (seg_row[None, :] < jnp.arange(CONT, dtype=jnp.int32)[:, None]).astype(jnp.int32), axis=1
    )
    first_pos = jnp.sum(
        jnp.where(
            seg_row[:, None] == jnp.arange(CONT, dtype=jnp.int32)[None, :], starts[None, :], 0
        ),
        axis=1,
    )
    cont_pos = PROMPT + jnp.arange(CTOK, dtype=jnp.int32) - first_pos
    position = jnp.concatenate([jnp.arange(PROMPT, dtype=jnp.int32), cont_pos])
    cos_part, sin_part = angles(position)
    group_inputs = after(
        tokens_group, token_of_row, place_column, first_row, more_rows, share_row_start, used_tiles, windows
    ).astype(F32)
    normed_group = group_inputs * inverse_root(group_inputs)
    hidden_one = (normed_group * gain_attn).astype(BF)
    projected = jnp.dot(hidden_one, packed, preferred_element_type=F32)
    query_pre = projected[:, :own_width]
    key_pre = projected[:, own_width : 2 * own_width]
    squares = jnp.stack([jnp.sum(query_pre * query_pre, axis=1), jnp.sum(key_pre * key_pre, axis=1)])
    roots = lax.rsqrt(sum_over_ctx(squares) / D + epsilon)
    root_query, root_key = roots[0][:, None], roots[1][:, None]
    normed_query = query_pre * root_query
    normed_key = key_pre * root_key
    query_rot, key_rot, value_low, context_low = attend(
        projected,
        roots.T,
        jnp.stack([gain_query, gain_key]),
        cos_part,
        sin_part,
        seg_ids,
        own_width,
    )
    branch_part = jnp.dot(context_low, out_full, preferred_element_type=F32)
    branch, unused, branch_there = scatter_group(after(branch_part, *first_near), slot_table, me)
    first_far = gather_expert_far(after_all(first_near, *branch_there))
    expert_weights = [build_expert(w_gate[0], w_down[0], first_near, first_far, me)]
    backs = [back_rows(row_tables[0], upstream_all, expert_weights[0][1])]
    for e in range(1, own_experts):
        near = gather_expert(*after_all((w_gate[e], w_up[e], w_down[e]), *branch_there), me)
        far = gather_expert_far(after_all(near, backs[e - 1][1]))
        expert_weights.append(build_expert(w_gate[e], w_down[e], near, far, me))
        backs.append(back_rows(row_tables[e], upstream_all, expert_weights[e][1]))

    inputs = tokens.astype(F32)
    middle = inputs + branch
    root_two = inverse_root(middle)
    normed_two = middle * root_two
    hidden_two = (normed_two * gain_ffn).astype(BF)
    hidden_all = lax.all_gather(hidden_two, "exp", axis=0, tiled=True)
    logits = jnp.dot(hidden_two, router_full, preferred_element_type=F32)
    router_prob = jax.nn.softmax(logits, axis=-1)

    every = range(own_experts)
    made = [
        expert_rows(
            row_tables[e],
            e,
            own_ids[:1],
            hidden_all,
            router_full,
            expert_weights[e][0],
            backs[e][1],
        )
        for e in every
    ]
    shares = [m[4].reshape(1, capacity) for m in made]
    grad_two_part, share_token = combine_rows(token_tables, [m[3] for m in made], shares)
    grad_two = lax.psum_scatter(grad_two_part, "exp", scatter_dimension=0, tiled=True)
    share_back = lax.all_to_all(
        share_token.reshape(exp_size, tok_rows, own_experts),
        "exp",
        split_axis=0,
        concat_axis=0,
        tiled=True,
    )
    grad_prob = jnp.swapaxes(share_back, 0, 1).reshape(tok_rows, experts)
    expert_grads = []
    for e in every:
        rows, hidden, grad_hidden = after_all(made[e][:3], grad_two_part)
        expert_grads.append(
            (
                lax.dot_general(rows, grad_hidden, TN, preferred_element_type=F32).astype(BF),
                lax.dot_general(hidden, backs[e][0], TN, preferred_element_type=F32).astype(BF),
            )
        )
    results = [
        jnp.dot(made[e][1], expert_weights[e][1], preferred_element_type=F32).astype(BF)
        for e in every
    ]
    grad_two = after(
        grad_two, *results, *(part for grads in expert_grads[1:] for part in grads)
    ).astype(F32)
    grad_logits = (
        router_prob * (grad_prob - jnp.sum(router_prob * grad_prob, axis=-1, keepdims=True))
    ).astype(BF)
    grad_router = jnp.einsum("td,te->ed", hidden_two, grad_logits, preferred_element_type=F32)
    grad_two = grad_two + jnp.einsum(
        "te,de->td", grad_logits, router_full, preferred_element_type=F32
    )
    grad_ffn_gain = jnp.sum(grad_two * normed_two, axis=0)
    grad_middle = cotangent.astype(F32) + norm_back(grad_two * gain_ffn, normed_two, root_two)

    sums = [scatter_expert_first(expert_grads[0], me)]
    more = [scatter_expert_second(expert_grads[0], after_all(sums[0], *results), me)]
    own_grad = after(grad_middle.astype(BF), *more[0])
    branch_grad, grad_there = gather_group(own_grad, slot_table, me)
    mixture_part, unused = combine_rows(token_tables, after_all(results, own_grad), shares)
    mixture = lax.psum_scatter(mixture_part, "exp", scatter_dimension=0, tiled=True).astype(F32)
    output = (middle + mixture).astype(BF)
    for e in range(1, own_experts):
        sums.append(scatter_expert_first(after_all(expert_grads[e], *grad_there), me))
    early_sums = sum_to_rows(jnp.concatenate([grad_router, grad_ffn_gain[None]]), me)
    branch_grad = after(branch_grad, mixture_part, early_sums)
    grad_context = lax.dot_general(branch_grad, out_full, NT, preferred_element_type=F32).astype(BF)
    out_grad = jnp.einsum("td,te->de", context_low, branch_grad, preferred_element_type=F32)
    grad_query_norm, grad_key_norm, grad_value = attend_back(
        query_rot, key_rot, value_low, grad_context, cos_part, sin_part, seg_ids
    )
    grad_query_gain = jnp.sum(grad_query_norm * normed_query, axis=0)
    grad_key_gain = jnp.sum(grad_key_norm * normed_key, axis=0)
    scaled_query = grad_query_norm * gain_query
    scaled_key = grad_key_norm * gain_key
    means = (
        sum_over_ctx(
            jnp.stack(
                [
                    jnp.sum(scaled_query * normed_query, axis=1),
                    jnp.sum(scaled_key * normed_key, axis=1),
                ]
            )
        )
        / D
    )
    grad_projected = jnp.concatenate(
        [
            root_query * (scaled_query - normed_query * means[0][:, None]),
            root_key * (scaled_key - normed_key * means[1][:, None]),
            grad_value,
        ],
        axis=1,
    ).astype(BF)
    grad_projected = after(grad_projected, *(piece for pieces in sums[1:] for piece in pieces))
    grad_packed = jnp.pad(grad_projected, ((0, 0), (0, 128)))
    grad_one_part = lax.dot_general(grad_packed, packed, NT, preferred_element_type=F32)
    grad_attn_gain = jnp.sum(grad_one_part * normed_group, axis=0)
    grad_one, one_sent, one_there = scatter_group(grad_one_part, slot_table, me)
    for e in range(1, own_experts):
        more.append(scatter_expert_second(expert_grads[e], after_all(sums[e], *one_there), me))
    weight_sums = [scatter_expert_end(expert_grads[e], sums[e], more[e], me) for e in every]
    gate_grad, up_grad, down_grad = (jnp.stack(parts) for parts in zip(*weight_sums))
    left, right = after_all((hidden_one, grad_projected), *one_sent)
    qkv_grad = lax.dot_general(left, right, TN, preferred_element_type=F32)
    out_sum = lax.psum_scatter(
        out_grad.astype(BF), "exp", scatter_dimension=0, tiled=True
    ).astype(F32)
    qkv_sum = lax.psum_scatter(
        qkv_grad.astype(BF).reshape(ctx_size, exp_size * part_rows, 3 * own_width),
        "exp",
        scatter_dimension=1,
        tiled=True,
    )
    qkv_own = exchange(qkv_sum, me).astype(F32)
    projection_grads = [
        jnp.swapaxes(qkv_own[:, :, i * own_width : (i + 1) * own_width], 0, 1).reshape(part_rows, D)
        for i in range(3)
    ]
    root_one = inverse_root(inputs)
    normed_one = inputs * root_one
    grad_input = grad_middle + norm_back(grad_one * gain_attn, normed_one, root_one)
    head_gains = lax.dynamic_update_slice(
        jnp.zeros((2, D), F32), jnp.stack([grad_query_gain, grad_key_gain]), (0, me * own_width)
    )
    late_sums = sum_to_rows(jnp.concatenate([grad_attn_gain[None], head_gains]), me)
    return (
        output,
        grad_input,
        projection_grads[0],
        projection_grads[1],
        projection_grads[2],
        out_sum,
        early_sums[:experts].T,
        late_sums[0],
        late_sums[1],
        late_sums[2],
        early_sums[experts],
        gate_grad,
        up_grad,
        down_grad,
    )


def solution(mesh):
    rows = P(BOTH, None)
    weights = P("exp", "ctx", None)
    in_specs = (
        (rows, rows, rows, P("exp", None), P("exp", None))
        + (rows,) * 5
        + (P(BOTH),) * 4
        + (weights,) * 3
    )
    out_specs = (rows,) * 7 + (P(BOTH),) * 4 + (weights,) * 3
    return jax.shard_map(local, mesh=mesh, in_specs=in_specs, out_specs=out_specs, check_vma=False)
```

time: 1480 us -> 1290 us (0.87)
  waiting for transfers between devices: 634 us -> 405 us
  local copies, waits for them, and re-layouts: 153 us -> 217 us
  blocking collectives: 42.5 us -> 0 us
  starting transfers between devices: 96 us -> 77 us
  other arithmetic: 119 us -> 134 us
    ppermute x18 -> x22, waiting for transfers between devices: 281 us -> 56.1 us  [send_y(): return lax.ppermute(value, 'ctx', Y_PAIRS)]
    reduce_scatter x1, waiting for transfers between devices: 97.1 us -> 4.58 us  [local(): lax.psum_scatter(grad_two_part, 'exp', scatter_dimension=0, tiled=True)]
    ppermute x18 -> x22, waiting for transfers between devices: 238 us -> 316 us  [send_x(): return lax.ppermute(value, 'ctx', X_PAIRS)]
    ppermute x10 -> x4, starting transfers between devices: 47.7 us -> 3.31 us  [send_xy(): return lax.ppermute(value, 'ctx', XY_PAIRS)]
    psum x1 -> x0, blocking collectives: 42.5 us -> none  [local(): lax.psum(jnp.concatenate([grad_attn_gain[None], head_gains]), BOTH)]
    another operation x6 -> x15, local copies, waits for them, and re-layouts: 4.62 us -> 26.5 us
    dynamic_update_slice x12, local copies, waits for them, and re-layouts: 4.32 us -> 23.3 us  [gather_group(): whole = lax.dynamic_update_slice(whole, part, (start, 0))]
    add x8 -> x10, other arithmetic: 37.2 us -> 18.3 us  [the longest x4 10 us: scatter_end(): first = take(me, 0).astype(F32) + low[0].astype(F32) + low_next.astype(F32)]
  transfers between devices with their start and end apart: 57 -> 60, of which waited for: 24 -> 28; matrix products, arithmetic and copies ran while one was open for 26% -> 37% of each run, Pallas kernels for 8% -> 10%
where the time goes in v3:
time: 1290 us; the launch traced here: 1280 us
  waiting for transfers between devices  405 us (31%)
  Pallas kernels  258 us (20%)
  local copies, waits for them, and re-layouts  217 us (17%)
  matrix products  168 us (13%)
  other arithmetic  134 us (10%)
  starting transfers between devices  77 us (6%)
  between operations  21.5 us (2%)
    ppermute x22, waiting for transfers between devices, send_x(): return lax.ppermute(value, 'ctx', X_PAIRS)  316 us
    pallas_call x2, Pallas kernels, expert_rows(): pl.pallas_call(functools.partial(expert_kernel, own), out_shape=[made(wid...  111 us
    ppermute x22, waiting for transfers between devices, send_y(): return lax.ppermute(value, 'ctx', Y_PAIRS)  56.1 us
    pallas_call x2, Pallas kernels, back_rows(): pl.pallas_call(back_rows_kernel, out_shape=[jax.ShapeDtypeStruct((capacit...  50.2 us
    dot_general x2, matrix products, local(): lax.dot_general(rows, grad_hidden, TN, preferred_element_type=F32)  45.4 us
    pallas_call x2, Pallas kernels, combine_rows(): pl.pallas_call(functools.partial(combine_kernel, experts), out_shape=[jax...  40.7 us
    pallas_call x1, Pallas kernels, attend_back(): pl.pallas_call(functools.partial(attend_back_kernel, tiles, 1.0 / math.sq...  30 us
    dynamic_update_slice x15, local copies, waits for them, and re-layouts, exchange(): whole = lax.dynamic_update_slice_in_dim(whole, part, me ^ away, 0)  29.4 us
  transfers between devices with their start and end apart: 60, of which 28 were waited for; matrix products, arithmetic and copies ran while one was open for 37% of the time, Pallas kernels for 10%

profile of v3, /device:TPU:0, one launch (start us, length us, event | category | flops | bytes accessed | tf_op | source)
XLA Modules:
  0.0 1280.4 jit_solution(16204565350327818115)
XLA Ops:
  19.9 4.5 collective-permute-done.4
  24.4 5.2 collective-permute-done.5
  34.2 4.9 all-to-all-start
  53.6 4.3 slice_bitcast_fusion.19
  57.8 4.6 fusion.55
  64.9 14.9 %select_reduce_fusion = s32[2,2048]{1,0:T(2,128)S(1)} fusion(s32[2,3072]{1,0:T(2,128)S(1)} %copy.330, pred[2,3072]{1,0:T(4,128)(4,1)S(1)} %bitcast.366), kind=kLoop, calls=%fused_computation | loop fusion | flops 50327552 | bytes 47104 | tf_op jit(solution)/shard_map/reduce_max | solution.py:759
  93.3 16.1 %collective-permute-done.3 = bf16[192,2048]{1,0:T(8,128)(2,1)} collective-permute-done((bf16[192,2048]{1,0:T(8,128)(2,1)S(1)}, bf16[192,2048]{1,0:T(8,128)(2,1)}, u32[]{:S(2)}, u32[]{:S(2)}) %collective-permute-start.3) | collective-permute-done | bytes 786464 | tf_op jit(solution)/shard_map/ppermute | solution.py:51
  120.6 4.1 fusion.5
  127.0 4.7 fusion.3
  131.8 12.2 fusion.106.qp_ref.kp_ref.vp_ref
  149.0 35.5 %collective-permute-done.7 = f32[2,1536]{1,0:T(2,128)S(1)} collective-permute-done((f32[2,1536]{1,0:T(2,128)S(1)}, f32[2,1536]{1,0:T(2,128)S(1)}, u32[]{:S(2)}, u32[]{:S(2)}) %collective-permute-start.7) | collective-permute-done | bytes 12320 | tf_op jit(solution)/shard_map/ppermute | solution.py:51
  190.8 25.7 %shard_map.272 = (bf16[1536,512]{1,0:T(8,128)(2,1)S(1)}, bf16[1536,512]{1,0:T(8,128)(2,1)}, bf16[1536,512]{1,0:T(8,128)(2,1)}, bf16[1536,512]{1,0:T(8,128)(2,1)}) custom-call(f32[1536,1664]{1,0:T(8,128)} %copy-done.19, f32[1536,1664]{1,0:T(8,128)} %copy-done.19, f32[1536,1664]{1,0:T(8,128)} %copy-done.19, f32[1536,2]{1,0:T(8,128)S(1)} %bitcast.339, ...), custom_call_target="tpu_custom_call" | custom-call | flops 3221225472 | bytes 15728640 | tf_op jit(solution)/shard_map/pallas_call | solution.py:359
  218.5 5.6 fusion.107
  227.4 31.3 %collective-permute-done.11 = bf16[2,192,2048]{2,1,0:T(8,128)(2,1)S(1)} collective-permute-done((bf16[2,192,2048]{2,1,0:T(8,128)(2,1)S(1)}, bf16[2,192,2048]{2,1,0:T(8,128)(2,1)S(1)}, u32[]{:S(2)}, u32[]{:S(2)}) %collective-permute-start.11) | collective-permute-done | bytes 1572896 | tf_op jit(solution)/shard_map/ppermute | solution.py:51
  262.3 14.8 %collective-permute-done.12 = bf16[192,2048]{1,0:T(8,128)(2,1)S(1)} collective-permute-done((bf16[192,2048]{1,0:T(8,128)(2,1)S(1)}, bf16[192,2048]{1,0:T(8,128)(2,1)S(1)}, u32[]{:S(2)}, u32[]{:S(2)}) %collective-permute-start.12) | collective-permute-done | bytes 786464 | tf_op jit(solution)/shard_map/ppermute | solution.py:55
  278.2 16.9 %collective-permute-done.14 = bf16[192,2048]{1,0:T(8,128)(2,1)S(1)} collective-permute-done((bf16[192,2048]{1,0:T(8,128)(2,1)S(1)}, bf16[192,2048]{1,0:T(8,128)(2,1)S(1)}, u32[]{:S(2)}, u32[]{:S(2)}) %collective-permute-start.14) | collective-permute-done | bytes 786464 | tf_op jit(solution)/shard_map/ppermute | solution.py:51
  303.3 4.8 broadcast.218.clone
  342.8 4.4 broadcast.218.clone.1
  349.2 73.0 %collective-permute-done.16 = bf16[768,1024]{1,0:T(8,128)(2,1)S(1)} collective-permute-done((bf16[768,1024]{1,0:T(8,128)(2,1)S(1)}, bf16[768,1024]{1,0:T(8,128)(2,1)S(1)}, u32[]{:S(2)}, u32[]{:S(2)}) %collective-permute-start.16) | collective-permute-done | bytes 1572896 | tf_op jit(solution)/shard_map/ppermute | solution.py:51
  431.5 25.0 %shard_map.273 = (bf16[2048,2048]{1,0:T(8,128)(2,1)}, f32[2048,1024]{1,0:T(8,128)}) custom-call(s32[1]{0:T(128)} %get-tuple-element.275.tiles_ref, s32[8]{0:T(128)S(1)} %get-tuple-element.293.low_ref, s32[8]{0:T(128)S(1)} %get-tuple-element.271.windows_ref, s32[2048,1]{1,0:T(8,128)S(1)} %copy.341.tok_ref, ...), custom_call_target="tpu_custom_call" | custom-call | flops 9663676416 | bytes 33554432 | tf_op jit(solution)/shard_map/pallas_call | solution.py:512
  469.2 20.2 %collective-permute-done.20 = bf16[768,1024]{1,0:T(8,128)(2,1)S(1)} collective-permute-done((bf16[768,1024]{1,0:T(8,128)(2,1)S(1)}, bf16[768,1024]{1,0:T(8,128)(2,1)S(1)}, u32[]{:S(2)}, u32[]{:S(2)}) %collective-permute-start.20) | collective-permute-done | bytes 1572896 | tf_op jit(solution)/shard_map/ppermute | solution.py:51
  496.7 25.2 %shard_map.275 = (bf16[2048,2048]{1,0:T(8,128)(2,1)}, f32[2048,1024]{1,0:T(8,128)}) custom-call(s32[1]{0:T(128)} %get-tuple-element.274.tiles_ref, s32[8]{0:T(128)S(1)} %get-tuple-element.294.low_ref, s32[8]{0:T(128)S(1)} %get-tuple-element.270.windows_ref, s32[2048,1]{1,0:T(8,128)S(1)} %copy-done.9, ...), custom_call_target="tpu_custom_call" | custom-call | flops 9663676416 | bytes 33554432 | tf_op jit(solution)/shard_map/pallas_call | solution.py:512
  521.9 56.7 %shard_map.276 = (bf16[2048,2048]{1,0:T(8,128)(2,1)}, bf16[2048,1024]{1,0:T(8,128)(2,1)}, bf16[2048,2048]{1,0:T(8,128)(2,1)}, bf16[2048,2048]{1,0:T(8,128)(2,1)}, f32[2048,1]{1,0:T(8,128)}) custom-call(s32[1]{0:T(128)} %get-tuple-element.274.tiles_ref, s32[8]{0:T(128)} %copy-done.15, s32[8]{0:T(128)} %copy-done.14, s32[1]{0:T(128)} %bitcast.376, ...), custom_call_target="tpu_custom_call" | custom-call | flops 28991029248 | bytes 58720256 | tf_op jit(solution)/shard_map/pallas_call | solution.py:600
  580.1 54.4 %shard_map.274 = (bf16[2048,2048]{1,0:T(8,128)(2,1)}, bf16[2048,1024]{1,0:T(8,128)(2,1)}, bf16[2048,2048]{1,0:T(8,128)(2,1)}, bf16[2048,2048]{1,0:T(8,128)(2,1)}, f32[2048,1]{1,0:T(8,128)}) custom-call(s32[1]{0:T(128)} %get-tuple-element.275.tiles_ref, s32[8]{0:T(128)} %copy-done.13, s32[8]{0:T(128)} %copy-done.12, s32[1]{0:T(128)} %bitcast.377, ...), custom_call_target="tpu_custom_call" | custom-call | flops 28991029248 | bytes 58720256 | tf_op jit(solution)/shard_map/pallas_call | solution.py:600
  637.4 20.4 %shard_map.277 = (bf16[3072,2048]{1,0:T(8,128)(2,1)}, f32[3072,2]{1,0:T(8,128)S(1)}) custom-call(s32[2,12]{1,0:T(2,128)S(1)} %copy.348.start_ref, s32[2,12]{1,0:T(2,128)S(1)} %copy.349.more_ref, s32[2,12]{1,0:T(2,128)S(1)} %copy.350.wide_ref, s32[3072,2]{1,0:T(8,128)S(1)} %copy-done.5, bf16[2048,2048]{1,0:T(8,128)(2,1)} %get-tuple-element.87.refs_0_, ...), custom_call_target="tpu_custom_call" | custom-call | flops 6442450944 | bytes 29360128 | tf_op jit(solution)/shard_map/pallas_call | solution.py:660
  661.3 12.8 %convolution_convert_fusion.5 = bf16[1024,2048]{1,0:T(8,128)(2,1)S(1)} fusion(bf16[2048,1024]{1,0:T(8,128)(2,1)} %get-tuple-element.104, bf16[2048,2048]{1,0:T(8,128)(2,1)} %get-tuple-element.105), kind=kOutput, calls=%fused_computation.24 | convolution fusion | flops 8592031744 | bytes 16777216 | tf_op jit(solution)/shard_map/dot_general | solution.py:864
  675.6 21.5 %convolution_convert_fusion.1 = bf16[2048,2048]{1,0:T(8,128)(2,1)S(1)} fusion(bf16[2048,2048]{1,0:T(8,128)(2,1)S(1)} %bitcast.383, bf16[2048,2048]{1,0:T(8,128)(2,1)} %get-tuple-element.103), kind=kOutput, calls=%fused_computation.11 | convolution fusion | flops 17184063488 | bytes 25165824 | tf_op jit(solution)/shard_map/dot_general | solution.py:863
  712.4 10.5 all-to-all-start.1
  722.9 14.1 %convolution_convert_fusion.6 = bf16[1024,2048]{1,0:T(8,128)(2,1)} fusion(bf16[2048,1024]{1,0:T(8,128)(2,1)} %get-tuple-element.96, bf16[2048,2048]{1,0:T(8,128)(2,1)} %get-tuple-element.97), kind=kOutput, calls=%fused_computation.25 | convolution fusion | flops 8592031744 | bytes 16777216 | tf_op jit(solution)/shard_map/dot_general | solution.py:864
  737.0 23.9 %convolution_convert_fusion.2 = bf16[2048,2048]{1,0:T(8,128)(2,1)} fusion(bf16[2048,2048]{1,0:T(8,128)(2,1)} %get-tuple-element.94, bf16[2048,2048]{1,0:T(8,128)(2,1)} %get-tuple-element.95), kind=kOutput, calls=%fused_computation.12 | convolution fusion | flops 17184063488 | bytes 25165824 | tf_op jit(solution)/shard_map/dot_general | solution.py:863
  761.0 13.3 %convolution_convert_fusion.3.refs_1_ = bf16[2048,2048]{1,0:T(8,128)(2,1)} fusion(bf16[2048,1024]{1,0:T(8,128)(2,1)S(1)} %copy-done.97, bf16[1024,2048]{1,0:T(8,128)(2,1)} %slice_dynamic-update-slice_fusion.8.wd_ref), kind=kOutput, calls=%fused_computation.13 | convolution fusion | flops 8594128896 | bytes 16777216 | tf_op jit(solution)/shard_map/dot_general | solution.py:868
  774.3 11.3 convolution_convert_fusion.4.refs_0_
  795.3 4.6 reduce-scatter.5.cloned.1.call-done
  799.9 3.9 multiply_reduce_fusion.4
  806.2 20.6 %collective-permute-done.24 = bf16[768,1024]{1,0:T(8,128)(2,1)} collective-permute-done((bf16[768,1024]{1,0:T(8,128)(2,1)}, bf16[768,1024]{1,0:T(8,128)(2,1)}, u32[]{:S(2)}, u32[]{:S(2)}) %collective-permute-start.24) | collective-permute-done | bytes 1572896 | tf_op jit(solution)/shard_map/ppermute | solution.py:51
  826.8 4.7 collective-permute-done.23
  840.2 4.7 all-to-all-start.2
  847.1 4.7 all-to-all-done.2
  853.4 13.9 %collective-permute-done.25 = bf16[384,2048]{1,0:T(8,128)(2,1)} collective-permute-done((bf16[384,2048]{1,0:T(8,128)(2,1)}, bf16[384,2048]{1,0:T(8,128)(2,1)}, u32[]{:S(2)}, u32[]{:S(2)}) %collective-permute-start.25) | collective-permute-done | bytes 1572896 | tf_op jit(solution)/shard_map/ppermute | solution.py:51
  880.9 20.4 %shard_map.278 = (bf16[3072,2048]{1,0:T(8,128)(2,1)}, f32[3072,2]{1,0:T(8,128)}) custom-call(s32[2,12]{1,0:T(2,128)S(1)} %copy.348.start_ref, s32[2,12]{1,0:T(2,128)S(1)} %copy.349.more_ref, s32[2,12]{1,0:T(2,128)S(1)} %copy.350.wide_ref, s32[3072,2]{1,0:T(8,128)S(1)} %copy-done.6, bf16[2048,2048]{1,0:T(8,128)(2,1)} %convolution_convert_fusion.4.refs_0_, ...), custom_call_target="tpu_custom_call" | custom-call | flops 6442450944 | bytes 29360128 | tf_op jit(solution)/shard_map/pallas_call | solution.py:660
  902.4 3.9 constant_dynamic-slice_fusion.56
  915.5 8.2 convolution_convert_fusion.8.d_ref
  923.7 30.0 %shard_map.279 = (f32[1536,512]{1,0:T(8,128)}, f32[1536,512]{1,0:T(8,128)}, f32[1536,512]{1,0:T(8,128)}) custom-call(bf16[1536,512]{1,0:T(8,128)(2,1)S(1)} %copy-done.17, bf16[1536,512]{1,0:T(8,128)(2,1)S(1)} %copy-done.18, bf16[1536,512]{1,0:T(8,128)(2,1)} %get-tuple-element.114.v_ref, bf16[1536,512]{1,0:T(8,128)(2,1)} %convolution_convert_fusion.8.d_ref, ...), custom_call_target="tpu_custom_call" | custom-call | flops 8053063680 | bytes 15728640 | tf_op jit(solution)/shard_map/pallas_call | solution.py:448
  953.8 5.7 multiply_reduce_fusion.1
  964.8 7.7 convolution_convert_fusion.7
  980.6 5.0 multiply_convert_fusion.1
  988.0 42.2 %collective-permute-done.34 = bf16[2,768,1024]{2,1,0:T(8,128)(2,1)} collective-permute-done((bf16[2,768,1024]{2,1,0:T(8,128)(2,1)}, bf16[2,768,1024]{2,1,0:T(8,128)(2,1)}, u32[]{:S(2)}, u32[]{:S(2)}) %collective-permute-start.34) | collective-permute-done | bytes 3145760 | tf_op jit(solution)/shard_map/ppermute | solution.py:51
  1030.2 16.4 %fusion.4 = (f32[2048]{0:T(1024)S(1)}, f32[1536,2048]{1,0:T(8,128)S(1)}) fusion(bf16[1536,2048]{1,0:T(8,128)(2,1)} %constant_dynamic-update-slice_fusion.10, f32[1536]{0:T(1024)S(1)} %copy-done.81, bf16[2048,1664]{1,0:T(8,128)(2,1)} %bitcast.356, bf16[1536,1536]{1,0:T(8,128)(2,1)} %pad_maximum_fusion), kind=kOutput, calls=%fused_computation.8 | convolution fusion | flops 10481563648 | bytes 30423040 | tf_op jit(solution)/shard_map/dot_general | solution.py:925
  1052.9 14.7 %convolution_convert_fusion = bf16[2048,1536]{1,0:T(8,128)(2,1)} fusion(bf16[1536,2048]{1,0:T(8,128)(2,1)} %copy-done.46, bf16[1536,1536]{1,0:T(8,128)(2,1)S(1)} %copy-done.48), kind=kOutput, calls=%fused_computation.10 | convolution fusion | flops 9666822144 | bytes 17301504 | tf_op jit(solution)/shard_map/dot_general | solution.py:933
  1072.1 4.6 constant_dynamic-slice_fusion.47
  1083.0 17.5 %collective-permute-done.36 = bf16[2,192,2048]{2,1,0:T(8,128)(2,1)S(1)} collective-permute-done((bf16[2,192,2048]{2,1,0:T(8,128)(2,1)}, bf16[2,192,2048]{2,1,0:T(8,128)(2,1)S(1)}, u32[]{:S(2)}, u32[]{:S(2)}) %collective-permute-start.36) | collective-permute-done | bytes 1572896 | tf_op jit(solution)/shard_map/ppermute | solution.py:51
  1108.8 11.6 collective-permute-done.38
  1121.5 9.9 collective-permute-done.37
  1131.5 4.1 fusion.26
  1136.8 4.4 all-to-all-start.3
  1141.7 5.1 all-to-all-done.3
  1168.5 24.5 %collective-permute-done.47 = bf16[768,1024]{1,0:T(8,128)(2,1)} collective-permute-done((bf16[768,1024]{1,0:T(8,128)(2,1)}, bf16[768,1024]{1,0:T(8,128)(2,1)}, u32[]{:S(2)}, u32[]{:S(2)}) %collective-permute-start.47) | collective-permute-done | bytes 1572896 | tf_op jit(solution)/shard_map/ppermute | solution.py:51
  1212.4 4.0 pad_maximum_fusion.1
  1217.8 7.2 dynamic_update_slice.259
  1225.3 7.2 dynamic_update_slice.260
  1232.8 7.2 dynamic_update_slice.261
  1240.3 7.2 dynamic_update_slice.262
  1251.9 15.0 %reduce-scatter.7.cloned.1.call-done = bf16[384,2048]{1,0:T(8,128)(2,1)} async-done(((bf16[3072,2048]{1,0:T(8,128)(2,1)}), bf16[384,2048]{1,0:T(8,128)(2,1)}) %reduce-scatter.7.cloned.1.call-update) | async-done | bytes 1572880 | tf_op jit(solution)/shard_map/reduce_scatter | solution.py:889
  1266.9 6.5 fusion.13
  (570 shorter events, 314.9 us)
Async XLA Ops:
  7.2 117.6 %all-gather.5.cloned.1.call-start = ((), (), s32[]{:S(2)}) async-start(), calls=%async_computation.8 | async-start | bytes 7667712 | tf_op jit(solution)/shard_map/all_gather | solution.py:731
  15.3 9.1 collective-permute-start.4
  18.3 11.3 collective-permute-start.5
  19.8 9.8 collective-permute-start.6
  30.6 187.9 %all-gather.7.cloned.1.call-start = ((), (), s32[]{:S(2)}) async-start(), calls=%async_computation.9 | async-start | bytes 2359296 | tf_op jit(solution)/shard_map/all_gather | solution.py:738
  31.4 48.9 %collective-permute-start = (bf16[384,2048]{1,0:T(8,128)(2,1)S(1)}, bf16[384,2048]{1,0:T(8,128)(2,1)}, u32[]{:S(2)}, u32[]{:S(2)}) collective-permute-start(bf16[384,2048]{1,0:T(8,128)(2,1)S(1)} %copy-done.24), channel_id=1, source_target_pairs={{0,8},{8,0},{16,24},{24,16},{1,9},{9,1},{17,25},{25,17},{2,10},{10... | collective-permute-start | bytes 4718600 | tf_op jit(solution)/shard_map/ppermute | solution.py:51
  32.7 52.3 %collective-permute-start.1 = (bf16[384,2048]{1,0:T(8,128)(2,1)S(1)}, bf16[384,2048]{1,0:T(8,128)(2,1)}, u32[]{:S(2)}, u32[]{:S(2)}) collective-permute-start(bf16[384,2048]{1,0:T(8,128)(2,1)S(1)} %copy-done.24), channel_id=1, source_target_pairs={{0,16},{8,24},{16,0},{24,8},{1,17},{9,25},{17,1},{25,9},{2,18},{10... | collective-permute-start | bytes 4718600 | tf_op jit(solution)/shard_map/ppermute | solution.py:55
  34.2 29.2 %all-to-all-start = ((s32[8,384,8]{1,2,0:T(8,128)}), s32[8,384,8]{1,2,0:T(8,128)S(1)}, u32[]{:S(2)}, u32[]{:S(2)}) async-start(s32[8,384,8]{1,2,0:T(8,128)} %broadcast_in_dim.154), calls=%async_computation | async-start | bytes 196608 | tf_op jit(solution)/shard_map/all_to_all | solution.py:739
  39.1 390.3 %all-gather.11.cloned.1.call-start = ((), (), s32[]{:S(2)}) async-start(), calls=%async_computation.11 | async-start | bytes 14155776 | tf_op jit(solution)/shard_map/all_gather | solution.py:746
  39.8 482.1 %all-gather.9.cloned.1.call-start = ((), (), s32[]{:S(2)}) async-start(), calls=%async_computation.10 | async-start | bytes 14155776 | tf_op jit(solution)/shard_map/all_gather | solution.py:830
  89.3 20.1 %collective-permute-start.3 = (bf16[192,2048]{1,0:T(8,128)(2,1)S(1)}, bf16[192,2048]{1,0:T(8,128)(2,1)}, u32[]{:S(2)}, u32[]{:S(2)}) collective-permute-start(bf16[192,2048]{1,0:T(8,128)(2,1)S(1)} %get-tuple-element.231), channel_id=1, source_target_pairs={{0,8},{8,0},{16,24},{24,16},{1,9},{9,1},{17,25},{25,17},{2,10},{10... | collective-permute-start | bytes 2359304 | tf_op jit(solution)/shard_map/ppermute | solution.py:51
  90.8 19.9 %collective-permute-start.2 = (bf16[192,2048]{1,0:T(8,128)(2,1)}, bf16[192,2048]{1,0:T(8,128)(2,1)}, u32[]{:S(2)}, u32[]{:S(2)}) collective-permute-start(bf16[192,2048]{1,0:T(8,128)(2,1)} %get-tuple-element.233), channel_id=1, source_target_pairs={{0,16},{8,24},{16,0},{24,8},{1,17},{9,25},{17,1},{25,9},{2,18},{10... | collective-permute-start | bytes 2359304 | tf_op jit(solution)/shard_map/ppermute | solution.py:55
  114.5 109.6 %collective-permute-start.10 = (bf16[1536,1024]{1,0:T(8,128)(2,1)}, bf16[1536,1024]{1,0:T(8,128)(2,1)}, u32[]{:S(2)}, u32[]{:S(2)}) collective-permute-start(bf16[1536,1024]{1,0:T(8,128)(2,1)} %pad_maximum_fusion.4), channel_id=1, source_target_pairs={{0,16},{8,24},{16,0},{24,8},{1,17},{9,25},{17,1},{25,9},{2,18},{10... | collective-permute-start | bytes 9437192 | tf_op jit(solution)/shard_map/ppermute | solution.py:55
  115.0 109.2 %collective-permute-start.9 = (bf16[1536,1024]{1,0:T(8,128)(2,1)}, bf16[1536,1024]{1,0:T(8,128)(2,1)}, u32[]{:S(2)}, u32[]{:S(2)}) collective-permute-start(bf16[1536,1024]{1,0:T(8,128)(2,1)} %pad_maximum_fusion.4), channel_id=1, source_target_pairs={{0,8},{8,0},{16,24},{24,16},{1,9},{9,1},{17,25},{25,17},{2,10},{10... | collective-permute-start | bytes 9437192 | tf_op jit(solution)/shard_map/ppermute | solution.py:51
  127.0 169.8 %copy-start.73 = (f32[2048]{0:T(1024)}, f32[2048]{0:T(1024)S(1)}, u32[]{:S(2)}) copy-start(f32[2048]{0:T(1024)S(1)} %get-tuple-element.136) | copy-start | bytes 24580
  144.6 39.9 %collective-permute-start.7 = (f32[2,1536]{1,0:T(2,128)S(1)}, f32[2,1536]{1,0:T(2,128)S(1)}, u32[]{:S(2)}, u32[]{:S(2)}) collective-permute-start(f32[2,1536]{1,0:T(2,128)S(1)} %pad_maximum_fusion.16), channel_id=1, source_target_pairs={{0,8},{8,0},{16,24},{24,16},{1,9},{9,1},{17,25},{25,17},{2,10},{10... | collective-permute-start | bytes 36872 | tf_op jit(solution)/shard_map/ppermute | solution.py:51
  184.5 3.8 collective-permute-start.8
  224.8 33.9 %collective-permute-start.11 = (bf16[2,192,2048]{2,1,0:T(8,128)(2,1)S(1)}, bf16[2,192,2048]{2,1,0:T(8,128)(2,1)S(1)}, u32[]{:S(2)}, u32[]{:S(2)}) collective-permute-start(bf16[2,192,2048]{2,1,0:T(8,128)(2,1)S(1)} %pad_maximum_fusion.10), channel_id=1, source_target_pairs={{0,8},{8,0},{16,24},{24,16},{1,9},{9,1},{17,25},{25,17},{2,10},{10... | collective-permute-start | bytes 4718600 | tf_op jit(solution)/shard_map/ppermute | solution.py:51
  226.5 35.8 %collective-permute-start.13 = (bf16[2,192,2048]{2,1,0:T(8,128)(2,1)S(1)}, bf16[2,192,2048]{2,1,0:T(8,128)(2,1)S(1)}, u32[]{:S(2)}, u32[]{:S(2)}) collective-permute-start(bf16[2,192,2048]{2,1,0:T(8,128)(2,1)S(1)} %pad_maximum_fusion.11), channel_id=1, source_target_pairs={{0,16},{8,24},{16,0},{24,8},{1,17},{9,25},{17,1},{25,9},{2,18},{10... | collective-permute-start | bytes 4718600 | tf_op jit(solution)/shard_map/ppermute | solution.py:55
  258.9 18.2 %collective-permute-start.12 = (bf16[192,2048]{1,0:T(8,128)(2,1)S(1)}, bf16[192,2048]{1,0:T(8,128)(2,1)S(1)}, u32[]{:S(2)}, u32[]{:S(2)}) collective-permute-start(bf16[192,2048]{1,0:T(8,128)(2,1)S(1)} %fusion.29), channel_id=1, source_target_pairs={{0,16},{8,24},{16,0},{24,8},{1,17},{9,25},{17,1},{25,9},{2,18},{10... | collective-permute-start | bytes 2359304 | tf_op jit(solution)/shard_map/ppermute | solution.py:55
  277.8 17.3 %collective-permute-start.14 = (bf16[192,2048]{1,0:T(8,128)(2,1)S(1)}, bf16[192,2048]{1,0:T(8,128)(2,1)S(1)}, u32[]{:S(2)}, u32[]{:S(2)}) collective-permute-start(bf16[192,2048]{1,0:T(8,128)(2,1)S(1)} %get-tuple-element.155), channel_id=1, source_target_pairs={{0,8},{8,0},{16,24},{24,16},{1,9},{9,1},{17,25},{25,17},{2,10},{10... | collective-permute-start | bytes 2359304 | tf_op jit(solution)/shard_map/ppermute | solution.py:51
  300.0 499.9 %reduce-scatter.5.cloned.1.call-start = ((), (), s32[]{:S(2)}) async-start(), calls=%async_computation.12 | async-start | bytes 14155776 | tf_op jit(solution)/shard_map/reduce_scatter | solution.py:849
  300.8 128.6 %copy-start.8 = (s32[2048,1]{1,0:T(8,128)}, s32[2048,1]{1,0:T(8,128)S(1)}, u32[]{:S(2)}) copy-start(s32[2048,1]{1,0:T(8,128)S(1)} %copy.341.tok_ref) | copy-start | bytes 24580
  303.2 193.4 %copy-start.14 = (s32[8]{0:T(128)}, s32[8]{0:T(128)S(1)}, u32[]{:S(2)}) copy-start(s32[8]{0:T(128)S(1)} %get-tuple-element.270.windows_ref) | copy-start | bytes 100
  303.2 193.4 %copy-start.15 = (s32[8]{0:T(128)}, s32[8]{0:T(128)S(1)}, u32[]{:S(2)}) copy-start(s32[8]{0:T(128)S(1)} %get-tuple-element.294.low_ref) | copy-start | bytes 100
  321.5 105.1 %collective-permute-start.17 = (bf16[1536,1024]{1,0:T(8,128)(2,1)}, bf16[1536,1024]{1,0:T(8,128)(2,1)S(1)}, u32[]{:S(2)}, u32[]{:S(2)}) collective-permute-start(bf16[1536,1024]{1,0:T(8,128)(2,1)} %pad_maximum_fusion.5), channel_id=1, source_target_pairs={{0,8},{8,0},{16,24},{24,16},{1,9},{9,1},{17,25},{25,17},{2,10},{10... | collective-permute-start | bytes 9437192 | tf_op jit(solution)/shard_map/ppermute | solution.py:51
  326.9 95.4 %collective-permute-start.16 = (bf16[768,1024]{1,0:T(8,128)(2,1)S(1)}, bf16[768,1024]{1,0:T(8,128)(2,1)S(1)}, u32[]{:S(2)}, u32[]{:S(2)}) collective-permute-start(bf16[768,1024]{1,0:T(8,128)(2,1)S(1)} %slice.382), channel_id=1, source_target_pairs={{0,8},{8,0},{16,24},{24,16},{1,9},{9,1},{17,25},{25,17},{2,10},{10... | collective-permute-start | bytes 4718600 | tf_op jit(solution)/shard_map/ppermute | solution.py:51
  334.6 89.3 %collective-permute-start.15 = (bf16[768,1024]{1,0:T(8,128)(2,1)S(1)}, bf16[768,1024]{1,0:T(8,128)(2,1)S(1)}, u32[]{:S(2)}, u32[]{:S(2)}) collective-permute-start(bf16[768,1024]{1,0:T(8,128)(2,1)S(1)} %slice.379), channel_id=1, source_target_pairs={{0,16},{8,24},{16,0},{24,8},{1,17},{9,25},{17,1},{25,9},{2,18},{10... | collective-permute-start | bytes 4718600 | tf_op jit(solution)/shard_map/ppermute | solution.py:55
  340.8 115.7 %collective-permute-start.18 = (bf16[1536,1024]{1,0:T(8,128)(2,1)}, bf16[1536,1024]{1,0:T(8,128)(2,1)}, u32[]{:S(2)}, u32[]{:S(2)}) collective-permute-start(bf16[1536,1024]{1,0:T(8,128)(2,1)} %pad_maximum_fusion.5), channel_id=1, source_target_pairs={{0,16},{8,24},{16,0},{24,8},{1,17},{9,25},{17,1},{25,9},{2,18},{10... | collective-permute-start | bytes 9437192 | tf_op jit(solution)/shard_map/ppermute | solution.py:55
  458.2 31.1 %collective-permute-start.20 = (bf16[768,1024]{1,0:T(8,128)(2,1)S(1)}, bf16[768,1024]{1,0:T(8,128)(2,1)S(1)}, u32[]{:S(2)}, u32[]{:S(2)}) collective-permute-start(bf16[768,1024]{1,0:T(8,128)(2,1)S(1)} %slice.406), channel_id=1, source_target_pairs={{0,8},{8,0},{16,24},{24,16},{1,9},{9,1},{17,25},{25,17},{2,10},{10... | collective-permute-start | bytes 4718600 | tf_op jit(solution)/shard_map/ppermute | solution.py:51
  461.6 32.3 %collective-permute-start.19 = (bf16[768,1024]{1,0:T(8,128)(2,1)S(1)}, bf16[768,1024]{1,0:T(8,128)(2,1)S(1)}, u32[]{:S(2)}, u32[]{:S(2)}) collective-permute-start(bf16[768,1024]{1,0:T(8,128)(2,1)S(1)} %slice.403), channel_id=1, source_target_pairs={{0,16},{8,24},{16,0},{24,8},{1,17},{9,25},{17,1},{25,9},{2,18},{10... | collective-permute-start | bytes 4718600 | tf_op jit(solution)/shard_map/ppermute | solution.py:55
  701.6 84.1 %collective-permute-start.22 = (bf16[2,768,1024]{2,1,0:T(8,128)(2,1)}, bf16[2,768,1024]{2,1,0:T(8,128)(2,1)}, u32[]{:S(2)}, u32[]{:S(2)}) collective-permute-start(bf16[2,768,1024]{2,1,0:T(8,128)(2,1)} %pad_maximum_fusion.7), channel_id=1, source_target_pairs={{0,16},{8,24},{16,0},{24,8},{1,17},{9,25},{17,1},{25,9},{2,18},{10... | collective-permute-start | bytes 9437192 | tf_op jit(solution)/shard_map/ppermute | solution.py:55
  706.3 79.4 %collective-permute-start.21 = (bf16[2,768,1024]{2,1,0:T(8,128)(2,1)}, bf16[2,768,1024]{2,1,0:T(8,128)(2,1)}, u32[]{:S(2)}, u32[]{:S(2)}) collective-permute-start(bf16[2,768,1024]{2,1,0:T(8,128)(2,1)} %pad_maximum_fusion.6), channel_id=1, source_target_pairs={{0,8},{8,0},{16,24},{24,16},{1,9},{9,1},{17,25},{25,17},{2,10},{10... | collective-permute-start | bytes 9437192 | tf_op jit(solution)/shard_map/ppermute | solution.py:51
  712.4 73.2 %all-to-all-start.1 = ((f32[8,384,2]{1,2,0:T(2,128)}), f32[8,384,2]{1,2,0:T(2,128)S(1)}, u32[]{:S(2)}, u32[]{:S(2)}) async-start(f32[8,384,2]{1,2,0:T(2,128)} %copy.347), calls=%async_computation.2 | async-start | bytes 49152 | tf_op jit(solution)/shard_map/all_to_all | solution.py:850
  789.6 37.2 %collective-permute-start.24 = (bf16[768,1024]{1,0:T(8,128)(2,1)}, bf16[768,1024]{1,0:T(8,128)(2,1)}, u32[]{:S(2)}, u32[]{:S(2)}) collective-permute-start(bf16[768,1024]{1,0:T(8,128)(2,1)} %fusion.21), channel_id=1, source_target_pairs={{0,8},{8,0},{16,24},{24,16},{1,9},{9,1},{17,25},{25,17},{2,10},{10... | collective-permute-start | bytes 4718600 | tf_op jit(solution)/shard_map/ppermute | solution.py:51
  794.9 36.6 %collective-permute-start.23 = (bf16[768,1024]{1,0:T(8,128)(2,1)}, bf16[768,1024]{1,0:T(8,128)(2,1)}, u32[]{:S(2)}, u32[]{:S(2)}) collective-permute-start(bf16[768,1024]{1,0:T(8,128)(2,1)} %fusion.22), channel_id=1, source_target_pairs={{0,16},{8,24},{16,0},{24,8},{1,17},{9,25},{17,1},{25,9},{2,18},{10... | collective-permute-start | bytes 4718600 | tf_op jit(solution)/shard_map/ppermute | solution.py:55
  831.5 35.8 %collective-permute-start.25 = (bf16[384,2048]{1,0:T(8,128)(2,1)}, bf16[384,2048]{1,0:T(8,128)(2,1)}, u32[]{:S(2)}, u32[]{:S(2)}) collective-permute-start(bf16[384,2048]{1,0:T(8,128)(2,1)} %fusion.90), channel_id=1, source_target_pairs={{0,8},{8,0},{16,24},{24,16},{1,9},{9,1},{17,25},{25,17},{2,10},{10... | collective-permute-start | bytes 4718600 | tf_op jit(solution)/shard_map/ppermute | solution.py:51
  833.0 38.6 %collective-permute-start.26 = (bf16[384,2048]{1,0:T(8,128)(2,1)}, bf16[384,2048]{1,0:T(8,128)(2,1)}, u32[]{:S(2)}, u32[]{:S(2)}) collective-permute-start(bf16[384,2048]{1,0:T(8,128)(2,1)} %fusion.90), channel_id=1, source_target_pairs={{0,16},{8,24},{16,0},{24,8},{1,17},{9,25},{17,1},{25,9},{2,18},{10... | collective-permute-start | bytes 4718600 | tf_op jit(solution)/shard_map/ppermute | solution.py:55
  840.2 11.6 all-to-all-start.2
  844.9 314.6 %reduce-scatter.11.cloned.1.call-start = ((), (), s32[]{:S(2)}) async-start(), calls=%async_computation.15 | async-start | bytes 2359296 | tf_op jit(solution)/shard_map/reduce_scatter | solution.py:934
  876.3 26.1 %collective-permute-start.28 = (bf16[192,2048]{1,0:T(8,128)(2,1)}, bf16[192,2048]{1,0:T(8,128)(2,1)}, u32[]{:S(2)}, u32[]{:S(2)}) collective-permute-start(bf16[192,2048]{1,0:T(8,128)(2,1)} %get-tuple-element.227), channel_id=1, source_target_pairs={{0,8},{8,0},{16,24},{24,16},{1,9},{9,1},{17,25},{25,17},{2,10},{10... | collective-permute-start | bytes 2359304 | tf_op jit(solution)/shard_map/ppermute | solution.py:51
  876.9 25.5 %collective-permute-start.27 = (bf16[192,2048]{1,0:T(8,128)(2,1)S(1)}, bf16[192,2048]{1,0:T(8,128)(2,1)}, u32[]{:S(2)}, u32[]{:S(2)}) collective-permute-start(bf16[192,2048]{1,0:T(8,128)(2,1)S(1)} %get-tuple-element.229), channel_id=1, source_target_pairs={{0,16},{8,24},{16,0},{24,8},{1,17},{9,25},{17,1},{25,9},{2,18},{10... | collective-permute-start | bytes 2359304 | tf_op jit(solution)/shard_map/ppermute | solution.py:55
  877.4 24.0 %collective-permute-start.29 = (f32[1,17,64]{2,0,1:T(1,128)S(1)}, f32[1,17,64]{2,0,1:T(1,128)S(1)}, u32[]{:S(2)}, u32[]{:S(2)}) collective-permute-start(f32[1,17,64]{2,0,1:T(1,128)S(1)} %get-tuple-element.254), channel_id=1, source_target_pairs={{0,8},{8,0},{16,24},{24,16},{1,9},{9,1},{17,25},{25,17},{2,10},{10... | collective-permute-start | bytes 13064 | tf_op jit(solution)/shard_map/ppermute | solution.py:51
  879.0 22.4 %collective-permute-start.30 = (f32[1,17,64]{2,0,1:T(1,128)S(1)}, f32[1,17,64]{2,0,1:T(1,128)S(1)}, u32[]{:S(2)}, u32[]{:S(2)}) collective-permute-start(f32[1,17,64]{2,0,1:T(1,128)S(1)} %get-tuple-element.253), channel_id=1, source_target_pairs={{0,16},{8,24},{16,0},{24,8},{1,17},{9,25},{17,1},{25,9},{2,18},{10... | collective-permute-start | bytes 13064 | tf_op jit(solution)/shard_map/ppermute | solution.py:55
  880.5 21.0 %collective-permute-start.31 = (f32[1,17,64]{2,0,1:T(1,128)S(1)}, f32[1,17,64]{2,0,1:T(1,128)S(1)}, u32[]{:S(2)}, u32[]{:S(2)}) collective-permute-start(f32[1,17,64]{2,0,1:T(1,128)S(1)} %get-tuple-element.252), channel_id=1, source_target_pairs={{0,24},{8,16},{16,8},{24,0},{1,25},{9,17},{17,9},{25,1},{2,26},{10... | collective-permute-start | bytes 13064 | tf_op jit(solution)/shard_map/ppermute | solution.py:59
  909.6 78.4 %collective-permute-start.35 = (bf16[2,768,1024]{2,1,0:T(8,128)(2,1)}, bf16[2,768,1024]{2,1,0:T(8,128)(2,1)}, u32[]{:S(2)}, u32[]{:S(2)}) collective-permute-start(bf16[2,768,1024]{2,1,0:T(8,128)(2,1)} %pad_maximum_fusion.9), channel_id=1, source_target_pairs={{0,16},{8,24},{16,0},{24,8},{1,17},{9,25},{17,1},{25,9},{2,18},{10... | collective-permute-start | bytes 9437192 | tf_op jit(solution)/shard_map/ppermute | solution.py:55
  959.5 4.6 collective-permute-start.32
  963.4 66.8 %collective-permute-start.34 = (bf16[2,768,1024]{2,1,0:T(8,128)(2,1)}, bf16[2,768,1024]{2,1,0:T(8,128)(2,1)}, u32[]{:S(2)}, u32[]{:S(2)}) collective-permute-start(bf16[2,768,1024]{2,1,0:T(8,128)(2,1)} %pad_maximum_fusion.8), channel_id=1, source_target_pairs={{0,8},{8,0},{16,24},{24,16},{1,9},{9,1},{17,25},{25,17},{2,10},{10... | collective-permute-start | bytes 9437192 | tf_op jit(solution)/shard_map/ppermute | solution.py:51
  964.2 13.0 %collective-permute-start.33 = (f32[2,1536]{1,0:T(2,128)S(1)}, f32[2,1536]{1,0:T(2,128)S(1)}, u32[]{:S(2)}, u32[]{:S(2)}) collective-permute-start(f32[2,1536]{1,0:T(2,128)S(1)} %fusion.85), channel_id=1, source_target_pairs={{0,16},{8,24},{16,0},{24,8},{1,17},{9,25},{17,1},{25,9},{2,18},{10... | collective-permute-start | bytes 36872 | tf_op jit(solution)/shard_map/ppermute | solution.py:55
  973.9 233.6 %reduce-scatter.9.cloned.1.call-start = ((), (), s32[]{:S(2)}) async-start(), calls=%async_computation.14 | async-start | bytes 7077888 | tf_op jit(solution)/shard_map/reduce_scatter | solution.py:937
  1067.6 199.3 %reduce-scatter.7.cloned.1.call-start = ((), (), s32[]{:S(2)}) async-start(), calls=%async_computation.13 | async-start | bytes 14155776 | tf_op jit(solution)/shard_map/reduce_scatter | solution.py:889
  1068.4 32.1 %collective-permute-start.36 = (bf16[2,192,2048]{2,1,0:T(8,128)(2,1)}, bf16[2,192,2048]{2,1,0:T(8,128)(2,1)S(1)}, u32[]{:S(2)}, u32[]{:S(2)}) collective-permute-start(bf16[2,192,2048]{2,1,0:T(8,128)(2,1)} %pad_maximum_fusion.12), channel_id=1, source_target_pairs={{0,8},{8,0},{16,24},{24,16},{1,9},{9,1},{17,25},{25,17},{2,10},{10... | collective-permute-start | bytes 4718600 | tf_op jit(solution)/shard_map/ppermute | solution.py:51
  1082.8 37.6 %collective-permute-start.38 = (bf16[2,192,2048]{2,1,0:T(8,128)(2,1)}, bf16[2,192,2048]{2,1,0:T(8,128)(2,1)S(1)}, u32[]{:S(2)}, u32[]{:S(2)}) collective-permute-start(bf16[2,192,2048]{2,1,0:T(8,128)(2,1)} %pad_maximum_fusion.13), channel_id=1, source_target_pairs={{0,16},{8,24},{16,0},{24,8},{1,17},{9,25},{17,1},{25,9},{2,18},{10... | collective-permute-start | bytes 4718600 | tf_op jit(solution)/shard_map/ppermute | solution.py:55
  1103.6 27.9 %collective-permute-start.37 = (bf16[192,2048]{1,0:T(8,128)(2,1)}, bf16[192,2048]{1,0:T(8,128)(2,1)}, u32[]{:S(2)}, u32[]{:S(2)}) collective-permute-start(bf16[192,2048]{1,0:T(8,128)(2,1)} %fusion.25), channel_id=1, source_target_pairs={{0,16},{8,24},{16,0},{24,8},{1,17},{9,25},{17,1},{25,9},{2,18},{10... | collective-permute-start | bytes 2359304 | tf_op jit(solution)/shard_map/ppermute | solution.py:55
  1135.5 18.6 %collective-permute-start.39 = (bf16[192,2048]{1,0:T(8,128)(2,1)}, bf16[192,2048]{1,0:T(8,128)(2,1)}, u32[]{:S(2)}, u32[]{:S(2)}) collective-permute-start(bf16[192,2048]{1,0:T(8,128)(2,1)} %get-tuple-element.149), channel_id=1, source_target_pairs={{0,8},{8,0},{16,24},{24,16},{1,9},{9,1},{17,25},{25,17},{2,10},{10... | collective-permute-start | bytes 2359304 | tf_op jit(solution)/shard_map/ppermute | solution.py:51
  1136.8 10.1 all-to-all-start.3
  1147.7 4.8 collective-permute-start.43
  1149.0 3.6 collective-permute-start.44
  1149.6 4.5 collective-permute-start.45
  1157.9 35.1 %collective-permute-start.47 = (bf16[768,1024]{1,0:T(8,128)(2,1)}, bf16[768,1024]{1,0:T(8,128)(2,1)}, u32[]{:S(2)}, u32[]{:S(2)}) collective-permute-start(bf16[768,1024]{1,0:T(8,128)(2,1)} %fusion.15), channel_id=1, source_target_pairs={{0,8},{8,0},{16,24},{24,16},{1,9},{9,1},{17,25},{25,17},{2,10},{10... | collective-permute-start | bytes 4718600 | tf_op jit(solution)/shard_map/ppermute | solution.py:51
  1164.0 36.0 %collective-permute-start.46 = (bf16[768,1024]{1,0:T(8,128)(2,1)S(1)}, bf16[768,1024]{1,0:T(8,128)(2,1)S(1)}, u32[]{:S(2)}, u32[]{:S(2)}) collective-permute-start(bf16[768,1024]{1,0:T(8,128)(2,1)S(1)} %fusion.18), channel_id=1, source_target_pairs={{0,16},{8,24},{16,0},{24,8},{1,17},{9,25},{17,1},{25,9},{2,18},{10... | collective-permute-start | bytes 4718600 | tf_op jit(solution)/shard_map/ppermute | solution.py:55
  1208.8 16.2 %collective-permute-start.40 = (bf16[1,64,1536]{2,1,0:T(8,128)(2,1)S(1)}, bf16[1,64,1536]{2,1,0:T(8,128)(2,1)S(1)}, u32[]{:S(2)}, u32[]{:S(2)}) collective-permute-start(bf16[1,64,1536]{2,1,0:T(8,128)(2,1)S(1)} %get-tuple-element.250), channel_id=1, source_target_pairs={{0,8},{8,0},{16,24},{24,16},{1,9},{9,1},{17,25},{25,17},{2,10},{10... | collective-permute-start | bytes 589832 | tf_op jit(solution)/shard_map/ppermute | solution.py:51
  1209.9 22.6 %collective-permute-start.41 = (bf16[1,64,1536]{2,1,0:T(8,128)(2,1)S(1)}, bf16[1,64,1536]{2,1,0:T(8,128)(2,1)S(1)}, u32[]{:S(2)}, u32[]{:S(2)}) collective-permute-start(bf16[1,64,1536]{2,1,0:T(8,128)(2,1)S(1)} %get-tuple-element.249), channel_id=1, source_target_pairs={{0,16},{8,24},{16,0},{24,8},{1,17},{9,25},{17,1},{25,9},{2,18},{10... | collective-permute-start | bytes 589832 | tf_op jit(solution)/shard_map/ppermute | solution.py:55
  1211.2 28.9 %collective-permute-start.42 = (bf16[1,64,1536]{2,1,0:T(8,128)(2,1)S(1)}, bf16[1,64,1536]{2,1,0:T(8,128)(2,1)S(1)}, u32[]{:S(2)}, u32[]{:S(2)}) collective-permute-start(bf16[1,64,1536]{2,1,0:T(8,128)(2,1)S(1)} %get-tuple-element.248), channel_id=1, source_target_pairs={{0,24},{8,16},{16,8},{24,0},{1,25},{9,17},{17,9},{25,1},{2,26},{10... | collective-permute-start | bytes 589832 | tf_op jit(solution)/shard_map/ppermute | solution.py:59
  (99 other events, 1301.2 us)
Sparse Core Ops, SparseCore 0:
  30.8 71.3 all-gather.4
  103.7 27.0 all-gather.6
  132.4 116.2 all-gather.10
  300.1 115.9 all-gather.8
  659.1 140.7 reduce-scatter.4
  974.0 36.1 reduce-scatter.10
  1067.7 69.2 reduce-scatter.8
  1139.3 127.5 reduce-scatter.6

commit v4 on v3

--- a/solution.py
+++ b/solution.py
@@ -102,11 +102,18 @@
     if lax.axis_size("ctx") != 4:
         return lax.all_to_all(blocks, "ctx", split_axis=0, concat_axis=0, tiled=True)
     sends = (lambda part: part, send_x, send_y, send_xy)
-    whole = jnp.zeros_like(blocks)
-    for away, send in enumerate(sends):
-        part = send(lax.dynamic_slice_in_dim(blocks, me ^ away, 1, 0))
-        whole = lax.dynamic_update_slice_in_dim(whole, part, me ^ away, 0)
-    return whole
+    parts = [
+        send(lax.dynamic_index_in_dim(blocks, me ^ away, 0, keepdims=False))
+        for away, send in enumerate(sends)
+    ]
+
+    def from_ctx(c):
+        chosen = parts[0]
+        for away in range(1, 4):
+            chosen = jnp.where((me ^ c) == away, parts[away], chosen)
+        return chosen
+
+    return jnp.stack([from_ctx(c) for c in range(4)])
 
 
 def sum_over_ctx(value):
@@ -132,15 +139,24 @@
             lax.all_gather(w_down, "ctx", axis=0, tiled=True),
         )
     width = w_gate.shape[1]
+    half = (w_gate.shape[0] + w_up.shape[0] + 2 * w_down.shape[0]) // 2
     packed = jnp.concatenate([w_gate, w_up, w_down[:, :width], w_down[:, width:]], axis=0)
-    return packed, send_x(packed), send_y(packed)
-
-
-def gather_expert_far(near):
+    low, high = packed[:half], packed[half:]
+    return (low, high), (send_x(low), send_y(low)), None
+
+
+def gather_expert_more(near, *others):
+    if lax.axis_size("ctx") != 4:
+        return near
+    high = after(near[0][1], *others)
+    return near[0], near[1], (send_x(high), send_y(high))
+
+
+def gather_expert_far(near, *others):
     if lax.axis_size("ctx") != 4:
         return ()
-    half = near[1].shape[0] // 2
-    return send_y(near[1][:half]), send_x(near[2][half:])
+    low, high = after_all((near[1][0], near[2][1]), *others)
+    return send_y(low), send_x(high)
 
 
 def build_expert(w_gate, w_down, near, far, me):
@@ -157,17 +173,15 @@
     def put_down(whole, part, owner, which):
         return lax.dynamic_update_slice(whole, part, (owner * half, which * width))
 
-    for away, part in enumerate(near):
-        both = put_both(both, part[:rows], me ^ away, 0, 0)
-        both = put_both(both, part[rows : 2 * rows], me ^ away, 1, 0)
-        down = put_down(down, part[2 * rows : 2 * rows + half], me ^ away, 0)
-        down = put_down(down, part[2 * rows + half :], me ^ away, 1)
-    low, high = far
-    both = put_both(both, low[:rows], me ^ 3, 0, 0)
-    both = put_both(both, low[rows:], me ^ 3, 1, 0)
-    both = put_both(both, high[:half], me ^ 3, 1, half)
-    down = put_down(down, high[half:rows], me ^ 3, 0)
-    down = put_down(down, high[rows:], me ^ 3, 1)
+    lows = (near[0][0],) + near[1] + (far[0],)
+    highs = (near[0][1],) + near[2] + (far[1],)
+    for away in range(4):
+        low, high, owner = lows[away], highs[away], me ^ away
+        both = put_both(both, low[:rows], owner, 0, 0)
+        both = put_both(both, low[rows:], owner, 1, 0)
+        both = put_both(both, high[:half], owner, 1, half)
+        down = put_down(down, high[half:rows], owner, 0)
+        down = put_down(down, high[rows:], owner, 1)
     return both, down
 
 
@@ -260,7 +274,7 @@
     if lax.axis_size("ctx") != 4:
         ordered = pick_blocks(partial.reshape(blocks, block, -1), slot_table).astype(BF)
         whole = lax.psum_scatter(ordered, "ctx", scatter_dimension=0, tiled=True)
-        return whole.astype(F32), (ordered,), (whole,)
+        return whole.astype(F32), (ordered,), (whole,), (whole,)
 
     def take(owner, part):
         start = slot_table[2 * owner + part] * block
@@ -269,7 +283,7 @@
     sent = scatter_payload(take, me)
     near = send_x(sent[0]), send_y(sent[1])
     far = scatter_second(take, me, *near)
-    return jnp.concatenate(scatter_end(take, me, *near, *far), axis=0), sent, far
+    return jnp.concatenate(scatter_end(take, me, *near, *far), axis=0), sent, near, far
 
 
 def prefix_count(member):
@@ -798,7 +812,11 @@
     query_pre = projected[:, :own_width]
     key_pre = projected[:, own_width : 2 * own_width]
     squares = jnp.stack([jnp.sum(query_pre * query_pre, axis=1), jnp.sum(key_pre * key_pre, axis=1)])
-    roots = lax.rsqrt(sum_over_ctx(squares) / D + epsilon)
+    if ctx_size == 4:
+        squares = after(squares, *first_near[1])
+    squares = sum_over_ctx(squares)
+    first_near = gather_expert_more(first_near, squares)
+    roots = lax.rsqrt(squares / D + epsilon)
     root_query, root_key = roots[0][:, None], roots[1][:, None]
     normed_query = query_pre * root_query
     normed_key = key_pre * root_key
@@ -812,15 +830,18 @@
         own_width,
     )
     branch_part = jnp.dot(context_low, out_full, preferred_element_type=F32)
-    branch, unused, branch_there = scatter_group(after(branch_part, *first_near), slot_table, me)
-    first_far = gather_expert_far(after_all(first_near, *branch_there))
-    expert_weights = [build_expert(w_gate[0], w_down[0], first_near, first_far, me)]
+    if ctx_size == 4:
+        branch_part = after(branch_part, *first_near[1], *first_near[2])
+    branch, unused, unused, branch_there = scatter_group(branch_part, slot_table, me)
+    far = gather_expert_far(first_near, *branch_there)
+    expert_weights = [build_expert(w_gate[0], w_down[0], first_near, far, me)]
     backs = [back_rows(row_tables[0], upstream_all, expert_weights[0][1])]
     for e in range(1, own_experts):
-        near = gather_expert(*after_all((w_gate[e], w_up[e], w_down[e]), *branch_there), me)
-        far = gather_expert_far(after_all(near, backs[e - 1][1]))
+        gates = far if ctx_size == 4 else branch_there
+        near = gather_expert(*after_all((w_gate[e], w_up[e], w_down[e]), *gates), me)
+        near = gather_expert_more(near)
+        far = gather_expert_far(near, backs[0][1])
         expert_weights.append(build_expert(w_gate[e], w_down[e], near, far, me))
-        backs.append(back_rows(row_tables[e], upstream_all, expert_weights[e][1]))
 
     inputs = tokens.astype(F32)
     middle = inputs + branch
@@ -832,18 +853,22 @@
     router_prob = jax.nn.softmax(logits, axis=-1)
 
     every = range(own_experts)
-    made = [
-        expert_rows(
-            row_tables[e],
-            e,
-            own_ids[:1],
-            hidden_all,
-            router_full,
-            expert_weights[e][0],
-            backs[e][1],
+    made = []
+    for e in every:
+        if e > 0:
+            upstream = after(upstream_all, made[-1][3])
+            backs.append(back_rows(row_tables[e], upstream, expert_weights[e][1]))
+        made.append(
+            expert_rows(
+                row_tables[e],
+                e,
+                own_ids[:1],
+                hidden_all,
+                router_full,
+                expert_weights[e][0],
+                backs[e][1],
+            )
         )
-        for e in every
-    ]
     shares = [m[4].reshape(1, capacity) for m in made]
     grad_two_part, share_token = combine_rows(token_tables, [m[3] for m in made], shares)
     grad_two = lax.psum_scatter(grad_two_part, "exp", scatter_dimension=0, tiled=True)
@@ -856,20 +881,30 @@
     )
     grad_prob = jnp.swapaxes(share_back, 0, 1).reshape(tok_rows, experts)
     expert_grads = []
+    results, mixture_part = [], grad_two_part
     for e in every:
-        rows, hidden, grad_hidden = after_all(made[e][:3], grad_two_part)
+        rows, hidden, grad_hidden = after_all(made[e][:3], mixture_part)
         expert_grads.append(
             (
                 lax.dot_general(rows, grad_hidden, TN, preferred_element_type=F32).astype(BF),
                 lax.dot_general(hidden, backs[e][0], TN, preferred_element_type=F32).astype(BF),
             )
         )
-    results = [
-        jnp.dot(made[e][1], expert_weights[e][1], preferred_element_type=F32).astype(BF)
-        for e in every
-    ]
+        if e == 0:
+            results = [
+                jnp.dot(
+                    after(made[k][1], *expert_grads[0]),
+                    expert_weights[k][1],
+                    preferred_element_type=F32,
+                ).astype(BF)
+                for k in every
+            ]
+            mixture_part, unused = combine_rows(token_tables, results, shares)
+    mixture = lax.psum_scatter(mixture_part, "exp", scatter_dimension=0, tiled=True)
+    output = (middle + mixture.astype(F32)).astype(BF)
+
     grad_two = after(
-        grad_two, *results, *(part for grads in expert_grads[1:] for part in grads)
+        grad_two, mixture_part, *(part for grads in expert_grads[1:] for part in grads)
     ).astype(F32)
     grad_logits = (
         router_prob * (grad_prob - jnp.sum(router_prob * grad_prob, axis=-1, keepdims=True))
@@ -882,16 +917,13 @@
     grad_middle = cotangent.astype(F32) + norm_back(grad_two * gain_ffn, normed_two, root_two)
 
     sums = [scatter_expert_first(expert_grads[0], me)]
-    more = [scatter_expert_second(expert_grads[0], after_all(sums[0], *results), me)]
+    more = [scatter_expert_second(expert_grads[0], after_all(sums[0], mixture_part), me)]
     own_grad = after(grad_middle.astype(BF), *more[0])
     branch_grad, grad_there = gather_group(own_grad, slot_table, me)
-    mixture_part, unused = combine_rows(token_tables, after_all(results, own_grad), shares)
-    mixture = lax.psum_scatter(mixture_part, "exp", scatter_dimension=0, tiled=True).astype(F32)
-    output = (middle + mixture).astype(BF)
     for e in range(1, own_experts):
         sums.append(scatter_expert_first(after_all(expert_grads[e], *grad_there), me))
     early_sums = sum_to_rows(jnp.concatenate([grad_router, grad_ffn_gain[None]]), me)
-    branch_grad = after(branch_grad, mixture_part, early_sums)
+    branch_grad = after(branch_grad, early_sums)
     grad_context = lax.dot_general(branch_grad, out_full, NT, preferred_element_type=F32).astype(BF)
     out_grad = jnp.einsum("td,te->de", context_low, branch_grad, preferred_element_type=F32)
     grad_query_norm, grad_key_norm, grad_value = attend_back(
@@ -901,17 +933,13 @@
     grad_key_gain = jnp.sum(grad_key_norm * normed_key, axis=0)
     scaled_query = grad_query_norm * gain_query
     scaled_key = grad_key_norm * gain_key
-    means = (
-        sum_over_ctx(
-            jnp.stack(
-                [
-                    jnp.sum(scaled_query * normed_query, axis=1),
-                    jnp.sum(scaled_key * normed_key, axis=1),
-                ]
-            )
-        )
-        / D
-    )
+    products = jnp.stack(
+        [jnp.sum(scaled_query * normed_query, axis=1), jnp.sum(scaled_key * normed_key, axis=1)]
+    )
+    products = after(products, *(piece for pieces in sums[1:] for piece in pieces))
+    means = sum_over_ctx(products) / D
+    for e in range(1, own_experts):
+        more.append(scatter_expert_second(expert_grads[e], after_all(sums[e], means), me))
     grad_projected = jnp.concatenate(
         [
             root_query * (scaled_query - normed_query * means[0][:, None]),
@@ -920,19 +948,18 @@
         ],
         axis=1,
     ).astype(BF)
-    grad_projected = after(grad_projected, *(piece for pieces in sums[1:] for piece in pieces))
     grad_packed = jnp.pad(grad_projected, ((0, 0), (0, 128)))
     grad_one_part = lax.dot_general(grad_packed, packed, NT, preferred_element_type=F32)
     grad_attn_gain = jnp.sum(grad_one_part * normed_group, axis=0)
-    grad_one, one_sent, one_there = scatter_group(grad_one_part, slot_table, me)
-    for e in range(1, own_experts):
-        more.append(scatter_expert_second(expert_grads[e], after_all(sums[e], *one_there), me))
+    grad_one, one_sent, one_near, unused = scatter_group(
+        after(grad_one_part, *(piece for pieces in more[1:] for piece in pieces)), slot_table, me
+    )
     weight_sums = [scatter_expert_end(expert_grads[e], sums[e], more[e], me) for e in every]
     gate_grad, up_grad, down_grad = (jnp.stack(parts) for parts in zip(*weight_sums))
     left, right = after_all((hidden_one, grad_projected), *one_sent)
     qkv_grad = lax.dot_general(left, right, TN, preferred_element_type=F32)
     out_sum = lax.psum_scatter(
-        out_grad.astype(BF), "exp", scatter_dimension=0, tiled=True
+        after(out_grad.astype(BF), mixture), "exp", scatter_dimension=0, tiled=True
     ).astype(F32)
     qkv_sum = lax.psum_scatter(
         qkv_grad.astype(BF).reshape(ctx_size, exp_size * part_rows, 3 * own_width),
@@ -951,7 +978,9 @@
     head_gains = lax.dynamic_update_slice(
         jnp.zeros((2, D), F32), jnp.stack([grad_query_gain, grad_key_gain]), (0, me * own_width)
     )
-    late_sums = sum_to_rows(jnp.concatenate([grad_attn_gain[None], head_gains]), me)
+    late_sums = sum_to_rows(
+        after(jnp.concatenate([grad_attn_gain[None], head_gains]), *one_near), me
+    )
     return (
         output,
         grad_input,

time: 1290 us -> 1200 us (0.930)
  waiting for transfers between devices: 405 us -> 340 us
  local copies, waits for them, and re-layouts: 217 us -> 177 us
  starting transfers between devices: 77 us -> 95 us
    ppermute x22 -> x24, waiting for transfers between devices: 316 us -> 218 us  [send_x(): return lax.ppermute(value, 'ctx', X_PAIRS)]
    ppermute x22 -> x24, waiting for transfers between devices: 56.1 us -> 98.4 us  [send_y(): return lax.ppermute(value, 'ctx', Y_PAIRS)]
    dynamic_update_slice x15 -> x0, local copies, waits for them, and re-layouts: 29.4 us -> none  [exchange(): whole = lax.dynamic_update_slice_in_dim(whole, part, me ^ away, 0)]
    ppermute x4, waiting for transfers between devices: 1.46 us -> 19 us  [send_xy(): return lax.ppermute(value, 'ctx', XY_PAIRS)]
    reduce_scatter x1, waiting for transfers between devices: 15 us -> 0.02 us  [local(): lax.psum_scatter(mixture_part, 'exp', scatter_dimension=0, tiled=True)]
    unnamed x214 -> x212, local copies, waits for them, and re-layouts: 26.2 us -> 16.2 us
    ppermute x22 -> x24, starting transfers between devices: 21.1 us -> 28 us  [send_y(): return lax.ppermute(value, 'ctx', Y_PAIRS)]
    ppermute x22 -> x24, starting transfers between devices: 27.6 us -> 23.2 us  [send_x(): return lax.ppermute(value, 'ctx', X_PAIRS)]
  transfers between devices with their start and end apart: 60 -> 64, of which waited for: 28 -> 34; matrix products, arithmetic and copies ran while one was open for 37% -> 38% of each run, Pallas kernels for 10% -> 8%
where the time goes in v4:
time: 1200 us; the launch traced here: 1190 us
  waiting for transfers between devices  340 us (28%)
  Pallas kernels  250 us (21%)
  local copies, waits for them, and re-layouts  177 us (15%)
  matrix products  170 us (14%)
  other arithmetic  134 us (11%)
  starting transfers between devices  95 us (8%)
  between operations  21.5 us (2%)
    ppermute x24, waiting for transfers between devices, send_x(): return lax.ppermute(value, 'ctx', X_PAIRS)  218 us
    pallas_call x2, Pallas kernels, expert_rows(): pl.pallas_call(functools.partial(expert_kernel, own), out_shape=[made(wid...  103 us
    ppermute x24, waiting for transfers between devices, send_y(): return lax.ppermute(value, 'ctx', Y_PAIRS)  98.4 us
    pallas_call x2, Pallas kernels, back_rows(): pl.pallas_call(back_rows_kernel, out_shape=[jax.ShapeDtypeStruct((capacit...  50.1 us
    dot_general x2, matrix products, local(): lax.dot_general(rows, grad_hidden, TN, preferred_element_type=F32)  46.8 us
    pallas_call x2, Pallas kernels, combine_rows(): pl.pallas_call(functools.partial(combine_kernel, experts), out_shape=[jax...  40.8 us
    pallas_call x1, Pallas kernels, attend_back(): pl.pallas_call(functools.partial(attend_back_kernel, tiles, 1.0 / math.sq...  30.1 us
    dynamic_update_slice x24, local copies, waits for them, and re-layouts, put_both(): lax.dynamic_update_slice(whole, part[None], (which, owner * rows + first,...  29.6 us
  transfers between devices with their start and end apart: 64, of which 34 were waited for; matrix products, arithmetic and copies ran while one was open for 38% of the time, Pallas kernels for 8%

profile of v4, /device:TPU:0, one launch (start us, length us, event | category | flops | bytes accessed | tf_op | source)
XLA Modules:
  0.0 1185.9 jit_solution(13399988674923329034)
XLA Ops:
  17.1 3.9 collective-permute-start.4
  21.6 5.8 collective-permute-done.4
  27.4 3.7 collective-permute-done.5
  36.2 4.9 all-to-all-start
  47.4 3.5 broadcast.205.clone
  52.8 4.4 slice_bitcast_fusion.15
  62.6 14.7 %select_reduce_fusion = s32[2,2048]{1,0:T(2,128)S(1)} fusion(s32[2,3072]{1,0:T(2,128)S(1)} %copy.317, pred[2,3072]{1,0:T(4,128)(4,1)S(1)} %bitcast.536), kind=kLoop, calls=%fused_computation | loop fusion | flops 50327552 | bytes 47104 | tf_op jit(solution)/shard_map/reduce_max | solution.py:773
  90.8 9.7 collective-permute-done.2
  100.5 7.6 collective-permute-done.3
  120.5 4.1 fusion.5
  126.8 4.7 fusion.3
  131.6 12.6 %fusion.145.qp_ref.kp_ref.vp_ref = f32[1536,1664]{1,0:T(8,128)S(1)} fusion(bf16[1536,2048]{1,0:T(8,128)(2,1)S(1)} %fusion.3, bf16[2048,1664]{1,0:T(8,128)(2,1)S(1)} %bitcast.529), kind=kOutput, calls=%fused_computation.488 | convolution fusion | flops 10468982784 | bytes 23330816 | tf_op jit(solution)/shard_map/dot_general | solution.py:811
  144.7 5.6 collective-permute-done.7
  164.1 25.5 %shard_map.272 = (bf16[1536,512]{1,0:T(8,128)(2,1)S(1)}, bf16[1536,512]{1,0:T(8,128)(2,1)}, bf16[1536,512]{1,0:T(8,128)(2,1)}, bf16[1536,512]{1,0:T(8,128)(2,1)}) custom-call(f32[1536,1664]{1,0:T(8,128)} %copy-done.14, f32[1536,1664]{1,0:T(8,128)} %copy-done.14, f32[1536,1664]{1,0:T(8,128)} %copy-done.14, f32[1536,2]{1,0:T(8,128)S(1)} %fusion.129.root_ref.key_root_ref, ...), custom_call_target="tpu_custom_call" | custom-call | flops 3221225472 | bytes 15728640 | tf_op jit(solution)/shard_map/pallas_call | solution.py:373
  190.8 5.6 fusion.146
  199.8 30.0 %collective-permute-done.13 = bf16[2,192,2048]{2,1,0:T(8,128)(2,1)S(1)} collective-permute-done((bf16[2,192,2048]{2,1,0:T(8,128)(2,1)S(1)}, bf16[2,192,2048]{2,1,0:T(8,128)(2,1)S(1)}, u32[]{:S(2)}, u32[]{:S(2)}) %collective-permute-start.13) | collective-permute-done | bytes 1572896 | tf_op jit(solution)/shard_map/ppermute | solution.py:51
  232.9 14.6 %collective-permute-done.14 = bf16[192,2048]{1,0:T(8,128)(2,1)S(1)} collective-permute-done((bf16[192,2048]{1,0:T(8,128)(2,1)S(1)}, bf16[192,2048]{1,0:T(8,128)(2,1)S(1)}, u32[]{:S(2)}, u32[]{:S(2)}) %collective-permute-start.14) | collective-permute-done | bytes 786464 | tf_op jit(solution)/shard_map/ppermute | solution.py:55
  249.3 15.4 %collective-permute-done.16 = bf16[192,2048]{1,0:T(8,128)(2,1)S(1)} collective-permute-done((bf16[192,2048]{1,0:T(8,128)(2,1)S(1)}, bf16[192,2048]{1,0:T(8,128)(2,1)S(1)}, u32[]{:S(2)}, u32[]{:S(2)}) %collective-permute-start.16) | collective-permute-done | bytes 786464 | tf_op jit(solution)/shard_map/ppermute | solution.py:51
  273.5 4.9 broadcast.218.clone
  302.8 16.3 %collective-permute-done.17 = bf16[768,1024]{1,0:T(8,128)(2,1)S(1)} collective-permute-done((bf16[768,1024]{1,0:T(8,128)(2,1)S(1)}, bf16[768,1024]{1,0:T(8,128)(2,1)S(1)}, u32[]{:S(2)}, u32[]{:S(2)}) %collective-permute-start.17) | collective-permute-done | bytes 1572896 | tf_op jit(solution)/shard_map/ppermute | solution.py:55
  331.2 4.4 broadcast.218.clone.1
  342.6 22.0 %collective-permute-done.19 = bf16[768,1024]{1,0:T(8,128)(2,1)S(1)} collective-permute-done((bf16[768,1024]{1,0:T(8,128)(2,1)}, bf16[768,1024]{1,0:T(8,128)(2,1)S(1)}, u32[]{:S(2)}, u32[]{:S(2)}) %collective-permute-start.19) | collective-permute-done | bytes 1572896 | tf_op jit(solution)/shard_map/ppermute | solution.py:51
  367.0 25.0 %collective-permute-done.20 = bf16[768,1024]{1,0:T(8,128)(2,1)S(1)} collective-permute-done((bf16[768,1024]{1,0:T(8,128)(2,1)}, bf16[768,1024]{1,0:T(8,128)(2,1)S(1)}, u32[]{:S(2)}, u32[]{:S(2)}) %collective-permute-start.20) | collective-permute-done | bytes 1572896 | tf_op jit(solution)/shard_map/ppermute | solution.py:51
  395.3 24.0 %shard_map.273 = (bf16[2048,2048]{1,0:T(8,128)(2,1)}, f32[2048,1024]{1,0:T(8,128)}) custom-call(s32[1]{0:T(128)} %get-tuple-element.298.tiles_ref, s32[8]{0:T(128)S(1)} %get-tuple-element.316.low_ref, s32[8]{0:T(128)S(1)} %get-tuple-element.294.windows_ref, s32[2048,1]{1,0:T(8,128)S(1)} %copy-done.4, ...), custom_call_target="tpu_custom_call" | custom-call | flops 9663676416 | bytes 33554432 | tf_op jit(solution)/shard_map/pallas_call | solution.py:526
  435.2 17.1 %collective-permute-done.23 = bf16[768,1024]{1,0:T(8,128)(2,1)S(1)} collective-permute-done((bf16[768,1024]{1,0:T(8,128)(2,1)S(1)}, bf16[768,1024]{1,0:T(8,128)(2,1)S(1)}, u32[]{:S(2)}, u32[]{:S(2)}) %collective-permute-start.23) | collective-permute-done | bytes 1572896 | tf_op jit(solution)/shard_map/ppermute | solution.py:55
  459.7 48.9 %shard_map.274 = (bf16[2048,2048]{1,0:T(8,128)(2,1)}, bf16[2048,1024]{1,0:T(8,128)(2,1)}, bf16[2048,2048]{1,0:T(8,128)(2,1)}, bf16[2048,2048]{1,0:T(8,128)(2,1)}, f32[2048,1]{1,0:T(8,128)}) custom-call(s32[1]{0:T(128)} %get-tuple-element.298.tiles_ref, s32[8]{0:T(128)} %copy-done.10, s32[8]{0:T(128)} %copy-done.9, s32[1]{0:T(128)} %bitcast.554, ...), custom_call_target="tpu_custom_call" | custom-call | flops 28991029248 | bytes 58720256 | tf_op jit(solution)/shard_map/pallas_call | solution.py:614
  510.1 26.1 %shard_map.275 = (bf16[2048,2048]{1,0:T(8,128)(2,1)}, f32[2048,1024]{1,0:T(8,128)}) custom-call(s32[1]{0:T(128)} %get-tuple-element.297.tiles_ref, s32[8]{0:T(128)S(1)} %get-tuple-element.317.low_ref, s32[8]{0:T(128)S(1)} %get-tuple-element.293.windows_ref, s32[2048,1]{1,0:T(8,128)S(1)} %copy.330.tok_ref, ...), custom_call_target="tpu_custom_call" | custom-call | flops 9663676416 | bytes 33554432 | tf_op jit(solution)/shard_map/pallas_call | solution.py:526
  536.2 54.4 %shard_map.276 = (bf16[2048,2048]{1,0:T(8,128)(2,1)}, bf16[2048,1024]{1,0:T(8,128)(2,1)}, bf16[2048,2048]{1,0:T(8,128)(2,1)}, bf16[2048,2048]{1,0:T(8,128)(2,1)}, f32[2048,1]{1,0:T(8,128)}) custom-call(s32[1]{0:T(128)} %get-tuple-element.297.tiles_ref, s32[8]{0:T(128)} %copy-done.8, s32[8]{0:T(128)} %copy-done.7, s32[1]{0:T(128)} %bitcast.555, ...), custom_call_target="tpu_custom_call" | custom-call | flops 28991029248 | bytes 58720256 | tf_op jit(solution)/shard_map/pallas_call | solution.py:614
  593.6 20.3 %shard_map.277 = (bf16[3072,2048]{1,0:T(8,128)(2,1)}, f32[3072,2]{1,0:T(8,128)S(1)}) custom-call(s32[2,12]{1,0:T(2,128)S(1)} %copy.334.start_ref, s32[2,12]{1,0:T(2,128)S(1)} %copy.335.more_ref, s32[2,12]{1,0:T(2,128)S(1)} %copy.336.wide_ref, s32[3072,2]{1,0:T(8,128)S(1)} %copy-done, bf16[2048,2048]{1,0:T(8,128)(2,1)} %get-tuple-element.90.refs_0_, ...), custom_call_target="tpu_custom_call" | custom-call | flops 6442450944 | bytes 29360128 | tf_op jit(solution)/shard_map/pallas_call | solution.py:674
  615.1 14.3 %convolution_convert_fusion.6 = bf16[1024,2048]{1,0:T(8,128)(2,1)} fusion(bf16[2048,1024]{1,0:T(8,128)(2,1)} %get-tuple-element.106, bf16[2048,2048]{1,0:T(8,128)(2,1)} %get-tuple-element.105), kind=kOutput, calls=%fused_computation.25 | convolution fusion | flops 8592031744 | bytes 16777216 | tf_op jit(solution)/shard_map/dot_general | solution.py:890
  629.5 23.9 %convolution_convert_fusion.4 = bf16[2048,2048]{1,0:T(8,128)(2,1)} fusion(bf16[2048,2048]{1,0:T(8,128)(2,1)} %get-tuple-element.102, bf16[2048,2048]{1,0:T(8,128)(2,1)} %get-tuple-element.103), kind=kOutput, calls=%fused_computation.14 | convolution fusion | flops 17184063488 | bytes 25165824 | tf_op jit(solution)/shard_map/dot_general | solution.py:889
  653.3 13.2 %convolution_convert_fusion.3.refs_0_ = bf16[2048,2048]{1,0:T(8,128)(2,1)} fusion(bf16[2048,1024]{1,0:T(8,128)(2,1)S(1)} %copy-done.93, bf16[1024,2048]{1,0:T(8,128)(2,1)} %slice_dynamic-update-slice_fusion.14.wd_ref), kind=kOutput, calls=%fused_computation.13 | convolution fusion | flops 8594128896 | bytes 16777216 | tf_op jit(solution)/shard_map/dot_general | solution.py:895
  666.5 13.1 %convolution_convert_fusion.2.refs_1_ = bf16[2048,2048]{1,0:T(8,128)(2,1)} fusion(bf16[2048,1024]{1,0:T(8,128)(2,1)S(1)} %copy-done.91, bf16[1024,2048]{1,0:T(8,128)(2,1)} %slice_dynamic-update-slice_fusion.8.wd_ref), kind=kOutput, calls=%fused_computation.12 | convolution fusion | flops 8594128896 | bytes 16777216 | tf_op jit(solution)/shard_map/dot_general | solution.py:895
  679.6 20.5 %shard_map.278 = (bf16[3072,2048]{1,0:T(8,128)(2,1)}, f32[3072,2]{1,0:T(8,128)}) custom-call(s32[2,12]{1,0:T(2,128)S(1)} %copy.334.start_ref, s32[2,12]{1,0:T(2,128)S(1)} %copy.335.more_ref, s32[2,12]{1,0:T(2,128)S(1)} %copy.336.wide_ref, s32[3072,2]{1,0:T(8,128)S(1)} %copy-done.1, bf16[2048,2048]{1,0:T(8,128)(2,1)} %convolution_convert_fusion.3.refs_0_, ...), custom_call_target="tpu_custom_call" | custom-call | flops 6442450944 | bytes 29360128 | tf_op jit(solution)/shard_map/pallas_call | solution.py:674
  704.8 20.5 %all-to-all-start.1 = ((f32[8,384,2]{1,2,0:T(2,128)}), f32[8,384,2]{1,2,0:T(2,128)S(1)}, u32[]{:S(2)}, u32[]{:S(2)}) async-start(f32[8,384,2]{1,2,0:T(2,128)} %copy.337), calls=%async_computation.3 | async-start | bytes 49152 | tf_op jit(solution)/shard_map/all_to_all | solution.py:875
  725.2 3.6 constant_dynamic-slice_fusion.1
  728.9 5.9 constant_dynamic-slice_fusion.43
  741.0 22.9 %convolution_convert_fusion.1 = bf16[2048,2048]{1,0:T(8,128)(2,1)} fusion(bf16[2048,2048]{1,0:T(8,128)(2,1)S(1)} %bitcast.563, bf16[2048,2048]{1,0:T(8,128)(2,1)} %get-tuple-element.113), kind=kOutput, calls=%fused_computation.11 | convolution fusion | flops 17184063488 | bytes 25165824 | tf_op jit(solution)/shard_map/dot_general | solution.py:889
  763.9 11.1 convolution_convert_fusion.5
  775.2 32.6 %collective-permute-done.25 = bf16[2,768,1024]{2,1,0:T(8,128)(2,1)} collective-permute-done((bf16[2,768,1024]{2,1,0:T(8,128)(2,1)}, bf16[2,768,1024]{2,1,0:T(8,128)(2,1)}, u32[]{:S(2)}, u32[]{:S(2)}) %collective-permute-start.25) | collective-permute-done | bytes 3145760 | tf_op jit(solution)/shard_map/ppermute | solution.py:51
  810.0 3.7 fusion.22
  820.0 4.0 multiply_reduce_fusion.4
  825.7 24.3 %collective-permute-done.27 = bf16[768,1024]{1,0:T(8,128)(2,1)} collective-permute-done((bf16[768,1024]{1,0:T(8,128)(2,1)}, bf16[768,1024]{1,0:T(8,128)(2,1)}, u32[]{:S(2)}, u32[]{:S(2)}) %collective-permute-start.27) | collective-permute-done | bytes 1572896 | tf_op jit(solution)/shard_map/ppermute | solution.py:55
  850.0 4.3 collective-permute-done.28
  856.4 3.4 broadcast.205
  861.6 27.3 %collective-permute-done.29 = bf16[384,2048]{1,0:T(8,128)(2,1)S(1)} collective-permute-done((bf16[384,2048]{1,0:T(8,128)(2,1)S(1)}, bf16[384,2048]{1,0:T(8,128)(2,1)S(1)}, u32[]{:S(2)}, u32[]{:S(2)}) %collective-permute-start.29) | collective-permute-done | bytes 1572896 | tf_op jit(solution)/shard_map/ppermute | solution.py:51
  898.7 4.0 all-to-all-start.2
  904.0 4.0 constant_dynamic-slice_fusion.41
  929.8 7.8 convolution_convert_fusion.8.d_ref
  937.7 30.1 %shard_map.279 = (f32[1536,512]{1,0:T(8,128)}, f32[1536,512]{1,0:T(8,128)}, f32[1536,512]{1,0:T(8,128)}) custom-call(bf16[1536,512]{1,0:T(8,128)(2,1)S(1)} %copy-done.12, bf16[1536,512]{1,0:T(8,128)(2,1)S(1)} %copy-done.13, bf16[1536,512]{1,0:T(8,128)(2,1)} %get-tuple-element.120.v_ref, bf16[1536,512]{1,0:T(8,128)(2,1)} %convolution_convert_fusion.8.d_ref, ...), custom_call_target="tpu_custom_call" | custom-call | flops 8053063680 | bytes 15728640 | tf_op jit(solution)/shard_map/pallas_call | solution.py:462
  967.8 6.1 multiply_reduce_fusion.1
  973.9 17.7 %collective-permute-done.36 = bf16[2,768,1024]{2,1,0:T(8,128)(2,1)S(1)} collective-permute-done((bf16[2,768,1024]{2,1,0:T(8,128)(2,1)S(1)}, bf16[2,768,1024]{2,1,0:T(8,128)(2,1)S(1)}, u32[]{:S(2)}, u32[]{:S(2)}) %collective-permute-start.36) | collective-permute-done | bytes 3145760 | tf_op jit(solution)/shard_map/ppermute | solution.py:51
  998.4 8.1 convolution_convert_fusion.7
  1011.9 3.4 fusion.20
  1020.9 3.8 multiply_convert_fusion.1
  1027.1 16.5 %fusion.4 = (f32[2048]{0:T(1024)S(1)}, f32[1536,2048]{1,0:T(8,128)S(1)}) fusion(bf16[1536,2048]{1,0:T(8,128)(2,1)} %constant_dynamic-update-slice_fusion.7, f32[1536]{0:T(1024)S(1)} %copy-done.78, bf16[2048,1664]{1,0:T(8,128)(2,1)} %bitcast.526, bf16[1536,1536]{1,0:T(8,128)(2,1)} %pad_maximum_fusion), kind=kOutput, calls=%fused_computation.8 | convolution fusion | flops 10481563648 | bytes 30423040 | tf_op jit(solution)/shard_map/dot_general | solution.py:952
  1043.6 4.5 collective-permute-done.40
  1048.1 4.2 collective-permute-done.41
  1056.3 14.3 %convolution_convert_fusion = bf16[2048,1536]{1,0:T(8,128)(2,1)} fusion(bf16[1536,2048]{1,0:T(8,128)(2,1)} %copy-done.40, bf16[1536,1536]{1,0:T(8,128)(2,1)S(1)} %copy-done.41), kind=kOutput, calls=%fused_computation.10 | convolution fusion | flops 9666822144 | bytes 17301504 | tf_op jit(solution)/shard_map/dot_general | solution.py:960
  1095.7 20.1 %collective-permute-done.42 = bf16[2,192,2048]{2,1,0:T(8,128)(2,1)S(1)} collective-permute-done((bf16[2,192,2048]{2,1,0:T(8,128)(2,1)}, bf16[2,192,2048]{2,1,0:T(8,128)(2,1)S(1)}, u32[]{:S(2)}, u32[]{:S(2)}) %collective-permute-start.42) | collective-permute-done | bytes 1572896 | tf_op jit(solution)/shard_map/ppermute | solution.py:51
  1123.4 5.2 all-to-all-start.3
  1128.6 4.9 pad_maximum_fusion.1
  1145.5 13.3 %collective-permute-done.49 = f32[3,64]{1,0:T(4,128)S(1)} collective-permute-done((f32[3,64]{1,0:T(4,128)S(1)}, f32[3,64]{1,0:T(4,128)S(1)}, u32[]{:S(2)}, u32[]{:S(2)}) %collective-permute-start.49) | collective-permute-done | bytes 800 | tf_op jit(solution)/shard_map/ppermute | solution.py:59
  1167.7 6.5 fusion.13
  (565 shorter events, 301.9 us)
Async XLA Ops:
  7.2 117.4 %all-gather.5.cloned.1.call-start = ((), (), s32[]{:S(2)}) async-start(), calls=%async_computation.8 | async-start | bytes 7667712 | tf_op jit(solution)/shard_map/all_gather | solution.py:745
  17.1 10.2 collective-permute-start.4
  21.0 10.0 collective-permute-start.5
  21.5 9.8 collective-permute-start.6
  32.8 158.0 %all-gather.7.cloned.1.call-start = ((), (), s32[]{:S(2)}) async-start(), calls=%async_computation.9 | async-start | bytes 2359296 | tf_op jit(solution)/shard_map/all_gather | solution.py:752
  33.5 50.5 %collective-permute-start.1 = (bf16[384,2048]{1,0:T(8,128)(2,1)S(1)}, bf16[384,2048]{1,0:T(8,128)(2,1)}, u32[]{:S(2)}, u32[]{:S(2)}) collective-permute-start(bf16[384,2048]{1,0:T(8,128)(2,1)S(1)} %copy-done.19), channel_id=1, source_target_pairs={{0,16},{8,24},{16,0},{24,8},{1,17},{9,25},{17,1},{25,9},{2,18},{10... | collective-permute-start | bytes 4718600 | tf_op jit(solution)/shard_map/ppermute | solution.py:55
  35.0 42.8 %collective-permute-start = (bf16[384,2048]{1,0:T(8,128)(2,1)S(1)}, bf16[384,2048]{1,0:T(8,128)(2,1)}, u32[]{:S(2)}, u32[]{:S(2)}) collective-permute-start(bf16[384,2048]{1,0:T(8,128)(2,1)S(1)} %copy-done.19), channel_id=1, source_target_pairs={{0,8},{8,0},{16,24},{24,16},{1,9},{9,1},{17,25},{25,17},{2,10},{10... | collective-permute-start | bytes 4718600 | tf_op jit(solution)/shard_map/ppermute | solution.py:51
  36.2 24.9 %all-to-all-start = ((s32[8,384,8]{1,2,0:T(8,128)}), s32[8,384,8]{1,2,0:T(8,128)S(1)}, u32[]{:S(2)}, u32[]{:S(2)}) async-start(s32[8,384,8]{1,2,0:T(8,128)} %broadcast_in_dim.162), calls=%async_computation | async-start | bytes 196608 | tf_op jit(solution)/shard_map/all_to_all | solution.py:753
  41.1 352.9 %all-gather.11.cloned.1.call-start = ((), (), s32[]{:S(2)}) async-start(), calls=%async_computation.11 | async-start | bytes 14155776 | tf_op jit(solution)/shard_map/all_gather | solution.py:760
  41.9 417.8 %all-gather.9.cloned.1.call-start = ((), (), s32[]{:S(2)}) async-start(), calls=%async_computation.10 | async-start | bytes 14155776 | tf_op jit(solution)/shard_map/all_gather | solution.py:851
  80.4 20.1 %collective-permute-start.2 = (bf16[192,2048]{1,0:T(8,128)(2,1)}, bf16[192,2048]{1,0:T(8,128)(2,1)}, u32[]{:S(2)}, u32[]{:S(2)}) collective-permute-start(bf16[192,2048]{1,0:T(8,128)(2,1)} %get-tuple-element.250), channel_id=1, source_target_pairs={{0,16},{8,24},{16,0},{24,8},{1,17},{9,25},{17,1},{25,9},{2,18},{10... | collective-permute-start | bytes 2359304 | tf_op jit(solution)/shard_map/ppermute | solution.py:55
  88.4 19.7 %collective-permute-start.3 = (bf16[192,2048]{1,0:T(8,128)(2,1)S(1)}, bf16[192,2048]{1,0:T(8,128)(2,1)}, u32[]{:S(2)}, u32[]{:S(2)}) collective-permute-start(bf16[192,2048]{1,0:T(8,128)(2,1)S(1)} %get-tuple-element.248), channel_id=1, source_target_pairs={{0,8},{8,0},{16,24},{24,16},{1,9},{9,1},{17,25},{25,17},{2,10},{10... | collective-permute-start | bytes 2359304 | tf_op jit(solution)/shard_map/ppermute | solution.py:51
  114.4 35.8 %collective-permute-start.7 = (bf16[768,1024]{1,0:T(8,128)(2,1)}, bf16[768,1024]{1,0:T(8,128)(2,1)S(1)}, u32[]{:S(2)}, u32[]{:S(2)}) collective-permute-start(bf16[768,1024]{1,0:T(8,128)(2,1)} %get-tuple-element.268), channel_id=1, source_target_pairs={{0,8},{8,0},{16,24},{24,16},{1,9},{9,1},{17,25},{25,17},{2,10},{10... | collective-permute-start | bytes 4718600 | tf_op jit(solution)/shard_map/ppermute | solution.py:51
  115.0 35.8 %collective-permute-start.8 = (bf16[768,1024]{1,0:T(8,128)(2,1)}, bf16[768,1024]{1,0:T(8,128)(2,1)}, u32[]{:S(2)}, u32[]{:S(2)}) collective-permute-start(bf16[768,1024]{1,0:T(8,128)(2,1)} %get-tuple-element.268), channel_id=1, source_target_pairs={{0,16},{8,24},{16,0},{24,8},{1,17},{9,25},{17,1},{25,9},{2,18},{10... | collective-permute-start | bytes 4718600 | tf_op jit(solution)/shard_map/ppermute | solution.py:55
  150.8 4.3 collective-permute-start.9
  155.1 3.8 collective-permute-start.10
  162.3 34.2 %collective-permute-start.11 = (bf16[768,1024]{1,0:T(8,128)(2,1)}, bf16[768,1024]{1,0:T(8,128)(2,1)}, u32[]{:S(2)}, u32[]{:S(2)}) collective-permute-start(bf16[768,1024]{1,0:T(8,128)(2,1)} %get-tuple-element.82), channel_id=1, source_target_pairs={{0,8},{8,0},{16,24},{24,16},{1,9},{9,1},{17,25},{25,17},{2,10},{10... | collective-permute-start | bytes 4718600 | tf_op jit(solution)/shard_map/ppermute | solution.py:51
  163.0 33.7 %collective-permute-start.12 = (bf16[768,1024]{1,0:T(8,128)(2,1)}, bf16[768,1024]{1,0:T(8,128)(2,1)}, u32[]{:S(2)}, u32[]{:S(2)}) collective-permute-start(bf16[768,1024]{1,0:T(8,128)(2,1)} %get-tuple-element.82), channel_id=1, source_target_pairs={{0,16},{8,24},{16,0},{24,8},{1,17},{9,25},{17,1},{25,9},{2,18},{10... | collective-permute-start | bytes 4718600 | tf_op jit(solution)/shard_map/ppermute | solution.py:55
  197.3 32.5 %collective-permute-start.13 = (bf16[2,192,2048]{2,1,0:T(8,128)(2,1)S(1)}, bf16[2,192,2048]{2,1,0:T(8,128)(2,1)S(1)}, u32[]{:S(2)}, u32[]{:S(2)}) collective-permute-start(bf16[2,192,2048]{2,1,0:T(8,128)(2,1)S(1)} %pad_maximum_fusion.14), channel_id=1, source_target_pairs={{0,8},{8,0},{16,24},{24,16},{1,9},{9,1},{17,25},{25,17},{2,10},{10... | collective-permute-start | bytes 4718600 | tf_op jit(solution)/shard_map/ppermute | solution.py:51
  198.6 34.3 %collective-permute-start.15 = (bf16[2,192,2048]{2,1,0:T(8,128)(2,1)S(1)}, bf16[2,192,2048]{2,1,0:T(8,128)(2,1)S(1)}, u32[]{:S(2)}, u32[]{:S(2)}) collective-permute-start(bf16[2,192,2048]{2,1,0:T(8,128)(2,1)S(1)} %pad_maximum_fusion.15), channel_id=1, source_target_pairs={{0,16},{8,24},{16,0},{24,8},{1,17},{9,25},{17,1},{25,9},{2,18},{10... | collective-permute-start | bytes 4718600 | tf_op jit(solution)/shard_map/ppermute | solution.py:55
  230.0 17.4 %collective-permute-start.14 = (bf16[192,2048]{1,0:T(8,128)(2,1)S(1)}, bf16[192,2048]{1,0:T(8,128)(2,1)S(1)}, u32[]{:S(2)}, u32[]{:S(2)}) collective-permute-start(bf16[192,2048]{1,0:T(8,128)(2,1)S(1)} %fusion.29), channel_id=1, source_target_pairs={{0,16},{8,24},{16,0},{24,8},{1,17},{9,25},{17,1},{25,9},{2,18},{10... | collective-permute-start | bytes 2359304 | tf_op jit(solution)/shard_map/ppermute | solution.py:55
  248.1 16.6 %collective-permute-start.16 = (bf16[192,2048]{1,0:T(8,128)(2,1)S(1)}, bf16[192,2048]{1,0:T(8,128)(2,1)S(1)}, u32[]{:S(2)}, u32[]{:S(2)}) collective-permute-start(bf16[192,2048]{1,0:T(8,128)(2,1)S(1)} %get-tuple-element.169), channel_id=1, source_target_pairs={{0,8},{8,0},{16,24},{24,16},{1,9},{9,1},{17,25},{25,17},{2,10},{10... | collective-permute-start | bytes 2359304 | tf_op jit(solution)/shard_map/ppermute | solution.py:51
  269.6 550.3 %reduce-scatter.7.cloned.1.call-start = ((), (), s32[]{:S(2)}) async-start(), calls=%async_computation.13 | async-start | bytes 14155776 | tf_op jit(solution)/shard_map/reduce_scatter | solution.py:874
  286.7 32.4 %collective-permute-start.17 = (bf16[768,1024]{1,0:T(8,128)(2,1)S(1)}, bf16[768,1024]{1,0:T(8,128)(2,1)S(1)}, u32[]{:S(2)}, u32[]{:S(2)}) collective-permute-start(bf16[768,1024]{1,0:T(8,128)(2,1)S(1)} %copy-done.50), channel_id=1, source_target_pairs={{0,16},{8,24},{16,0},{24,8},{1,17},{9,25},{17,1},{25,9},{2,18},{10... | collective-permute-start | bytes 4718600 | tf_op jit(solution)/shard_map/ppermute | solution.py:55
  288.8 32.0 %collective-permute-start.18 = (bf16[768,1024]{1,0:T(8,128)(2,1)}, bf16[768,1024]{1,0:T(8,128)(2,1)S(1)}, u32[]{:S(2)}, u32[]{:S(2)}) collective-permute-start(bf16[768,1024]{1,0:T(8,128)(2,1)} %collective-permute-done.12), channel_id=1, source_target_pairs={{0,8},{8,0},{16,24},{24,16},{1,9},{9,1},{17,25},{25,17},{2,10},{10... | collective-permute-start | bytes 4718600 | tf_op jit(solution)/shard_map/ppermute | solution.py:51
  327.1 37.5 %collective-permute-start.19 = (bf16[768,1024]{1,0:T(8,128)(2,1)}, bf16[768,1024]{1,0:T(8,128)(2,1)S(1)}, u32[]{:S(2)}, u32[]{:S(2)}) collective-permute-start(bf16[768,1024]{1,0:T(8,128)(2,1)} %get-tuple-element.263), channel_id=1, source_target_pairs={{0,8},{8,0},{16,24},{24,16},{1,9},{9,1},{17,25},{25,17},{2,10},{10... | collective-permute-start | bytes 4718600 | tf_op jit(solution)/shard_map/ppermute | solution.py:51
  327.8 93.0 %collective-permute-start.21 = (bf16[768,1024]{1,0:T(8,128)(2,1)}, bf16[768,1024]{1,0:T(8,128)(2,1)}, u32[]{:S(2)}, u32[]{:S(2)}) collective-permute-start(bf16[768,1024]{1,0:T(8,128)(2,1)} %get-tuple-element.263), channel_id=1, source_target_pairs={{0,16},{8,24},{16,0},{24,8},{1,17},{9,25},{17,1},{25,9},{2,18},{10... | collective-permute-start | bytes 4718600 | tf_op jit(solution)/shard_map/ppermute | solution.py:55
  328.9 63.1 %collective-permute-start.20 = (bf16[768,1024]{1,0:T(8,128)(2,1)}, bf16[768,1024]{1,0:T(8,128)(2,1)S(1)}, u32[]{:S(2)}, u32[]{:S(2)}) collective-permute-start(bf16[768,1024]{1,0:T(8,128)(2,1)} %get-tuple-element.262), channel_id=1, source_target_pairs={{0,8},{8,0},{16,24},{24,16},{1,9},{9,1},{17,25},{25,17},{2,10},{10... | collective-permute-start | bytes 4718600 | tf_op jit(solution)/shard_map/ppermute | solution.py:51
  329.4 89.9 %collective-permute-start.22 = (bf16[768,1024]{1,0:T(8,128)(2,1)}, bf16[768,1024]{1,0:T(8,128)(2,1)}, u32[]{:S(2)}, u32[]{:S(2)}) collective-permute-start(bf16[768,1024]{1,0:T(8,128)(2,1)} %get-tuple-element.262), channel_id=1, source_target_pairs={{0,16},{8,24},{16,0},{24,8},{1,17},{9,25},{17,1},{25,9},{2,18},{10... | collective-permute-start | bytes 4718600 | tf_op jit(solution)/shard_map/ppermute | solution.py:55
  419.3 32.9 %collective-permute-start.23 = (bf16[768,1024]{1,0:T(8,128)(2,1)S(1)}, bf16[768,1024]{1,0:T(8,128)(2,1)S(1)}, u32[]{:S(2)}, u32[]{:S(2)}) collective-permute-start(bf16[768,1024]{1,0:T(8,128)(2,1)S(1)} %copy-done.52), channel_id=1, source_target_pairs={{0,16},{8,24},{16,0},{24,8},{1,17},{9,25},{17,1},{25,9},{2,18},{10... | collective-permute-start | bytes 4718600 | tf_op jit(solution)/shard_map/ppermute | solution.py:55
  424.9 32.3 %collective-permute-start.24 = (bf16[768,1024]{1,0:T(8,128)(2,1)}, bf16[768,1024]{1,0:T(8,128)(2,1)S(1)}, u32[]{:S(2)}, u32[]{:S(2)}) collective-permute-start(bf16[768,1024]{1,0:T(8,128)(2,1)} %collective-permute-done.22), channel_id=1, source_target_pairs={{0,8},{8,0},{16,24},{24,16},{1,9},{9,1},{17,25},{25,17},{2,10},{10... | collective-permute-start | bytes 4718600 | tf_op jit(solution)/shard_map/ppermute | solution.py:51
  615.1 393.5 %reduce-scatter.5.cloned.1.call-start = ((), (), s32[]{:S(2)}) async-start(), calls=%async_computation.12 | async-start | bytes 14155776 | tf_op jit(solution)/shard_map/reduce_scatter | solution.py:903
  704.8 70.3 %all-to-all-start.1 = ((f32[8,384,2]{1,2,0:T(2,128)}), f32[8,384,2]{1,2,0:T(2,128)S(1)}, u32[]{:S(2)}, u32[]{:S(2)}) async-start(f32[8,384,2]{1,2,0:T(2,128)} %copy.337), calls=%async_computation.3 | async-start | bytes 49152 | tf_op jit(solution)/shard_map/all_to_all | solution.py:875
  737.0 70.8 %collective-permute-start.25 = (bf16[2,768,1024]{2,1,0:T(8,128)(2,1)}, bf16[2,768,1024]{2,1,0:T(8,128)(2,1)}, u32[]{:S(2)}, u32[]{:S(2)}) collective-permute-start(bf16[2,768,1024]{2,1,0:T(8,128)(2,1)} %pad_maximum_fusion.4), channel_id=1, source_target_pairs={{0,8},{8,0},{16,24},{24,16},{1,9},{9,1},{17,25},{25,17},{2,10},{10... | collective-permute-start | bytes 9437192 | tf_op jit(solution)/shard_map/ppermute | solution.py:51
  739.2 70.8 %collective-permute-start.26 = (bf16[2,768,1024]{2,1,0:T(8,128)(2,1)}, bf16[2,768,1024]{2,1,0:T(8,128)(2,1)}, u32[]{:S(2)}, u32[]{:S(2)}) collective-permute-start(bf16[2,768,1024]{2,1,0:T(8,128)(2,1)} %pad_maximum_fusion.5), channel_id=1, source_target_pairs={{0,16},{8,24},{16,0},{24,8},{1,17},{9,25},{17,1},{25,9},{2,18},{10... | collective-permute-start | bytes 9437192 | tf_op jit(solution)/shard_map/ppermute | solution.py:55
  813.7 36.3 %collective-permute-start.27 = (bf16[768,1024]{1,0:T(8,128)(2,1)}, bf16[768,1024]{1,0:T(8,128)(2,1)}, u32[]{:S(2)}, u32[]{:S(2)}) collective-permute-start(bf16[768,1024]{1,0:T(8,128)(2,1)} %fusion.22), channel_id=1, source_target_pairs={{0,16},{8,24},{16,0},{24,8},{1,17},{9,25},{17,1},{25,9},{2,18},{10... | collective-permute-start | bytes 4718600 | tf_op jit(solution)/shard_map/ppermute | solution.py:55
  818.4 35.9 %collective-permute-start.28 = (bf16[768,1024]{1,0:T(8,128)(2,1)}, bf16[768,1024]{1,0:T(8,128)(2,1)}, u32[]{:S(2)}, u32[]{:S(2)}) collective-permute-start(bf16[768,1024]{1,0:T(8,128)(2,1)} %fusion.21), channel_id=1, source_target_pairs={{0,8},{8,0},{16,24},{24,16},{1,9},{9,1},{17,25},{25,17},{2,10},{10... | collective-permute-start | bytes 4718600 | tf_op jit(solution)/shard_map/ppermute | solution.py:51
  854.3 34.6 %collective-permute-start.29 = (bf16[384,2048]{1,0:T(8,128)(2,1)S(1)}, bf16[384,2048]{1,0:T(8,128)(2,1)S(1)}, u32[]{:S(2)}, u32[]{:S(2)}) collective-permute-start(bf16[384,2048]{1,0:T(8,128)(2,1)S(1)} %fusion.130), channel_id=1, source_target_pairs={{0,8},{8,0},{16,24},{24,16},{1,9},{9,1},{17,25},{25,17},{2,10},{10... | collective-permute-start | bytes 4718600 | tf_op jit(solution)/shard_map/ppermute | solution.py:51
  855.6 36.5 %collective-permute-start.30 = (bf16[384,2048]{1,0:T(8,128)(2,1)S(1)}, bf16[384,2048]{1,0:T(8,128)(2,1)S(1)}, u32[]{:S(2)}, u32[]{:S(2)}) collective-permute-start(bf16[384,2048]{1,0:T(8,128)(2,1)S(1)} %fusion.130), channel_id=1, source_target_pairs={{0,16},{8,24},{16,0},{24,8},{1,17},{9,25},{17,1},{25,9},{2,18},{10... | collective-permute-start | bytes 4718600 | tf_op jit(solution)/shard_map/ppermute | solution.py:55
  890.3 27.8 %collective-permute-start.31 = (bf16[192,2048]{1,0:T(8,128)(2,1)}, bf16[192,2048]{1,0:T(8,128)(2,1)}, u32[]{:S(2)}, u32[]{:S(2)}) collective-permute-start(bf16[192,2048]{1,0:T(8,128)(2,1)} %get-tuple-element.246), channel_id=1, source_target_pairs={{0,16},{8,24},{16,0},{24,8},{1,17},{9,25},{17,1},{25,9},{2,18},{10... | collective-permute-start | bytes 2359304 | tf_op jit(solution)/shard_map/ppermute | solution.py:55
  894.3 23.8 %collective-permute-start.32 = (bf16[192,2048]{1,0:T(8,128)(2,1)}, bf16[192,2048]{1,0:T(8,128)(2,1)}, u32[]{:S(2)}, u32[]{:S(2)}) collective-permute-start(bf16[192,2048]{1,0:T(8,128)(2,1)} %get-tuple-element.244), channel_id=1, source_target_pairs={{0,8},{8,0},{16,24},{24,16},{1,9},{9,1},{17,25},{25,17},{2,10},{10... | collective-permute-start | bytes 2359304 | tf_op jit(solution)/shard_map/ppermute | solution.py:51
  898.7 10.9 all-to-all-start.2
  902.7 179.8 %reduce-scatter.11.cloned.1.call-start = ((), (), s32[]{:S(2)}) async-start(), calls=%async_computation.15 | async-start | bytes 2359296 | tf_op jit(solution)/shard_map/reduce_scatter | solution.py:961
  914.5 11.0 collective-permute-start.33
  915.9 9.6 collective-permute-start.34
  917.0 8.6 collective-permute-start.35
  923.0 68.7 %collective-permute-start.36 = (bf16[2,768,1024]{2,1,0:T(8,128)(2,1)S(1)}, bf16[2,768,1024]{2,1,0:T(8,128)(2,1)S(1)}, u32[]{:S(2)}, u32[]{:S(2)}) collective-permute-start(bf16[2,768,1024]{2,1,0:T(8,128)(2,1)S(1)} %pad_maximum_fusion.6), channel_id=1, source_target_pairs={{0,8},{8,0},{16,24},{24,16},{1,9},{9,1},{17,25},{25,17},{2,10},{10... | collective-permute-start | bytes 9437192 | tf_op jit(solution)/shard_map/ppermute | solution.py:51
  924.5 68.5 %collective-permute-start.37 = (bf16[2,768,1024]{2,1,0:T(8,128)(2,1)S(1)}, bf16[2,768,1024]{2,1,0:T(8,128)(2,1)}, u32[]{:S(2)}, u32[]{:S(2)}) collective-permute-start(bf16[2,768,1024]{2,1,0:T(8,128)(2,1)S(1)} %pad_maximum_fusion.7), channel_id=1, source_target_pairs={{0,16},{8,24},{16,0},{24,8},{1,17},{9,25},{17,1},{25,9},{2,18},{10... | collective-permute-start | bytes 9437192 | tf_op jit(solution)/shard_map/ppermute | solution.py:55
  993.0 3.7 collective-permute-start.38
  997.4 11.3 collective-permute-start.39
  1008.6 154.4 %reduce-scatter.9.cloned.1.call-start = ((), (), s32[]{:S(2)}) async-start(), calls=%async_computation.14 | async-start | bytes 7077888 | tf_op jit(solution)/shard_map/reduce_scatter | solution.py:964
  1015.4 32.8 %collective-permute-start.40 = (bf16[768,1024]{1,0:T(8,128)(2,1)}, bf16[768,1024]{1,0:T(8,128)(2,1)}, u32[]{:S(2)}, u32[]{:S(2)}) collective-permute-start(bf16[768,1024]{1,0:T(8,128)(2,1)} %fusion.20), channel_id=1, source_target_pairs={{0,16},{8,24},{16,0},{24,8},{1,17},{9,25},{17,1},{25,9},{2,18},{10... | collective-permute-start | bytes 4718600 | tf_op jit(solution)/shard_map/ppermute | solution.py:55
  1019.7 32.6 %collective-permute-start.41 = (bf16[768,1024]{1,0:T(8,128)(2,1)}, bf16[768,1024]{1,0:T(8,128)(2,1)}, u32[]{:S(2)}, u32[]{:S(2)}) collective-permute-start(bf16[768,1024]{1,0:T(8,128)(2,1)} %fusion.19), channel_id=1, source_target_pairs={{0,8},{8,0},{16,24},{24,16},{1,9},{9,1},{17,25},{25,17},{2,10},{10... | collective-permute-start | bytes 4718600 | tf_op jit(solution)/shard_map/ppermute | solution.py:51
  1084.2 31.6 %collective-permute-start.42 = (bf16[2,192,2048]{2,1,0:T(8,128)(2,1)}, bf16[2,192,2048]{2,1,0:T(8,128)(2,1)S(1)}, u32[]{:S(2)}, u32[]{:S(2)}) collective-permute-start(bf16[2,192,2048]{2,1,0:T(8,128)(2,1)} %pad_maximum_fusion.16), channel_id=1, source_target_pairs={{0,8},{8,0},{16,24},{24,16},{1,9},{9,1},{17,25},{25,17},{2,10},{10... | collective-permute-start | bytes 4718600 | tf_op jit(solution)/shard_map/ppermute | solution.py:51
  1085.4 37.2 %collective-permute-start.44 = (bf16[2,192,2048]{2,1,0:T(8,128)(2,1)}, bf16[2,192,2048]{2,1,0:T(8,128)(2,1)}, u32[]{:S(2)}, u32[]{:S(2)}) collective-permute-start(bf16[2,192,2048]{2,1,0:T(8,128)(2,1)} %pad_maximum_fusion.17), channel_id=1, source_target_pairs={{0,16},{8,24},{16,0},{24,8},{1,17},{9,25},{17,1},{25,9},{2,18},{10... | collective-permute-start | bytes 4718600 | tf_op jit(solution)/shard_map/ppermute | solution.py:55
  1118.9 16.6 %collective-permute-start.43 = (bf16[192,2048]{1,0:T(8,128)(2,1)}, bf16[192,2048]{1,0:T(8,128)(2,1)S(1)}, u32[]{:S(2)}, u32[]{:S(2)}) collective-permute-start(bf16[192,2048]{1,0:T(8,128)(2,1)} %fusion.25), channel_id=1, source_target_pairs={{0,16},{8,24},{16,0},{24,8},{1,17},{9,25},{17,1},{25,9},{2,18},{10... | collective-permute-start | bytes 2359304 | tf_op jit(solution)/shard_map/ppermute | solution.py:55
  1123.4 11.2 all-to-all-start.3
  1138.5 20.8 %collective-permute-start.45 = (bf16[192,2048]{1,0:T(8,128)(2,1)S(1)}, bf16[192,2048]{1,0:T(8,128)(2,1)S(1)}, u32[]{:S(2)}, u32[]{:S(2)}) collective-permute-start(bf16[192,2048]{1,0:T(8,128)(2,1)S(1)} %get-tuple-element.163), channel_id=1, source_target_pairs={{0,8},{8,0},{16,24},{24,16},{1,9},{9,1},{17,25},{25,17},{2,10},{10... | collective-permute-start | bytes 2359304 | tf_op jit(solution)/shard_map/ppermute | solution.py:51
  1139.6 19.2 %collective-permute-start.49 = (f32[3,64]{1,0:T(4,128)S(1)}, f32[3,64]{1,0:T(4,128)S(1)}, u32[]{:S(2)}, u32[]{:S(2)}) collective-permute-start(f32[3,64]{1,0:T(4,128)S(1)} %bitcast.551), channel_id=1, source_target_pairs={{0,24},{8,16},{16,8},{24,0},{1,25},{9,17},{17,9},{25,1},{2,26},{10... | collective-permute-start | bytes 2312 | tf_op jit(solution)/shard_map/ppermute | solution.py:59
  1141.4 17.4 %collective-permute-start.50 = (f32[3,64]{1,0:T(4,128)S(1)}, f32[3,64]{1,0:T(4,128)S(1)}, u32[]{:S(2)}, u32[]{:S(2)}) collective-permute-start(f32[3,64]{1,0:T(4,128)S(1)} %bitcast.552), channel_id=1, source_target_pairs={{0,16},{8,24},{16,0},{24,8},{1,17},{9,25},{17,1},{25,9},{2,18},{10... | collective-permute-start | bytes 2312 | tf_op jit(solution)/shard_map/ppermute | solution.py:55
  1142.2 16.6 %collective-permute-start.51 = (f32[3,64]{1,0:T(4,128)S(1)}, f32[3,64]{1,0:T(4,128)S(1)}, u32[]{:S(2)}, u32[]{:S(2)}) collective-permute-start(f32[3,64]{1,0:T(4,128)S(1)} %bitcast.553), channel_id=1, source_target_pairs={{0,8},{8,0},{16,24},{24,16},{1,9},{9,1},{17,25},{25,17},{2,10},{10... | collective-permute-start | bytes 2312 | tf_op jit(solution)/shard_map/ppermute | solution.py:51
  1164.1 10.1 collective-permute-start.46
  1165.4 9.5 collective-permute-start.47
  1166.5 8.5 collective-permute-start.48
  (100 other events, 2095.2 us)
Sparse Core Ops, SparseCore 0:
  32.9 71.2 all-gather.4
  105.8 27.0 all-gather.6
  134.5 116.2 all-gather.10
  269.7 116.3 all-gather.8
  615.2 144.3 reduce-scatter.6
  761.8 127.5 reduce-scatter.4
  1008.7 35.2 reduce-scatter.10
  1070.7 70.4 reduce-scatter.8

commit v5 on v4

--- a/solution.py
+++ b/solution.py
@@ -67,35 +67,34 @@
     return lax.optimization_barrier(tuple(values) + others)[: len(values)]
 
 
-def gather_pieces(value, half):
-    from_x = send_x(value)
-    from_y = send_y(value)
-    far_low = send_y(from_x[:half])
-    far_high = send_x(from_y[half:])
-    return from_x, from_y, far_low, far_high
-
-
-def scatter_payload(take, me):
-    low = jnp.stack([take(me ^ 1, 0), take(me ^ 3, 0)]).astype(BF)
-    high = jnp.stack([take(me ^ 2, 1), take(me ^ 3, 1)]).astype(BF)
-    return low, high
-
-
-def scatter_first(take, me):
-    low, high = scatter_payload(take, me)
+def gather_pieces(low, high):
+    low_x, high_y = send_x(low), send_y(high)
+    high_x, low_y = send_x(high), send_y(low)
+    return (low_x, low_y, send_y(low_x)), (high_x, high_y, send_x(high_y))
+
+
+def scatter_ahead(take, me):
+    return send_x(take(me ^ 3, 0).astype(BF)), send_y(take(me ^ 3, 1).astype(BF))
+
+
+def scatter_direct(take, me, *others):
+    low, high = take(me ^ 1, 0).astype(BF), take(me ^ 2, 1).astype(BF)
+    if others:
+        low, high = after_all((low, high), *others)
     return send_x(low), send_y(high)
 
 
-def scatter_second(take, me, low, high):
-    low_next = send_y((take(me ^ 2, 0).astype(F32) + low[1].astype(F32)).astype(BF))
-    high_next = send_x((take(me ^ 1, 1).astype(F32) + high[1].astype(F32)).astype(BF))
-    return low_next, high_next
-
-
-def scatter_end(take, me, low, high, low_next, high_next):
-    first = take(me, 0).astype(F32) + low[0].astype(F32) + low_next.astype(F32)
-    second = take(me, 1).astype(F32) + high[0].astype(F32) + high_next.astype(F32)
-    return first, second
+def scatter_last(take, me, ahead):
+    low = (take(me ^ 2, 0).astype(F32) + ahead[0].astype(F32)).astype(BF)
+    high = (take(me ^ 1, 1).astype(F32) + ahead[1].astype(F32)).astype(BF)
+    return send_y(low), send_x(high)
+
+
+def scatter_end(take, me, direct, last):
+    return [
+        take(me, part).astype(F32) + direct[part].astype(F32) + last[part].astype(F32)
+        for part in range(2)
+    ]
 
 
 def exchange(blocks, me):
@@ -132,57 +131,18 @@
     return jnp.sum(exchange(parts, me), axis=0)
 
 
-def gather_expert(w_gate, w_up, w_down, me):
-    if lax.axis_size("ctx") != 4:
-        return (
-            lax.all_gather(jnp.stack([w_gate, w_up]), "ctx", axis=1, tiled=True),
-            lax.all_gather(w_down, "ctx", axis=0, tiled=True),
-        )
-    width = w_gate.shape[1]
-    half = (w_gate.shape[0] + w_up.shape[0] + 2 * w_down.shape[0]) // 2
-    packed = jnp.concatenate([w_gate, w_up, w_down[:, :width], w_down[:, width:]], axis=0)
-    low, high = packed[:half], packed[half:]
-    return (low, high), (send_x(low), send_y(low)), None
-
-
-def gather_expert_more(near, *others):
-    if lax.axis_size("ctx") != 4:
-        return near
-    high = after(near[0][1], *others)
-    return near[0], near[1], (send_x(high), send_y(high))
-
-
-def gather_expert_far(near, *others):
-    if lax.axis_size("ctx") != 4:
-        return ()
-    low, high = after_all((near[1][0], near[2][1]), *others)
-    return send_y(low), send_x(high)
-
-
-def build_expert(w_gate, w_down, near, far, me):
-    if lax.axis_size("ctx") != 4:
-        return near
-    rows, width = w_gate.shape
-    half = rows // 2
-    both = jnp.zeros((2, 4 * rows, width), BF)
-    down = jnp.zeros((2 * rows, 2 * width), BF)
-
-    def put_both(whole, part, owner, which, first):
-        return lax.dynamic_update_slice(whole, part[None], (which, owner * rows + first, 0))
-
-    def put_down(whole, part, owner, which):
-        return lax.dynamic_update_slice(whole, part, (owner * half, which * width))
-
-    lows = (near[0][0],) + near[1] + (far[0],)
-    highs = (near[0][1],) + near[2] + (far[1],)
-    for away in range(4):
-        low, high, owner = lows[away], highs[away], me ^ away
-        both = put_both(both, low[:rows], owner, 0, 0)
-        both = put_both(both, low[rows:], owner, 1, 0)
-        both = put_both(both, high[:half], owner, 1, half)
-        down = put_down(down, high[half:rows], owner, 0)
-        down = put_down(down, high[rows:], owner, 1)
-    return both, down
+def pack_expert(w_gate, w_up, w_down):
+    half, width = w_up.shape[0] // 2, w_up.shape[1]
+    low = jnp.concatenate([w_gate, w_up[:half]], axis=0)
+    high = jnp.concatenate([w_up[half:], w_down[:, :width], w_down[:, width:]], axis=0)
+    return low, high
+
+
+def whole_expert(w_gate, w_up, w_down):
+    return (
+        lax.all_gather(jnp.stack([w_gate, w_up]), "ctx", axis=1, tiled=True),
+        lax.all_gather(w_down, "ctx", axis=0, tiled=True),
+    )
 
 
 def expert_take(grads):
@@ -209,21 +169,24 @@
         return tuple(
             lax.psum_scatter(grad, "ctx", scatter_dimension=0, tiled=True) for grad in grads
         )
-    return scatter_first(expert_take(grads), me)
-
-
-def scatter_expert_second(grads, sums, me):
+    take = expert_take(grads)
+    low = send_x(jnp.stack([take(me ^ 1, 0), take(me ^ 3, 0)]).astype(BF))
+    high = send_y(jnp.stack([take(me ^ 2, 1), take(me ^ 3, 1)]).astype(BF))
+    return low, high
+
+
+def split_sums(sums):
     if lax.axis_size("ctx") != 4:
-        return ()
-    return scatter_second(expert_take(grads), me, *sums)
-
-
-def scatter_expert_end(grads, sums, more, me):
+        return sums, sums
+    return (sums[0][1], sums[1][1]), (sums[0][0], sums[1][0])
+
+
+def scatter_expert_end(grads, direct, last, me):
     if lax.axis_size("ctx") != 4:
-        gate_up, down = (part.astype(F32) for part in sums)
+        gate_up, down = (part.astype(F32) for part in direct)
         width = gate_up.shape[1] // 2
         return gate_up[:, :width], gate_up[:, width:], down
-    first, second = scatter_end(expert_take(grads), me, *sums, *more)
+    first, second = scatter_end(expert_take(grads), me, direct, last)
     rows, half = grads[0].shape[0] // 4, grads[1].shape[0] // 8
     down = [
         jnp.concatenate([part[rows : rows + half], part[rows + half :]], axis=1)
@@ -250,22 +213,14 @@
         match = slot_table[None, :] == jnp.arange(blocks, dtype=jnp.int32)[:, None]
         order = jnp.sum(jnp.where(match, jnp.arange(blocks, dtype=jnp.int32)[None, :], 0), axis=1)
         return pick_blocks(whole, order), ()
-    from_x, from_y, far_low, far_high = gather_pieces(rows, block)
-    parts = (
-        (rows[:block], me, 0),
-        (rows[block:], me, 1),
-        (from_x[:block], me ^ 1, 0),
-        (from_x[block:], me ^ 1, 1),
-        (from_y[:block], me ^ 2, 0),
-        (from_y[block:], me ^ 2, 1),
-        (far_low, me ^ 3, 0),
-        (far_high, me ^ 3, 1),
-    )
+    pieces = gather_pieces(rows[:block], rows[block:])
     whole = jnp.zeros((8 * block, rows.shape[1]), rows.dtype)
-    for part, owner, slot in parts:
-        start = slot_table[2 * owner + slot] * block
-        whole = lax.dynamic_update_slice(whole, part, (start, 0))
-    return whole, (far_low, far_high)
+    for slot in range(2):
+        for away in range(4):
+            part = pieces[slot][away - 1] if away else rows[slot * block : (slot + 1) * block]
+            start = slot_table[2 * (me ^ away) + slot] * block
+            whole = lax.dynamic_update_slice(whole, part, (start, 0))
+    return whole, (pieces[0][2], pieces[1][2])
 
 
 def scatter_group(partial, slot_table, me):
@@ -274,16 +229,16 @@
     if lax.axis_size("ctx") != 4:
         ordered = pick_blocks(partial.reshape(blocks, block, -1), slot_table).astype(BF)
         whole = lax.psum_scatter(ordered, "ctx", scatter_dimension=0, tiled=True)
-        return whole.astype(F32), (ordered,), (whole,), (whole,)
+        return whole.astype(F32), (whole,), (whole,)
 
     def take(owner, part):
         start = slot_table[2 * owner + part] * block
         return lax.dynamic_slice(partial, (start, 0), (block, partial.shape[1]))
 
-    sent = scatter_payload(take, me)
-    near = send_x(sent[0]), send_y(sent[1])
-    far = scatter_second(take, me, *near)
-    return jnp.concatenate(scatter_end(take, me, *near, *far), axis=0), sent, near, far
+    ahead = scatter_ahead(take, me)
+    direct = scatter_direct(take, me)
+    last = scatter_last(take, me, ahead)
+    return jnp.concatenate(scatter_end(take, me, direct, last), axis=0), ahead, last
 
 
 def prefix_count(member):
@@ -500,16 +455,41 @@
     return acc_ref[...].astype(BF)
 
 
-def back_rows_kernel(
-    tiles_ref, low_ref, windows_ref, tok_ref, dy_ref, wd_ref, rows_ref, raw_ref, acc_ref
-):
+def copy_all(copies):
+    for copy in copies:
+        copy.start()
+    for copy in copies:
+        copy.wait()
+
+
+def back_rows_kernel(tiles_ref, low_ref, windows_ref, me_ref, tok_ref, dy_ref, *refs):
+    parts, (rows_ref, raw_ref, down_ref, acc_ref, sems) = refs[:-5], refs[-5:]
     i = pl.program_id(0)
+
+    @pl.when(i == 0)
+    def _():
+        if len(parts) == 1:
+            copy_all([pltpu.make_async_copy(parts[0], down_ref, sems.at[0])])
+            return
+        rows, width = down_ref.shape[0] // 4, down_ref.shape[1] // 2
+        copies = []
+        for away, part in enumerate(parts):
+            owner = pl.multiple_of((me_ref[0] ^ away) * rows, rows)
+            for k in range(2):
+                copies.append(
+                    pltpu.make_async_copy(
+                        part.at[pl.ds((k + 1) * rows, rows)],
+                        down_ref.at[pl.ds(owner, rows), pl.ds(k * width, width)],
+                        sems.at[len(copies)],
+                    )
+                )
+        copy_all(copies)
 
     @pl.when(i < tiles_ref[0])
     def _():
         rows = pick_rows(tok_ref[...], low_ref[i], windows_ref[i], dy_ref, acc_ref)
         rows_ref[...] = rows
-        raw_ref[...] = dot(rows, wd_ref[...], NT)
+        raw_ref[...] = dot(rows, down_ref[...], NT)
 
     @pl.when(i >= tiles_ref[0])
     def _():
@@ -517,9 +497,8 @@
         raw_ref[...] = jnp.zeros_like(raw_ref)
 
 
-def back_rows(tables, upstream, w_down):
+def back_rows(tables, me, upstream, parts, ff):
     total, width = upstream.shape
-    ff = w_down.shape[0]
     capacity = tables[3].shape[0]
     tile = lambda n: pl.BlockSpec((TILE, n), lambda i, *_: (i, 0))
     once = lambda shape: pl.BlockSpec(shape, lambda i, *_: (0, 0), pipeline_mode=pl.Buffered(1))
@@ -528,44 +507,60 @@
         out_shape=[
             jax.ShapeDtypeStruct((capacity, width), BF),
             jax.ShapeDtypeStruct((capacity, ff), F32),
+            jax.ShapeDtypeStruct((ff, width), BF),
         ],
         grid_spec=pltpu.PrefetchScalarGridSpec(
-            num_scalar_prefetch=3,
+            num_scalar_prefetch=4,
             grid=(capacity // TILE,),
-            in_specs=[tile(1), once((total, width)), once((ff, width))],
-            out_specs=[tile(width), tile(ff)],
-            scratch_shapes=[pltpu.VMEM((TILE, width), F32)],
+            in_specs=[tile(1), once((total, width))]
+            + [pl.BlockSpec(memory_space=pl.ANY)] * len(parts),
+            out_specs=[tile(width), tile(ff), pl.BlockSpec((ff, width), lambda i, *_: (0, 0))],
+            scratch_shapes=[
+                pltpu.VMEM((TILE, width), F32),
+                pltpu.SemaphoreType.DMA((2 * len(parts),)),
+            ],
         ),
         compiler_params=pltpu.CompilerParams(vmem_limit_bytes=48 << 20),
         cost_estimate=pl.CostEstimate(
             flops=total * (width * ff + WIN * width),
-            bytes_accessed=2 * total * width + 2 * ff * width + capacity * (2 * width + 4 * ff),
+            bytes_accessed=2 * total * width + 4 * ff * width + capacity * (2 * width + 4 * ff),
             transcendentals=0,
         ),
-    )(*tables, upstream, w_down)
+    )(*tables[:3], me, tables[3], upstream, *parts)
 
 
 def expert_kernel(
-    own,
-    tiles_ref,
-    low_ref,
-    windows_ref,
-    id_ref,
-    tok_ref,
-    h_ref,
-    router_ref,
-    wg_ref,
-    wu_ref,
-    raw_ref,
-    rows_ref,
-    hid_ref,
-    dab_ref,
-    dh_ref,
-    share_ref,
-    acc_ref,
+    own, tiles_ref, low_ref, windows_ref, ids_ref, tok_ref, h_ref, router_ref, raw_ref, *refs
 ):
+    parts = refs[:-8]
+    rows_ref, hid_ref, dab_ref, dh_ref, share_ref, both_ref, acc_ref, sems = refs[-8:]
+    wg_ref, wu_ref = both_ref.at[0], both_ref.at[1]
     i = pl.program_id(0)
     ff = wg_ref.shape[1]
+
+    @pl.when(i == 0)
+    def _():
+        if len(parts) == 1:
+            copy_all([pltpu.make_async_copy(parts[0], both_ref, sems.at[0])])
+            return
+        rows = wg_ref.shape[0] // 4
+        half = rows // 2
+        copies = []
+        for away in range(4):
+            owner = pl.multiple_of((ids_ref[1] ^ away) * rows, rows)
+            for part, first, count, which, shift in (
+                (parts[away], 0, rows, 0, 0),
+                (parts[away], rows, half, 1, 0),
+                (parts[4 + away], 0, half, 1, half),
+            ):
+                copies.append(
+                    pltpu.make_async_copy(
+                        part.at[pl.ds(first, count)],
+                        both_ref.at[which, pl.ds(owner + shift, count)],
+                        sems.at[len(copies)],
+                    )
+                )
+        copy_all(copies)
 
     @pl.when(i < tiles_ref[0])
     def _():
@@ -574,7 +569,7 @@
         logits = dot(rows, router_ref[...])
         probs = jnp.exp(logits - jnp.max(logits, axis=1, keepdims=True))
         column = lax.broadcasted_iota(jnp.int32, probs.shape, 1)
-        mine = jnp.sum(jnp.where(column == id_ref[0] + own, probs, 0.0), axis=1, keepdims=True)
+        mine = jnp.sum(jnp.where(column == ids_ref[0] + own, probs, 0.0), axis=1, keepdims=True)
         gate = mine / jnp.sum(probs, axis=1, keepdims=True)
         share = 0.0
         part = ff // 4
@@ -601,15 +596,11 @@
             ref[...] = jnp.zeros_like(ref)
 
 
-def expert_rows(tables, own, first_id, hidden, router, gate_up, raw):
+def expert_rows(tables, own, ids, hidden, router, parts, raw):
     total, width = hidden.shape
-    ff = gate_up.shape[2]
-    capacity = tables[3].shape[0]
+    capacity, ff = raw.shape
     tile = lambda n: pl.BlockSpec((TILE, n), lambda i, *_: (i, 0))
     once = lambda shape: pl.BlockSpec(shape, lambda i, *_: (0, 0), pipeline_mode=pl.Buffered(1))
-    half = lambda k: pl.BlockSpec(
-        (None, width, ff), lambda i, *_: (k, 0, 0), pipeline_mode=pl.Buffered(1)
-    )
     made = lambda n, dtype=BF: jax.ShapeDtypeStruct((capacity, n), dtype)
     return pl.pallas_call(
         functools.partial(expert_kernel, own),
@@ -617,16 +608,14 @@
         grid_spec=pltpu.PrefetchScalarGridSpec(
             num_scalar_prefetch=4,
             grid=(capacity // TILE,),
-            in_specs=[
-                tile(1),
-                once((total, width)),
-                once(router.shape),
-                half(0),
-                half(1),
-                tile(ff),
+            in_specs=[tile(1), once((total, width)), once(router.shape), tile(ff)]
+            + [pl.BlockSpec(memory_space=pl.ANY)] * len(parts),
+            out_specs=[tile(width), tile(ff), tile(2 * ff), tile(width), tile(1)],
+            scratch_shapes=[
+                pltpu.VMEM((2, width, ff), BF),
+                pltpu.VMEM((TILE, width), F32),
+                pltpu.SemaphoreType.DMA((12,)),
             ],
-            out_specs=[tile(width), tile(ff), tile(2 * ff), tile(width), tile(1)],
-            scratch_shapes=[pltpu.VMEM((TILE, width), F32)],
         ),
         compiler_params=pltpu.CompilerParams(vmem_limit_bytes=56 << 20),
         cost_estimate=pl.CostEstimate(
@@ -634,7 +623,7 @@
             bytes_accessed=2 * total * width + 4 * ff * width + capacity * (4 * width + 10 * ff),
             transcendentals=total * ff,
         ),
-    )(*tables[:3], first_id, tables[3], hidden, router, gate_up, gate_up, raw)
+    )(*tables[:3], ids, tables[3], hidden, router, raw, *parts)
 
 
 def combine_kernel(experts, start_ref, more_ref, wide_ref, pos_ref, *refs):
@@ -758,7 +747,10 @@
         tiled=True,
     ).reshape(exp_size * tok_rows, TOP)
     upstream_all = lax.all_gather(cotangent, "exp", axis=0, tiled=True)
-    first_near = gather_expert(*after_all((w_gate[0], w_up[0], w_down[0]), *tokens_there), me)
+    packs = [pack_expert(w_gate[e], w_up[e], w_down[e]) for e in range(own_experts)]
+    if ctx_size == 4:
+        ahead = after_all(packs[0], *tokens_there)
+        ahead = send_x(ahead[0]), send_y(ahead[1])
 
     own_ids = exp_index * own_experts + jnp.arange(own_experts, dtype=jnp.int32)
     member = jnp.any(routes_all[:, :, None] == own_ids[None, None, :], axis=1)
@@ -813,9 +805,11 @@
     key_pre = projected[:, own_width : 2 * own_width]
     squares = jnp.stack([jnp.sum(query_pre * query_pre, axis=1), jnp.sum(key_pre * key_pre, axis=1)])
     if ctx_size == 4:
-        squares = after(squares, *first_near[1])
+        squares = after(squares, *ahead)
     squares = sum_over_ctx(squares)
-    first_near = gather_expert_more(first_near, squares)
+    if ctx_size == 4:
+        direct = after_all(packs[0], squares)
+        direct = send_x(direct[1]), send_y(direct[0])
     roots = lax.rsqrt(squares / D + epsilon)
     root_query, root_key = roots[0][:, None], roots[1][:, None]
     normed_query = query_pre * root_query
@@ -831,17 +825,33 @@
     )
     branch_part = jnp.dot(context_low, out_full, preferred_element_type=F32)
     if ctx_size == 4:
-        branch_part = after(branch_part, *first_near[1], *first_near[2])
-    branch, unused, unused, branch_there = scatter_group(branch_part, slot_table, me)
-    far = gather_expert_far(first_near, *branch_there)
-    expert_weights = [build_expert(w_gate[0], w_down[0], first_near, far, me)]
-    backs = [back_rows(row_tables[0], upstream_all, expert_weights[0][1])]
-    for e in range(1, own_experts):
-        gates = far if ctx_size == 4 else branch_there
-        near = gather_expert(*after_all((w_gate[e], w_up[e], w_down[e]), *gates), me)
-        near = gather_expert_more(near)
-        far = gather_expert_far(near, backs[0][1])
-        expert_weights.append(build_expert(w_gate[e], w_down[e], near, far, me))
+        branch_part = after(branch_part, *direct)
+    branch, unused, branch_there = scatter_group(branch_part, slot_table, me)
+    me_table = jnp.reshape(me, (1,)).astype(jnp.int32)
+    ids = jnp.stack([own_ids[0], me.astype(jnp.int32)])
+    width = w_gate.shape[2]
+    lows, highs, backs = [], [], []
+    if ctx_size == 4:
+        passed = after_all(ahead, *branch_there)
+        passed = send_y(passed[0]), send_x(passed[1])
+        lows.append((packs[0][0], ahead[0], direct[1], passed[0]))
+        highs.append((packs[0][1], direct[0], ahead[1], passed[1]))
+        upstream = upstream_all
+        for e in range(1, own_experts):
+            low, high = after_all(packs[e], *passed)
+            ahead = send_x(low), send_y(high)
+            direct = send_x(high), send_y(low)
+            passed = send_y(ahead[0]), send_x(ahead[1])
+            lows.append((packs[e][0], ahead[0], direct[1], passed[0]))
+            highs.append((packs[e][1], direct[0], ahead[1], passed[1]))
+            upstream = after(upstream, *ahead)
+        backs.append(back_rows(row_tables[0], me_table, upstream, highs[0], width))
+    else:
+        for e in range(own_experts):
+            both, down = whole_expert(*after_all((w_gate[e], w_up[e], w_down[e]), *branch_there))
+            lows.append((both,))
+            highs.append((down,))
+        backs.append(back_rows(row_tables[0], me_table, upstream_all, highs[0], width))
 
     inputs = tokens.astype(F32)
     middle = inputs + branch
@@ -857,17 +867,11 @@
     for e in every:
         if e > 0:
             upstream = after(upstream_all, made[-1][3])
-            backs.append(back_rows(row_tables[e], upstream, expert_weights[e][1]))
+            highs[e] = after_all(highs[e], made[-1][3])
+            backs.append(back_rows(row_tables[e], me_table, upstream, highs[e], width))
+        parts = tuple(lows[e]) + tuple(highs[e]) if ctx_size == 4 else lows[e]
         made.append(
-            expert_rows(
-                row_tables[e],
-                e,
-                own_ids[:1],
-                hidden_all,
-                router_full,
-                expert_weights[e][0],
-                backs[e][1],
-            )
+            expert_rows(row_tables[e], e, ids, hidden_all, router_full, parts, backs[e][1])
         )
     shares = [m[4].reshape(1, capacity) for m in made]
     grad_two_part, share_token = combine_rows(token_tables, [m[3] for m in made], shares)
@@ -881,7 +885,7 @@
     )
     grad_prob = jnp.swapaxes(share_back, 0, 1).reshape(tok_rows, experts)
     expert_grads = []
-    results, mixture_part = [], grad_two_part
+    mixture_part = grad_two_part
     for e in every:
         rows, hidden, grad_hidden = after_all(made[e][:3], mixture_part)
         expert_grads.append(
@@ -893,13 +897,20 @@
         if e == 0:
             results = [
                 jnp.dot(
-                    after(made[k][1], *expert_grads[0]),
-                    expert_weights[k][1],
-                    preferred_element_type=F32,
+                    after(made[k][1], *expert_grads[0]), backs[k][2], preferred_element_type=F32
                 ).astype(BF)
                 for k in every
             ]
+            if ctx_size == 4:
+                take = expert_take(expert_grads[0])
+                ahead = scatter_ahead(take, me)
+                results = after_all(results, *ahead)
+                direct = scatter_direct(take, me, *ahead)
+                last = scatter_last(take, me, ahead)
+            else:
+                direct, last = scatter_expert_first(expert_grads[0], me), ()
             mixture_part, unused = combine_rows(token_tables, results, shares)
+    directs, lasts = [direct], [last]
     mixture = lax.psum_scatter(mixture_part, "exp", scatter_dimension=0, tiled=True)
     output = (middle + mixture.astype(F32)).astype(BF)
 
@@ -916,16 +927,15 @@
     grad_ffn_gain = jnp.sum(grad_two * normed_two, axis=0)
     grad_middle = cotangent.astype(F32) + norm_back(grad_two * gain_ffn, normed_two, root_two)
 
-    sums = [scatter_expert_first(expert_grads[0], me)]
-    more = [scatter_expert_second(expert_grads[0], after_all(sums[0], mixture_part), me)]
-    own_grad = after(grad_middle.astype(BF), *more[0])
+    own_grad = after(grad_middle.astype(BF), *directs[0], *lasts[0])
     branch_grad, grad_there = gather_group(own_grad, slot_table, me)
+    sums = []
     for e in range(1, own_experts):
         sums.append(scatter_expert_first(after_all(expert_grads[e], *grad_there), me))
-    early_sums = sum_to_rows(jnp.concatenate([grad_router, grad_ffn_gain[None]]), me)
-    branch_grad = after(branch_grad, early_sums)
     grad_context = lax.dot_general(branch_grad, out_full, NT, preferred_element_type=F32).astype(BF)
-    out_grad = jnp.einsum("td,te->de", context_low, branch_grad, preferred_element_type=F32)
+    out_grad = lax.dot_general(
+        context_low, branch_grad, TN, preferred_element_type=F32
+    ).astype(BF)
     grad_query_norm, grad_key_norm, grad_value = attend_back(
         query_rot, key_rot, value_low, grad_context, cos_part, sin_part, seg_ids
     )
@@ -936,10 +946,14 @@
     products = jnp.stack(
         [jnp.sum(scaled_query * normed_query, axis=1), jnp.sum(scaled_key * normed_key, axis=1)]
     )
-    products = after(products, *(piece for pieces in sums[1:] for piece in pieces))
+    products = after(products, out_grad, *(piece for pieces in sums for piece in pieces))
     means = sum_over_ctx(products) / D
     for e in range(1, own_experts):
-        more.append(scatter_expert_second(expert_grads[e], after_all(sums[e], means), me))
+        ahead, direct = split_sums(sums[e - 1])
+        directs.append(direct)
+        ahead = after_all(ahead, means)
+        take = expert_take(expert_grads[e])
+        lasts.append(scatter_last(take, me, ahead) if ctx_size == 4 else ())
     grad_projected = jnp.concatenate(
         [
             root_query * (scaled_query - normed_query * means[0][:, None]),
@@ -951,18 +965,22 @@
     grad_packed = jnp.pad(grad_projected, ((0, 0), (0, 128)))
     grad_one_part = lax.dot_general(grad_packed, packed, NT, preferred_element_type=F32)
     grad_attn_gain = jnp.sum(grad_one_part * normed_group, axis=0)
-    grad_one, one_sent, one_near, unused = scatter_group(
-        after(grad_one_part, *(piece for pieces in more[1:] for piece in pieces)), slot_table, me
-    )
-    weight_sums = [scatter_expert_end(expert_grads[e], sums[e], more[e], me) for e in every]
+    qkv_grad = lax.dot_general(hidden_one, grad_projected, TN, preferred_element_type=F32).astype(BF)
+    grad_one, one_ahead, unused = scatter_group(
+        after(grad_one_part, *(piece for pieces in lasts[1:] for piece in pieces)), slot_table, me
+    )
+    weight_sums = [
+        scatter_expert_end(
+            expert_grads[e], after_all(directs[e], *one_ahead), after_all(lasts[e], *one_ahead), me
+        )
+        for e in every
+    ]
     gate_grad, up_grad, down_grad = (jnp.stack(parts) for parts in zip(*weight_sums))
-    left, right = after_all((hidden_one, grad_projected), *one_sent)
-    qkv_grad = lax.dot_general(left, right, TN, preferred_element_type=F32)
     out_sum = lax.psum_scatter(
-        after(out_grad.astype(BF), mixture), "exp", scatter_dimension=0, tiled=True
+        after(out_grad, mixture), "exp", scatter_dimension=0, tiled=True
     ).astype(F32)
     qkv_sum = lax.psum_scatter(
-        qkv_grad.astype(BF).reshape(ctx_size, exp_size * part_rows, 3 * own_width),
+        qkv_grad.reshape(ctx_size, exp_size * part_rows, 3 * own_width),
         "exp",
         scatter_dimension=1,
         tiled=True,
@@ -978,9 +996,10 @@
     head_gains = lax.dynamic_update_slice(
         jnp.zeros((2, D), F32), jnp.stack([grad_query_gain, grad_key_gain]), (0, me * own_width)
     )
-    late_sums = sum_to_rows(
-        after(jnp.concatenate([grad_attn_gain[None], head_gains]), *one_near), me
-    )
+    small_sums = jnp.concatenate(
+        [grad_router, jnp.stack([grad_ffn_gain, grad_attn_gain]), head_gains]
+    )
+    small_sums = sum_to_rows(after(small_sums, *one_ahead), me)
     return (
         output,
         grad_input,
@@ -988,11 +1007,11 @@
         projection_grads[1],
         projection_grads[2],
         out_sum,
-        early_sums[:experts].T,
-        late_sums[0],
-        late_sums[1],
-        late_sums[2],
-        early_sums[experts],
+        small_sums[:experts].T,
+        small_sums[experts + 1],
+        small_sums[experts + 2],
+        small_sums[experts + 3],
+        small_sums[experts],
         gate_grad,
         up_grad,
         down_grad,

time: 1200 us -> 1050 us (0.88)
  local copies, waits for them, and re-layouts: 177 us -> 93.4 us
  waiting for transfers between devices: 340 us -> 284 us
  Pallas kernels: 250 us -> 264 us
  starting transfers between devices: 95 us -> 82.2 us
    ppermute x24 -> x28, waiting for transfers between devices: 218 us -> 113 us  [send_x(): return lax.ppermute(value, 'ctx', X_PAIRS)]
    ppermute x24 -> x28, waiting for transfers between devices: 98.4 us -> 151 us  [send_y(): return lax.ppermute(value, 'ctx', Y_PAIRS)]
    dynamic_update_slice x40 -> x0, local copies, waits for them, and re-layouts: 49.4 us -> none  [the longest x24 29.6 us: put_both(): lax.dynamic_update_slice(whole, part[None], (which, owner * rows + first,...]
    another operation x8 -> x2, local copies, waits for them, and re-layouts: 22.1 us -> 4.18 us
    all_to_all x1, starting transfers between devices: 20.5 us -> 3.34 us  [local(): lax.all_to_all(share_token.reshape(exp_size, tok_rows, own_experts), 'exp...]
    ppermute x4 -> x3, waiting for transfers between devices: 19 us -> 5.49 us  [send_xy(): return lax.ppermute(value, 'ctx', XY_PAIRS)]
    ppermute x24 -> x28, starting transfers between devices: 23.2 us -> 36.5 us  [send_x(): return lax.ppermute(value, 'ctx', X_PAIRS)]
    convert_element_type x9 -> x8, other arithmetic: 24.3 us -> 16.5 us  [the longest x4 9.78 us: scatter_last(): low = (take(me ^ 2, 0).astype(F32) + ahead[0].astype(F32)).astype(BF)]
  transfers between devices with their start and end apart: 64 -> 70, of which waited for: 34 -> 35; matrix products, arithmetic and copies ran while one was open for 38% -> 34% of each run, Pallas kernels for 8% -> 19%
where the time goes in v5:
time: 1050 us; the launch traced here: 1040 us
  waiting for transfers between devices  284 us (27%)
  Pallas kernels  264 us (25%)
  matrix products  168 us (16%)
  other arithmetic  127 us (12%)
  local copies, waits for them, and re-layouts  93.4 us (9%)
  starting transfers between devices  82.2 us (8%)
  between operations  21.5 us (2%)
    ppermute x28, waiting for transfers between devices, send_y(): return lax.ppermute(value, 'ctx', Y_PAIRS)  151 us
    ppermute x28, waiting for transfers between devices, send_x(): return lax.ppermute(value, 'ctx', X_PAIRS)  113 us
    pallas_call x2, Pallas kernels, expert_rows(): pl.pallas_call(functools.partial(expert_kernel, own), out_shape=[made(wid...  112 us
    pallas_call x2, Pallas kernels, back_rows(): pl.pallas_call(back_rows_kernel, out_shape=[jax.ShapeDtypeStruct((capacit...  55.6 us
    dot_general x2, matrix products, local(): lax.dot_general(rows, grad_hidden, TN, preferred_element_type=F32)  47.1 us
    pallas_call x2, Pallas kernels, combine_rows(): pl.pallas_call(functools.partial(combine_kernel, experts), out_shape=[jax...  40.8 us
    ppermute x28, starting transfers between devices, send_x(): return lax.ppermute(value, 'ctx', X_PAIRS)  36.5 us
    pallas_call x1, Pallas kernels, attend_back(): pl.pallas_call(functools.partial(attend_back_kernel, tiles, 1.0 / math.sq...  30.2 us
  transfers between devices with their start and end apart: 70, of which 35 were waited for; matrix products, arithmetic and copies ran while one was open for 34% of the time, Pallas kernels for 19%

profile of v5, /device:TPU:0, one launch (start us, length us, event | category | flops | bytes accessed | tf_op | source)
XLA Modules:
  0.0 1040.1 jit_solution(17723950930423174030)
XLA Ops:
  16.5 4.0 collective-permute-start.6
  21.1 5.5 collective-permute-done.6
  26.6 3.7 collective-permute-done.7
  34.8 3.4 broadcast.199.clone
  44.5 4.9 all-to-all-start
  55.8 2.9 slice_bitcast_fusion.8
  68.5 16.4 %select_reduce_fusion = s32[2,2048]{1,0:T(2,128)} fusion(s32[2,3072]{1,0:T(2,128)} %copy.272, pred[2,3072]{1,0:T(4,128)(4,1)S(1)} %bitcast.322), kind=kLoop, calls=%fused_computation | loop fusion | flops 50327552 | bytes 47104 | tf_op jit(solution)/shard_map/reduce_max | solution.py:765
  93.9 12.7 %collective-permute-done.2 = bf16[192,2048]{1,0:T(8,128)(2,1)S(1)} collective-permute-done((bf16[192,2048]{1,0:T(8,128)(2,1)}, bf16[192,2048]{1,0:T(8,128)(2,1)S(1)}, u32[]{:S(2)}, u32[]{:S(2)}) %collective-permute-start.2) | collective-permute-done | bytes 786464 | tf_op jit(solution)/shard_map/ppermute | solution.py:55
  115.9 4.1 fusion.5
  122.2 16.2 %fusion.16.qp_ref.kp_ref.vp_ref = f32[1536,1664]{1,0:T(8,128)S(1)} fusion(bf16[2048,1664]{1,0:T(8,128)(2,1)} %bitcast.311, bf16[1536,2048]{1,0:T(8,128)(2,1)} %constant_dynamic-update-slice_fusion.9, f32[2048]{0:T(1024)S(1)} %get-tuple-element.171, f32[1536]{0:T(1024)S(1)} %add_rsqrt_fusion.1), kind=kOutput, calls=%fused_computation.73 | convolution fusion | flops 10481565696 | bytes 23345152 | tf_op jit(solution)/shard_map/dot_general | solution.py:803
  139.1 10.8 %collective-permute-done.9.refs_1_ = bf16[768,1024]{1,0:T(8,128)(2,1)} collective-permute-done((bf16[768,1024]{1,0:T(8,128)(2,1)}, bf16[768,1024]{1,0:T(8,128)(2,1)}, u32[]{:S(2)}, u32[]{:S(2)}) %collective-permute-start.9) | collective-permute-done | bytes 1572896 | tf_op jit(solution)/shard_map/ppermute | solution.py:51
  151.5 2.8 fusion.20
  164.0 25.9 %shard_map.272 = (bf16[1536,512]{1,0:T(8,128)(2,1)S(1)}, bf16[1536,512]{1,0:T(8,128)(2,1)}, bf16[1536,512]{1,0:T(8,128)(2,1)}, bf16[1536,512]{1,0:T(8,128)(2,1)}) custom-call(f32[1536,1664]{1,0:T(8,128)} %copy-done.16, f32[1536,1664]{1,0:T(8,128)} %copy-done.16, f32[1536,1664]{1,0:T(8,128)} %copy-done.16, f32[1536,2]{1,0:T(8,128)S(1)} %fusion.79.root_ref.key_root_ref, ...), custom_call_target="tpu_custom_call" | custom-call | flops 3221225472 | bytes 15728640 | tf_op jit(solution)/shard_map/pallas_call | solution.py:328
  191.0 5.6 fusion.95
  200.5 17.4 %collective-permute-done.16 = bf16[192,2048]{1,0:T(8,128)(2,1)S(1)} collective-permute-done((bf16[192,2048]{1,0:T(8,128)(2,1)S(1)}, bf16[192,2048]{1,0:T(8,128)(2,1)S(1)}, u32[]{:S(2)}, u32[]{:S(2)}) %collective-permute-start.16) | collective-permute-done | bytes 786464 | tf_op jit(solution)/shard_map/ppermute | solution.py:51
  220.2 11.0 %collective-permute-done.15 = bf16[192,2048]{1,0:T(8,128)(2,1)S(1)} collective-permute-done((bf16[192,2048]{1,0:T(8,128)(2,1)S(1)}, bf16[192,2048]{1,0:T(8,128)(2,1)S(1)}, u32[]{:S(2)}, u32[]{:S(2)}) %collective-permute-start.15) | collective-permute-done | bytes 786464 | tf_op jit(solution)/shard_map/ppermute | solution.py:51
  231.1 7.5 collective-permute-done.17
  240.4 8.3 collective-permute-done.18
  262.1 27.5 %collective-permute-done.21.refs_3_ = bf16[768,1024]{1,0:T(8,128)(2,1)S(1)} collective-permute-done((bf16[768,1024]{1,0:T(8,128)(2,1)}, bf16[768,1024]{1,0:T(8,128)(2,1)S(1)}, u32[]{:S(2)}, u32[]{:S(2)}) %collective-permute-start.21) | collective-permute-done | bytes 1572896 | tf_op jit(solution)/shard_map/ppermute | solution.py:55
  300.9 27.8 %collective-permute-done.24.refs_2_.refs_6_ = bf16[768,1024]{1,0:T(8,128)(2,1)} collective-permute-done((bf16[768,1024]{1,0:T(8,128)(2,1)}, bf16[768,1024]{1,0:T(8,128)(2,1)}, u32[]{:S(2)}, u32[]{:S(2)}) %collective-permute-start.24) | collective-permute-done | bytes 1572896 | tf_op jit(solution)/shard_map/ppermute | solution.py:55
  333.4 29.1 %shard_map.273 = (bf16[2048,2048]{1,0:T(8,128)(2,1)}, f32[2048,1024]{1,0:T(8,128)}, bf16[1024,2048]{1,0:T(8,128)(2,1)}) custom-call(s32[1]{0:T(128)} %get-tuple-element.315.tiles_ref, s32[8]{0:T(128)S(1)} %get-tuple-element.333.low_ref, s32[8]{0:T(128)S(1)} %get-tuple-element.311.windows_ref, s32[1]{0:T(128)} %bitcast.36.me_ref, s32[2048,1]{1,0:T(8,128)S(1)} %copy-done.4, ...), custom_call_target="tpu_custom_call" | custom-call | flops 9663676416 | bytes 37748736 | tf_op jit(solution)/shard_map/pallas_call | solution.py:505
  362.5 11.2 %all-gather.9.cloned.1.call-done.h_ref = bf16[3072,2048]{1,0:T(8,128)(2,1)} async-done(((bf16[384,2048]{1,0:T(8,128)(2,1)}), bf16[3072,2048]{1,0:T(8,128)(2,1)}) %all-gather.9.cloned.1.call-update) | async-done | bytes 12582928 | tf_op jit(solution)/shard_map/all_gather | solution.py:861
  373.7 62.0 %shard_map.274 = (bf16[2048,2048]{1,0:T(8,128)(2,1)}, bf16[2048,1024]{1,0:T(8,128)(2,1)}, bf16[2048,2048]{1,0:T(8,128)(2,1)}, bf16[2048,2048]{1,0:T(8,128)(2,1)}, f32[2048,1]{1,0:T(8,128)}) custom-call(s32[1]{0:T(128)} %get-tuple-element.315.tiles_ref, s32[8]{0:T(128)} %copy-done.10, s32[8]{0:T(128)} %copy-done.9, s32[2]{0:T(128)} %pad_add_fusion.ids_ref, ...), custom_call_target="tpu_custom_call" | custom-call | flops 28991029248 | bytes 58720256 | tf_op jit(solution)/shard_map/pallas_call | solution.py:605
  437.3 26.5 %shard_map.275 = (bf16[2048,2048]{1,0:T(8,128)(2,1)}, f32[2048,1024]{1,0:T(8,128)}, bf16[1024,2048]{1,0:T(8,128)(2,1)}) custom-call(s32[1]{0:T(128)} %get-tuple-element.314.tiles_ref, s32[8]{0:T(128)S(1)} %get-tuple-element.334.low_ref, s32[8]{0:T(128)S(1)} %get-tuple-element.310.windows_ref, s32[1]{0:T(128)} %bitcast.36.me_ref, ...), custom_call_target="tpu_custom_call" | custom-call | flops 9663676416 | bytes 37748736 | tf_op jit(solution)/shard_map/pallas_call | solution.py:505
  463.9 49.8 %shard_map.276 = (bf16[2048,2048]{1,0:T(8,128)(2,1)}, bf16[2048,1024]{1,0:T(8,128)(2,1)}, bf16[2048,2048]{1,0:T(8,128)(2,1)}, bf16[2048,2048]{1,0:T(8,128)(2,1)}, f32[2048,1]{1,0:T(8,128)}) custom-call(s32[1]{0:T(128)} %get-tuple-element.314.tiles_ref, s32[8]{0:T(128)} %copy-done.8, s32[8]{0:T(128)} %copy-done.7, s32[2]{0:T(128)} %pad_add_fusion.ids_ref, ...), custom_call_target="tpu_custom_call" | custom-call | flops 28991029248 | bytes 58720256 | tf_op jit(solution)/shard_map/pallas_call | solution.py:605
  516.7 20.3 %shard_map.277 = (bf16[3072,2048]{1,0:T(8,128)(2,1)}, f32[3072,2]{1,0:T(8,128)S(1)}) custom-call(s32[2,12]{1,0:T(2,128)S(1)} %copy.289.start_ref, s32[2,12]{1,0:T(2,128)S(1)} %copy.290.more_ref, s32[2,12]{1,0:T(2,128)S(1)} %copy.291.wide_ref, s32[3072,2]{1,0:T(8,128)S(1)} %copy-done, bf16[2048,2048]{1,0:T(8,128)(2,1)} %get-tuple-element.104.refs_0_, ...), custom_call_target="tpu_custom_call" | custom-call | flops 6442450944 | bytes 29360128 | tf_op jit(solution)/shard_map/pallas_call | solution.py:663
  538.3 13.1 %convolution_convert_fusion.6 = bf16[1024,2048]{1,0:T(8,128)(2,1)S(1)} fusion(bf16[2048,1024]{1,0:T(8,128)(2,1)} %get-tuple-element.119, bf16[2048,2048]{1,0:T(8,128)(2,1)} %get-tuple-element.118), kind=kOutput, calls=%fused_computation.25 | convolution fusion | flops 8592031744 | bytes 16777216 | tf_op jit(solution)/shard_map/dot_general | solution.py:894
  551.4 22.4 %convolution_convert_fusion.4 = bf16[2048,2048]{1,0:T(8,128)(2,1)S(1)} fusion(bf16[2048,2048]{1,0:T(8,128)(2,1)} %get-tuple-element.115, bf16[2048,2048]{1,0:T(8,128)(2,1)} %get-tuple-element.116), kind=kOutput, calls=%fused_computation.14 | convolution fusion | flops 17184063488 | bytes 25165824 | tf_op jit(solution)/shard_map/dot_general | solution.py:893
  578.3 8.8 collective-permute-start.29
  588.8 13.7 %convolution_convert_fusion.3.refs_0_ = bf16[2048,2048]{1,0:T(8,128)(2,1)} fusion(bf16[2048,1024]{1,0:T(8,128)(2,1)} %get-tuple-element.119, bf16[1024,2048]{1,0:T(8,128)(2,1)S(1)} %copy-done.104), kind=kOutput, calls=%fused_computation.13 | convolution fusion | flops 8594128896 | bytes 16777216 | tf_op jit(solution)/shard_map/dot_general | solution.py:899
  602.5 10.9 %convolution_convert_fusion.2.refs_1_ = bf16[2048,2048]{1,0:T(8,128)(2,1)} fusion(bf16[2048,1024]{1,0:T(8,128)(2,1)S(1)} %copy-done.106, bf16[1024,2048]{1,0:T(8,128)(2,1)S(1)} %copy-done.105), kind=kOutput, calls=%fused_computation.12 | convolution fusion | flops 8594128896 | bytes 16777216 | tf_op jit(solution)/shard_map/dot_general | solution.py:899
  613.4 7.7 collective-permute-done.29
  622.8 20.5 %shard_map.278 = (bf16[3072,2048]{1,0:T(8,128)(2,1)}, f32[3072,2]{1,0:T(8,128)}) custom-call(s32[2,12]{1,0:T(2,128)S(1)} %copy.289.start_ref, s32[2,12]{1,0:T(2,128)S(1)} %copy.290.more_ref, s32[2,12]{1,0:T(2,128)S(1)} %copy.291.wide_ref, s32[3072,2]{1,0:T(8,128)S(1)} %copy-done.1, bf16[2048,2048]{1,0:T(8,128)(2,1)} %convolution_convert_fusion.3.refs_0_, ...), custom_call_target="tpu_custom_call" | custom-call | flops 6442450944 | bytes 29360128 | tf_op jit(solution)/shard_map/pallas_call | solution.py:663
  647.9 3.3 all-to-all-start.1
  658.0 3.8 add_convert_fusion.3
  667.2 24.8 %convolution_convert_fusion.1 = bf16[2048,2048]{1,0:T(8,128)(2,1)} fusion(bf16[2048,2048]{1,0:T(8,128)(2,1)} %get-tuple-element.129, bf16[2048,2048]{1,0:T(8,128)(2,1)} %get-tuple-element.130), kind=kOutput, calls=%fused_computation.11 | convolution fusion | flops 17184063488 | bytes 25165824 | tf_op jit(solution)/shard_map/dot_general | solution.py:893
  692.0 11.3 %convolution_convert_fusion.5 = bf16[1024,2048]{1,0:T(8,128)(2,1)} fusion(bf16[2048,1024]{1,0:T(8,128)(2,1)S(1)} %copy-done.107, bf16[2048,2048]{1,0:T(8,128)(2,1)S(1)} %bitcast.342), kind=kOutput, calls=%fused_computation.24 | convolution fusion | flops 8592031744 | bytes 16777216 | tf_op jit(solution)/shard_map/dot_general | solution.py:894
  703.5 4.7 multiply_reduce_fusion.2
  709.8 18.2 %collective-permute-done.33 = bf16[768,1024]{1,0:T(8,128)(2,1)} collective-permute-done((bf16[768,1024]{1,0:T(8,128)(2,1)}, bf16[768,1024]{1,0:T(8,128)(2,1)}, u32[]{:S(2)}, u32[]{:S(2)}) %collective-permute-start.33) | collective-permute-done | bytes 1572896 | tf_op jit(solution)/shard_map/ppermute | solution.py:55
  733.4 14.1 %collective-permute-done.35 = bf16[192,2048]{1,0:T(8,128)(2,1)S(1)} collective-permute-done((bf16[192,2048]{1,0:T(8,128)(2,1)S(1)}, bf16[192,2048]{1,0:T(8,128)(2,1)S(1)}, u32[]{:S(2)}, u32[]{:S(2)}) %collective-permute-start.35) | collective-permute-done | bytes 786464 | tf_op jit(solution)/shard_map/ppermute | solution.py:51
  747.9 3.2 collective-permute-done.39
  756.6 11.4 %collective-permute-done.36 = bf16[192,2048]{1,0:T(8,128)(2,1)S(1)} collective-permute-done((bf16[192,2048]{1,0:T(8,128)(2,1)S(1)}, bf16[192,2048]{1,0:T(8,128)(2,1)S(1)}, u32[]{:S(2)}, u32[]{:S(2)}) %collective-permute-start.36) | collective-permute-done | bytes 786464 | tf_op jit(solution)/shard_map/ppermute | solution.py:55
  768.0 14.3 %collective-permute-done.37 = bf16[192,2048]{1,0:T(8,128)(2,1)S(1)} collective-permute-done((bf16[192,2048]{1,0:T(8,128)(2,1)S(1)}, bf16[192,2048]{1,0:T(8,128)(2,1)S(1)}, u32[]{:S(2)}, u32[]{:S(2)}) %collective-permute-start.37) | collective-permute-done | bytes 786464 | tf_op jit(solution)/shard_map/ppermute | solution.py:55
  790.0 4.8 convolution_convert_fusion.8.d_ref
  794.8 30.2 %shard_map.279 = (f32[1536,512]{1,0:T(8,128)}, f32[1536,512]{1,0:T(8,128)}, f32[1536,512]{1,0:T(8,128)}) custom-call(bf16[1536,512]{1,0:T(8,128)(2,1)S(1)} %copy-done.12, bf16[1536,512]{1,0:T(8,128)(2,1)S(1)} %copy-done.13, bf16[1536,512]{1,0:T(8,128)(2,1)} %get-tuple-element.137.v_ref, bf16[1536,512]{1,0:T(8,128)(2,1)} %convolution_convert_fusion.8.d_ref, ...), custom_call_target="tpu_custom_call" | custom-call | flops 8053063680 | bytes 15728640 | tf_op jit(solution)/shard_map/pallas_call | solution.py:417
  825.1 3.4 convert.12
  828.5 5.4 multiply_reduce_fusion.1
  833.9 4.6 convolution_convert_fusion.7
  838.6 14.6 %collective-permute-done.41 = bf16[2,768,1024]{2,1,0:T(8,128)(2,1)} collective-permute-done((bf16[2,768,1024]{2,1,0:T(8,128)(2,1)}, bf16[2,768,1024]{2,1,0:T(8,128)(2,1)}, u32[]{:S(2)}, u32[]{:S(2)}) %collective-permute-start.41) | collective-permute-done | bytes 3145760 | tf_op jit(solution)/shard_map/ppermute | solution.py:51
  857.1 3.9 slice_bitcast_fusion.5
  867.6 3.9 slice_bitcast_fusion.4
  875.1 4.1 multiply_convert_fusion.1
  879.2 15.4 %convolution_convert_fusion = bf16[2048,1536]{1,0:T(8,128)(2,1)} fusion(bf16[1536,2048]{1,0:T(8,128)(2,1)} %constant_dynamic-update-slice_fusion.9, f32[2048]{0:T(1024)S(1)} %copy-done.75, f32[1536]{0:T(1024)S(1)} %copy-done.94, bf16[1536,512]{1,0:T(8,128)(2,1)S(1)} %copy-done.37, bf16[1536,512]{1,0:T(8,128)(2,1)S(1)} %get-tuple-element.197, ...), kind=kOutput, calls=%fused_computation.10 | convolution fusion | flops 9693560832 | bytes 17315840 | tf_op jit(solution)/shard_map/dot_general | solution.py:968
  896.4 3.1 add_convert_fusion.1
  905.9 17.1 %fusion.4 = (f32[2048]{0:T(1024)}, f32[1536,2048]{1,0:T(8,128)S(1)}) fusion(bf16[1536,2048]{1,0:T(8,128)(2,1)} %constant_dynamic-update-slice_fusion.9, f32[1536]{0:T(1024)S(1)} %copy-done.94, bf16[2048,1664]{1,0:T(8,128)(2,1)} %bitcast.315, bf16[1536,1536]{1,0:T(8,128)(2,1)} %pad_maximum_fusion), kind=kOutput, calls=%fused_computation.8 | convolution fusion | flops 10481563648 | bytes 30423040 | tf_op jit(solution)/shard_map/dot_general | solution.py:966
  923.0 9.1 collective-permute-done.45
  932.1 3.4 collective-permute-done.46
  944.5 13.7 %collective-permute-done.48 = bf16[192,2048]{1,0:T(8,128)(2,1)} collective-permute-done((bf16[192,2048]{1,0:T(8,128)(2,1)}, bf16[192,2048]{1,0:T(8,128)(2,1)}, u32[]{:S(2)}, u32[]{:S(2)}) %collective-permute-start.48) | collective-permute-done | bytes 786464 | tf_op jit(solution)/shard_map/ppermute | solution.py:51
  962.6 3.8 all-to-all-start.2
  972.1 3.0 convert_add_fusion.2
  975.2 2.9 convert_add_fusion.4
  991.2 3.1 convert_add_fusion.7
  998.8 14.7 %collective-permute-done.52 = bf16[192,2048]{1,0:T(8,128)(2,1)S(1)} collective-permute-done((bf16[192,2048]{1,0:T(8,128)(2,1)S(1)}, bf16[192,2048]{1,0:T(8,128)(2,1)S(1)}, u32[]{:S(2)}, u32[]{:S(2)}) %collective-permute-start.52) | collective-permute-done | bytes 786464 | tf_op jit(solution)/shard_map/ppermute | solution.py:51
  1021.8 6.5 fusion.13
  (541 shorter events, 224.4 us)
Async XLA Ops:
  7.2 112.9 %all-gather.5.cloned.1.call-start = ((), (), s32[]{:S(2)}) async-start(), calls=%async_computation.7 | async-start | bytes 7667712 | tf_op jit(solution)/shard_map/all_gather | solution.py:734
  16.5 10.1 collective-permute-start.6
  20.4 9.8 collective-permute-start.7
  20.9 9.6 collective-permute-start.8
  31.9 159.1 %all-gather.7.cloned.1.call-start = ((), (), s32[]{:S(2)}) async-start(), calls=%async_computation.8 | async-start | bytes 2359296 | tf_op jit(solution)/shard_map/all_gather | solution.py:741
  32.7 298.1 %all-gather.11.cloned.1.call-start = ((), (), s32[]{:S(2)}) async-start(), calls=%async_computation.10 | async-start | bytes 14155776 | tf_op jit(solution)/shard_map/all_gather | solution.py:749
  39.8 46.6 %collective-permute-start = (bf16[192,2048]{1,0:T(8,128)(2,1)}, bf16[192,2048]{1,0:T(8,128)(2,1)}, u32[]{:S(2)}, u32[]{:S(2)}) collective-permute-start(bf16[192,2048]{1,0:T(8,128)(2,1)} %get-tuple-element.277), channel_id=1, source_target_pairs={{0,8},{8,0},{16,24},{24,16},{1,9},{9,1},{17,25},{25,17},{2,10},{10... | collective-permute-start | bytes 2359304 | tf_op jit(solution)/shard_map/ppermute | solution.py:51
  41.3 50.5 %collective-permute-start.1 = (bf16[192,2048]{1,0:T(8,128)(2,1)}, bf16[192,2048]{1,0:T(8,128)(2,1)}, u32[]{:S(2)}, u32[]{:S(2)}) collective-permute-start(bf16[192,2048]{1,0:T(8,128)(2,1)} %get-tuple-element.277), channel_id=1, source_target_pairs={{0,16},{8,24},{16,0},{24,8},{1,17},{9,25},{17,1},{25,9},{2,18},{10... | collective-permute-start | bytes 2359304 | tf_op jit(solution)/shard_map/ppermute | solution.py:55
  41.9 66.6 %collective-permute-start.3 = (bf16[192,2048]{1,0:T(8,128)(2,1)}, bf16[192,2048]{1,0:T(8,128)(2,1)}, u32[]{:S(2)}, u32[]{:S(2)}) collective-permute-start(bf16[192,2048]{1,0:T(8,128)(2,1)} %get-tuple-element.275), channel_id=1, source_target_pairs={{0,8},{8,0},{16,24},{24,16},{1,9},{9,1},{17,25},{25,17},{2,10},{10... | collective-permute-start | bytes 2359304 | tf_op jit(solution)/shard_map/ppermute | solution.py:51
  43.2 45.6 %collective-permute-start.4 = (bf16[192,2048]{1,0:T(8,128)(2,1)}, bf16[192,2048]{1,0:T(8,128)(2,1)}, u32[]{:S(2)}, u32[]{:S(2)}) collective-permute-start(bf16[192,2048]{1,0:T(8,128)(2,1)} %get-tuple-element.275), channel_id=1, source_target_pairs={{0,16},{8,24},{16,0},{24,8},{1,17},{9,25},{17,1},{25,9},{2,18},{10... | collective-permute-start | bytes 2359304 | tf_op jit(solution)/shard_map/ppermute | solution.py:55
  44.5 19.3 %all-to-all-start = ((s32[8,384,8]{1,2,0:T(8,128)}), s32[8,384,8]{1,2,0:T(8,128)S(1)}, u32[]{:S(2)}, u32[]{:S(2)}) async-start(s32[8,384,8]{1,2,0:T(8,128)} %broadcast_in_dim.46), calls=%async_computation | async-start | bytes 196608 | tf_op jit(solution)/shard_map/all_to_all | solution.py:742
  49.3 324.4 %all-gather.9.cloned.1.call-start = ((), (), s32[]{:S(2)}) async-start(), calls=%async_computation.9 | async-start | bytes 14155776 | tf_op jit(solution)/shard_map/all_gather | solution.py:861
  86.4 20.2 %collective-permute-start.2 = (bf16[192,2048]{1,0:T(8,128)(2,1)}, bf16[192,2048]{1,0:T(8,128)(2,1)S(1)}, u32[]{:S(2)}, u32[]{:S(2)}) collective-permute-start(bf16[192,2048]{1,0:T(8,128)(2,1)} %collective-permute-done), channel_id=1, source_target_pairs={{0,16},{8,24},{16,0},{24,8},{1,17},{9,25},{17,1},{25,9},{2,18},{10... | collective-permute-start | bytes 2359304 | tf_op jit(solution)/shard_map/ppermute | solution.py:55
  88.8 23.9 %collective-permute-start.5 = (bf16[192,2048]{1,0:T(8,128)(2,1)}, bf16[192,2048]{1,0:T(8,128)(2,1)S(1)}, u32[]{:S(2)}, u32[]{:S(2)}) collective-permute-start(bf16[192,2048]{1,0:T(8,128)(2,1)} %collective-permute-done.4), channel_id=1, source_target_pairs={{0,8},{8,0},{16,24},{24,16},{1,9},{9,1},{17,25},{25,17},{2,10},{10... | collective-permute-start | bytes 2359304 | tf_op jit(solution)/shard_map/ppermute | solution.py:51
  113.7 36.2 %collective-permute-start.9 = (bf16[768,1024]{1,0:T(8,128)(2,1)}, bf16[768,1024]{1,0:T(8,128)(2,1)}, u32[]{:S(2)}, u32[]{:S(2)}) collective-permute-start(bf16[768,1024]{1,0:T(8,128)(2,1)} %get-tuple-element.93.refs_0_), channel_id=1, source_target_pairs={{0,8},{8,0},{16,24},{24,16},{1,9},{9,1},{17,25},{25,17},{2,10},{10... | collective-permute-start | bytes 4718600 | tf_op jit(solution)/shard_map/ppermute | solution.py:51
  115.2 35.9 %collective-permute-start.10 = (bf16[768,1024]{1,0:T(8,128)(2,1)}, bf16[768,1024]{1,0:T(8,128)(2,1)S(1)}, u32[]{:S(2)}, u32[]{:S(2)}) collective-permute-start(bf16[768,1024]{1,0:T(8,128)(2,1)} %get-tuple-element.92.refs_0_.refs_4_), channel_id=1, source_target_pairs={{0,16},{8,24},{16,0},{24,8},{1,17},{9,25},{17,1},{25,9},{2,18},{10... | collective-permute-start | bytes 4718600 | tf_op jit(solution)/shard_map/ppermute | solution.py:55
  161.8 34.8 %collective-permute-start.13 = (bf16[768,1024]{1,0:T(8,128)(2,1)}, bf16[768,1024]{1,0:T(8,128)(2,1)}, u32[]{:S(2)}, u32[]{:S(2)}) collective-permute-start(bf16[768,1024]{1,0:T(8,128)(2,1)} %get-tuple-element.92.refs_0_.refs_4_), channel_id=1, source_target_pairs={{0,8},{8,0},{16,24},{24,16},{1,9},{9,1},{17,25},{25,17},{2,10},{10... | collective-permute-start | bytes 4718600 | tf_op jit(solution)/shard_map/ppermute | solution.py:51
  163.0 33.9 %collective-permute-start.14 = (bf16[768,1024]{1,0:T(8,128)(2,1)}, bf16[768,1024]{1,0:T(8,128)(2,1)}, u32[]{:S(2)}, u32[]{:S(2)}) collective-permute-start(bf16[768,1024]{1,0:T(8,128)(2,1)} %get-tuple-element.93.refs_0_), channel_id=1, source_target_pairs={{0,16},{8,24},{16,0},{24,8},{1,17},{9,25},{17,1},{25,9},{2,18},{10... | collective-permute-start | bytes 4718600 | tf_op jit(solution)/shard_map/ppermute | solution.py:55
  197.3 20.5 %collective-permute-start.16 = (bf16[192,2048]{1,0:T(8,128)(2,1)S(1)}, bf16[192,2048]{1,0:T(8,128)(2,1)S(1)}, u32[]{:S(2)}, u32[]{:S(2)}) collective-permute-start(bf16[192,2048]{1,0:T(8,128)(2,1)S(1)} %get-tuple-element.195), channel_id=1, source_target_pairs={{0,8},{8,0},{16,24},{24,16},{1,9},{9,1},{17,25},{25,17},{2,10},{10... | collective-permute-start | bytes 2359304 | tf_op jit(solution)/shard_map/ppermute | solution.py:51
  198.4 32.7 %collective-permute-start.15 = (bf16[192,2048]{1,0:T(8,128)(2,1)S(1)}, bf16[192,2048]{1,0:T(8,128)(2,1)S(1)}, u32[]{:S(2)}, u32[]{:S(2)}) collective-permute-start(bf16[192,2048]{1,0:T(8,128)(2,1)S(1)} %get-tuple-element.192), channel_id=1, source_target_pairs={{0,8},{8,0},{16,24},{24,16},{1,9},{9,1},{17,25},{25,17},{2,10},{10... | collective-permute-start | bytes 2359304 | tf_op jit(solution)/shard_map/ppermute | solution.py:51
  199.4 31.7 %collective-permute-start.19 = (bf16[192,2048]{1,0:T(8,128)(2,1)S(1)}, bf16[192,2048]{1,0:T(8,128)(2,1)S(1)}, u32[]{:S(2)}, u32[]{:S(2)}) collective-permute-start(bf16[192,2048]{1,0:T(8,128)(2,1)S(1)} %get-tuple-element.193), channel_id=1, source_target_pairs={{0,16},{8,24},{16,0},{24,8},{1,17},{9,25},{17,1},{25,9},{2,18},{10... | collective-permute-start | bytes 2359304 | tf_op jit(solution)/shard_map/ppermute | solution.py:55
  218.1 20.5 %collective-permute-start.17 = (bf16[192,2048]{1,0:T(8,128)(2,1)S(1)}, bf16[192,2048]{1,0:T(8,128)(2,1)S(1)}, u32[]{:S(2)}, u32[]{:S(2)}) collective-permute-start(bf16[192,2048]{1,0:T(8,128)(2,1)S(1)} %add_convert_fusion.8), channel_id=1, source_target_pairs={{0,16},{8,24},{16,0},{24,8},{1,17},{9,25},{17,1},{25,9},{2,18},{10... | collective-permute-start | bytes 2359304 | tf_op jit(solution)/shard_map/ppermute | solution.py:55
  219.2 29.4 %collective-permute-start.18 = (bf16[192,2048]{1,0:T(8,128)(2,1)S(1)}, bf16[192,2048]{1,0:T(8,128)(2,1)S(1)}, u32[]{:S(2)}, u32[]{:S(2)}) collective-permute-start(bf16[192,2048]{1,0:T(8,128)(2,1)S(1)} %get-tuple-element.194), channel_id=1, source_target_pairs={{0,16},{8,24},{16,0},{24,8},{1,17},{9,25},{17,1},{25,9},{2,18},{10... | collective-permute-start | bytes 2359304 | tf_op jit(solution)/shard_map/ppermute | solution.py:55
  239.3 12.1 %collective-permute-start.20 = (bf16[192,2048]{1,0:T(8,128)(2,1)S(1)}, bf16[192,2048]{1,0:T(8,128)(2,1)S(1)}, u32[]{:S(2)}, u32[]{:S(2)}) collective-permute-start(bf16[192,2048]{1,0:T(8,128)(2,1)S(1)} %get-tuple-element.191), channel_id=1, source_target_pairs={{0,8},{8,0},{16,24},{24,16},{1,9},{9,1},{17,25},{25,17},{2,10},{10... | collective-permute-start | bytes 2359304 | tf_op jit(solution)/shard_map/ppermute | solution.py:51
  256.3 447.1 %reduce-scatter.7.cloned.1.call-start = ((), (), s32[]{:S(2)}) async-start(), calls=%async_computation.12 | async-start | bytes 14155776 | tf_op jit(solution)/shard_map/reduce_scatter | solution.py:878
  256.3 33.2 %collective-permute-start.21 = (bf16[768,1024]{1,0:T(8,128)(2,1)}, bf16[768,1024]{1,0:T(8,128)(2,1)S(1)}, u32[]{:S(2)}, u32[]{:S(2)}) collective-permute-start(bf16[768,1024]{1,0:T(8,128)(2,1)} %collective-permute-done.9.refs_1_), channel_id=1, source_target_pairs={{0,16},{8,24},{16,0},{24,8},{1,17},{9,25},{17,1},{25,9},{2,18},{10... | collective-permute-start | bytes 4718600 | tf_op jit(solution)/shard_map/ppermute | solution.py:55
  258.1 32.9 %collective-permute-start.22 = (bf16[768,1024]{1,0:T(8,128)(2,1)}, bf16[768,1024]{1,0:T(8,128)(2,1)S(1)}, u32[]{:S(2)}, u32[]{:S(2)}) collective-permute-start(bf16[768,1024]{1,0:T(8,128)(2,1)} %copy-done.14), channel_id=1, source_target_pairs={{0,8},{8,0},{16,24},{24,16},{1,9},{9,1},{17,25},{25,17},{2,10},{10... | collective-permute-start | bytes 4718600 | tf_op jit(solution)/shard_map/ppermute | solution.py:51
  291.1 37.7 %collective-permute-start.24 = (bf16[768,1024]{1,0:T(8,128)(2,1)}, bf16[768,1024]{1,0:T(8,128)(2,1)}, u32[]{:S(2)}, u32[]{:S(2)}) collective-permute-start(bf16[768,1024]{1,0:T(8,128)(2,1)} %pad_maximum_fusion.9.refs_0_.refs_4_), channel_id=1, source_target_pairs={{0,16},{8,24},{16,0},{24,8},{1,17},{9,25},{17,1},{25,9},{2,18},{10... | collective-permute-start | bytes 4718600 | tf_op jit(solution)/shard_map/ppermute | solution.py:55
  292.9 37.6 %collective-permute-start.23 = (bf16[768,1024]{1,0:T(8,128)(2,1)}, bf16[768,1024]{1,0:T(8,128)(2,1)}, u32[]{:S(2)}, u32[]{:S(2)}) collective-permute-start(bf16[768,1024]{1,0:T(8,128)(2,1)} %pad_maximum_fusion.8.refs_0_), channel_id=1, source_target_pairs={{0,8},{8,0},{16,24},{24,16},{1,9},{9,1},{17,25},{25,17},{2,10},{10... | collective-permute-start | bytes 4718600 | tf_op jit(solution)/shard_map/ppermute | solution.py:51
  298.9 136.9 %collective-permute-start.25 = (bf16[768,1024]{1,0:T(8,128)(2,1)}, bf16[768,1024]{1,0:T(8,128)(2,1)}, u32[]{:S(2)}, u32[]{:S(2)}) collective-permute-start(bf16[768,1024]{1,0:T(8,128)(2,1)} %pad_maximum_fusion.9.refs_0_.refs_4_), channel_id=1, source_target_pairs={{0,8},{8,0},{16,24},{24,16},{1,9},{9,1},{17,25},{25,17},{2,10},{10... | collective-permute-start | bytes 4718600 | tf_op jit(solution)/shard_map/ppermute | solution.py:51
  300.7 163.2 %collective-permute-start.27 = (bf16[768,1024]{1,0:T(8,128)(2,1)}, bf16[768,1024]{1,0:T(8,128)(2,1)}, u32[]{:S(2)}, u32[]{:S(2)}) collective-permute-start(bf16[768,1024]{1,0:T(8,128)(2,1)} %pad_maximum_fusion.8.refs_0_), channel_id=1, source_target_pairs={{0,16},{8,24},{16,0},{24,8},{1,17},{9,25},{17,1},{25,9},{2,18},{10... | collective-permute-start | bytes 4718600 | tf_op jit(solution)/shard_map/ppermute | solution.py:55
  328.7 107.0 %collective-permute-start.26 = (bf16[768,1024]{1,0:T(8,128)(2,1)}, bf16[768,1024]{1,0:T(8,128)(2,1)}, u32[]{:S(2)}, u32[]{:S(2)}) collective-permute-start(bf16[768,1024]{1,0:T(8,128)(2,1)} %collective-permute-done.24.refs_2_.refs_6_), channel_id=1, source_target_pairs={{0,8},{8,0},{16,24},{24,16},{1,9},{9,1},{17,25},{25,17},{2,10},{10... | collective-permute-start | bytes 4718600 | tf_op jit(solution)/shard_map/ppermute | solution.py:51
  330.5 133.4 %collective-permute-start.28 = (bf16[768,1024]{1,0:T(8,128)(2,1)}, bf16[768,1024]{1,0:T(8,128)(2,1)}, u32[]{:S(2)}, u32[]{:S(2)}) collective-permute-start(bf16[768,1024]{1,0:T(8,128)(2,1)} %collective-permute-done.23.refs_1_), channel_id=1, source_target_pairs={{0,16},{8,24},{16,0},{24,8},{1,17},{9,25},{17,1},{25,9},{2,18},{10... | collective-permute-start | bytes 4718600 | tf_op jit(solution)/shard_map/ppermute | solution.py:55
  538.2 300.3 %reduce-scatter.5.cloned.1.call-start = ((), (), s32[]{:S(2)}) async-start(), calls=%async_computation.11 | async-start | bytes 14155776 | tf_op jit(solution)/shard_map/reduce_scatter | solution.py:914
  578.3 42.8 %collective-permute-start.29 = (bf16[768,1024]{1,0:T(8,128)(2,1)S(1)}, bf16[768,1024]{1,0:T(8,128)(2,1)S(1)}, u32[]{:S(2)}, u32[]{:S(2)}) collective-permute-start(bf16[768,1024]{1,0:T(8,128)(2,1)S(1)} %pad_maximum_fusion.10), channel_id=1, source_target_pairs={{0,8},{8,0},{16,24},{24,16},{1,9},{9,1},{17,25},{25,17},{2,10},{10... | collective-permute-start | bytes 4718600 | tf_op jit(solution)/shard_map/ppermute | solution.py:51
  587.2 35.5 %collective-permute-start.30 = (bf16[768,1024]{1,0:T(8,128)(2,1)S(1)}, bf16[768,1024]{1,0:T(8,128)(2,1)S(1)}, u32[]{:S(2)}, u32[]{:S(2)}) collective-permute-start(bf16[768,1024]{1,0:T(8,128)(2,1)S(1)} %pad_maximum_fusion.11), channel_id=1, source_target_pairs={{0,16},{8,24},{16,0},{24,8},{1,17},{9,25},{17,1},{25,9},{2,18},{10... | collective-permute-start | bytes 4718600 | tf_op jit(solution)/shard_map/ppermute | solution.py:55
  647.9 9.3 all-to-all-start.1
  651.3 288.4 %reduce-scatter.11.cloned.1.call-start = ((), (), s32[]{:S(2)}) async-start(), calls=%async_computation.14 | async-start | bytes 2359296 | tf_op jit(solution)/shard_map/reduce_scatter | solution.py:979
  657.4 52.4 %collective-permute-start.31 = (bf16[768,1024]{1,0:T(8,128)(2,1)}, bf16[768,1024]{1,0:T(8,128)(2,1)}, u32[]{:S(2)}, u32[]{:S(2)}) collective-permute-start(bf16[768,1024]{1,0:T(8,128)(2,1)} %pad_maximum_fusion.12), channel_id=1, source_target_pairs={{0,8},{8,0},{16,24},{24,16},{1,9},{9,1},{17,25},{25,17},{2,10},{10... | collective-permute-start | bytes 4718600 | tf_op jit(solution)/shard_map/ppermute | solution.py:51
  657.9 51.8 %collective-permute-start.32 = (bf16[768,1024]{1,0:T(8,128)(2,1)}, bf16[768,1024]{1,0:T(8,128)(2,1)}, u32[]{:S(2)}, u32[]{:S(2)}) collective-permute-start(bf16[768,1024]{1,0:T(8,128)(2,1)} %pad_maximum_fusion.13), channel_id=1, source_target_pairs={{0,16},{8,24},{16,0},{24,8},{1,17},{9,25},{17,1},{25,9},{2,18},{10... | collective-permute-start | bytes 4718600 | tf_op jit(solution)/shard_map/ppermute | solution.py:55
  661.8 66.2 %collective-permute-start.33 = (bf16[768,1024]{1,0:T(8,128)(2,1)}, bf16[768,1024]{1,0:T(8,128)(2,1)}, u32[]{:S(2)}, u32[]{:S(2)}) collective-permute-start(bf16[768,1024]{1,0:T(8,128)(2,1)} %add_convert_fusion.3), channel_id=1, source_target_pairs={{0,16},{8,24},{16,0},{24,8},{1,17},{9,25},{17,1},{25,9},{2,18},{10... | collective-permute-start | bytes 4718600 | tf_op jit(solution)/shard_map/ppermute | solution.py:55
  665.7 62.3 %collective-permute-start.34 = (bf16[768,1024]{1,0:T(8,128)(2,1)}, bf16[768,1024]{1,0:T(8,128)(2,1)}, u32[]{:S(2)}, u32[]{:S(2)}) collective-permute-start(bf16[768,1024]{1,0:T(8,128)(2,1)} %add_convert_fusion.2), channel_id=1, source_target_pairs={{0,8},{8,0},{16,24},{24,16},{1,9},{9,1},{17,25},{25,17},{2,10},{10... | collective-permute-start | bytes 4718600 | tf_op jit(solution)/shard_map/ppermute | solution.py:51
  729.0 18.4 %collective-permute-start.35 = (bf16[192,2048]{1,0:T(8,128)(2,1)S(1)}, bf16[192,2048]{1,0:T(8,128)(2,1)S(1)}, u32[]{:S(2)}, u32[]{:S(2)}) collective-permute-start(bf16[192,2048]{1,0:T(8,128)(2,1)S(1)} %get-tuple-element.274), channel_id=1, source_target_pairs={{0,8},{8,0},{16,24},{24,16},{1,9},{9,1},{17,25},{25,17},{2,10},{10... | collective-permute-start | bytes 2359304 | tf_op jit(solution)/shard_map/ppermute | solution.py:51
  730.6 20.5 %collective-permute-start.39 = (bf16[192,2048]{1,0:T(8,128)(2,1)S(1)}, bf16[192,2048]{1,0:T(8,128)(2,1)S(1)}, u32[]{:S(2)}, u32[]{:S(2)}) collective-permute-start(bf16[192,2048]{1,0:T(8,128)(2,1)S(1)} %get-tuple-element.272), channel_id=1, source_target_pairs={{0,16},{8,24},{16,0},{24,8},{1,17},{9,25},{17,1},{25,9},{2,18},{10... | collective-permute-start | bytes 2359304 | tf_op jit(solution)/shard_map/ppermute | solution.py:55
  730.9 37.0 %collective-permute-start.36 = (bf16[192,2048]{1,0:T(8,128)(2,1)S(1)}, bf16[192,2048]{1,0:T(8,128)(2,1)S(1)}, u32[]{:S(2)}, u32[]{:S(2)}) collective-permute-start(bf16[192,2048]{1,0:T(8,128)(2,1)S(1)} %get-tuple-element.274), channel_id=1, source_target_pairs={{0,16},{8,24},{16,0},{24,8},{1,17},{9,25},{17,1},{25,9},{2,18},{10... | collective-permute-start | bytes 2359304 | tf_op jit(solution)/shard_map/ppermute | solution.py:55
  747.5 34.9 %collective-permute-start.37 = (bf16[192,2048]{1,0:T(8,128)(2,1)S(1)}, bf16[192,2048]{1,0:T(8,128)(2,1)S(1)}, u32[]{:S(2)}, u32[]{:S(2)}) collective-permute-start(bf16[192,2048]{1,0:T(8,128)(2,1)S(1)} %collective-permute-done.35), channel_id=1, source_target_pairs={{0,16},{8,24},{16,0},{24,8},{1,17},{9,25},{17,1},{25,9},{2,18},{10... | collective-permute-start | bytes 2359304 | tf_op jit(solution)/shard_map/ppermute | solution.py:55
  751.1 31.2 %collective-permute-start.40 = (bf16[192,2048]{1,0:T(8,128)(2,1)S(1)}, bf16[192,2048]{1,0:T(8,128)(2,1)S(1)}, u32[]{:S(2)}, u32[]{:S(2)}) collective-permute-start(bf16[192,2048]{1,0:T(8,128)(2,1)S(1)} %collective-permute-done.39), channel_id=1, source_target_pairs={{0,8},{8,0},{16,24},{24,16},{1,9},{9,1},{17,25},{25,17},{2,10},{10... | collective-permute-start | bytes 2359304 | tf_op jit(solution)/shard_map/ppermute | solution.py:51
  755.0 33.5 %collective-permute-start.38 = (bf16[192,2048]{1,0:T(8,128)(2,1)S(1)}, bf16[192,2048]{1,0:T(8,128)(2,1)S(1)}, u32[]{:S(2)}, u32[]{:S(2)}) collective-permute-start(bf16[192,2048]{1,0:T(8,128)(2,1)S(1)} %get-tuple-element.272), channel_id=1, source_target_pairs={{0,8},{8,0},{16,24},{24,16},{1,9},{9,1},{17,25},{25,17},{2,10},{10... | collective-permute-start | bytes 2359304 | tf_op jit(solution)/shard_map/ppermute | solution.py:51
  785.1 68.1 %collective-permute-start.41 = (bf16[2,768,1024]{2,1,0:T(8,128)(2,1)}, bf16[2,768,1024]{2,1,0:T(8,128)(2,1)}, u32[]{:S(2)}, u32[]{:S(2)}) collective-permute-start(bf16[2,768,1024]{2,1,0:T(8,128)(2,1)} %pad_maximum_fusion.4), channel_id=1, source_target_pairs={{0,8},{8,0},{16,24},{24,16},{1,9},{9,1},{17,25},{25,17},{2,10},{10... | collective-permute-start | bytes 9437192 | tf_op jit(solution)/shard_map/ppermute | solution.py:51
  787.9 67.9 %collective-permute-start.42 = (bf16[2,768,1024]{2,1,0:T(8,128)(2,1)}, bf16[2,768,1024]{2,1,0:T(8,128)(2,1)}, u32[]{:S(2)}, u32[]{:S(2)}) collective-permute-start(bf16[2,768,1024]{2,1,0:T(8,128)(2,1)} %pad_maximum_fusion.5), channel_id=1, source_target_pairs={{0,16},{8,24},{16,0},{24,8},{1,17},{9,25},{17,1},{25,9},{2,18},{10... | collective-permute-start | bytes 9437192 | tf_op jit(solution)/shard_map/ppermute | solution.py:55
  838.6 178.6 %reduce-scatter.9.cloned.1.call-start = ((), (), s32[]{:S(2)}) async-start(), calls=%async_computation.13 | async-start | bytes 7077888 | tf_op jit(solution)/shard_map/reduce_scatter | solution.py:982
  899.4 32.7 %collective-permute-start.45 = (bf16[768,1024]{1,0:T(8,128)(2,1)}, bf16[768,1024]{1,0:T(8,128)(2,1)}, u32[]{:S(2)}, u32[]{:S(2)}) collective-permute-start(bf16[768,1024]{1,0:T(8,128)(2,1)} %add_convert_fusion.1), channel_id=1, source_target_pairs={{0,16},{8,24},{16,0},{24,8},{1,17},{9,25},{17,1},{25,9},{2,18},{10... | collective-permute-start | bytes 4718600 | tf_op jit(solution)/shard_map/ppermute | solution.py:55
  902.9 32.6 %collective-permute-start.46 = (bf16[768,1024]{1,0:T(8,128)(2,1)}, bf16[768,1024]{1,0:T(8,128)(2,1)}, u32[]{:S(2)}, u32[]{:S(2)}) collective-permute-start(bf16[768,1024]{1,0:T(8,128)(2,1)} %add_convert_fusion), channel_id=1, source_target_pairs={{0,8},{8,0},{16,24},{24,16},{1,9},{9,1},{17,25},{25,17},{2,10},{10... | collective-permute-start | bytes 4718600 | tf_op jit(solution)/shard_map/ppermute | solution.py:51
  937.4 20.8 %collective-permute-start.48 = (bf16[192,2048]{1,0:T(8,128)(2,1)}, bf16[192,2048]{1,0:T(8,128)(2,1)}, u32[]{:S(2)}, u32[]{:S(2)}) collective-permute-start(bf16[192,2048]{1,0:T(8,128)(2,1)} %get-tuple-element.189), channel_id=1, source_target_pairs={{0,8},{8,0},{16,24},{24,16},{1,9},{9,1},{17,25},{25,17},{2,10},{10... | collective-permute-start | bytes 2359304 | tf_op jit(solution)/shard_map/ppermute | solution.py:51
  939.0 22.4 %collective-permute-start.51 = (bf16[192,2048]{1,0:T(8,128)(2,1)}, bf16[192,2048]{1,0:T(8,128)(2,1)}, u32[]{:S(2)}, u32[]{:S(2)}) collective-permute-start(bf16[192,2048]{1,0:T(8,128)(2,1)} %get-tuple-element.187), channel_id=1, source_target_pairs={{0,16},{8,24},{16,0},{24,8},{1,17},{9,25},{17,1},{25,9},{2,18},{10... | collective-permute-start | bytes 2359304 | tf_op jit(solution)/shard_map/ppermute | solution.py:55
  941.7 48.3 %collective-permute-start.47 = (bf16[192,2048]{1,0:T(8,128)(2,1)}, bf16[192,2048]{1,0:T(8,128)(2,1)}, u32[]{:S(2)}, u32[]{:S(2)}) collective-permute-start(bf16[192,2048]{1,0:T(8,128)(2,1)} %get-tuple-element.186), channel_id=1, source_target_pairs={{0,8},{8,0},{16,24},{24,16},{1,9},{9,1},{17,25},{25,17},{2,10},{10... | collective-permute-start | bytes 2359304 | tf_op jit(solution)/shard_map/ppermute | solution.py:51
  942.9 55.8 %collective-permute-start.50 = (bf16[192,2048]{1,0:T(8,128)(2,1)}, bf16[192,2048]{1,0:T(8,128)(2,1)}, u32[]{:S(2)}, u32[]{:S(2)}) collective-permute-start(bf16[192,2048]{1,0:T(8,128)(2,1)} %get-tuple-element.188), channel_id=1, source_target_pairs={{0,16},{8,24},{16,0},{24,8},{1,17},{9,25},{17,1},{25,9},{2,18},{10... | collective-permute-start | bytes 2359304 | tf_op jit(solution)/shard_map/ppermute | solution.py:55
  961.0 30.2 %collective-permute-start.49 = (bf16[192,2048]{1,0:T(8,128)(2,1)}, bf16[192,2048]{1,0:T(8,128)(2,1)}, u32[]{:S(2)}, u32[]{:S(2)}) collective-permute-start(bf16[192,2048]{1,0:T(8,128)(2,1)} %add_convert_fusion.6), channel_id=1, source_target_pairs={{0,16},{8,24},{16,0},{24,8},{1,17},{9,25},{17,1},{25,9},{2,18},{10... | collective-permute-start | bytes 2359304 | tf_op jit(solution)/shard_map/ppermute | solution.py:55
  962.6 23.0 %all-to-all-start.2 = ((f32[8,1,5120]{2,1,0:T(1,128)}), f32[8,1,5120]{2,1,0:T(1,128)S(1)}, u32[]{:S(2)}, u32[]{:S(2)}) async-start(f32[8,1,5120]{2,1,0:T(1,128)} %reshape.256), calls=%async_computation.6 | async-start | bytes 327680 | tf_op jit(solution)/shard_map/all_to_all | solution.py:130
  987.5 10.0 collective-permute-start.56
  994.3 19.2 %collective-permute-start.52 = (bf16[192,2048]{1,0:T(8,128)(2,1)S(1)}, bf16[192,2048]{1,0:T(8,128)(2,1)S(1)}, u32[]{:S(2)}, u32[]{:S(2)}) collective-permute-start(bf16[192,2048]{1,0:T(8,128)(2,1)S(1)} %get-tuple-element.185), channel_id=1, source_target_pairs={{0,8},{8,0},{16,24},{24,16},{1,9},{9,1},{17,25},{25,17},{2,10},{10... | collective-permute-start | bytes 2359304 | tf_op jit(solution)/shard_map/ppermute | solution.py:51
  1018.3 10.1 collective-permute-start.53
  1020.2 8.8 collective-permute-start.54
  1020.7 8.5 collective-permute-start.55
  (118 other events, 1656.4 us)
Sparse Core Ops, SparseCore 0:
  32.1 71.5 all-gather.4
  105.3 27.6 all-gather.6
  134.6 116.2 all-gather.10
  256.4 117.2 all-gather.8
  538.3 142.1 reduce-scatter.6
  682.6 127.5 reduce-scatter.4
  838.7 35.5 reduce-scatter.10
  894.8 69.0 reduce-scatter.8

commit v6 on v5

--- a/solution.py
+++ b/solution.py
@@ -27,7 +27,7 @@
 NT = (((1,), (1,)), ((), ()))
 TN = (((0,), (0,)), ((), ()))
 TILE = 256
-WIN = 512
+WIN = 768
 NOWHERE = -(1 << 20)
 
 
@@ -84,9 +84,14 @@
     return send_x(low), send_y(high)
 
 
-def scatter_last(take, me, ahead):
+def scatter_last_payload(take, me, ahead):
     low = (take(me ^ 2, 0).astype(F32) + ahead[0].astype(F32)).astype(BF)
     high = (take(me ^ 1, 1).astype(F32) + ahead[1].astype(F32)).astype(BF)
+    return low, high
+
+
+def scatter_last(take, me, ahead):
+    low, high = scatter_last_payload(take, me, ahead)
     return send_y(low), send_x(high)
 
 
@@ -169,7 +174,10 @@
         return tuple(
             lax.psum_scatter(grad, "ctx", scatter_dimension=0, tiled=True) for grad in grads
         )
-    take = expert_take(grads)
+    return scatter_joined(expert_take(grads), me)
+
+
+def scatter_joined(take, me):
     low = send_x(jnp.stack([take(me ^ 1, 0), take(me ^ 3, 0)]).astype(BF))
     high = send_y(jnp.stack([take(me ^ 2, 1), take(me ^ 3, 1)]).astype(BF))
     return low, high
@@ -223,22 +231,25 @@
     return whole, (pieces[0][2], pieces[1][2])
 
 
-def scatter_group(partial, slot_table, me):
+def scatter_group(partial, slot_table, me, joined=False):
     blocks = slot_table.shape[0]
     block = partial.shape[0] // blocks
     if lax.axis_size("ctx") != 4:
         ordered = pick_blocks(partial.reshape(blocks, block, -1), slot_table).astype(BF)
         whole = lax.psum_scatter(ordered, "ctx", scatter_dimension=0, tiled=True)
-        return whole.astype(F32), (whole,), (whole,)
+        return whole.astype(F32), (whole,), (whole,), (whole,)
 
     def take(owner, part):
         start = slot_table[2 * owner + part] * block
         return lax.dynamic_slice(partial, (start, 0), (block, partial.shape[1]))
 
-    ahead = scatter_ahead(take, me)
-    direct = scatter_direct(take, me)
-    last = scatter_last(take, me, ahead)
-    return jnp.concatenate(scatter_end(take, me, direct, last), axis=0), ahead, last
+    if joined:
+        ahead, direct = split_sums(scatter_joined(take, me))
+    else:
+        ahead, direct = scatter_ahead(take, me), scatter_direct(take, me)
+    sent = scatter_last_payload(take, me, ahead)
+    last = send_y(sent[0]), send_x(sent[1])
+    return jnp.concatenate(scatter_end(take, me, direct, last), axis=0), ahead, sent, last
 
 
 def prefix_count(member):
@@ -752,8 +763,76 @@
         ahead = after_all(packs[0], *tokens_there)
         ahead = send_x(ahead[0]), send_y(ahead[1])
 
+    seg_ids = jnp.concatenate([jnp.full((PROMPT,), -1, jnp.int32), seg_row])
+    starts = jnp.sum(
+        (seg_row[None, :] < jnp.arange(CONT, dtype=jnp.int32)[:, None]).astype(jnp.int32), axis=1
+    )
+    first_pos = jnp.sum(
+        jnp.where(
+            seg_row[:, None] == jnp.arange(CONT, dtype=jnp.int32)[None, :], starts[None, :], 0
+        ),
+        axis=1,
+    )
+    cont_pos = PROMPT + jnp.arange(CTOK, dtype=jnp.int32) - first_pos
+    position = jnp.concatenate([jnp.arange(PROMPT, dtype=jnp.int32), cont_pos])
+    cos_part, sin_part = angles(position)
+    group_inputs = tokens_group.astype(F32)
+    normed_group = group_inputs * inverse_root(group_inputs)
+    hidden_one = (normed_group * gain_attn).astype(BF)
+    projected = jnp.dot(hidden_one, packed, preferred_element_type=F32)
+    query_pre = projected[:, :own_width]
+    key_pre = projected[:, own_width : 2 * own_width]
+    squares = jnp.stack([jnp.sum(query_pre * query_pre, axis=1), jnp.sum(key_pre * key_pre, axis=1)])
+    if ctx_size == 4:
+        squares = after(squares, *ahead)
+    squares = sum_over_ctx(squares)
+    if ctx_size == 4:
+        direct = after_all(packs[0], squares)
+        direct = send_x(direct[1]), send_y(direct[0])
+    roots = lax.rsqrt(squares / D + epsilon)
+    root_query, root_key = roots[0][:, None], roots[1][:, None]
+    normed_query = query_pre * root_query
+    normed_key = key_pre * root_key
+    query_rot, key_rot, value_low, context_low = attend(
+        projected,
+        roots.T,
+        jnp.stack([gain_query, gain_key]),
+        cos_part,
+        sin_part,
+        seg_ids,
+        own_width,
+    )
+    branch_part = jnp.dot(context_low, out_full, preferred_element_type=F32)
+    if ctx_size == 4:
+        branch_part = after(branch_part, *direct)
+    branch, unused, unused, branch_there = scatter_group(branch_part, slot_table, me)
+    me_table = jnp.reshape(me, (1,)).astype(jnp.int32)
+    width = w_gate.shape[2]
+    lows, highs, backs = [], [], []
+    if ctx_size == 4:
+        passed = after_all(ahead, *branch_there)
+        passed = send_y(passed[0]), send_x(passed[1])
+        lows.append((packs[0][0], ahead[0], direct[1], passed[0]))
+        highs.append((packs[0][1], direct[0], ahead[1], passed[1]))
+        upstream, first_passed = upstream_all, passed
+        for e in range(1, own_experts):
+            low, high = after_all(packs[e], *passed)
+            ahead = send_x(low), send_y(high)
+            direct = send_x(high), send_y(low)
+            passed = send_y(ahead[0]), send_x(ahead[1])
+            lows.append((packs[e][0], ahead[0], direct[1], passed[0]))
+            highs.append((packs[e][1], direct[0], ahead[1], passed[1]))
+            upstream = after(upstream, *ahead)
+    else:
+        for e in range(own_experts):
+            both, down = whole_expert(*after_all((w_gate[e], w_up[e], w_down[e]), *branch_there))
+            lows.append((both,))
+            highs.append((down,))
+        upstream = upstream_all
+        first_passed = branch_there
+
     own_ids = exp_index * own_experts + jnp.arange(own_experts, dtype=jnp.int32)
-    member = jnp.any(routes_all[:, :, None] == own_ids[None, None, :], axis=1)
+    member = jnp.any(after(routes_all, *first_passed)[:, :, None] == own_ids[None, None, :], axis=1)
     place_of = prefix_count(member)
     capacity = exp_size * 8 * ((5 * tok_rows * TOP // (4 * experts) + 7) // 8)
     row_tiles = (capacity + TILE - 1) // TILE
@@ -782,76 +861,8 @@
     share_row_start = jnp.minimum(first_place // 128 * 128, capacity - 384)
     token_tables = (first_row, more_rows, share_row_start, place_column)
 
-    seg_ids = jnp.concatenate([jnp.full((PROMPT,), -1, jnp.int32), seg_row])
-    starts = jnp.sum(
-        (seg_row[None, :] < jnp.arange(CONT, dtype=jnp.int32)[:, None]).astype(jnp.int32), axis=1
-    )
-    first_pos = jnp.sum(
-        jnp.where(
-            seg_row[:, None] == jnp.arange(CONT, dtype=jnp.int32)[None, :], starts[None, :], 0
-        ),
-        axis=1,
-    )
-    cont_pos = PROMPT + jnp.arange(CTOK, dtype=jnp.int32) - first_pos
-    position = jnp.concatenate([jnp.arange(PROMPT, dtype=jnp.int32), cont_pos])
-    cos_part, sin_part = angles(position)
-    group_inputs = after(
-        tokens_group, token_of_row, place_column, first_row, more_rows, share_row_start, used_tiles, windows
-    ).astype(F32)
-    normed_group = group_inputs * inverse_root(group_inputs)
-    hidden_one = (normed_group * gain_attn).astype(BF)
-    projected = jnp.dot(hidden_one, packed, preferred_element_type=F32)
-    query_pre = projected[:, :own_width]
-    key_pre = projected[:, own_width : 2 * own_width]
-    squares = jnp.stack([jnp.sum(query_pre * query_pre, axis=1), jnp.sum(key_pre * key_pre, axis=1)])
-    if ctx_size == 4:
-        squares = after(squares, *ahead)
-    squares = sum_over_ctx(squares)
-    if ctx_size == 4:
-        direct = after_all(packs[0], squares)
-        direct = send_x(direct[1]), send_y(direct[0])
-    roots = lax.rsqrt(squares / D + epsilon)
-    root_query, root_key = roots[0][:, None], roots[1][:, None]
-    normed_query = query_pre * root_query
-    normed_key = key_pre * root_key
-    query_rot, key_rot, value_low, context_low = attend(
-        projected,
-        roots.T,
-        jnp.stack([gain_query, gain_key]),
-        cos_part,
-        sin_part,
-        seg_ids,
-        own_width,
-    )
-    branch_part = jnp.dot(context_low, out_full, preferred_element_type=F32)
-    if ctx_size == 4:
-        branch_part = after(branch_part, *direct)
-    branch, unused, branch_there = scatter_group(branch_part, slot_table, me)
-    me_table = jnp.reshape(me, (1,)).astype(jnp.int32)
     ids = jnp.stack([own_ids[0], me.astype(jnp.int32)])
-    width = w_gate.shape[2]
-    lows, highs, backs = [], [], []
-    if ctx_size == 4:
-        passed = after_all(ahead, *branch_there)
-        passed = send_y(passed[0]), send_x(passed[1])
-        lows.append((packs[0][0], ahead[0], direct[1], passed[0]))
-        highs.append((packs[0][1], direct[0], ahead[1], passed[1]))
-        upstream = upstream_all
-        for e in range(1, own_experts):
-            low, high = after_all(packs[e], *passed)
-            ahead = send_x(low), send_y(high)
-            direct = send_x(high), send_y(low)
-            passed = send_y(ahead[0]), send_x(ahead[1])
-            lows.append((packs[e][0], ahead[0], direct[1], passed[0]))
-            highs.append((packs[e][1], direct[0], ahead[1], passed[1]))
-            upstream = after(upstream, *ahead)
-        backs.append(back_rows(row_tables[0], me_table, upstream, highs[0], width))
-    else:
-        for e in range(own_experts):
-            both, down = whole_expert(*after_all((w_gate[e], w_up[e], w_down[e]), *branch_there))
-            lows.append((both,))
-            highs.append((down,))
-        backs.append(back_rows(row_tables[0], me_table, upstream_all, highs[0], width))
+    backs.append(back_rows(row_tables[0], me_table, upstream, highs[0], width))
 
     inputs = tokens.astype(F32)
     middle = inputs + branch
@@ -884,39 +895,37 @@
         tiled=True,
     )
     grad_prob = jnp.swapaxes(share_back, 0, 1).reshape(tok_rows, experts)
-    expert_grads = []
-    mixture_part = grad_two_part
-    for e in every:
-        rows, hidden, grad_hidden = after_all(made[e][:3], mixture_part)
-        expert_grads.append(
-            (
-                lax.dot_general(rows, grad_hidden, TN, preferred_element_type=F32).astype(BF),
-                lax.dot_general(hidden, backs[e][0], TN, preferred_element_type=F32).astype(BF),
-            )
+    def weight_grads(e, *others):
+        rows, hidden, grad_hidden = after_all(made[e][:3], *others)
+        return (
+            lax.dot_general(rows, grad_hidden, TN, preferred_element_type=F32).astype(BF),
+            lax.dot_general(hidden, backs[e][0], TN, preferred_element_type=F32).astype(BF),
         )
-        if e == 0:
-            results = [
-                jnp.dot(
-                    after(made[k][1], *expert_grads[0]), backs[k][2], preferred_element_type=F32
-                ).astype(BF)
-                for k in every
-            ]
-            if ctx_size == 4:
-                take = expert_take(expert_grads[0])
-                ahead = scatter_ahead(take, me)
-                results = after_all(results, *ahead)
-                direct = scatter_direct(take, me, *ahead)
-                last = scatter_last(take, me, ahead)
-            else:
-                direct, last = scatter_expert_first(expert_grads[0], me), ()
-            mixture_part, unused = combine_rows(token_tables, results, shares)
+
+    expert_grads = [weight_grads(0, grad_two_part)]
+    results = [
+        jnp.dot(
+            after(made[e][1], share_back, *expert_grads[0]),
+            backs[e][2],
+            preferred_element_type=F32,
+        ).astype(BF)
+        for e in every
+    ]
+    if ctx_size == 4:
+        take = expert_take(expert_grads[0])
+        ahead = scatter_ahead(take, me)
+        results = after_all(results, *ahead)
+    mixture_part, unused = combine_rows(token_tables, results, shares)
+    if ctx_size == 4:
+        direct = scatter_direct(take, me, mixture_part)
+        last = scatter_last(take, me, after_all(ahead, mixture_part))
+    else:
+        direct, last = scatter_expert_first(expert_grads[0], me), ()
     directs, lasts = [direct], [last]
+
     mixture = lax.psum_scatter(mixture_part, "exp", scatter_dimension=0, tiled=True)
     output = (middle + mixture.astype(F32)).astype(BF)
-
-    grad_two = after(
-        grad_two, mixture_part, *(part for grads in expert_grads[1:] for part in grads)
-    ).astype(F32)
+    grad_two = after(grad_two, mixture_part).astype(F32)
     grad_logits = (
         router_prob * (grad_prob - jnp.sum(router_prob * grad_prob, axis=-1, keepdims=True))
     ).astype(BF)
@@ -931,6 +940,7 @@
     branch_grad, grad_there = gather_group(own_grad, slot_table, me)
     sums = []
     for e in range(1, own_experts):
+        expert_grads.append(weight_grads(e, own_grad))
         sums.append(scatter_expert_first(after_all(expert_grads[e], *grad_there), me))
     grad_context = lax.dot_general(branch_grad, out_full, NT, preferred_element_type=F32).astype(BF)
     out_grad = lax.dot_general(
@@ -966,21 +976,24 @@
     grad_one_part = lax.dot_general(grad_packed, packed, NT, preferred_element_type=F32)
     grad_attn_gain = jnp.sum(grad_one_part * normed_group, axis=0)
     qkv_grad = lax.dot_general(hidden_one, grad_projected, TN, preferred_element_type=F32).astype(BF)
-    grad_one, one_ahead, unused = scatter_group(
-        after(grad_one_part, *(piece for pieces in lasts[1:] for piece in pieces)), slot_table, me
+    grad_one, one_ahead, one_sent, unused = scatter_group(
+        after(grad_one_part, *(piece for pieces in lasts[1:] for piece in pieces)),
+        slot_table,
+        me,
+        joined=True,
     )
     weight_sums = [
         scatter_expert_end(
-            expert_grads[e], after_all(directs[e], *one_ahead), after_all(lasts[e], *one_ahead), me
+            expert_grads[e], after_all(directs[e], *one_sent), after_all(lasts[e], *one_sent), me
         )
         for e in every
     ]
     gate_grad, up_grad, down_grad = (jnp.stack(parts) for parts in zip(*weight_sums))
     out_sum = lax.psum_scatter(
-        after(out_grad, mixture), "exp", scatter_dimension=0, tiled=True
+        out_grad, "exp", scatter_dimension=0, tiled=True
     ).astype(F32)
     qkv_sum = lax.psum_scatter(
-        qkv_grad.reshape(ctx_size, exp_size * part_rows, 3 * own_width),
+        after(qkv_grad, mixture).reshape(ctx_size, exp_size * part_rows, 3 * own_width),
         "exp",
         scatter_dimension=1,
         tiled=True,
@@ -999,7 +1012,7 @@
     small_sums = jnp.concatenate(
         [grad_router, jnp.stack([grad_ffn_gain, grad_attn_gain]), head_gains]
     )
-    small_sums = sum_to_rows(after(small_sums, *one_ahead), me)
+    small_sums = sum_to_rows(after(small_sums, *one_sent), me)
     return (
         output,
         grad_input,

time: 1050 us -> 1070 us (1.019)
  Pallas kernels: 264 us -> 282 us
  starting transfers between devices: 82.2 us -> 70.3 us
    ppermute x28 -> x27, waiting for transfers between devices: 113 us -> 155 us  [send_x(): return lax.ppermute(value, 'ctx', X_PAIRS)]
    ppermute x28 -> x27, waiting for transfers between devices: 151 us -> 128 us  [send_y(): return lax.ppermute(value, 'ctx', Y_PAIRS)]
    pallas_call x2, Pallas kernels: 112 us -> 126 us  [expert_rows(): pl.pallas_call(functools.partial(expert_kernel, own), out_shape=[made(wid...]
    ppermute x28 -> x27, starting transfers between devices: 36.5 us -> 25 us  [send_x(): return lax.ppermute(value, 'ctx', X_PAIRS)]
    all_gather x1, waiting for transfers between devices: 11.2 us -> 0.02 us  [local(): hidden_all = lax.all_gather(hidden_two, 'exp', axis=0, tiled=True)]
    ppermute x28 -> x27, starting transfers between devices: 25.1 us -> 27.2 us  [send_y(): return lax.ppermute(value, 'ctx', Y_PAIRS)]
  transfers between devices with their start and end apart: 70 -> 68, of which waited for: 35 -> 32; matrix products, arithmetic and copies ran while one was open for 34% -> 34% of each run, Pallas kernels for 19% -> 19%
where the time goes in v6:
time: 1070 us; the launch traced here: 1060 us
  waiting for transfers between devices  292 us (27%)
  Pallas kernels  282 us (26%)
  matrix products  166 us (16%)
  other arithmetic  131 us (12%)
  local copies, waits for them, and re-layouts  99.6 us (9%)
  starting transfers between devices  70.3 us (7%)
  between operations  21.4 us (2%)
    ppermute x27, waiting for transfers between devices, send_x(): return lax.ppermute(value, 'ctx', X_PAIRS)  155 us
    ppermute x27, waiting for transfers between devices, send_y(): return lax.ppermute(value, 'ctx', Y_PAIRS)  128 us
    pallas_call x2, Pallas kernels, expert_rows(): pl.pallas_call(functools.partial(expert_kernel, own), out_shape=[made(wid...  126 us
    pallas_call x2, Pallas kernels, back_rows(): pl.pallas_call(back_rows_kernel, out_shape=[jax.ShapeDtypeStruct((capacit...  59.7 us
    dot_general x2, matrix products, weight_grads(): lax.dot_general(rows, grad_hidden, TN, preferred_element_type=F32)  45 us
    pallas_call x2, Pallas kernels, combine_rows(): pl.pallas_call(functools.partial(combine_kernel, experts), out_shape=[jax...  40.8 us
    pallas_call x1, Pallas kernels, attend_back(): pl.pallas_call(functools.partial(attend_back_kernel, tiles, 1.0 / math.sq...  30 us
    ppermute x27, starting transfers between devices, send_y(): return lax.ppermute(value, 'ctx', Y_PAIRS)  27.2 us
  transfers between devices with their start and end apart: 68, of which 32 were waited for; matrix products, arithmetic and copies ran while one was open for 34% of the time, Pallas kernels for 19%

profile of v6, /device:TPU:0, one launch (start us, length us, event | category | flops | bytes accessed | tf_op | source)
XLA Modules:
  0.0 1062.0 jit_solution(478610925452442029)
XLA Ops:
  16.5 4.0 collective-permute-start.6
  21.1 5.5 collective-permute-done.6
  26.6 3.7 collective-permute-done.7
  34.8 3.4 broadcast.176.clone
  54.7 5.7 collective-permute-done
  61.8 17.0 %collective-permute-done.4 = bf16[192,2048]{1,0:T(8,128)(2,1)S(1)} collective-permute-done((bf16[192,2048]{1,0:T(8,128)(2,1)}, bf16[192,2048]{1,0:T(8,128)(2,1)S(1)}, u32[]{:S(2)}, u32[]{:S(2)}) %collective-permute-start.4) | collective-permute-done | bytes 786464 | tf_op jit(solution)/shard_map/ppermute | solution.py:55
  84.5 9.8 collective-permute-done.2
  103.8 4.1 fusion.5
  110.2 16.1 %fusion.16.qp_ref.kp_ref.vp_ref = f32[1536,1664]{1,0:T(8,128)S(1)} fusion(bf16[2048,1664]{1,0:T(8,128)(2,1)} %bitcast.337, bf16[1536,2048]{1,0:T(8,128)(2,1)} %constant_dynamic-update-slice_fusion.9, f32[2048]{0:T(1024)S(1)} %get-tuple-element.175, f32[1536]{0:T(1024)S(1)} %add_rsqrt_fusion.1), kind=kOutput, calls=%fused_computation.73 | convolution fusion | flops 10481565696 | bytes 23345152 | tf_op jit(solution)/shard_map/dot_general | solution.py:782
  126.8 3.0 collective-permute-done.9.refs_1_
  143.7 25.7 %shard_map.272 = (bf16[1536,512]{1,0:T(8,128)(2,1)S(1)}, bf16[1536,512]{1,0:T(8,128)(2,1)}, bf16[1536,512]{1,0:T(8,128)(2,1)}, bf16[1536,512]{1,0:T(8,128)(2,1)}) custom-call(f32[1536,1664]{1,0:T(8,128)} %copy-done.17, f32[1536,1664]{1,0:T(8,128)} %copy-done.17, f32[1536,1664]{1,0:T(8,128)} %copy-done.17, f32[1536,2]{1,0:T(8,128)S(1)} %fusion.87.root_ref.key_root_ref, ...), custom_call_target="tpu_custom_call" | custom-call | flops 3221225472 | bytes 15728640 | tf_op jit(solution)/shard_map/pallas_call | solution.py:339
  170.6 5.6 fusion.103
  179.7 17.6 %collective-permute-done.16 = bf16[192,2048]{1,0:T(8,128)(2,1)S(1)} collective-permute-done((bf16[192,2048]{1,0:T(8,128)(2,1)S(1)}, bf16[192,2048]{1,0:T(8,128)(2,1)S(1)}, u32[]{:S(2)}, u32[]{:S(2)}) %collective-permute-start.16) | collective-permute-done | bytes 786464 | tf_op jit(solution)/shard_map/ppermute | solution.py:51
  199.5 11.0 %collective-permute-done.15 = bf16[192,2048]{1,0:T(8,128)(2,1)S(1)} collective-permute-done((bf16[192,2048]{1,0:T(8,128)(2,1)S(1)}, bf16[192,2048]{1,0:T(8,128)(2,1)S(1)}, u32[]{:S(2)}, u32[]{:S(2)}) %collective-permute-start.15) | collective-permute-done | bytes 786464 | tf_op jit(solution)/shard_map/ppermute | solution.py:51
  210.5 7.0 collective-permute-done.17
  218.6 8.3 collective-permute-done.18
  226.9 8.5 collective-permute-done.20
  242.2 5.2 all-to-all-start
  254.2 8.8 collective-permute-done.21.refs_3_
  262.9 5.6 collective-permute-done.22.refs_3_.refs_7_
  279.5 14.7 %select_reduce_fusion = s32[2,2048]{1,0:T(2,128)S(1)} fusion(s32[2,3072]{1,0:T(2,128)S(1)} %copy.283, pred[2,3072]{1,0:T(4,128)(4,1)S(1)} %bitcast.348), kind=kLoop, calls=%fused_computation | loop fusion | flops 50327552 | bytes 47104 | tf_op jit(solution)/shard_map/reduce_max | solution.py:844
  297.6 2.9 broadcast_select_fusion.pos_ref
  300.5 7.1 collective-permute-done.24.refs_2_.refs_6_
  307.6 33.7 %collective-permute-done.23.refs_1_ = bf16[768,1024]{1,0:T(8,128)(2,1)} collective-permute-done((bf16[768,1024]{1,0:T(8,128)(2,1)}, bf16[768,1024]{1,0:T(8,128)(2,1)}, u32[]{:S(2)}, u32[]{:S(2)}) %collective-permute-start.23) | collective-permute-done | bytes 1572896 | tf_op jit(solution)/shard_map/ppermute | solution.py:51
  345.9 29.7 %shard_map.273 = (bf16[2048,2048]{1,0:T(8,128)(2,1)}, f32[2048,1024]{1,0:T(8,128)}, bf16[1024,2048]{1,0:T(8,128)(2,1)}) custom-call(s32[1]{0:T(128)} %get-tuple-element.319.tiles_ref, s32[8]{0:T(128)S(1)} %get-tuple-element.317.low_ref, s32[8]{0:T(128)S(1)} %get-tuple-element.315.windows_ref, s32[1]{0:T(128)} %bitcast.36.me_ref, s32[2048,1]{1,0:T(8,128)S(1)} %copy-done.5, ...), custom_call_target="tpu_custom_call" | custom-call | flops 11274289152 | bytes 37748736 | tf_op jit(solution)/shard_map/pallas_call | solution.py:516
  375.6 62.7 %shard_map.274 = (bf16[2048,2048]{1,0:T(8,128)(2,1)}, bf16[2048,1024]{1,0:T(8,128)(2,1)}, bf16[2048,2048]{1,0:T(8,128)(2,1)}, bf16[2048,2048]{1,0:T(8,128)(2,1)}, f32[2048,1]{1,0:T(8,128)}) custom-call(s32[1]{0:T(128)} %get-tuple-element.319.tiles_ref, s32[8]{0:T(128)} %copy-done.10, s32[8]{0:T(128)} %copy-done.11, s32[2]{0:T(128)} %pad_add_fusion.ids_ref, ...), custom_call_target="tpu_custom_call" | custom-call | flops 30601641984 | bytes 58720256 | tf_op jit(solution)/shard_map/pallas_call | solution.py:616
  441.4 30.0 %shard_map.275 = (bf16[2048,2048]{1,0:T(8,128)(2,1)}, f32[2048,1024]{1,0:T(8,128)}, bf16[1024,2048]{1,0:T(8,128)(2,1)}) custom-call(s32[1]{0:T(128)} %get-tuple-element.318.tiles_ref, s32[8]{0:T(128)S(1)} %get-tuple-element.316.low_ref, s32[8]{0:T(128)S(1)} %get-tuple-element.314.windows_ref, s32[1]{0:T(128)} %bitcast.36.me_ref, ...), custom_call_target="tpu_custom_call" | custom-call | flops 11274289152 | bytes 37748736 | tf_op jit(solution)/shard_map/pallas_call | solution.py:516
  471.5 62.8 %shard_map.276 = (bf16[2048,2048]{1,0:T(8,128)(2,1)}, bf16[2048,1024]{1,0:T(8,128)(2,1)}, bf16[2048,2048]{1,0:T(8,128)(2,1)}, bf16[2048,2048]{1,0:T(8,128)(2,1)}, f32[2048,1]{1,0:T(8,128)}) custom-call(s32[1]{0:T(128)} %get-tuple-element.318.tiles_ref, s32[8]{0:T(128)} %copy-done.8, s32[8]{0:T(128)} %copy-done.9, s32[2]{0:T(128)} %pad_add_fusion.ids_ref, ...), custom_call_target="tpu_custom_call" | custom-call | flops 30601641984 | bytes 58720256 | tf_op jit(solution)/shard_map/pallas_call | solution.py:616
  537.3 20.3 %shard_map.277 = (bf16[3072,2048]{1,0:T(8,128)(2,1)}, f32[3072,2]{1,0:T(8,128)S(1)}) custom-call(s32[2,12]{1,0:T(2,128)S(1)} %copy.292.start_ref, s32[2,12]{1,0:T(2,128)S(1)} %copy.293.more_ref, s32[2,12]{1,0:T(2,128)S(1)} %copy.294.wide_ref, s32[3072,2]{1,0:T(8,128)S(1)} %copy-done, bf16[2048,2048]{1,0:T(8,128)(2,1)} %get-tuple-element.104.refs_0_, ...), custom_call_target="tpu_custom_call" | custom-call | flops 6442450944 | bytes 29360128 | tf_op jit(solution)/shard_map/pallas_call | solution.py:674
  561.3 3.3 all-to-all-start.1
  564.6 12.9 %convolution_convert_fusion.6 = bf16[1024,2048]{1,0:T(8,128)(2,1)S(1)} fusion(bf16[2048,1024]{1,0:T(8,128)(2,1)} %get-tuple-element.122, bf16[2048,2048]{1,0:T(8,128)(2,1)} %get-tuple-element.121), kind=kOutput, calls=%fused_computation.25 | convolution fusion | flops 8592031744 | bytes 16777216 | tf_op jit(solution)/shard_map/dot_general | solution.py:902
  579.1 22.4 %convolution_convert_fusion.4 = bf16[2048,2048]{1,0:T(8,128)(2,1)S(1)} fusion(bf16[2048,2048]{1,0:T(8,128)(2,1)} %get-tuple-element.118, bf16[2048,2048]{1,0:T(8,128)(2,1)} %get-tuple-element.119), kind=kOutput, calls=%fused_computation.14 | convolution fusion | flops 17184063488 | bytes 25165824 | tf_op jit(solution)/shard_map/dot_general | solution.py:901
  601.5 2.9 constant_dynamic-slice_fusion.39
  607.1 14.7 %convolution_convert_fusion.3.refs_0_ = bf16[2048,2048]{1,0:T(8,128)(2,1)} fusion(bf16[2048,1024]{1,0:T(8,128)(2,1)} %get-tuple-element.122, bf16[1024,2048]{1,0:T(8,128)(2,1)} %get-tuple-element.123), kind=kOutput, calls=%fused_computation.13 | convolution fusion | flops 8594128896 | bytes 16777216 | tf_op jit(solution)/shard_map/dot_general | solution.py:907
  621.8 10.8 %convolution_convert_fusion.2.refs_1_ = bf16[2048,2048]{1,0:T(8,128)(2,1)} fusion(bf16[2048,1024]{1,0:T(8,128)(2,1)S(1)} %copy-done.98, bf16[1024,2048]{1,0:T(8,128)(2,1)S(1)} %copy-done.99), kind=kOutput, calls=%fused_computation.12 | convolution fusion | flops 8594128896 | bytes 16777216 | tf_op jit(solution)/shard_map/dot_general | solution.py:907
  632.6 10.2 collective-permute-done.29
  644.2 20.5 %shard_map.278 = (bf16[3072,2048]{1,0:T(8,128)(2,1)}, f32[3072,2]{1,0:T(8,128)}) custom-call(s32[2,12]{1,0:T(2,128)S(1)} %copy.292.start_ref, s32[2,12]{1,0:T(2,128)S(1)} %copy.293.more_ref, s32[2,12]{1,0:T(2,128)S(1)} %copy.294.wide_ref, s32[3072,2]{1,0:T(8,128)S(1)} %copy-done.1, bf16[2048,2048]{1,0:T(8,128)(2,1)} %convolution_convert_fusion.3.refs_0_, ...), custom_call_target="tpu_custom_call" | custom-call | flops 6442450944 | bytes 29360128 | tf_op jit(solution)/shard_map/pallas_call | solution.py:674
  673.9 3.7 add_convert_fusion.3
  679.6 3.3 add_convert_fusion.2
  684.4 4.5 multiply_reduce_fusion.2
  690.6 18.9 %collective-permute-done.31 = bf16[768,1024]{1,0:T(8,128)(2,1)} collective-permute-done((bf16[768,1024]{1,0:T(8,128)(2,1)}, bf16[768,1024]{1,0:T(8,128)(2,1)}, u32[]{:S(2)}, u32[]{:S(2)}) %collective-permute-start.31) | collective-permute-done | bytes 1572896 | tf_op jit(solution)/shard_map/ppermute | solution.py:51
  711.3 31.8 %collective-permute-done.33 = bf16[768,1024]{1,0:T(8,128)(2,1)} collective-permute-done((bf16[768,1024]{1,0:T(8,128)(2,1)}, bf16[768,1024]{1,0:T(8,128)(2,1)}, u32[]{:S(2)}, u32[]{:S(2)}) %collective-permute-start.33) | collective-permute-done | bytes 1572896 | tf_op jit(solution)/shard_map/ppermute | solution.py:55
  749.1 22.6 %convolution_convert_fusion.1 = bf16[2048,2048]{1,0:T(8,128)(2,1)S(1)} fusion(bf16[2048,2048]{1,0:T(8,128)(2,1)} %get-tuple-element.143, bf16[2048,2048]{1,0:T(8,128)(2,1)} %get-tuple-element.144), kind=kOutput, calls=%fused_computation.11 | convolution fusion | flops 17184063488 | bytes 25165824 | tf_op jit(solution)/shard_map/dot_general | solution.py:901
  771.7 12.7 %convolution_convert_fusion.5 = bf16[1024,2048]{1,0:T(8,128)(2,1)S(1)} fusion(bf16[2048,1024]{1,0:T(8,128)(2,1)} %get-tuple-element.145, bf16[2048,2048]{1,0:T(8,128)(2,1)} %get-tuple-element.146), kind=kOutput, calls=%fused_computation.24 | convolution fusion | flops 8592031744 | bytes 16777216 | tf_op jit(solution)/shard_map/dot_general | solution.py:902
  789.2 11.8 %collective-permute-done.37 = bf16[192,2048]{1,0:T(8,128)(2,1)S(1)} collective-permute-done((bf16[192,2048]{1,0:T(8,128)(2,1)S(1)}, bf16[192,2048]{1,0:T(8,128)(2,1)S(1)}, u32[]{:S(2)}, u32[]{:S(2)}) %collective-permute-start.37) | collective-permute-done | bytes 786464 | tf_op jit(solution)/shard_map/ppermute | solution.py:55
  810.5 5.2 convolution_convert_fusion.8.d_ref
  815.6 30.0 %shard_map.279 = (f32[1536,512]{1,0:T(8,128)}, f32[1536,512]{1,0:T(8,128)}, f32[1536,512]{1,0:T(8,128)}) custom-call(bf16[1536,512]{1,0:T(8,128)(2,1)S(1)} %copy-done.13, bf16[1536,512]{1,0:T(8,128)(2,1)S(1)} %copy-done.14, bf16[1536,512]{1,0:T(8,128)(2,1)} %get-tuple-element.133.v_ref, bf16[1536,512]{1,0:T(8,128)(2,1)} %convolution_convert_fusion.8.d_ref, ...), custom_call_target="tpu_custom_call" | custom-call | flops 8053063680 | bytes 15728640 | tf_op jit(solution)/shard_map/pallas_call | solution.py:428
  845.7 3.4 convert.32
  849.1 5.4 multiply_reduce_fusion.1
  854.5 4.6 convolution_convert_fusion.7
  859.3 11.7 %collective-permute-done.41 = bf16[2,768,1024]{2,1,0:T(8,128)(2,1)} collective-permute-done((bf16[2,768,1024]{2,1,0:T(8,128)(2,1)}, bf16[2,768,1024]{2,1,0:T(8,128)(2,1)}, u32[]{:S(2)}, u32[]{:S(2)}) %collective-permute-start.41) | collective-permute-done | bytes 3145760 | tf_op jit(solution)/shard_map/ppermute | solution.py:51
  874.9 3.8 slice_bitcast_fusion.5
  885.9 3.9 slice_bitcast_fusion.4
  893.0 3.3 add_convert_fusion.1
  901.0 3.9 multiply_convert_fusion.1
  906.6 14.4 %convolution_convert_fusion = bf16[2048,1536]{1,0:T(8,128)(2,1)} fusion(bf16[1536,2048]{1,0:T(8,128)(2,1)} %constant_dynamic-update-slice_fusion.9, f32[2048]{0:T(1024)S(1)} %copy-done.73, f32[1536]{0:T(1024)S(1)} %copy-done.93, bf16[1536,512]{1,0:T(8,128)(2,1)S(1)} %copy-done.35, bf16[1536,512]{1,0:T(8,128)(2,1)S(1)} %get-tuple-element.201, ...), kind=kOutput, calls=%fused_computation.10 | convolution fusion | flops 9693560832 | bytes 17315840 | tf_op jit(solution)/shard_map/dot_general | solution.py:978
  921.0 3.7 pad_maximum_fusion
  924.8 17.2 %fusion.4 = (f32[2048]{0:T(1024)}, f32[1536,2048]{1,0:T(8,128)S(1)}) fusion(bf16[1536,2048]{1,0:T(8,128)(2,1)} %constant_dynamic-update-slice_fusion.9, f32[1536]{0:T(1024)S(1)} %copy-done.93, bf16[2048,1664]{1,0:T(8,128)(2,1)} %bitcast.341, bf16[1536,1536]{1,0:T(8,128)(2,1)} %pad_maximum_fusion), kind=kOutput, calls=%fused_computation.8 | convolution fusion | flops 10481563648 | bytes 30423040 | tf_op jit(solution)/shard_map/dot_general | solution.py:976
  946.1 27.1 %collective-permute-done.47 = bf16[2,192,2048]{2,1,0:T(8,128)(2,1)S(1)} collective-permute-done((bf16[2,192,2048]{2,1,0:T(8,128)(2,1)S(1)}, bf16[2,192,2048]{2,1,0:T(8,128)(2,1)S(1)}, u32[]{:S(2)}, u32[]{:S(2)}) %collective-permute-start.47) | collective-permute-done | bytes 1572896 | tf_op jit(solution)/shard_map/ppermute | solution.py:51
  979.9 12.3 %collective-permute-done.48 = bf16[192,2048]{1,0:T(8,128)(2,1)} collective-permute-done((bf16[192,2048]{1,0:T(8,128)(2,1)}, bf16[192,2048]{1,0:T(8,128)(2,1)}, u32[]{:S(2)}, u32[]{:S(2)}) %collective-permute-start.48) | collective-permute-done | bytes 786464 | tf_op jit(solution)/shard_map/ppermute | solution.py:55
  992.1 4.6 fusion.21
  999.2 4.0 all-to-all-start.2
  1030.2 4.0 pad_maximum_fusion.2
  1043.9 6.5 fusion.13
  (514 shorter events, 225.1 us)
Async XLA Ops:
  7.2 100.8 %all-gather.5.cloned.1.call-start = ((), (), s32[]{:S(2)}) async-start(), calls=%async_computation.7 | async-start | bytes 7667712 | tf_op jit(solution)/shard_map/all_gather | solution.py:745
  16.5 10.1 collective-permute-start.6
  20.4 9.8 collective-permute-start.7
  20.9 9.6 collective-permute-start.8
  31.9 138.6 %all-gather.7.cloned.1.call-start = ((), (), s32[]{:S(2)}) async-start(), calls=%async_computation.8 | async-start | bytes 2359296 | tf_op jit(solution)/shard_map/all_gather | solution.py:752
  32.7 310.6 %all-gather.11.cloned.1.call-start = ((), (), s32[]{:S(2)}) async-start(), calls=%async_computation.10 | async-start | bytes 14155776 | tf_op jit(solution)/shard_map/all_gather | solution.py:760
  33.4 342.2 %all-gather.9.cloned.1.call-start = ((), (), s32[]{:S(2)}) async-start(), calls=%async_computation.9 | async-start | bytes 14155776 | tf_op jit(solution)/shard_map/all_gather | solution.py:872
  39.8 20.7 %collective-permute-start = (bf16[192,2048]{1,0:T(8,128)(2,1)}, bf16[192,2048]{1,0:T(8,128)(2,1)S(1)}, u32[]{:S(2)}, u32[]{:S(2)}) collective-permute-start(bf16[192,2048]{1,0:T(8,128)(2,1)} %get-tuple-element.281), channel_id=1, source_target_pairs={{0,8},{8,0},{16,24},{24,16},{1,9},{9,1},{17,25},{25,17},{2,10},{10... | collective-permute-start | bytes 2359304 | tf_op jit(solution)/shard_map/ppermute | solution.py:51
  41.3 41.0 %collective-permute-start.1 = (bf16[192,2048]{1,0:T(8,128)(2,1)}, bf16[192,2048]{1,0:T(8,128)(2,1)}, u32[]{:S(2)}, u32[]{:S(2)}) collective-permute-start(bf16[192,2048]{1,0:T(8,128)(2,1)} %get-tuple-element.281), channel_id=1, source_target_pairs={{0,16},{8,24},{16,0},{24,8},{1,17},{9,25},{17,1},{25,9},{2,18},{10... | collective-permute-start | bytes 2359304 | tf_op jit(solution)/shard_map/ppermute | solution.py:55
  41.9 57.9 %collective-permute-start.3 = (bf16[192,2048]{1,0:T(8,128)(2,1)}, bf16[192,2048]{1,0:T(8,128)(2,1)}, u32[]{:S(2)}, u32[]{:S(2)}) collective-permute-start(bf16[192,2048]{1,0:T(8,128)(2,1)} %get-tuple-element.279), channel_id=1, source_target_pairs={{0,8},{8,0},{16,24},{24,16},{1,9},{9,1},{17,25},{25,17},{2,10},{10... | collective-permute-start | bytes 2359304 | tf_op jit(solution)/shard_map/ppermute | solution.py:51
  43.2 35.6 %collective-permute-start.4 = (bf16[192,2048]{1,0:T(8,128)(2,1)}, bf16[192,2048]{1,0:T(8,128)(2,1)S(1)}, u32[]{:S(2)}, u32[]{:S(2)}) collective-permute-start(bf16[192,2048]{1,0:T(8,128)(2,1)} %get-tuple-element.279), channel_id=1, source_target_pairs={{0,16},{8,24},{16,0},{24,8},{1,17},{9,25},{17,1},{25,9},{2,18},{10... | collective-permute-start | bytes 2359304 | tf_op jit(solution)/shard_map/ppermute | solution.py:55
  60.4 33.8 %collective-permute-start.2 = (bf16[192,2048]{1,0:T(8,128)(2,1)S(1)}, bf16[192,2048]{1,0:T(8,128)(2,1)S(1)}, u32[]{:S(2)}, u32[]{:S(2)}) collective-permute-start(bf16[192,2048]{1,0:T(8,128)(2,1)S(1)} %collective-permute-done), channel_id=1, source_target_pairs={{0,16},{8,24},{16,0},{24,8},{1,17},{9,25},{17,1},{25,9},{2,18},{10... | collective-permute-start | bytes 2359304 | tf_op jit(solution)/shard_map/ppermute | solution.py:55
  78.8 16.9 %collective-permute-start.5 = (bf16[192,2048]{1,0:T(8,128)(2,1)S(1)}, bf16[192,2048]{1,0:T(8,128)(2,1)S(1)}, u32[]{:S(2)}, u32[]{:S(2)}) collective-permute-start(bf16[192,2048]{1,0:T(8,128)(2,1)S(1)} %collective-permute-done.4), channel_id=1, source_target_pairs={{0,8},{8,0},{16,24},{24,16},{1,9},{9,1},{17,25},{25,17},{2,10},{10... | collective-permute-start | bytes 2359304 | tf_op jit(solution)/shard_map/ppermute | solution.py:51
  95.7 34.2 %collective-permute-start.9 = (bf16[768,1024]{1,0:T(8,128)(2,1)}, bf16[768,1024]{1,0:T(8,128)(2,1)}, u32[]{:S(2)}, u32[]{:S(2)}) collective-permute-start(bf16[768,1024]{1,0:T(8,128)(2,1)} %get-tuple-element.94.refs_0_), channel_id=1, source_target_pairs={{0,8},{8,0},{16,24},{24,16},{1,9},{9,1},{17,25},{25,17},{2,10},{10... | collective-permute-start | bytes 4718600 | tf_op jit(solution)/shard_map/ppermute | solution.py:51
  96.0 33.9 %collective-permute-start.10 = (bf16[768,1024]{1,0:T(8,128)(2,1)}, bf16[768,1024]{1,0:T(8,128)(2,1)S(1)}, u32[]{:S(2)}, u32[]{:S(2)}) collective-permute-start(bf16[768,1024]{1,0:T(8,128)(2,1)} %get-tuple-element.93.refs_0_.refs_4_), channel_id=1, source_target_pairs={{0,16},{8,24},{16,0},{24,8},{1,17},{9,25},{17,1},{25,9},{2,18},{10... | collective-permute-start | bytes 4718600 | tf_op jit(solution)/shard_map/ppermute | solution.py:55
  141.4 34.8 %collective-permute-start.13 = (bf16[768,1024]{1,0:T(8,128)(2,1)}, bf16[768,1024]{1,0:T(8,128)(2,1)}, u32[]{:S(2)}, u32[]{:S(2)}) collective-permute-start(bf16[768,1024]{1,0:T(8,128)(2,1)} %get-tuple-element.93.refs_0_.refs_4_), channel_id=1, source_target_pairs={{0,8},{8,0},{16,24},{24,16},{1,9},{9,1},{17,25},{25,17},{2,10},{10... | collective-permute-start | bytes 4718600 | tf_op jit(solution)/shard_map/ppermute | solution.py:51
  142.3 33.9 %collective-permute-start.14 = (bf16[768,1024]{1,0:T(8,128)(2,1)}, bf16[768,1024]{1,0:T(8,128)(2,1)}, u32[]{:S(2)}, u32[]{:S(2)}) collective-permute-start(bf16[768,1024]{1,0:T(8,128)(2,1)} %get-tuple-element.94.refs_0_), channel_id=1, source_target_pairs={{0,16},{8,24},{16,0},{24,8},{1,17},{9,25},{17,1},{25,9},{2,18},{10... | collective-permute-start | bytes 4718600 | tf_op jit(solution)/shard_map/ppermute | solution.py:55
  176.7 20.5 %collective-permute-start.16 = (bf16[192,2048]{1,0:T(8,128)(2,1)S(1)}, bf16[192,2048]{1,0:T(8,128)(2,1)S(1)}, u32[]{:S(2)}, u32[]{:S(2)}) collective-permute-start(bf16[192,2048]{1,0:T(8,128)(2,1)S(1)} %get-tuple-element.199), channel_id=1, source_target_pairs={{0,8},{8,0},{16,24},{24,16},{1,9},{9,1},{17,25},{25,17},{2,10},{10... | collective-permute-start | bytes 2359304 | tf_op jit(solution)/shard_map/ppermute | solution.py:51
  177.8 32.7 %collective-permute-start.15 = (bf16[192,2048]{1,0:T(8,128)(2,1)S(1)}, bf16[192,2048]{1,0:T(8,128)(2,1)S(1)}, u32[]{:S(2)}, u32[]{:S(2)}) collective-permute-start(bf16[192,2048]{1,0:T(8,128)(2,1)S(1)} %get-tuple-element.196), channel_id=1, source_target_pairs={{0,8},{8,0},{16,24},{24,16},{1,9},{9,1},{17,25},{25,17},{2,10},{10... | collective-permute-start | bytes 2359304 | tf_op jit(solution)/shard_map/ppermute | solution.py:51
  178.8 31.7 %collective-permute-start.19 = (bf16[192,2048]{1,0:T(8,128)(2,1)S(1)}, bf16[192,2048]{1,0:T(8,128)(2,1)S(1)}, u32[]{:S(2)}, u32[]{:S(2)}) collective-permute-start(bf16[192,2048]{1,0:T(8,128)(2,1)S(1)} %get-tuple-element.197), channel_id=1, source_target_pairs={{0,16},{8,24},{16,0},{24,8},{1,17},{9,25},{17,1},{25,9},{2,18},{10... | collective-permute-start | bytes 2359304 | tf_op jit(solution)/shard_map/ppermute | solution.py:55
  197.4 20.0 %collective-permute-start.17 = (bf16[192,2048]{1,0:T(8,128)(2,1)S(1)}, bf16[192,2048]{1,0:T(8,128)(2,1)S(1)}, u32[]{:S(2)}, u32[]{:S(2)}) collective-permute-start(bf16[192,2048]{1,0:T(8,128)(2,1)S(1)} %add_convert_fusion.6), channel_id=1, source_target_pairs={{0,16},{8,24},{16,0},{24,8},{1,17},{9,25},{17,1},{25,9},{2,18},{10... | collective-permute-start | bytes 2359304 | tf_op jit(solution)/shard_map/ppermute | solution.py:55
  198.4 28.5 %collective-permute-start.18 = (bf16[192,2048]{1,0:T(8,128)(2,1)S(1)}, bf16[192,2048]{1,0:T(8,128)(2,1)S(1)}, u32[]{:S(2)}, u32[]{:S(2)}) collective-permute-start(bf16[192,2048]{1,0:T(8,128)(2,1)S(1)} %get-tuple-element.198), channel_id=1, source_target_pairs={{0,16},{8,24},{16,0},{24,8},{1,17},{9,25},{17,1},{25,9},{2,18},{10... | collective-permute-start | bytes 2359304 | tf_op jit(solution)/shard_map/ppermute | solution.py:55
  218.1 17.2 %collective-permute-start.20 = (bf16[192,2048]{1,0:T(8,128)(2,1)S(1)}, bf16[192,2048]{1,0:T(8,128)(2,1)S(1)}, u32[]{:S(2)}, u32[]{:S(2)}) collective-permute-start(bf16[192,2048]{1,0:T(8,128)(2,1)S(1)} %get-tuple-element.195), channel_id=1, source_target_pairs={{0,8},{8,0},{16,24},{24,16},{1,9},{9,1},{17,25},{25,17},{2,10},{10... | collective-permute-start | bytes 2359304 | tf_op jit(solution)/shard_map/ppermute | solution.py:51
  240.2 22.7 %collective-permute-start.21 = (bf16[768,1024]{1,0:T(8,128)(2,1)}, bf16[768,1024]{1,0:T(8,128)(2,1)}, u32[]{:S(2)}, u32[]{:S(2)}) collective-permute-start(bf16[768,1024]{1,0:T(8,128)(2,1)} %collective-permute-done.9.refs_1_), channel_id=1, source_target_pairs={{0,16},{8,24},{16,0},{24,8},{1,17},{9,25},{17,1},{25,9},{2,18},{10... | collective-permute-start | bytes 4718600 | tf_op jit(solution)/shard_map/ppermute | solution.py:55
  240.3 28.2 %collective-permute-start.22 = (bf16[768,1024]{1,0:T(8,128)(2,1)}, bf16[768,1024]{1,0:T(8,128)(2,1)}, u32[]{:S(2)}, u32[]{:S(2)}) collective-permute-start(bf16[768,1024]{1,0:T(8,128)(2,1)} %copy-done.15), channel_id=1, source_target_pairs={{0,8},{8,0},{16,24},{24,16},{1,9},{9,1},{17,25},{25,17},{2,10},{10... | collective-permute-start | bytes 4718600 | tf_op jit(solution)/shard_map/ppermute | solution.py:51
  242.2 12.0 %all-to-all-start = ((s32[8,384,8]{1,2,0:T(8,128)}), s32[8,384,8]{1,2,0:T(8,128)S(1)}, u32[]{:S(2)}, u32[]{:S(2)}) async-start(s32[8,384,8]{1,2,0:T(8,128)} %broadcast_in_dim.55), calls=%async_computation | async-start | bytes 196608 | tf_op jit(solution)/shard_map/all_to_all | solution.py:753
  247.3 437.0 %reduce-scatter.7.cloned.1.call-start = ((), (), s32[]{:S(2)}) async-start(), calls=%async_computation.12 | async-start | bytes 14155776 | tf_op jit(solution)/shard_map/reduce_scatter | solution.py:889
  269.9 37.6 %collective-permute-start.24 = (bf16[768,1024]{1,0:T(8,128)(2,1)}, bf16[768,1024]{1,0:T(8,128)(2,1)}, u32[]{:S(2)}, u32[]{:S(2)}) collective-permute-start(bf16[768,1024]{1,0:T(8,128)(2,1)} %pad_maximum_fusion.9.refs_0_.refs_4_), channel_id=1, source_target_pairs={{0,16},{8,24},{16,0},{24,8},{1,17},{9,25},{17,1},{25,9},{2,18},{10... | collective-permute-start | bytes 4718600 | tf_op jit(solution)/shard_map/ppermute | solution.py:55
  269.9 168.5 %collective-permute-start.25 = (bf16[768,1024]{1,0:T(8,128)(2,1)}, bf16[768,1024]{1,0:T(8,128)(2,1)}, u32[]{:S(2)}, u32[]{:S(2)}) collective-permute-start(bf16[768,1024]{1,0:T(8,128)(2,1)} %pad_maximum_fusion.9.refs_0_.refs_4_), channel_id=1, source_target_pairs={{0,8},{8,0},{16,24},{24,16},{1,9},{9,1},{17,25},{25,17},{2,10},{10... | collective-permute-start | bytes 4718600 | tf_op jit(solution)/shard_map/ppermute | solution.py:51
  271.1 70.1 %collective-permute-start.23 = (bf16[768,1024]{1,0:T(8,128)(2,1)}, bf16[768,1024]{1,0:T(8,128)(2,1)}, u32[]{:S(2)}, u32[]{:S(2)}) collective-permute-start(bf16[768,1024]{1,0:T(8,128)(2,1)} %pad_maximum_fusion.8.refs_0_), channel_id=1, source_target_pairs={{0,8},{8,0},{16,24},{24,16},{1,9},{9,1},{17,25},{25,17},{2,10},{10... | collective-permute-start | bytes 4718600 | tf_op jit(solution)/shard_map/ppermute | solution.py:51
  271.9 199.5 %collective-permute-start.27 = (bf16[768,1024]{1,0:T(8,128)(2,1)}, bf16[768,1024]{1,0:T(8,128)(2,1)}, u32[]{:S(2)}, u32[]{:S(2)}) collective-permute-start(bf16[768,1024]{1,0:T(8,128)(2,1)} %pad_maximum_fusion.8.refs_0_), channel_id=1, source_target_pairs={{0,16},{8,24},{16,0},{24,8},{1,17},{9,25},{17,1},{25,9},{2,18},{10... | collective-permute-start | bytes 4718600 | tf_op jit(solution)/shard_map/ppermute | solution.py:55
  307.6 130.8 %collective-permute-start.26 = (bf16[768,1024]{1,0:T(8,128)(2,1)}, bf16[768,1024]{1,0:T(8,128)(2,1)}, u32[]{:S(2)}, u32[]{:S(2)}) collective-permute-start(bf16[768,1024]{1,0:T(8,128)(2,1)} %collective-permute-done.24.refs_2_.refs_6_), channel_id=1, source_target_pairs={{0,8},{8,0},{16,24},{24,16},{1,9},{9,1},{17,25},{25,17},{2,10},{10... | collective-permute-start | bytes 4718600 | tf_op jit(solution)/shard_map/ppermute | solution.py:51
  341.3 130.2 %collective-permute-start.28 = (bf16[768,1024]{1,0:T(8,128)(2,1)}, bf16[768,1024]{1,0:T(8,128)(2,1)}, u32[]{:S(2)}, u32[]{:S(2)}) collective-permute-start(bf16[768,1024]{1,0:T(8,128)(2,1)} %collective-permute-done.23.refs_1_), channel_id=1, source_target_pairs={{0,16},{8,24},{16,0},{24,8},{1,17},{9,25},{17,1},{25,9},{2,18},{10... | collective-permute-start | bytes 4718600 | tf_op jit(solution)/shard_map/ppermute | solution.py:55
  561.3 45.8 %all-to-all-start.1 = ((f32[8,384,2]{1,2,0:T(2,128)}), f32[8,384,2]{1,2,0:T(2,128)S(1)}, u32[]{:S(2)}, u32[]{:S(2)}) async-start(f32[8,384,2]{1,2,0:T(2,128)} %copy.291), calls=%async_computation.1 | async-start | bytes 49152 | tf_op jit(solution)/shard_map/all_to_all | solution.py:890
  564.6 356.5 %reduce-scatter.5.cloned.1.call-start = ((), (), s32[]{:S(2)}) async-start(), calls=%async_computation.11 | async-start | bytes 14155776 | tf_op jit(solution)/shard_map/reduce_scatter | solution.py:926
  605.7 37.1 %collective-permute-start.29 = (bf16[768,1024]{1,0:T(8,128)(2,1)}, bf16[768,1024]{1,0:T(8,128)(2,1)}, u32[]{:S(2)}, u32[]{:S(2)}) collective-permute-start(bf16[768,1024]{1,0:T(8,128)(2,1)} %pad_maximum_fusion.10), channel_id=1, source_target_pairs={{0,8},{8,0},{16,24},{24,16},{1,9},{9,1},{17,25},{25,17},{2,10},{10... | collective-permute-start | bytes 4718600 | tf_op jit(solution)/shard_map/ppermute | solution.py:51
  607.0 37.1 %collective-permute-start.30 = (bf16[768,1024]{1,0:T(8,128)(2,1)}, bf16[768,1024]{1,0:T(8,128)(2,1)}, u32[]{:S(2)}, u32[]{:S(2)}) collective-permute-start(bf16[768,1024]{1,0:T(8,128)(2,1)} %pad_maximum_fusion.11), channel_id=1, source_target_pairs={{0,16},{8,24},{16,0},{24,8},{1,17},{9,25},{17,1},{25,9},{2,18},{10... | collective-permute-start | bytes 4718600 | tf_op jit(solution)/shard_map/ppermute | solution.py:55
  664.7 311.0 %reduce-scatter.11.cloned.1.call-start = ((), (), s32[]{:S(2)}) async-start(), calls=%async_computation.14 | async-start | bytes 2359296 | tf_op jit(solution)/shard_map/reduce_scatter | solution.py:992
  671.8 37.7 %collective-permute-start.31 = (bf16[768,1024]{1,0:T(8,128)(2,1)}, bf16[768,1024]{1,0:T(8,128)(2,1)}, u32[]{:S(2)}, u32[]{:S(2)}) collective-permute-start(bf16[768,1024]{1,0:T(8,128)(2,1)} %pad_maximum_fusion.12), channel_id=1, source_target_pairs={{0,8},{8,0},{16,24},{24,16},{1,9},{9,1},{17,25},{25,17},{2,10},{10... | collective-permute-start | bytes 4718600 | tf_op jit(solution)/shard_map/ppermute | solution.py:51
  673.7 37.6 %collective-permute-start.32 = (bf16[768,1024]{1,0:T(8,128)(2,1)}, bf16[768,1024]{1,0:T(8,128)(2,1)}, u32[]{:S(2)}, u32[]{:S(2)}) collective-permute-start(bf16[768,1024]{1,0:T(8,128)(2,1)} %pad_maximum_fusion.13), channel_id=1, source_target_pairs={{0,16},{8,24},{16,0},{24,8},{1,17},{9,25},{17,1},{25,9},{2,18},{10... | collective-permute-start | bytes 4718600 | tf_op jit(solution)/shard_map/ppermute | solution.py:55
  677.6 65.5 %collective-permute-start.33 = (bf16[768,1024]{1,0:T(8,128)(2,1)}, bf16[768,1024]{1,0:T(8,128)(2,1)}, u32[]{:S(2)}, u32[]{:S(2)}) collective-permute-start(bf16[768,1024]{1,0:T(8,128)(2,1)} %add_convert_fusion.3), channel_id=1, source_target_pairs={{0,16},{8,24},{16,0},{24,8},{1,17},{9,25},{17,1},{25,9},{2,18},{10... | collective-permute-start | bytes 4718600 | tf_op jit(solution)/shard_map/ppermute | solution.py:55
  682.9 60.3 %collective-permute-start.34 = (bf16[768,1024]{1,0:T(8,128)(2,1)}, bf16[768,1024]{1,0:T(8,128)(2,1)}, u32[]{:S(2)}, u32[]{:S(2)}) collective-permute-start(bf16[768,1024]{1,0:T(8,128)(2,1)} %add_convert_fusion.2), channel_id=1, source_target_pairs={{0,8},{8,0},{16,24},{24,16},{1,9},{9,1},{17,25},{25,17},{2,10},{10... | collective-permute-start | bytes 4718600 | tf_op jit(solution)/shard_map/ppermute | solution.py:51
  745.0 39.4 %collective-permute-start.35 = (bf16[192,2048]{1,0:T(8,128)(2,1)S(1)}, bf16[192,2048]{1,0:T(8,128)(2,1)S(1)}, u32[]{:S(2)}, u32[]{:S(2)}) collective-permute-start(bf16[192,2048]{1,0:T(8,128)(2,1)S(1)} %get-tuple-element.278), channel_id=1, source_target_pairs={{0,8},{8,0},{16,24},{24,16},{1,9},{9,1},{17,25},{25,17},{2,10},{10... | collective-permute-start | bytes 2359304 | tf_op jit(solution)/shard_map/ppermute | solution.py:51
  745.6 43.5 %collective-permute-start.36 = (bf16[192,2048]{1,0:T(8,128)(2,1)S(1)}, bf16[192,2048]{1,0:T(8,128)(2,1)S(1)}, u32[]{:S(2)}, u32[]{:S(2)}) collective-permute-start(bf16[192,2048]{1,0:T(8,128)(2,1)S(1)} %get-tuple-element.278), channel_id=1, source_target_pairs={{0,16},{8,24},{16,0},{24,8},{1,17},{9,25},{17,1},{25,9},{2,18},{10... | collective-permute-start | bytes 2359304 | tf_op jit(solution)/shard_map/ppermute | solution.py:55
  746.1 62.8 %collective-permute-start.38 = (bf16[192,2048]{1,0:T(8,128)(2,1)}, bf16[192,2048]{1,0:T(8,128)(2,1)S(1)}, u32[]{:S(2)}, u32[]{:S(2)}) collective-permute-start(bf16[192,2048]{1,0:T(8,128)(2,1)} %get-tuple-element.276), channel_id=1, source_target_pairs={{0,8},{8,0},{16,24},{24,16},{1,9},{9,1},{17,25},{25,17},{2,10},{10... | collective-permute-start | bytes 2359304 | tf_op jit(solution)/shard_map/ppermute | solution.py:51
  747.6 37.6 %collective-permute-start.39 = (bf16[192,2048]{1,0:T(8,128)(2,1)}, bf16[192,2048]{1,0:T(8,128)(2,1)S(1)}, u32[]{:S(2)}, u32[]{:S(2)}) collective-permute-start(bf16[192,2048]{1,0:T(8,128)(2,1)} %get-tuple-element.276), channel_id=1, source_target_pairs={{0,16},{8,24},{16,0},{24,8},{1,17},{9,25},{17,1},{25,9},{2,18},{10... | collective-permute-start | bytes 2359304 | tf_op jit(solution)/shard_map/ppermute | solution.py:55
  784.4 16.6 %collective-permute-start.37 = (bf16[192,2048]{1,0:T(8,128)(2,1)S(1)}, bf16[192,2048]{1,0:T(8,128)(2,1)S(1)}, u32[]{:S(2)}, u32[]{:S(2)}) collective-permute-start(bf16[192,2048]{1,0:T(8,128)(2,1)S(1)} %collective-permute-done.35), channel_id=1, source_target_pairs={{0,16},{8,24},{16,0},{24,8},{1,17},{9,25},{17,1},{25,9},{2,18},{10... | collective-permute-start | bytes 2359304 | tf_op jit(solution)/shard_map/ppermute | solution.py:55
  785.2 16.4 %collective-permute-start.40 = (bf16[192,2048]{1,0:T(8,128)(2,1)S(1)}, bf16[192,2048]{1,0:T(8,128)(2,1)S(1)}, u32[]{:S(2)}, u32[]{:S(2)}) collective-permute-start(bf16[192,2048]{1,0:T(8,128)(2,1)S(1)} %collective-permute-done.39), channel_id=1, source_target_pairs={{0,8},{8,0},{16,24},{24,16},{1,9},{9,1},{17,25},{25,17},{2,10},{10... | collective-permute-start | bytes 2359304 | tf_op jit(solution)/shard_map/ppermute | solution.py:51
  804.5 66.5 %collective-permute-start.41 = (bf16[2,768,1024]{2,1,0:T(8,128)(2,1)}, bf16[2,768,1024]{2,1,0:T(8,128)(2,1)}, u32[]{:S(2)}, u32[]{:S(2)}) collective-permute-start(bf16[2,768,1024]{2,1,0:T(8,128)(2,1)} %pad_maximum_fusion.4), channel_id=1, source_target_pairs={{0,8},{8,0},{16,24},{24,16},{1,9},{9,1},{17,25},{25,17},{2,10},{10... | collective-permute-start | bytes 9437192 | tf_op jit(solution)/shard_map/ppermute | solution.py:51
  807.4 66.5 %collective-permute-start.42 = (bf16[2,768,1024]{2,1,0:T(8,128)(2,1)}, bf16[2,768,1024]{2,1,0:T(8,128)(2,1)}, u32[]{:S(2)}, u32[]{:S(2)}) collective-permute-start(bf16[2,768,1024]{2,1,0:T(8,128)(2,1)} %pad_maximum_fusion.5), channel_id=1, source_target_pairs={{0,16},{8,24},{16,0},{24,8},{1,17},{9,25},{17,1},{25,9},{2,18},{10... | collective-permute-start | bytes 9437192 | tf_op jit(solution)/shard_map/ppermute | solution.py:55
  859.2 179.6 %reduce-scatter.9.cloned.1.call-start = ((), (), s32[]{:S(2)}) async-start(), calls=%async_computation.13 | async-start | bytes 7077888 | tf_op jit(solution)/shard_map/reduce_scatter | solution.py:995
  873.9 6.1 collective-permute-start.43
  896.3 45.7 %collective-permute-start.45 = (bf16[768,1024]{1,0:T(8,128)(2,1)}, bf16[768,1024]{1,0:T(8,128)(2,1)}, u32[]{:S(2)}, u32[]{:S(2)}) collective-permute-start(bf16[768,1024]{1,0:T(8,128)(2,1)} %add_convert_fusion.1), channel_id=1, source_target_pairs={{0,16},{8,24},{16,0},{24,8},{1,17},{9,25},{17,1},{25,9},{2,18},{10... | collective-permute-start | bytes 4718600 | tf_op jit(solution)/shard_map/ppermute | solution.py:55
  899.3 42.7 %collective-permute-start.46 = (bf16[768,1024]{1,0:T(8,128)(2,1)}, bf16[768,1024]{1,0:T(8,128)(2,1)}, u32[]{:S(2)}, u32[]{:S(2)}) collective-permute-start(bf16[768,1024]{1,0:T(8,128)(2,1)} %add_convert_fusion), channel_id=1, source_target_pairs={{0,8},{8,0},{16,24},{24,16},{1,9},{9,1},{17,25},{25,17},{2,10},{10... | collective-permute-start | bytes 4718600 | tf_op jit(solution)/shard_map/ppermute | solution.py:51
  942.6 30.5 %collective-permute-start.47 = (bf16[2,192,2048]{2,1,0:T(8,128)(2,1)S(1)}, bf16[2,192,2048]{2,1,0:T(8,128)(2,1)S(1)}, u32[]{:S(2)}, u32[]{:S(2)}) collective-permute-start(bf16[2,192,2048]{2,1,0:T(8,128)(2,1)S(1)} %pad_maximum_fusion.14), channel_id=1, source_target_pairs={{0,8},{8,0},{16,24},{24,16},{1,9},{9,1},{17,25},{25,17},{2,10},{10... | collective-permute-start | bytes 4718600 | tf_op jit(solution)/shard_map/ppermute | solution.py:51
  945.0 34.8 %collective-permute-start.49 = (bf16[2,192,2048]{2,1,0:T(8,128)(2,1)}, bf16[2,192,2048]{2,1,0:T(8,128)(2,1)}, u32[]{:S(2)}, u32[]{:S(2)}) collective-permute-start(bf16[2,192,2048]{2,1,0:T(8,128)(2,1)} %pad_maximum_fusion.15), channel_id=1, source_target_pairs={{0,16},{8,24},{16,0},{24,8},{1,17},{9,25},{17,1},{25,9},{2,18},{10... | collective-permute-start | bytes 4718600 | tf_op jit(solution)/shard_map/ppermute | solution.py:55
  974.4 17.7 %collective-permute-start.48 = (bf16[192,2048]{1,0:T(8,128)(2,1)}, bf16[192,2048]{1,0:T(8,128)(2,1)}, u32[]{:S(2)}, u32[]{:S(2)}) collective-permute-start(bf16[192,2048]{1,0:T(8,128)(2,1)} %fusion.20), channel_id=1, source_target_pairs={{0,16},{8,24},{16,0},{24,8},{1,17},{9,25},{17,1},{25,9},{2,18},{10... | collective-permute-start | bytes 2359304 | tf_op jit(solution)/shard_map/ppermute | solution.py:55
  996.8 38.7 %collective-permute-start.50 = (bf16[192,2048]{1,0:T(8,128)(2,1)}, bf16[192,2048]{1,0:T(8,128)(2,1)}, u32[]{:S(2)}, u32[]{:S(2)}) collective-permute-start(bf16[192,2048]{1,0:T(8,128)(2,1)} %get-tuple-element.189), channel_id=1, source_target_pairs={{0,8},{8,0},{16,24},{24,16},{1,9},{9,1},{17,25},{25,17},{2,10},{10... | collective-permute-start | bytes 2359304 | tf_op jit(solution)/shard_map/ppermute | solution.py:51
  999.2 25.5 %all-to-all-start.2 = ((f32[8,1,5120]{2,1,0:T(1,128)}), f32[8,1,5120]{2,1,0:T(1,128)S(1)}, u32[]{:S(2)}, u32[]{:S(2)}) async-start(f32[8,1,5120]{2,1,0:T(1,128)} %reshape.270), calls=%async_computation.6 | async-start | bytes 327680 | tf_op jit(solution)/shard_map/all_to_all | solution.py:135
  1026.7 7.6 collective-permute-start.54
  1027.1 7.2 collective-permute-start.55
  1040.3 10.1 collective-permute-start.51
  1040.7 10.4 collective-permute-start.52
  1042.1 9.0 collective-permute-start.53
  (104 other events, 1429.2 us)
Sparse Core Ops, SparseCore 0:
  32.1 69.4 all-gather.4
  103.2 27.7 all-gather.6
  132.6 116.2 all-gather.10
  250.4 114.9 all-gather.8
  558.8 125.4 reduce-scatter.6
  686.5 127.1 reduce-scatter.4
  859.3 35.0 reduce-scatter.10
  924.9 68.5 reduce-scatter.8

commit v7 on v6

--- a/solution.py
+++ b/solution.py
@@ -127,12 +127,13 @@
     return value + send_y(value)
 
 
-def sum_to_rows(values, me):
+def sum_to_rows(values, me, *others):
     ctx_size, exp_size = lax.axis_size("ctx"), lax.axis_size("exp")
     count, width = values.shape
     parts = values.reshape(count, ctx_size, exp_size, width // (ctx_size * exp_size))
     parts = jnp.transpose(parts, (2, 1, 0, 3))
-    parts = jnp.sum(lax.all_to_all(parts, "exp", split_axis=0, concat_axis=0, tiled=True), axis=0)
+    parts = lax.all_to_all(parts, "exp", split_axis=0, concat_axis=0, tiled=True)
+    parts = jnp.sum(after(parts, *others), axis=0)
     return jnp.sum(exchange(parts, me), axis=0)
 
 
@@ -178,8 +179,13 @@
 
 
 def scatter_joined(take, me):
-    low = send_x(jnp.stack([take(me ^ 1, 0), take(me ^ 3, 0)]).astype(BF))
-    high = send_y(jnp.stack([take(me ^ 2, 1), take(me ^ 3, 1)]).astype(BF))
+    low, high = joined_payload(take, me)
+    return send_x(low), send_y(high)
+
+
+def joined_payload(take, me):
+    low = jnp.stack([take(me ^ 1, 0), take(me ^ 3, 0)]).astype(BF)
+    high = jnp.stack([take(me ^ 2, 1), take(me ^ 3, 1)]).astype(BF)
     return low, high
 
 
@@ -243,13 +249,15 @@
         start = slot_table[2 * owner + part] * block
         return lax.dynamic_slice(partial, (start, 0), (block, partial.shape[1]))
 
+    first = ()
     if joined:
-        ahead, direct = split_sums(scatter_joined(take, me))
+        first = joined_payload(take, me)
+        ahead, direct = split_sums((send_x(first[0]), send_y(first[1])))
     else:
         ahead, direct = scatter_ahead(take, me), scatter_direct(take, me)
     sent = scatter_last_payload(take, me, ahead)
     last = send_y(sent[0]), send_x(sent[1])
-    return jnp.concatenate(scatter_end(take, me, direct, last), axis=0), ahead, sent, last
+    return jnp.concatenate(scatter_end(take, me, direct, last), axis=0), first, sent, last
 
 
 def prefix_count(member):
@@ -818,6 +826,7 @@
         for e in range(1, own_experts):
             low, high = after_all(packs[e], *passed)
             ahead = send_x(low), send_y(high)
+            low, high = after_all((low, high), *ahead)
             direct = send_x(high), send_y(low)
             passed = send_y(ahead[0]), send_x(ahead[1])
             lows.append((packs[e][0], ahead[0], direct[1], passed[0]))
@@ -903,24 +912,25 @@
         )
 
     expert_grads = [weight_grads(0, grad_two_part)]
+    if ctx_size == 4:
+        take = expert_take(expert_grads[0])
+        payload = joined_payload(take, me)
+    else:
+        payload = expert_grads[0]
     results = [
         jnp.dot(
-            after(made[e][1], share_back, *expert_grads[0]),
-            backs[e][2],
-            preferred_element_type=F32,
+            after(made[e][1], share_back, *payload), backs[e][2], preferred_element_type=F32
         ).astype(BF)
         for e in every
     ]
     if ctx_size == 4:
-        take = expert_take(expert_grads[0])
-        ahead = scatter_ahead(take, me)
-        results = after_all(results, *ahead)
-    mixture_part, unused = combine_rows(token_tables, results, shares)
-    if ctx_size == 4:
-        direct = scatter_direct(take, me, mixture_part)
-        last = scatter_last(take, me, after_all(ahead, mixture_part))
+        ahead, direct = split_sums((send_x(payload[0]), send_y(payload[1])))
+        last = scatter_last_payload(take, me, ahead)
+        results = after_all(results, *last)
+        last = send_y(last[0]), send_x(last[1])
     else:
         direct, last = scatter_expert_first(expert_grads[0], me), ()
+    mixture_part, unused = combine_rows(token_tables, results, shares)
     directs, lasts = [direct], [last]
 
     mixture = lax.psum_scatter(mixture_part, "exp", scatter_dimension=0, tiled=True)
@@ -956,7 +966,10 @@
     products = jnp.stack(
         [jnp.sum(scaled_query * normed_query, axis=1), jnp.sum(scaled_key * normed_key, axis=1)]
     )
-    products = after(products, out_grad, *(piece for pieces in sums for piece in pieces))
+    weight_sums = [scatter_expert_end(expert_grads[0], directs[0], lasts[0], me)]
+    products = after(
+        products, out_grad, *weight_sums[0], *(piece for pieces in sums for piece in pieces)
+    )
     means = sum_over_ctx(products) / D
     for e in range(1, own_experts):
         ahead, direct = split_sums(sums[e - 1])
@@ -976,18 +989,15 @@
     grad_one_part = lax.dot_general(grad_packed, packed, NT, preferred_element_type=F32)
     grad_attn_gain = jnp.sum(grad_one_part * normed_group, axis=0)
     qkv_grad = lax.dot_general(hidden_one, grad_projected, TN, preferred_element_type=F32).astype(BF)
-    grad_one, one_ahead, one_sent, unused = scatter_group(
+    grad_one, one_first, one_sent, unused = scatter_group(
         after(grad_one_part, *(piece for pieces in lasts[1:] for piece in pieces)),
         slot_table,
         me,
         joined=True,
     )
-    weight_sums = [
-        scatter_expert_end(
-            expert_grads[e], after_all(directs[e], *one_sent), after_all(lasts[e], *one_sent), me
-        )
-        for e in every
-    ]
+    for e in range(1, own_experts):
+        direct, last = after_all(directs[e], *one_sent), after_all(lasts[e], *one_sent)
+        weight_sums.append(scatter_expert_end(expert_grads[e], direct, last, me))
     gate_grad, up_grad, down_grad = (jnp.stack(parts) for parts in zip(*weight_sums))
     out_sum = lax.psum_scatter(
         out_grad, "exp", scatter_dimension=0, tiled=True
@@ -1012,7 +1022,7 @@
     small_sums = jnp.concatenate(
         [grad_router, jnp.stack([grad_ffn_gain, grad_attn_gain]), head_gains]
     )
-    small_sums = sum_to_rows(after(small_sums, *one_sent), me)
+    small_sums = sum_to_rows(after(small_sums, *one_first), me, *one_sent)
     return (
         output,
         grad_input,

time: 1070 us -> 1070 us (level)
  waiting for transfers between devices: 292 us -> 272 us
    ppermute x27 -> x26, waiting for transfers between devices: 128 us -> 104 us  [send_y(): return lax.ppermute(value, 'ctx', Y_PAIRS)]
    ppermute x27 -> x26, waiting for transfers between devices: 155 us -> 147 us  [send_x(): return lax.ppermute(value, 'ctx', X_PAIRS)]
    ppermute x27 -> x26, starting transfers between devices: 25 us -> 28.4 us  [send_x(): return lax.ppermute(value, 'ctx', X_PAIRS)]
    unnamed x207 -> x205, local copies, waits for them, and re-layouts: 20 us -> 22.8 us
    ppermute x27 -> x26, starting transfers between devices: 27.2 us -> 27.7 us  [send_y(): return lax.ppermute(value, 'ctx', Y_PAIRS)]
  transfers between devices with their start and end apart: 68 -> 66, of which waited for: 32 -> 30; matrix products, arithmetic and copies ran while one was open for 34% -> 35% of each run, Pallas kernels for 19% -> 19%
where the time goes in v7:
time: 1070 us; the launch traced here: 1060 us
  Pallas kernels  282 us (26%)
  waiting for transfers between devices  272 us (25%)
  matrix products  167 us (16%)
  other arithmetic  132 us (12%)
  local copies, waits for them, and re-layouts  108 us (10%)
  starting transfers between devices  75.3 us (7%)
  between operations  21.4 us (2%)
    ppermute x26, waiting for transfers between devices, send_x(): return lax.ppermute(value, 'ctx', X_PAIRS)  147 us
    pallas_call x2, Pallas kernels, expert_rows(): pl.pallas_call(functools.partial(expert_kernel, own), out_shape=[made(wid...  126 us
    ppermute x26, waiting for transfers between devices, send_y(): return lax.ppermute(value, 'ctx', Y_PAIRS)  104 us
    pallas_call x2, Pallas kernels, back_rows(): pl.pallas_call(back_rows_kernel, out_shape=[jax.ShapeDtypeStruct((capacit...  60 us
    dot_general x2, matrix products, weight_grads(): lax.dot_general(rows, grad_hidden, TN, preferred_element_type=F32)  45.1 us
    pallas_call x2, Pallas kernels, combine_rows(): pl.pallas_call(functools.partial(combine_kernel, experts), out_shape=[jax...  40.8 us
    pallas_call x1, Pallas kernels, attend_back(): pl.pallas_call(functools.partial(attend_back_kernel, tiles, 1.0 / math.sq...  30 us
    ppermute x26, starting transfers between devices, send_x(): return lax.ppermute(value, 'ctx', X_PAIRS)  28.4 us
  transfers between devices with their start and end apart: 66, of which 30 were waited for; matrix products, arithmetic and copies ran while one was open for 35% of the time, Pallas kernels for 19%

profile of v7, /device:TPU:0, one launch (start us, length us, event | category | flops | bytes accessed | tf_op | source)
XLA Modules:
  0.0 1058.2 jit_solution(17590713091141799203)
XLA Ops:
  16.5 4.0 collective-permute-start.6
  21.1 5.5 collective-permute-done.6
  26.6 3.7 collective-permute-done.7
  34.8 3.4 broadcast.176.clone
  54.7 5.7 collective-permute-done
  61.8 17.0 %collective-permute-done.4 = bf16[192,2048]{1,0:T(8,128)(2,1)S(1)} collective-permute-done((bf16[192,2048]{1,0:T(8,128)(2,1)}, bf16[192,2048]{1,0:T(8,128)(2,1)S(1)}, u32[]{:S(2)}, u32[]{:S(2)}) %collective-permute-start.4) | collective-permute-done | bytes 786464 | tf_op jit(solution)/shard_map/ppermute | solution.py:55
  84.5 9.8 collective-permute-done.2
  103.7 4.1 fusion.5
  110.1 16.1 %fusion.18.qp_ref.kp_ref.vp_ref = f32[1536,1664]{1,0:T(8,128)S(1)} fusion(bf16[2048,1664]{1,0:T(8,128)(2,1)} %bitcast.363, bf16[1536,2048]{1,0:T(8,128)(2,1)} %constant_dynamic-update-slice_fusion.9, f32[2048]{0:T(1024)S(1)} %get-tuple-element.165, f32[1536]{0:T(1024)S(1)} %add_rsqrt_fusion.1), kind=kOutput, calls=%fused_computation.75 | convolution fusion | flops 10481565696 | bytes 23345152 | tf_op jit(solution)/shard_map/dot_general | solution.py:790
  126.7 3.1 collective-permute-done.9.refs_1_
  143.7 25.7 %shard_map.272 = (bf16[1536,512]{1,0:T(8,128)(2,1)S(1)}, bf16[1536,512]{1,0:T(8,128)(2,1)}, bf16[1536,512]{1,0:T(8,128)(2,1)}, bf16[1536,512]{1,0:T(8,128)(2,1)}) custom-call(f32[1536,1664]{1,0:T(8,128)} %copy-done.16, f32[1536,1664]{1,0:T(8,128)} %copy-done.16, f32[1536,1664]{1,0:T(8,128)} %copy-done.16, f32[1536,2]{1,0:T(8,128)S(1)} %fusion.89.root_ref.key_root_ref, ...), custom_call_target="tpu_custom_call" | custom-call | flops 3221225472 | bytes 15728640 | tf_op jit(solution)/shard_map/pallas_call | solution.py:347
  170.6 5.6 fusion.106
  179.7 17.6 %collective-permute-done.16 = bf16[192,2048]{1,0:T(8,128)(2,1)S(1)} collective-permute-done((bf16[192,2048]{1,0:T(8,128)(2,1)S(1)}, bf16[192,2048]{1,0:T(8,128)(2,1)S(1)}, u32[]{:S(2)}, u32[]{:S(2)}) %collective-permute-start.16) | collective-permute-done | bytes 786464 | tf_op jit(solution)/shard_map/ppermute | solution.py:51
  199.5 11.0 %collective-permute-done.15 = bf16[192,2048]{1,0:T(8,128)(2,1)S(1)} collective-permute-done((bf16[192,2048]{1,0:T(8,128)(2,1)S(1)}, bf16[192,2048]{1,0:T(8,128)(2,1)S(1)}, u32[]{:S(2)}, u32[]{:S(2)}) %collective-permute-start.15) | collective-permute-done | bytes 786464 | tf_op jit(solution)/shard_map/ppermute | solution.py:51
  210.5 7.0 collective-permute-done.17
  218.6 8.2 collective-permute-done.18
  226.8 8.5 collective-permute-done.20
  242.1 5.2 all-to-all-start
  254.2 6.8 collective-permute-done.21.refs_3_
  261.0 3.0 collective-permute-done.22.refs_3_.refs_7_
  269.7 14.7 %select_reduce_fusion = s32[2,2048]{1,0:T(2,128)S(1)} fusion(s32[2,3072]{1,0:T(2,128)S(1)} %copy.283, pred[2,3072]{1,0:T(4,128)(4,1)S(1)} %bitcast.374), kind=kLoop, calls=%fused_computation | loop fusion | flops 50327552 | bytes 47104 | tf_op jit(solution)/shard_map/reduce_max | solution.py:853
  290.8 3.0 broadcast_select_fusion.pos_ref
  293.8 25.3 %collective-permute-done.23.refs_1_ = bf16[768,1024]{1,0:T(8,128)(2,1)} collective-permute-done((bf16[768,1024]{1,0:T(8,128)(2,1)}, bf16[768,1024]{1,0:T(8,128)(2,1)}, u32[]{:S(2)}, u32[]{:S(2)}) %collective-permute-start.23) | collective-permute-done | bytes 1572896 | tf_op jit(solution)/shard_map/ppermute | solution.py:51
  325.8 29.6 %shard_map.273 = (bf16[2048,2048]{1,0:T(8,128)(2,1)}, f32[2048,1024]{1,0:T(8,128)}, bf16[1024,2048]{1,0:T(8,128)(2,1)}) custom-call(s32[1]{0:T(128)} %get-tuple-element.309.tiles_ref, s32[8]{0:T(128)S(1)} %get-tuple-element.307.low_ref, s32[8]{0:T(128)S(1)} %get-tuple-element.305.windows_ref, s32[1]{0:T(128)} %bitcast.36.me_ref, s32[2048,1]{1,0:T(8,128)S(1)} %copy-done.4, ...), custom_call_target="tpu_custom_call" | custom-call | flops 11274289152 | bytes 37748736 | tf_op jit(solution)/shard_map/pallas_call | solution.py:524
  355.5 9.9 all-gather.9.cloned.1.call-done.h_ref
  365.4 62.8 %shard_map.274 = (bf16[2048,2048]{1,0:T(8,128)(2,1)}, bf16[2048,1024]{1,0:T(8,128)(2,1)}, bf16[2048,2048]{1,0:T(8,128)(2,1)}, bf16[2048,2048]{1,0:T(8,128)(2,1)}, f32[2048,1]{1,0:T(8,128)}) custom-call(s32[1]{0:T(128)} %get-tuple-element.309.tiles_ref, s32[8]{0:T(128)} %copy-done.9, s32[8]{0:T(128)} %copy-done.10, s32[2]{0:T(128)} %pad_add_fusion.ids_ref, ...), custom_call_target="tpu_custom_call" | custom-call | flops 30601641984 | bytes 58720256 | tf_op jit(solution)/shard_map/pallas_call | solution.py:624
  429.8 30.4 %shard_map.275 = (bf16[2048,2048]{1,0:T(8,128)(2,1)}, f32[2048,1024]{1,0:T(8,128)}, bf16[1024,2048]{1,0:T(8,128)(2,1)}) custom-call(s32[1]{0:T(128)} %get-tuple-element.308.tiles_ref, s32[8]{0:T(128)S(1)} %get-tuple-element.306.low_ref, s32[8]{0:T(128)S(1)} %get-tuple-element.304.windows_ref, s32[1]{0:T(128)} %bitcast.36.me_ref, ...), custom_call_target="tpu_custom_call" | custom-call | flops 11274289152 | bytes 37748736 | tf_op jit(solution)/shard_map/pallas_call | solution.py:524
  460.2 62.8 %shard_map.276 = (bf16[2048,2048]{1,0:T(8,128)(2,1)}, bf16[2048,1024]{1,0:T(8,128)(2,1)}, bf16[2048,2048]{1,0:T(8,128)(2,1)}, bf16[2048,2048]{1,0:T(8,128)(2,1)}, f32[2048,1]{1,0:T(8,128)}) custom-call(s32[1]{0:T(128)} %get-tuple-element.308.tiles_ref, s32[8]{0:T(128)} %copy-done.7, s32[8]{0:T(128)} %copy-done.8, s32[2]{0:T(128)} %pad_add_fusion.ids_ref, ...), custom_call_target="tpu_custom_call" | custom-call | flops 30601641984 | bytes 58720256 | tf_op jit(solution)/shard_map/pallas_call | solution.py:624
  526.0 20.3 %shard_map.277 = (bf16[3072,2048]{1,0:T(8,128)(2,1)}, f32[3072,2]{1,0:T(8,128)S(1)}) custom-call(s32[2,12]{1,0:T(2,128)S(1)} %copy.292.start_ref, s32[2,12]{1,0:T(2,128)S(1)} %copy.293.more_ref, s32[2,12]{1,0:T(2,128)S(1)} %copy.294.wide_ref, s32[3072,2]{1,0:T(8,128)S(1)} %copy-done, bf16[2048,2048]{1,0:T(8,128)(2,1)} %get-tuple-element.99.refs_0_, ...), custom_call_target="tpu_custom_call" | custom-call | flops 6442450944 | bytes 29360128 | tf_op jit(solution)/shard_map/pallas_call | solution.py:682
  550.0 3.3 all-to-all-start.1
  553.4 12.9 %convolution_convert_fusion.6 = bf16[1024,2048]{1,0:T(8,128)(2,1)S(1)} fusion(bf16[2048,1024]{1,0:T(8,128)(2,1)} %get-tuple-element.119, bf16[2048,2048]{1,0:T(8,128)(2,1)} %get-tuple-element.118), kind=kOutput, calls=%fused_computation.25 | convolution fusion | flops 8592031744 | bytes 16777216 | tf_op jit(solution)/shard_map/dot_general | solution.py:911
  567.8 22.5 %convolution_convert_fusion.4 = bf16[2048,2048]{1,0:T(8,128)(2,1)S(1)} fusion(bf16[2048,2048]{1,0:T(8,128)(2,1)} %get-tuple-element.115, bf16[2048,2048]{1,0:T(8,128)(2,1)} %get-tuple-element.116), kind=kOutput, calls=%fused_computation.14 | convolution fusion | flops 17184063488 | bytes 25165824 | tf_op jit(solution)/shard_map/dot_general | solution.py:910
  599.8 14.6 %convolution_convert_fusion.3.refs_0_ = bf16[2048,2048]{1,0:T(8,128)(2,1)} fusion(bf16[2048,1024]{1,0:T(8,128)(2,1)} %get-tuple-element.119, bf16[1024,2048]{1,0:T(8,128)(2,1)} %get-tuple-element.120), kind=kOutput, calls=%fused_computation.13 | convolution fusion | flops 8594128896 | bytes 16777216 | tf_op jit(solution)/shard_map/dot_general | solution.py:921
  614.5 10.9 %convolution_convert_fusion.2.refs_1_ = bf16[2048,2048]{1,0:T(8,128)(2,1)} fusion(bf16[2048,1024]{1,0:T(8,128)(2,1)S(1)} %copy-done.97, bf16[1024,2048]{1,0:T(8,128)(2,1)S(1)} %copy-done.98), kind=kOutput, calls=%fused_computation.12 | convolution fusion | flops 8594128896 | bytes 16777216 | tf_op jit(solution)/shard_map/dot_general | solution.py:921
  625.4 39.9 %collective-permute-done.29 = bf16[2,768,1024]{2,1,0:T(8,128)(2,1)} collective-permute-done((bf16[2,768,1024]{2,1,0:T(8,128)(2,1)}, bf16[2,768,1024]{2,1,0:T(8,128)(2,1)}, u32[]{:S(2)}, u32[]{:S(2)}) %collective-permute-start.29) | collective-permute-done | bytes 3145760 | tf_op jit(solution)/shard_map/ppermute | solution.py:51
  665.3 3.3 fusion.16
  668.6 3.4 fusion.15
  671.9 20.5 %shard_map.278 = (bf16[3072,2048]{1,0:T(8,128)(2,1)}, f32[3072,2]{1,0:T(8,128)}) custom-call(s32[2,12]{1,0:T(2,128)S(1)} %copy.292.start_ref, s32[2,12]{1,0:T(2,128)S(1)} %copy.293.more_ref, s32[2,12]{1,0:T(2,128)S(1)} %copy.294.wide_ref, s32[3072,2]{1,0:T(8,128)S(1)} %copy-done.1, bf16[2048,2048]{1,0:T(8,128)(2,1)} %convolution_convert_fusion.3.refs_0_, ...), custom_call_target="tpu_custom_call" | custom-call | flops 6442450944 | bytes 29360128 | tf_op jit(solution)/shard_map/pallas_call | solution.py:682
  702.0 4.5 multiply_reduce_fusion.2
  708.2 24.9 %collective-permute-done.31 = bf16[768,1024]{1,0:T(8,128)(2,1)} collective-permute-done((bf16[768,1024]{1,0:T(8,128)(2,1)}, bf16[768,1024]{1,0:T(8,128)(2,1)}, u32[]{:S(2)}, u32[]{:S(2)}) %collective-permute-start.31) | collective-permute-done | bytes 1572896 | tf_op jit(solution)/shard_map/ppermute | solution.py:55
  740.3 22.6 %convolution_convert_fusion.1 = bf16[2048,2048]{1,0:T(8,128)(2,1)S(1)} fusion(bf16[2048,2048]{1,0:T(8,128)(2,1)} %get-tuple-element.136, bf16[2048,2048]{1,0:T(8,128)(2,1)} %get-tuple-element.137), kind=kOutput, calls=%fused_computation.11 | convolution fusion | flops 17184063488 | bytes 25165824 | tf_op jit(solution)/shard_map/dot_general | solution.py:910
  762.9 12.8 %convolution_convert_fusion.5 = bf16[1024,2048]{1,0:T(8,128)(2,1)S(1)} fusion(bf16[2048,1024]{1,0:T(8,128)(2,1)} %get-tuple-element.138, bf16[2048,2048]{1,0:T(8,128)(2,1)} %get-tuple-element.139), kind=kOutput, calls=%fused_computation.24 | convolution fusion | flops 8592031744 | bytes 16777216 | tf_op jit(solution)/shard_map/dot_general | solution.py:911
  781.2 11.0 %collective-permute-done.35 = bf16[192,2048]{1,0:T(8,128)(2,1)S(1)} collective-permute-done((bf16[192,2048]{1,0:T(8,128)(2,1)S(1)}, bf16[192,2048]{1,0:T(8,128)(2,1)S(1)}, u32[]{:S(2)}, u32[]{:S(2)}) %collective-permute-start.35) | collective-permute-done | bytes 786464 | tf_op jit(solution)/shard_map/ppermute | solution.py:55
  802.3 5.0 convolution_convert_fusion.8.d_ref
  807.3 30.0 %shard_map.279 = (f32[1536,512]{1,0:T(8,128)}, f32[1536,512]{1,0:T(8,128)}, f32[1536,512]{1,0:T(8,128)}) custom-call(bf16[1536,512]{1,0:T(8,128)(2,1)S(1)} %copy-done.12, bf16[1536,512]{1,0:T(8,128)(2,1)S(1)} %copy-done.13, bf16[1536,512]{1,0:T(8,128)(2,1)} %get-tuple-element.130.v_ref, bf16[1536,512]{1,0:T(8,128)(2,1)} %convolution_convert_fusion.8.d_ref, ...), custom_call_target="tpu_custom_call" | custom-call | flops 8053063680 | bytes 15728640 | tf_op jit(solution)/shard_map/pallas_call | solution.py:436
  837.3 3.4 convert.34
  840.7 5.3 multiply_reduce_fusion.1
  846.7 4.6 convolution_convert_fusion.7
  853.1 8.8 collective-permute-done.39
  861.8 3.7 collective-permute-done.40
  865.8 3.9 slice_bitcast_fusion.3
  879.0 3.9 slice_bitcast_fusion.2
  887.2 3.8 multiply_convert_fusion.1
  892.7 14.3 %convolution_convert_fusion = bf16[2048,1536]{1,0:T(8,128)(2,1)} fusion(bf16[1536,2048]{1,0:T(8,128)(2,1)} %constant_dynamic-update-slice_fusion.9, f32[2048]{0:T(1024)S(1)} %copy-done.73, f32[1536]{0:T(1024)S(1)} %copy-done.91, bf16[1536,512]{1,0:T(8,128)(2,1)S(1)} %copy-done.37, bf16[1536,512]{1,0:T(8,128)(2,1)S(1)} %get-tuple-element.191, ...), kind=kOutput, calls=%fused_computation.10 | convolution fusion | flops 9693560832 | bytes 17315840 | tf_op jit(solution)/shard_map/dot_general | solution.py:991
  918.6 16.6 %fusion.4 = (f32[2048]{0:T(1024)S(1)}, f32[1536,2048]{1,0:T(8,128)S(1)}) fusion(bf16[1536,2048]{1,0:T(8,128)(2,1)} %constant_dynamic-update-slice_fusion.9, f32[1536]{0:T(1024)S(1)} %copy-done.92, bf16[2048,1664]{1,0:T(8,128)(2,1)} %bitcast.367, bf16[1536,1536]{1,0:T(8,128)(2,1)} %pad_maximum_fusion), kind=kOutput, calls=%fused_computation.8 | convolution fusion | flops 10481563648 | bytes 30423040 | tf_op jit(solution)/shard_map/dot_general | solution.py:989
  935.2 7.2 collective-permute-done.43
  942.5 6.0 collective-permute-done.44
  963.7 15.2 %collective-permute-done.45 = bf16[2,192,2048]{2,1,0:T(8,128)(2,1)S(1)} collective-permute-done((bf16[2,192,2048]{2,1,0:T(8,128)(2,1)S(1)}, bf16[2,192,2048]{2,1,0:T(8,128)(2,1)S(1)}, u32[]{:S(2)}, u32[]{:S(2)}) %collective-permute-start.45) | collective-permute-done | bytes 1572896 | tf_op jit(solution)/shard_map/ppermute | solution.py:51
  987.9 4.8 all-to-all-start.2
  996.1 3.9 all-to-all-done.2
  1001.8 3.4 collective-permute-done.46
  1005.1 4.7 fusion.23
  1014.8 3.0 convert_add_fusion.4
  1040.8 6.5 fusion.13
  (510 shorter events, 242.0 us)
Async XLA Ops:
  7.2 100.7 %all-gather.5.cloned.1.call-start = ((), (), s32[]{:S(2)}) async-start(), calls=%async_computation.7 | async-start | bytes 7667712 | tf_op jit(solution)/shard_map/all_gather | solution.py:753
  16.5 10.1 collective-permute-start.6
  20.4 9.8 collective-permute-start.7
  20.9 9.6 collective-permute-start.8
  31.9 138.6 %all-gather.7.cloned.1.call-start = ((), (), s32[]{:S(2)}) async-start(), calls=%async_computation.8 | async-start | bytes 2359296 | tf_op jit(solution)/shard_map/all_gather | solution.py:760
  32.7 290.5 %all-gather.11.cloned.1.call-start = ((), (), s32[]{:S(2)}) async-start(), calls=%async_computation.10 | async-start | bytes 14155776 | tf_op jit(solution)/shard_map/all_gather | solution.py:768
  33.4 332.0 %all-gather.9.cloned.1.call-start = ((), (), s32[]{:S(2)}) async-start(), calls=%async_computation.9 | async-start | bytes 14155776 | tf_op jit(solution)/shard_map/all_gather | solution.py:881
  39.8 20.7 %collective-permute-start = (bf16[192,2048]{1,0:T(8,128)(2,1)}, bf16[192,2048]{1,0:T(8,128)(2,1)S(1)}, u32[]{:S(2)}, u32[]{:S(2)}) collective-permute-start(bf16[192,2048]{1,0:T(8,128)(2,1)} %get-tuple-element.271), channel_id=1, source_target_pairs={{0,8},{8,0},{16,24},{24,16},{1,9},{9,1},{17,25},{25,17},{2,10},{10... | collective-permute-start | bytes 2359304 | tf_op jit(solution)/shard_map/ppermute | solution.py:51
  41.3 41.0 %collective-permute-start.1 = (bf16[192,2048]{1,0:T(8,128)(2,1)}, bf16[192,2048]{1,0:T(8,128)(2,1)}, u32[]{:S(2)}, u32[]{:S(2)}) collective-permute-start(bf16[192,2048]{1,0:T(8,128)(2,1)} %get-tuple-element.271), channel_id=1, source_target_pairs={{0,16},{8,24},{16,0},{24,8},{1,17},{9,25},{17,1},{25,9},{2,18},{10... | collective-permute-start | bytes 2359304 | tf_op jit(solution)/shard_map/ppermute | solution.py:55
  41.9 57.9 %collective-permute-start.3 = (bf16[192,2048]{1,0:T(8,128)(2,1)}, bf16[192,2048]{1,0:T(8,128)(2,1)}, u32[]{:S(2)}, u32[]{:S(2)}) collective-permute-start(bf16[192,2048]{1,0:T(8,128)(2,1)} %get-tuple-element.269), channel_id=1, source_target_pairs={{0,8},{8,0},{16,24},{24,16},{1,9},{9,1},{17,25},{25,17},{2,10},{10... | collective-permute-start | bytes 2359304 | tf_op jit(solution)/shard_map/ppermute | solution.py:51
  43.2 35.6 %collective-permute-start.4 = (bf16[192,2048]{1,0:T(8,128)(2,1)}, bf16[192,2048]{1,0:T(8,128)(2,1)S(1)}, u32[]{:S(2)}, u32[]{:S(2)}) collective-permute-start(bf16[192,2048]{1,0:T(8,128)(2,1)} %get-tuple-element.269), channel_id=1, source_target_pairs={{0,16},{8,24},{16,0},{24,8},{1,17},{9,25},{17,1},{25,9},{2,18},{10... | collective-permute-start | bytes 2359304 | tf_op jit(solution)/shard_map/ppermute | solution.py:55
  60.4 33.8 %collective-permute-start.2 = (bf16[192,2048]{1,0:T(8,128)(2,1)S(1)}, bf16[192,2048]{1,0:T(8,128)(2,1)S(1)}, u32[]{:S(2)}, u32[]{:S(2)}) collective-permute-start(bf16[192,2048]{1,0:T(8,128)(2,1)S(1)} %collective-permute-done), channel_id=1, source_target_pairs={{0,16},{8,24},{16,0},{24,8},{1,17},{9,25},{17,1},{25,9},{2,18},{10... | collective-permute-start | bytes 2359304 | tf_op jit(solution)/shard_map/ppermute | solution.py:55
  78.8 16.9 %collective-permute-start.5 = (bf16[192,2048]{1,0:T(8,128)(2,1)S(1)}, bf16[192,2048]{1,0:T(8,128)(2,1)S(1)}, u32[]{:S(2)}, u32[]{:S(2)}) collective-permute-start(bf16[192,2048]{1,0:T(8,128)(2,1)S(1)} %collective-permute-done.4), channel_id=1, source_target_pairs={{0,8},{8,0},{16,24},{24,16},{1,9},{9,1},{17,25},{25,17},{2,10},{10... | collective-permute-start | bytes 2359304 | tf_op jit(solution)/shard_map/ppermute | solution.py:51
  95.7 34.2 %collective-permute-start.9 = (bf16[768,1024]{1,0:T(8,128)(2,1)}, bf16[768,1024]{1,0:T(8,128)(2,1)}, u32[]{:S(2)}, u32[]{:S(2)}) collective-permute-start(bf16[768,1024]{1,0:T(8,128)(2,1)} %get-tuple-element.89.refs_0_), channel_id=1, source_target_pairs={{0,8},{8,0},{16,24},{24,16},{1,9},{9,1},{17,25},{25,17},{2,10},{10... | collective-permute-start | bytes 4718600 | tf_op jit(solution)/shard_map/ppermute | solution.py:51
  96.0 33.9 %collective-permute-start.10 = (bf16[768,1024]{1,0:T(8,128)(2,1)}, bf16[768,1024]{1,0:T(8,128)(2,1)S(1)}, u32[]{:S(2)}, u32[]{:S(2)}) collective-permute-start(bf16[768,1024]{1,0:T(8,128)(2,1)} %get-tuple-element.88.refs_0_.refs_4_), channel_id=1, source_target_pairs={{0,16},{8,24},{16,0},{24,8},{1,17},{9,25},{17,1},{25,9},{2,18},{10... | collective-permute-start | bytes 4718600 | tf_op jit(solution)/shard_map/ppermute | solution.py:55
  141.4 34.8 %collective-permute-start.13 = (bf16[768,1024]{1,0:T(8,128)(2,1)}, bf16[768,1024]{1,0:T(8,128)(2,1)}, u32[]{:S(2)}, u32[]{:S(2)}) collective-permute-start(bf16[768,1024]{1,0:T(8,128)(2,1)} %get-tuple-element.88.refs_0_.refs_4_), channel_id=1, source_target_pairs={{0,8},{8,0},{16,24},{24,16},{1,9},{9,1},{17,25},{25,17},{2,10},{10... | collective-permute-start | bytes 4718600 | tf_op jit(solution)/shard_map/ppermute | solution.py:51
  142.2 34.0 %collective-permute-start.14 = (bf16[768,1024]{1,0:T(8,128)(2,1)}, bf16[768,1024]{1,0:T(8,128)(2,1)}, u32[]{:S(2)}, u32[]{:S(2)}) collective-permute-start(bf16[768,1024]{1,0:T(8,128)(2,1)} %get-tuple-element.89.refs_0_), channel_id=1, source_target_pairs={{0,16},{8,24},{16,0},{24,8},{1,17},{9,25},{17,1},{25,9},{2,18},{10... | collective-permute-start | bytes 4718600 | tf_op jit(solution)/shard_map/ppermute | solution.py:55
  176.7 20.5 %collective-permute-start.16 = (bf16[192,2048]{1,0:T(8,128)(2,1)S(1)}, bf16[192,2048]{1,0:T(8,128)(2,1)S(1)}, u32[]{:S(2)}, u32[]{:S(2)}) collective-permute-start(bf16[192,2048]{1,0:T(8,128)(2,1)S(1)} %get-tuple-element.189), channel_id=1, source_target_pairs={{0,8},{8,0},{16,24},{24,16},{1,9},{9,1},{17,25},{25,17},{2,10},{10... | collective-permute-start | bytes 2359304 | tf_op jit(solution)/shard_map/ppermute | solution.py:51
  177.8 32.7 %collective-permute-start.15 = (bf16[192,2048]{1,0:T(8,128)(2,1)S(1)}, bf16[192,2048]{1,0:T(8,128)(2,1)S(1)}, u32[]{:S(2)}, u32[]{:S(2)}) collective-permute-start(bf16[192,2048]{1,0:T(8,128)(2,1)S(1)} %get-tuple-element.186), channel_id=1, source_target_pairs={{0,8},{8,0},{16,24},{24,16},{1,9},{9,1},{17,25},{25,17},{2,10},{10... | collective-permute-start | bytes 2359304 | tf_op jit(solution)/shard_map/ppermute | solution.py:51
  178.8 31.7 %collective-permute-start.19 = (bf16[192,2048]{1,0:T(8,128)(2,1)S(1)}, bf16[192,2048]{1,0:T(8,128)(2,1)S(1)}, u32[]{:S(2)}, u32[]{:S(2)}) collective-permute-start(bf16[192,2048]{1,0:T(8,128)(2,1)S(1)} %get-tuple-element.187), channel_id=1, source_target_pairs={{0,16},{8,24},{16,0},{24,8},{1,17},{9,25},{17,1},{25,9},{2,18},{10... | collective-permute-start | bytes 2359304 | tf_op jit(solution)/shard_map/ppermute | solution.py:55
  197.4 20.1 %collective-permute-start.17 = (bf16[192,2048]{1,0:T(8,128)(2,1)S(1)}, bf16[192,2048]{1,0:T(8,128)(2,1)S(1)}, u32[]{:S(2)}, u32[]{:S(2)}) collective-permute-start(bf16[192,2048]{1,0:T(8,128)(2,1)S(1)} %add_convert_fusion.4), channel_id=1, source_target_pairs={{0,16},{8,24},{16,0},{24,8},{1,17},{9,25},{17,1},{25,9},{2,18},{10... | collective-permute-start | bytes 2359304 | tf_op jit(solution)/shard_map/ppermute | solution.py:55
  198.4 28.4 %collective-permute-start.18 = (bf16[192,2048]{1,0:T(8,128)(2,1)S(1)}, bf16[192,2048]{1,0:T(8,128)(2,1)S(1)}, u32[]{:S(2)}, u32[]{:S(2)}) collective-permute-start(bf16[192,2048]{1,0:T(8,128)(2,1)S(1)} %get-tuple-element.188), channel_id=1, source_target_pairs={{0,16},{8,24},{16,0},{24,8},{1,17},{9,25},{17,1},{25,9},{2,18},{10... | collective-permute-start | bytes 2359304 | tf_op jit(solution)/shard_map/ppermute | solution.py:55
  218.1 17.1 %collective-permute-start.20 = (bf16[192,2048]{1,0:T(8,128)(2,1)S(1)}, bf16[192,2048]{1,0:T(8,128)(2,1)S(1)}, u32[]{:S(2)}, u32[]{:S(2)}) collective-permute-start(bf16[192,2048]{1,0:T(8,128)(2,1)S(1)} %get-tuple-element.185), channel_id=1, source_target_pairs={{0,8},{8,0},{16,24},{24,16},{1,9},{9,1},{17,25},{25,17},{2,10},{10... | collective-permute-start | bytes 2359304 | tf_op jit(solution)/shard_map/ppermute | solution.py:51
  240.2 20.8 %collective-permute-start.21 = (bf16[768,1024]{1,0:T(8,128)(2,1)}, bf16[768,1024]{1,0:T(8,128)(2,1)}, u32[]{:S(2)}, u32[]{:S(2)}) collective-permute-start(bf16[768,1024]{1,0:T(8,128)(2,1)} %collective-permute-done.9.refs_1_), channel_id=1, source_target_pairs={{0,16},{8,24},{16,0},{24,8},{1,17},{9,25},{17,1},{25,9},{2,18},{10... | collective-permute-start | bytes 4718600 | tf_op jit(solution)/shard_map/ppermute | solution.py:55
  240.3 23.8 %collective-permute-start.22 = (bf16[768,1024]{1,0:T(8,128)(2,1)}, bf16[768,1024]{1,0:T(8,128)(2,1)}, u32[]{:S(2)}, u32[]{:S(2)}) collective-permute-start(bf16[768,1024]{1,0:T(8,128)(2,1)} %copy-done.14), channel_id=1, source_target_pairs={{0,8},{8,0},{16,24},{24,16},{1,9},{9,1},{17,25},{25,17},{2,10},{10... | collective-permute-start | bytes 4718600 | tf_op jit(solution)/shard_map/ppermute | solution.py:51
  242.1 12.0 %all-to-all-start = ((s32[8,384,8]{1,2,0:T(8,128)}), s32[8,384,8]{1,2,0:T(8,128)S(1)}, u32[]{:S(2)}, u32[]{:S(2)}) async-start(s32[8,384,8]{1,2,0:T(8,128)} %broadcast_in_dim.55), calls=%async_computation | async-start | bytes 196608 | tf_op jit(solution)/shard_map/all_to_all | solution.py:761
  247.3 454.7 %reduce-scatter.7.cloned.1.call-start = ((), (), s32[]{:S(2)}) async-start(), calls=%async_computation.12 | async-start | bytes 14155776 | tf_op jit(solution)/shard_map/reduce_scatter | solution.py:898
  284.5 34.6 %collective-permute-start.23 = (bf16[768,1024]{1,0:T(8,128)(2,1)}, bf16[768,1024]{1,0:T(8,128)(2,1)}, u32[]{:S(2)}, u32[]{:S(2)}) collective-permute-start(bf16[768,1024]{1,0:T(8,128)(2,1)} %pad_maximum_fusion.10.refs_0_), channel_id=1, source_target_pairs={{0,8},{8,0},{16,24},{24,16},{1,9},{9,1},{17,25},{25,17},{2,10},{10... | collective-permute-start | bytes 4718600 | tf_op jit(solution)/shard_map/ppermute | solution.py:51
  285.0 34.1 %collective-permute-start.24 = (bf16[768,1024]{1,0:T(8,128)(2,1)}, bf16[768,1024]{1,0:T(8,128)(2,1)}, u32[]{:S(2)}, u32[]{:S(2)}) collective-permute-start(bf16[768,1024]{1,0:T(8,128)(2,1)} %pad_maximum_fusion.11.refs_0_.refs_4_), channel_id=1, source_target_pairs={{0,16},{8,24},{16,0},{24,8},{1,17},{9,25},{17,1},{25,9},{2,18},{10... | collective-permute-start | bytes 4718600 | tf_op jit(solution)/shard_map/ppermute | solution.py:55
  319.1 109.1 %collective-permute-start.25 = (bf16[768,1024]{1,0:T(8,128)(2,1)}, bf16[768,1024]{1,0:T(8,128)(2,1)}, u32[]{:S(2)}, u32[]{:S(2)}) collective-permute-start(bf16[768,1024]{1,0:T(8,128)(2,1)} %pad_maximum_fusion.11.refs_0_.refs_4_), channel_id=1, source_target_pairs={{0,8},{8,0},{16,24},{24,16},{1,9},{9,1},{17,25},{25,17},{2,10},{10... | collective-permute-start | bytes 4718600 | tf_op jit(solution)/shard_map/ppermute | solution.py:51
  320.5 139.7 %collective-permute-start.27 = (bf16[768,1024]{1,0:T(8,128)(2,1)}, bf16[768,1024]{1,0:T(8,128)(2,1)}, u32[]{:S(2)}, u32[]{:S(2)}) collective-permute-start(bf16[768,1024]{1,0:T(8,128)(2,1)} %pad_maximum_fusion.10.refs_0_), channel_id=1, source_target_pairs={{0,16},{8,24},{16,0},{24,8},{1,17},{9,25},{17,1},{25,9},{2,18},{10... | collective-permute-start | bytes 4718600 | tf_op jit(solution)/shard_map/ppermute | solution.py:55
  320.7 107.4 %collective-permute-start.26 = (bf16[768,1024]{1,0:T(8,128)(2,1)}, bf16[768,1024]{1,0:T(8,128)(2,1)}, u32[]{:S(2)}, u32[]{:S(2)}) collective-permute-start(bf16[768,1024]{1,0:T(8,128)(2,1)} %collective-permute-done.24.refs_2_.refs_6_), channel_id=1, source_target_pairs={{0,8},{8,0},{16,24},{24,16},{1,9},{9,1},{17,25},{25,17},{2,10},{10... | collective-permute-start | bytes 4718600 | tf_op jit(solution)/shard_map/ppermute | solution.py:51
  322.5 137.7 %collective-permute-start.28 = (bf16[768,1024]{1,0:T(8,128)(2,1)}, bf16[768,1024]{1,0:T(8,128)(2,1)}, u32[]{:S(2)}, u32[]{:S(2)}) collective-permute-start(bf16[768,1024]{1,0:T(8,128)(2,1)} %collective-permute-done.23.refs_1_), channel_id=1, source_target_pairs={{0,16},{8,24},{16,0},{24,8},{1,17},{9,25},{17,1},{25,9},{2,18},{10... | collective-permute-start | bytes 4718600 | tf_op jit(solution)/shard_map/ppermute | solution.py:55
  550.0 49.8 %all-to-all-start.1 = ((f32[8,384,2]{1,2,0:T(2,128)}), f32[8,384,2]{1,2,0:T(2,128)S(1)}, u32[]{:S(2)}, u32[]{:S(2)}) async-start(f32[8,384,2]{1,2,0:T(2,128)} %copy.291), calls=%async_computation.1 | async-start | bytes 49152 | tf_op jit(solution)/shard_map/all_to_all | solution.py:899
  553.3 353.7 %reduce-scatter.5.cloned.1.call-start = ((), (), s32[]{:S(2)}) async-start(), calls=%async_computation.11 | async-start | bytes 14155776 | tf_op jit(solution)/shard_map/reduce_scatter | solution.py:936
  594.7 70.5 %collective-permute-start.29 = (bf16[2,768,1024]{2,1,0:T(8,128)(2,1)}, bf16[2,768,1024]{2,1,0:T(8,128)(2,1)}, u32[]{:S(2)}, u32[]{:S(2)}) collective-permute-start(bf16[2,768,1024]{2,1,0:T(8,128)(2,1)} %pad_maximum_fusion.4), channel_id=1, source_target_pairs={{0,8},{8,0},{16,24},{24,16},{1,9},{9,1},{17,25},{25,17},{2,10},{10... | collective-permute-start | bytes 9437192 | tf_op jit(solution)/shard_map/ppermute | solution.py:51
  597.2 71.3 %collective-permute-start.30 = (bf16[2,768,1024]{2,1,0:T(8,128)(2,1)}, bf16[2,768,1024]{2,1,0:T(8,128)(2,1)}, u32[]{:S(2)}, u32[]{:S(2)}) collective-permute-start(bf16[2,768,1024]{2,1,0:T(8,128)(2,1)} %pad_maximum_fusion.5), channel_id=1, source_target_pairs={{0,16},{8,24},{16,0},{24,8},{1,17},{9,25},{17,1},{25,9},{2,18},{10... | collective-permute-start | bytes 9437192 | tf_op jit(solution)/shard_map/ppermute | solution.py:55
  692.5 301.8 %reduce-scatter.11.cloned.1.call-start = ((), (), s32[]{:S(2)}) async-start(), calls=%async_computation.14 | async-start | bytes 2359296 | tf_op jit(solution)/shard_map/reduce_scatter | solution.py:1002
  697.1 36.1 %collective-permute-start.31 = (bf16[768,1024]{1,0:T(8,128)(2,1)}, bf16[768,1024]{1,0:T(8,128)(2,1)}, u32[]{:S(2)}, u32[]{:S(2)}) collective-permute-start(bf16[768,1024]{1,0:T(8,128)(2,1)} %fusion.16), channel_id=1, source_target_pairs={{0,16},{8,24},{16,0},{24,8},{1,17},{9,25},{17,1},{25,9},{2,18},{10... | collective-permute-start | bytes 4718600 | tf_op jit(solution)/shard_map/ppermute | solution.py:55
  698.6 35.7 %collective-permute-start.32 = (bf16[768,1024]{1,0:T(8,128)(2,1)}, bf16[768,1024]{1,0:T(8,128)(2,1)}, u32[]{:S(2)}, u32[]{:S(2)}) collective-permute-start(bf16[768,1024]{1,0:T(8,128)(2,1)} %fusion.15), channel_id=1, source_target_pairs={{0,8},{8,0},{16,24},{24,16},{1,9},{9,1},{17,25},{25,17},{2,10},{10... | collective-permute-start | bytes 4718600 | tf_op jit(solution)/shard_map/ppermute | solution.py:51
  736.2 39.5 %collective-permute-start.33 = (bf16[192,2048]{1,0:T(8,128)(2,1)S(1)}, bf16[192,2048]{1,0:T(8,128)(2,1)S(1)}, u32[]{:S(2)}, u32[]{:S(2)}) collective-permute-start(bf16[192,2048]{1,0:T(8,128)(2,1)S(1)} %get-tuple-element.268), channel_id=1, source_target_pairs={{0,8},{8,0},{16,24},{24,16},{1,9},{9,1},{17,25},{25,17},{2,10},{10... | collective-permute-start | bytes 2359304 | tf_op jit(solution)/shard_map/ppermute | solution.py:51
  737.7 43.4 %collective-permute-start.34 = (bf16[192,2048]{1,0:T(8,128)(2,1)S(1)}, bf16[192,2048]{1,0:T(8,128)(2,1)S(1)}, u32[]{:S(2)}, u32[]{:S(2)}) collective-permute-start(bf16[192,2048]{1,0:T(8,128)(2,1)S(1)} %get-tuple-element.268), channel_id=1, source_target_pairs={{0,16},{8,24},{16,0},{24,8},{1,17},{9,25},{17,1},{25,9},{2,18},{10... | collective-permute-start | bytes 2359304 | tf_op jit(solution)/shard_map/ppermute | solution.py:55
  738.1 62.6 %collective-permute-start.36 = (bf16[192,2048]{1,0:T(8,128)(2,1)}, bf16[192,2048]{1,0:T(8,128)(2,1)S(1)}, u32[]{:S(2)}, u32[]{:S(2)}) collective-permute-start(bf16[192,2048]{1,0:T(8,128)(2,1)} %get-tuple-element.266), channel_id=1, source_target_pairs={{0,8},{8,0},{16,24},{24,16},{1,9},{9,1},{17,25},{25,17},{2,10},{10... | collective-permute-start | bytes 2359304 | tf_op jit(solution)/shard_map/ppermute | solution.py:51
  738.8 37.6 %collective-permute-start.37 = (bf16[192,2048]{1,0:T(8,128)(2,1)}, bf16[192,2048]{1,0:T(8,128)(2,1)S(1)}, u32[]{:S(2)}, u32[]{:S(2)}) collective-permute-start(bf16[192,2048]{1,0:T(8,128)(2,1)} %get-tuple-element.266), channel_id=1, source_target_pairs={{0,16},{8,24},{16,0},{24,8},{1,17},{9,25},{17,1},{25,9},{2,18},{10... | collective-permute-start | bytes 2359304 | tf_op jit(solution)/shard_map/ppermute | solution.py:55
  775.7 16.4 %collective-permute-start.35 = (bf16[192,2048]{1,0:T(8,128)(2,1)S(1)}, bf16[192,2048]{1,0:T(8,128)(2,1)S(1)}, u32[]{:S(2)}, u32[]{:S(2)}) collective-permute-start(bf16[192,2048]{1,0:T(8,128)(2,1)S(1)} %collective-permute-done.33), channel_id=1, source_target_pairs={{0,16},{8,24},{16,0},{24,8},{1,17},{9,25},{17,1},{25,9},{2,18},{10... | collective-permute-start | bytes 2359304 | tf_op jit(solution)/shard_map/ppermute | solution.py:55
  776.4 16.2 %collective-permute-start.38 = (bf16[192,2048]{1,0:T(8,128)(2,1)S(1)}, bf16[192,2048]{1,0:T(8,128)(2,1)S(1)}, u32[]{:S(2)}, u32[]{:S(2)}) collective-permute-start(bf16[192,2048]{1,0:T(8,128)(2,1)S(1)} %collective-permute-done.37), channel_id=1, source_target_pairs={{0,8},{8,0},{16,24},{24,16},{1,9},{9,1},{17,25},{25,17},{2,10},{10... | collective-permute-start | bytes 2359304 | tf_op jit(solution)/shard_map/ppermute | solution.py:51
  795.5 66.4 %collective-permute-start.39 = (bf16[2,768,1024]{2,1,0:T(8,128)(2,1)}, bf16[2,768,1024]{2,1,0:T(8,128)(2,1)}, u32[]{:S(2)}, u32[]{:S(2)}) collective-permute-start(bf16[2,768,1024]{2,1,0:T(8,128)(2,1)} %pad_maximum_fusion.6), channel_id=1, source_target_pairs={{0,8},{8,0},{16,24},{24,16},{1,9},{9,1},{17,25},{25,17},{2,10},{10... | collective-permute-start | bytes 9437192 | tf_op jit(solution)/shard_map/ppermute | solution.py:51
  799.2 66.3 %collective-permute-start.40 = (bf16[2,768,1024]{2,1,0:T(8,128)(2,1)}, bf16[2,768,1024]{2,1,0:T(8,128)(2,1)}, u32[]{:S(2)}, u32[]{:S(2)}) collective-permute-start(bf16[2,768,1024]{2,1,0:T(8,128)(2,1)} %pad_maximum_fusion.7), channel_id=1, source_target_pairs={{0,16},{8,24},{16,0},{24,8},{1,17},{9,25},{17,1},{25,9},{2,18},{10... | collective-permute-start | bytes 9437192 | tf_op jit(solution)/shard_map/ppermute | solution.py:55
  851.3 184.3 %reduce-scatter.9.cloned.1.call-start = ((), (), s32[]{:S(2)}) async-start(), calls=%async_computation.13 | async-start | bytes 7077888 | tf_op jit(solution)/shard_map/reduce_scatter | solution.py:1005
  865.5 6.1 collective-permute-start.41
  877.9 5.1 collective-permute-start.42
  911.7 30.8 %collective-permute-start.43 = (bf16[768,1024]{1,0:T(8,128)(2,1)}, bf16[768,1024]{1,0:T(8,128)(2,1)}, u32[]{:S(2)}, u32[]{:S(2)}) collective-permute-start(bf16[768,1024]{1,0:T(8,128)(2,1)} %add_convert_fusion.1), channel_id=1, source_target_pairs={{0,16},{8,24},{16,0},{24,8},{1,17},{9,25},{17,1},{25,9},{2,18},{10... | collective-permute-start | bytes 4718600 | tf_op jit(solution)/shard_map/ppermute | solution.py:55
  914.5 34.0 %collective-permute-start.44 = (bf16[768,1024]{1,0:T(8,128)(2,1)}, bf16[768,1024]{1,0:T(8,128)(2,1)}, u32[]{:S(2)}, u32[]{:S(2)}) collective-permute-start(bf16[768,1024]{1,0:T(8,128)(2,1)} %add_convert_fusion), channel_id=1, source_target_pairs={{0,8},{8,0},{16,24},{24,16},{1,9},{9,1},{17,25},{25,17},{2,10},{10... | collective-permute-start | bytes 4718600 | tf_op jit(solution)/shard_map/ppermute | solution.py:51
  949.2 29.8 %collective-permute-start.45 = (bf16[2,192,2048]{2,1,0:T(8,128)(2,1)S(1)}, bf16[2,192,2048]{2,1,0:T(8,128)(2,1)S(1)}, u32[]{:S(2)}, u32[]{:S(2)}) collective-permute-start(bf16[2,192,2048]{2,1,0:T(8,128)(2,1)S(1)} %pad_maximum_fusion.12), channel_id=1, source_target_pairs={{0,8},{8,0},{16,24},{24,16},{1,9},{9,1},{17,25},{25,17},{2,10},{10... | collective-permute-start | bytes 4718600 | tf_op jit(solution)/shard_map/ppermute | solution.py:51
  961.8 39.9 %collective-permute-start.47 = (bf16[2,192,2048]{2,1,0:T(8,128)(2,1)}, bf16[2,192,2048]{2,1,0:T(8,128)(2,1)}, u32[]{:S(2)}, u32[]{:S(2)}) collective-permute-start(bf16[2,192,2048]{2,1,0:T(8,128)(2,1)} %pad_maximum_fusion.13), channel_id=1, source_target_pairs={{0,16},{8,24},{16,0},{24,8},{1,17},{9,25},{17,1},{25,9},{2,18},{10... | collective-permute-start | bytes 4718600 | tf_op jit(solution)/shard_map/ppermute | solution.py:55
  982.6 22.5 %collective-permute-start.46 = (bf16[192,2048]{1,0:T(8,128)(2,1)}, bf16[192,2048]{1,0:T(8,128)(2,1)}, u32[]{:S(2)}, u32[]{:S(2)}) collective-permute-start(bf16[192,2048]{1,0:T(8,128)(2,1)} %fusion.22), channel_id=1, source_target_pairs={{0,16},{8,24},{16,0},{24,8},{1,17},{9,25},{17,1},{25,9},{2,18},{10... | collective-permute-start | bytes 2359304 | tf_op jit(solution)/shard_map/ppermute | solution.py:55
  987.9 12.0 %all-to-all-start.2 = ((f32[8,1,5120]{2,1,0:T(1,128)}), f32[8,1,5120]{2,1,0:T(1,128)S(1)}, u32[]{:S(2)}, u32[]{:S(2)}) async-start(f32[8,1,5120]{2,1,0:T(1,128)} %reshape.276), calls=%async_computation.6 | async-start | bytes 327680 | tf_op jit(solution)/shard_map/all_to_all | solution.py:135
  1009.8 22.6 %collective-permute-start.48 = (bf16[192,2048]{1,0:T(8,128)(2,1)}, bf16[192,2048]{1,0:T(8,128)(2,1)}, u32[]{:S(2)}, u32[]{:S(2)}) collective-permute-start(bf16[192,2048]{1,0:T(8,128)(2,1)} %get-tuple-element.179), channel_id=1, source_target_pairs={{0,8},{8,0},{16,24},{24,16},{1,9},{9,1},{17,25},{25,17},{2,10},{10... | collective-permute-start | bytes 2359304 | tf_op jit(solution)/shard_map/ppermute | solution.py:51
  1011.3 19.9 %collective-permute-start.52 = (f32[20,64]{1,0:T(8,128)S(1)}, f32[20,64]{1,0:T(8,128)S(1)}, u32[]{:S(2)}, u32[]{:S(2)}) collective-permute-start(f32[20,64]{1,0:T(8,128)S(1)} %bitcast.382), channel_id=1, source_target_pairs={{0,24},{8,16},{16,8},{24,0},{1,25},{9,17},{17,9},{25,1},{2,26},{10... | collective-permute-start | bytes 15368 | tf_op jit(solution)/shard_map/ppermute | solution.py:59
  1011.7 19.5 %collective-permute-start.53 = (f32[20,64]{1,0:T(8,128)S(1)}, f32[20,64]{1,0:T(8,128)S(1)}, u32[]{:S(2)}, u32[]{:S(2)}) collective-permute-start(f32[20,64]{1,0:T(8,128)S(1)} %bitcast.383), channel_id=1, source_target_pairs={{0,16},{8,24},{16,0},{24,8},{1,17},{9,25},{17,1},{25,9},{2,18},{10... | collective-permute-start | bytes 15368 | tf_op jit(solution)/shard_map/ppermute | solution.py:55
  1013.5 17.7 %collective-permute-start.54 = (f32[20,64]{1,0:T(8,128)S(1)}, f32[20,64]{1,0:T(8,128)S(1)}, u32[]{:S(2)}, u32[]{:S(2)}) collective-permute-start(f32[20,64]{1,0:T(8,128)S(1)} %bitcast.384), channel_id=1, source_target_pairs={{0,8},{8,0},{16,24},{24,16},{1,9},{9,1},{17,25},{25,17},{2,10},{10... | collective-permute-start | bytes 15368 | tf_op jit(solution)/shard_map/ppermute | solution.py:51
  1037.2 10.1 collective-permute-start.49
  1037.6 9.7 collective-permute-start.50
  1039.4 7.9 collective-permute-start.51
  (101 other events, 1531.0 us)
Sparse Core Ops, SparseCore 0:
  32.1 69.4 all-gather.4
  103.2 27.7 all-gather.6
  132.6 116.2 all-gather.10
  250.4 114.9 all-gather.8
  547.6 127.7 reduce-scatter.6
  692.6 130.1 reduce-scatter.4
  851.4 34.7 reduce-scatter.10
  907.2 70.2 reduce-scatter.8

commit v8 on v7

--- a/solution.py
+++ b/solution.py
@@ -749,7 +749,8 @@
     by_owner = jnp.concatenate(
         [by_owner, jnp.broadcast_to(small, (ctx_size,) + small.shape)], axis=2
     )
-    own_columns = exchange(by_owner, me)
+    out_full = lax.all_gather(w_out, "exp", axis=0, tiled=True)
+    own_columns, out_full = after_all((exchange(by_owner, me), out_full))
     packed = lax.all_gather(own_columns, "exp", axis=1, tiled=True).reshape(D, 3 * own_width + 128)
     small_full = packed[:, 3 * own_width :]
     router_full = small_full[:, :experts]
@@ -757,7 +758,6 @@
     gain_attn, gain_ffn = gains[:, 0], gains[:, 3]
     own_gains = lax.dynamic_slice(gains, (me * own_width, 0), (own_width, 4))
     gain_query, gain_key = own_gains[:, 1], own_gains[:, 2]
-    out_full = lax.all_gather(w_out, "exp", axis=0, tiled=True)
     routes_all = lax.all_to_all(
         jnp.broadcast_to(routes[None], (exp_size,) + routes.shape),
         "exp",
@@ -896,14 +896,6 @@
     shares = [m[4].reshape(1, capacity) for m in made]
     grad_two_part, share_token = combine_rows(token_tables, [m[3] for m in made], shares)
     grad_two = lax.psum_scatter(grad_two_part, "exp", scatter_dimension=0, tiled=True)
-    share_back = lax.all_to_all(
-        share_token.reshape(exp_size, tok_rows, own_experts),
-        "exp",
-        split_axis=0,
-        concat_axis=0,
-        tiled=True,
-    )
-    grad_prob = jnp.swapaxes(share_back, 0, 1).reshape(tok_rows, experts)
     def weight_grads(e, *others):
         rows, hidden, grad_hidden = after_all(made[e][:3], *others)
         return (
@@ -919,10 +911,18 @@
         payload = expert_grads[0]
     results = [
         jnp.dot(
-            after(made[e][1], share_back, *payload), backs[e][2], preferred_element_type=F32
+            after(made[e][1], *payload), backs[e][2], preferred_element_type=F32
         ).astype(BF)
         for e in every
     ]
+    share_back = lax.all_to_all(
+        after(share_token, *results).reshape(exp_size, tok_rows, own_experts),
+        "exp",
+        split_axis=0,
+        concat_axis=0,
+        tiled=True,
+    )
+    grad_prob = jnp.swapaxes(share_back, 0, 1).reshape(tok_rows, experts)
     if ctx_size == 4:
         ahead, direct = split_sums((send_x(payload[0]), send_y(payload[1])))
         last = scatter_last_payload(take, me, ahead)
@@ -967,8 +967,8 @@
         [jnp.sum(scaled_query * normed_query, axis=1), jnp.sum(scaled_key * normed_key, axis=1)]
     )
     weight_sums = [scatter_expert_end(expert_grads[0], directs[0], lasts[0], me)]
-    products = after(
-        products, out_grad, *weight_sums[0], *(piece for pieces in sums for piece in pieces)
+    *weight_sums[0], products = after_all(
+        (*weight_sums[0], products), out_grad, *(piece for pieces in sums for piece in pieces)
     )
     means = sum_over_ctx(products) / D
     for e in range(1, own_experts):
@@ -976,7 +976,12 @@
         directs.append(direct)
         ahead = after_all(ahead, means)
         take = expert_take(expert_grads[e])
-        lasts.append(scatter_last(take, me, ahead) if ctx_size == 4 else ())
+        if ctx_size == 4:
+            last_sent = scatter_last_payload(take, me, ahead)
+            lasts.append((send_y(last_sent[0]), send_x(last_sent[1])))
+        else:
+            last_sent = direct
+            lasts.append(())
     grad_projected = jnp.concatenate(
         [
             root_query * (scaled_query - normed_query * means[0][:, None]),
@@ -988,7 +993,8 @@
     grad_packed = jnp.pad(grad_projected, ((0, 0), (0, 128)))
     grad_one_part = lax.dot_general(grad_packed, packed, NT, preferred_element_type=F32)
     grad_attn_gain = jnp.sum(grad_one_part * normed_group, axis=0)
-    qkv_grad = lax.dot_general(hidden_one, grad_projected, TN, preferred_element_type=F32).astype(BF)
+    left, right = after_all((hidden_one, grad_projected), *last_sent)
+    qkv_grad = lax.dot_general(left, right, TN, preferred_element_type=F32).astype(BF)
     grad_one, one_first, one_sent, unused = scatter_group(
         after(grad_one_part, *(piece for pieces in lasts[1:] for piece in pieces)),
         slot_table,

time: 1070 us -> 1040 us (0.972); the launches traced: 1060 us -> 1040 us
  Pallas kernels: 282 us -> 270 us
    unnamed x205 -> x211, local copies, waits for them, and re-layouts: 22.8 us -> 31.6 us
  transfers between devices with their start and end apart: 66 -> 66, of which waited for: 30 -> 31; matrix products, arithmetic and copies ran while one was open for 35% -> 34% of each run, Pallas kernels for 19% -> 18%
where the time goes in v8:
time: 1040 us
  waiting for transfers between devices  280 us (27%)
  Pallas kernels  270 us (26%)
  matrix products  161 us (15%)
  other arithmetic  125 us (12%)
  local copies, waits for them, and re-layouts  111 us (11%)
  starting transfers between devices  72.5 us (7%)
  between operations  21.6 us (2%)
    ppermute x26, waiting for transfers between devices, send_x(): return lax.ppermute(value, 'ctx', X_PAIRS)  156 us
    pallas_call x2, Pallas kernels, expert_rows(): pl.pallas_call(functools.partial(expert_kernel, own), out_shape=[made(wid...  116 us
    ppermute x26, waiting for transfers between devices, send_y(): return lax.ppermute(value, 'ctx', Y_PAIRS)  96.7 us
    pallas_call x2, Pallas kernels, back_rows(): pl.pallas_call(back_rows_kernel, out_shape=[jax.ShapeDtypeStruct((capacit...  56.9 us
    dot_general x2, matrix products, weight_grads(): lax.dot_general(rows, grad_hidden, TN, preferred_element_type=F32)  45 us
    pallas_call x2, Pallas kernels, combine_rows(): pl.pallas_call(functools.partial(combine_kernel, experts), out_shape=[jax...  40.8 us
    unnamed x211, local copies, waits for them, and re-layouts  31.6 us
    pallas_call x1, Pallas kernels, attend_back(): pl.pallas_call(functools.partial(attend_back_kernel, tiles, 1.0 / math.sq...  30 us
  transfers between devices with their start and end apart: 66, of which 31 were waited for; matrix products, arithmetic and copies ran while one was open for 34% of the time, Pallas kernels for 18%

profile of v8, /device:TPU:0, one launch (start us, length us, event | category | flops | bytes accessed | tf_op | source)
XLA Modules:
  0.0 1041.6 jit_solution(16658915200905842886)
XLA Ops:
  17.2 4.0 collective-permute-start.6
  21.8 5.5 collective-permute-done.6
  27.3 3.7 collective-permute-done.7
  32.6 8.8 all-gather.5.cloned.1.call-done
  43.8 3.4 broadcast.176.clone
  62.7 6.9 collective-permute-done
  71.0 16.8 %collective-permute-done.4 = bf16[192,2048]{1,0:T(8,128)(2,1)S(1)} collective-permute-done((bf16[192,2048]{1,0:T(8,128)(2,1)}, bf16[192,2048]{1,0:T(8,128)(2,1)S(1)}, u32[]{:S(2)}, u32[]{:S(2)}) %collective-permute-start.4) | collective-permute-done | bytes 786464 | tf_op jit(solution)/shard_map/ppermute | solution.py:55
  89.8 2.7 constant_dynamic-update-slice_fusion.15
  94.7 8.9 collective-permute-done.2
  113.4 4.1 fusion.5
  120.7 6.2 fusion.3
  127.0 12.5 %fusion.102.qp_ref.kp_ref.vp_ref = f32[1536,1664]{1,0:T(8,128)S(1)} fusion(bf16[1536,2048]{1,0:T(8,128)(2,1)S(1)} %fusion.3, bf16[2048,1664]{1,0:T(8,128)(2,1)S(1)} %bitcast.374), kind=kOutput, calls=%fused_computation.385 | convolution fusion | flops 10468982784 | bytes 23330816 | tf_op jit(solution)/shard_map/dot_general | solution.py:790
  141.7 2.8 fusion.27
  153.7 25.9 %shard_map.272 = (bf16[1536,512]{1,0:T(8,128)(2,1)S(1)}, bf16[1536,512]{1,0:T(8,128)(2,1)}, bf16[1536,512]{1,0:T(8,128)(2,1)}, bf16[1536,512]{1,0:T(8,128)(2,1)}) custom-call(f32[1536,1664]{1,0:T(8,128)} %copy-done.22, f32[1536,1664]{1,0:T(8,128)} %copy-done.22, f32[1536,1664]{1,0:T(8,128)} %copy-done.22, f32[1536,2]{1,0:T(8,128)S(1)} %fusion.86.root_ref.key_root_ref, ...), custom_call_target="tpu_custom_call" | custom-call | flops 3221225472 | bytes 15728640 | tf_op jit(solution)/shard_map/pallas_call | solution.py:347
  179.5 5.6 fusion.103
  189.9 17.4 %collective-permute-done.16 = bf16[192,2048]{1,0:T(8,128)(2,1)S(1)} collective-permute-done((bf16[192,2048]{1,0:T(8,128)(2,1)S(1)}, bf16[192,2048]{1,0:T(8,128)(2,1)S(1)}, u32[]{:S(2)}, u32[]{:S(2)}) %collective-permute-start.16) | collective-permute-done | bytes 786464 | tf_op jit(solution)/shard_map/ppermute | solution.py:51
  209.6 11.0 %collective-permute-done.15 = bf16[192,2048]{1,0:T(8,128)(2,1)S(1)} collective-permute-done((bf16[192,2048]{1,0:T(8,128)(2,1)S(1)}, bf16[192,2048]{1,0:T(8,128)(2,1)S(1)}, u32[]{:S(2)}, u32[]{:S(2)}) %collective-permute-start.15) | collective-permute-done | bytes 786464 | tf_op jit(solution)/shard_map/ppermute | solution.py:51
  220.5 6.8 collective-permute-done.17
  229.4 7.5 collective-permute-done.18
  236.8 7.2 collective-permute-done.20
  252.8 3.4 all-to-all-start
  263.2 6.9 collective-permute-done.21.refs_3_
  270.0 3.8 collective-permute-done.22.refs_3_.refs_7_
  279.5 14.7 %select_reduce_fusion = s32[2,2048]{1,0:T(2,128)S(1)} fusion(s32[2,3072]{1,0:T(2,128)S(1)} %copy.283, pred[2,3072]{1,0:T(4,128)(4,1)S(1)} %bitcast.381), kind=kLoop, calls=%fused_computation | loop fusion | flops 50327552 | bytes 47104 | tf_op jit(solution)/shard_map/reduce_max | solution.py:853
  301.6 2.9 broadcast_select_fusion.pos_ref
  304.5 24.4 %collective-permute-done.23.refs_1_ = bf16[768,1024]{1,0:T(8,128)(2,1)} collective-permute-done((bf16[768,1024]{1,0:T(8,128)(2,1)}, bf16[768,1024]{1,0:T(8,128)(2,1)}, u32[]{:S(2)}, u32[]{:S(2)}) %collective-permute-start.23) | collective-permute-done | bytes 1572896 | tf_op jit(solution)/shard_map/ppermute | solution.py:51
  338.5 26.9 %shard_map.273 = (bf16[2048,2048]{1,0:T(8,128)(2,1)}, f32[2048,1024]{1,0:T(8,128)}, bf16[1024,2048]{1,0:T(8,128)(2,1)}) custom-call(s32[1]{0:T(128)} %get-tuple-element.325.tiles_ref, s32[8]{0:T(128)S(1)} %get-tuple-element.323.low_ref, s32[8]{0:T(128)S(1)} %get-tuple-element.321.windows_ref, s32[1]{0:T(128)} %bitcast.36.me_ref, s32[2048,1]{1,0:T(8,128)S(1)} %copy-done.8, ...), custom_call_target="tpu_custom_call" | custom-call | flops 11274289152 | bytes 37748736 | tf_op jit(solution)/shard_map/pallas_call | solution.py:524
  366.2 53.5 %shard_map.274 = (bf16[2048,2048]{1,0:T(8,128)(2,1)}, bf16[2048,1024]{1,0:T(8,128)(2,1)}, bf16[2048,2048]{1,0:T(8,128)(2,1)}, bf16[2048,2048]{1,0:T(8,128)(2,1)}, f32[2048,1]{1,0:T(8,128)}) custom-call(s32[1]{0:T(128)} %get-tuple-element.325.tiles_ref, s32[8]{0:T(128)} %copy-done.13, s32[8]{0:T(128)} %copy-done.14, s32[2]{0:T(128)} %pad_add_fusion.ids_ref, ...), custom_call_target="tpu_custom_call" | custom-call | flops 30601641984 | bytes 58720256 | tf_op jit(solution)/shard_map/pallas_call | solution.py:624
  422.7 30.0 %shard_map.275 = (bf16[2048,2048]{1,0:T(8,128)(2,1)}, f32[2048,1024]{1,0:T(8,128)}, bf16[1024,2048]{1,0:T(8,128)(2,1)}) custom-call(s32[1]{0:T(128)} %get-tuple-element.324.tiles_ref, s32[8]{0:T(128)S(1)} %get-tuple-element.322.low_ref, s32[8]{0:T(128)S(1)} %get-tuple-element.320.windows_ref, s32[1]{0:T(128)} %bitcast.36.me_ref, ...), custom_call_target="tpu_custom_call" | custom-call | flops 11274289152 | bytes 37748736 | tf_op jit(solution)/shard_map/pallas_call | solution.py:524
  452.7 62.8 %shard_map.276 = (bf16[2048,2048]{1,0:T(8,128)(2,1)}, bf16[2048,1024]{1,0:T(8,128)(2,1)}, bf16[2048,2048]{1,0:T(8,128)(2,1)}, bf16[2048,2048]{1,0:T(8,128)(2,1)}, f32[2048,1]{1,0:T(8,128)}) custom-call(s32[1]{0:T(128)} %get-tuple-element.324.tiles_ref, s32[8]{0:T(128)} %copy-done.11, s32[8]{0:T(128)} %copy-done.12, s32[2]{0:T(128)} %pad_add_fusion.ids_ref, ...), custom_call_target="tpu_custom_call" | custom-call | flops 30601641984 | bytes 58720256 | tf_op jit(solution)/shard_map/pallas_call | solution.py:624
  518.5 20.3 %shard_map.277 = (bf16[3072,2048]{1,0:T(8,128)(2,1)}, f32[3072,2]{1,0:T(8,128)S(1)}) custom-call(s32[2,12]{1,0:T(2,128)S(1)} %copy.291.start_ref, s32[2,12]{1,0:T(2,128)S(1)} %copy.292.more_ref, s32[2,12]{1,0:T(2,128)S(1)} %copy.293.wide_ref, s32[3072,2]{1,0:T(8,128)S(1)} %copy-done, bf16[2048,2048]{1,0:T(8,128)(2,1)} %get-tuple-element.111.refs_0_, ...), custom_call_target="tpu_custom_call" | custom-call | flops 6442450944 | bytes 29360128 | tf_op jit(solution)/shard_map/pallas_call | solution.py:682
  540.1 12.9 %convolution_convert_fusion.6 = bf16[1024,2048]{1,0:T(8,128)(2,1)S(1)} fusion(bf16[2048,1024]{1,0:T(8,128)(2,1)} %get-tuple-element.128, bf16[2048,2048]{1,0:T(8,128)(2,1)} %get-tuple-element.127), kind=kOutput, calls=%fused_computation.25 | convolution fusion | flops 8592031744 | bytes 16777216 | tf_op jit(solution)/shard_map/dot_general | solution.py:903
  554.3 22.4 %convolution_convert_fusion.4 = bf16[2048,2048]{1,0:T(8,128)(2,1)S(1)} fusion(bf16[2048,2048]{1,0:T(8,128)(2,1)} %get-tuple-element.124, bf16[2048,2048]{1,0:T(8,128)(2,1)} %get-tuple-element.125), kind=kOutput, calls=%fused_computation.14 | convolution fusion | flops 17184063488 | bytes 25165824 | tf_op jit(solution)/shard_map/dot_general | solution.py:902
  582.4 13.7 %convolution_convert_fusion.3.refs_0_ = bf16[2048,2048]{1,0:T(8,128)(2,1)} fusion(bf16[2048,1024]{1,0:T(8,128)(2,1)S(1)} %copy-done.97, bf16[1024,2048]{1,0:T(8,128)(2,1)} %get-tuple-element.129), kind=kOutput, calls=%fused_computation.13 | convolution fusion | flops 8594128896 | bytes 16777216 | tf_op jit(solution)/shard_map/dot_general | solution.py:913
  596.2 13.0 %convolution_convert_fusion.2.refs_1_ = bf16[2048,2048]{1,0:T(8,128)(2,1)} fusion(bf16[2048,1024]{1,0:T(8,128)(2,1)S(1)} %copy-done.96, bf16[1024,2048]{1,0:T(8,128)(2,1)} %get-tuple-element.132), kind=kOutput, calls=%fused_computation.12 | convolution fusion | flops 8594128896 | bytes 16777216 | tf_op jit(solution)/shard_map/dot_general | solution.py:913
  609.2 37.6 %collective-permute-done.29 = bf16[2,768,1024]{2,1,0:T(8,128)(2,1)S(1)} collective-permute-done((bf16[2,768,1024]{2,1,0:T(8,128)(2,1)S(1)}, bf16[2,768,1024]{2,1,0:T(8,128)(2,1)S(1)}, u32[]{:S(2)}, u32[]{:S(2)}) %collective-permute-start.29) | collective-permute-done | bytes 3145760 | tf_op jit(solution)/shard_map/ppermute | solution.py:51
  651.6 20.5 %shard_map.278 = (bf16[3072,2048]{1,0:T(8,128)(2,1)}, f32[3072,2]{1,0:T(8,128)}) custom-call(s32[2,12]{1,0:T(2,128)S(1)} %copy.291.start_ref, s32[2,12]{1,0:T(2,128)S(1)} %copy.292.more_ref, s32[2,12]{1,0:T(2,128)S(1)} %copy.293.wide_ref, s32[3072,2]{1,0:T(8,128)S(1)} %copy-done.1, bf16[2048,2048]{1,0:T(8,128)(2,1)} %convolution_convert_fusion.3.refs_0_, ...), custom_call_target="tpu_custom_call" | custom-call | flops 6442450944 | bytes 29360128 | tf_op jit(solution)/shard_map/pallas_call | solution.py:682
  678.5 6.5 all-to-all-start.1
  685.1 5.9 all-to-all-done.1
  691.1 16.1 %collective-permute-done.31 = bf16[768,1024]{1,0:T(8,128)(2,1)} collective-permute-done((bf16[768,1024]{1,0:T(8,128)(2,1)}, bf16[768,1024]{1,0:T(8,128)(2,1)}, u32[]{:S(2)}, u32[]{:S(2)}) %collective-permute-start.31) | collective-permute-done | bytes 1572896 | tf_op jit(solution)/shard_map/ppermute | solution.py:55
  707.2 3.1 convert_add_fusion.6
  719.4 3.9 multiply_reduce_fusion.2
  730.9 22.6 %convolution_convert_fusion.1 = bf16[2048,2048]{1,0:T(8,128)(2,1)S(1)} fusion(bf16[2048,2048]{1,0:T(8,128)(2,1)} %get-tuple-element.147, bf16[2048,2048]{1,0:T(8,128)(2,1)} %get-tuple-element.148), kind=kOutput, calls=%fused_computation.11 | convolution fusion | flops 17184063488 | bytes 25165824 | tf_op jit(solution)/shard_map/dot_general | solution.py:902
  753.5 12.8 %convolution_convert_fusion.5 = bf16[1024,2048]{1,0:T(8,128)(2,1)S(1)} fusion(bf16[2048,1024]{1,0:T(8,128)(2,1)} %get-tuple-element.149, bf16[2048,2048]{1,0:T(8,128)(2,1)} %get-tuple-element.150), kind=kOutput, calls=%fused_computation.24 | convolution fusion | flops 8592031744 | bytes 16777216 | tf_op jit(solution)/shard_map/dot_general | solution.py:903
  772.7 11.3 %collective-permute-done.35 = bf16[192,2048]{1,0:T(8,128)(2,1)S(1)} collective-permute-done((bf16[192,2048]{1,0:T(8,128)(2,1)S(1)}, bf16[192,2048]{1,0:T(8,128)(2,1)S(1)}, u32[]{:S(2)}, u32[]{:S(2)}) %collective-permute-start.35) | collective-permute-done | bytes 786464 | tf_op jit(solution)/shard_map/ppermute | solution.py:55
  794.5 5.1 convolution_convert_fusion.8.d_ref
  799.7 30.0 %shard_map.279 = (f32[1536,512]{1,0:T(8,128)}, f32[1536,512]{1,0:T(8,128)}, f32[1536,512]{1,0:T(8,128)}) custom-call(bf16[1536,512]{1,0:T(8,128)(2,1)S(1)} %copy-done.16, bf16[1536,512]{1,0:T(8,128)(2,1)S(1)} %copy-done.17, bf16[1536,512]{1,0:T(8,128)(2,1)} %get-tuple-element.141.v_ref, bf16[1536,512]{1,0:T(8,128)(2,1)} %convolution_convert_fusion.8.d_ref, ...), custom_call_target="tpu_custom_call" | custom-call | flops 8053063680 | bytes 15728640 | tf_op jit(solution)/shard_map/pallas_call | solution.py:436
  829.7 3.4 convert.34
  833.1 4.8 multiply_reduce_fusion.1
  838.0 4.6 convolution_convert_fusion.7
  842.7 13.7 %collective-permute-done.39 = bf16[2,768,1024]{2,1,0:T(8,128)(2,1)} collective-permute-done((bf16[2,768,1024]{2,1,0:T(8,128)(2,1)}, bf16[2,768,1024]{2,1,0:T(8,128)(2,1)}, u32[]{:S(2)}, u32[]{:S(2)}) %collective-permute-start.39) | collective-permute-done | bytes 3145760 | tf_op jit(solution)/shard_map/ppermute | solution.py:51
  856.4 3.7 collective-permute-done.40
  860.4 3.9 slice_bitcast_fusion.3
  871.1 3.9 slice_bitcast_fusion.2
  878.1 3.4 add_convert_fusion.1
  884.2 3.9 multiply_convert_fusion.1
  890.6 12.4 %convolution_convert_fusion = bf16[2048,1536]{1,0:T(8,128)(2,1)} fusion(bf16[1536,2048]{1,0:T(8,128)(2,1)S(1)} %bitcast.363, bf16[1536,1536]{1,0:T(8,128)(2,1)S(1)} %pad_maximum_fusion), kind=kOutput, calls=%fused_computation.10 | convolution fusion | flops 9666822144 | bytes 17301504 | tf_op jit(solution)/shard_map/dot_general | solution.py:997
  906.3 17.0 %fusion.4 = (f32[2048]{0:T(1024)S(1)}, f32[1536,2048]{1,0:T(8,128)S(1)}) fusion(bf16[1536,2048]{1,0:T(8,128)(2,1)} %constant_dynamic-update-slice_fusion.9, f32[1536]{0:T(1024)S(1)} %copy-done.81, bf16[2048,1664]{1,0:T(8,128)(2,1)} %bitcast.371, bf16[1536,1536]{1,0:T(8,128)(2,1)} %copy-done.49), kind=kOutput, calls=%fused_computation.8 | convolution fusion | flops 10481563648 | bytes 30423040 | tf_op jit(solution)/shard_map/dot_general | solution.py:994
  923.3 12.6 %collective-permute-done.43 = bf16[768,1024]{1,0:T(8,128)(2,1)} collective-permute-done((bf16[768,1024]{1,0:T(8,128)(2,1)}, bf16[768,1024]{1,0:T(8,128)(2,1)}, u32[]{:S(2)}, u32[]{:S(2)}) %collective-permute-start.43) | collective-permute-done | bytes 1572896 | tf_op jit(solution)/shard_map/ppermute | solution.py:55
  942.9 27.5 %collective-permute-done.45 = bf16[2,192,2048]{2,1,0:T(8,128)(2,1)S(1)} collective-permute-done((bf16[2,192,2048]{2,1,0:T(8,128)(2,1)S(1)}, bf16[2,192,2048]{2,1,0:T(8,128)(2,1)S(1)}, u32[]{:S(2)}, u32[]{:S(2)}) %collective-permute-start.45) | collective-permute-done | bytes 1572896 | tf_op jit(solution)/shard_map/ppermute | solution.py:51
  974.1 3.6 all-to-all-start.2
  979.6 5.3 all-to-all-done.2
  988.5 4.6 fusion.20
  1024.1 6.5 fusion.13
  (521 shorter events, 230.7 us)
Async XLA Ops:
  7.2 34.3 %all-gather.5.cloned.1.call-start = ((), (), s32[]{:S(2)}) async-start(), calls=%async_computation.7 | async-start | bytes 2359296 | tf_op jit(solution)/shard_map/all_gather | solution.py:752
  7.9 109.6 %all-gather.7.cloned.1.call-start = ((), (), s32[]{:S(2)}) async-start(), calls=%async_computation.8 | async-start | bytes 7667712 | tf_op jit(solution)/shard_map/all_gather | solution.py:754
  17.2 10.1 collective-permute-start.6
  21.2 9.8 collective-permute-start.7
  21.7 9.6 collective-permute-start.8
  41.5 263.0 %all-gather.11.cloned.1.call-start = ((), (), s32[]{:S(2)}) async-start(), calls=%async_computation.10 | async-start | bytes 14155776 | tf_op jit(solution)/shard_map/all_gather | solution.py:768
  42.2 324.0 %all-gather.9.cloned.1.call-start = ((), (), s32[]{:S(2)}) async-start(), calls=%async_computation.9 | async-start | bytes 14155776 | tf_op jit(solution)/shard_map/all_gather | solution.py:881
  48.8 20.7 %collective-permute-start = (bf16[192,2048]{1,0:T(8,128)(2,1)}, bf16[192,2048]{1,0:T(8,128)(2,1)}, u32[]{:S(2)}, u32[]{:S(2)}) collective-permute-start(bf16[192,2048]{1,0:T(8,128)(2,1)} %get-tuple-element.287), channel_id=1, source_target_pairs={{0,8},{8,0},{16,24},{24,16},{1,9},{9,1},{17,25},{25,17},{2,10},{10... | collective-permute-start | bytes 2359304 | tf_op jit(solution)/shard_map/ppermute | solution.py:51
  50.3 42.2 %collective-permute-start.1 = (bf16[192,2048]{1,0:T(8,128)(2,1)}, bf16[192,2048]{1,0:T(8,128)(2,1)}, u32[]{:S(2)}, u32[]{:S(2)}) collective-permute-start(bf16[192,2048]{1,0:T(8,128)(2,1)} %get-tuple-element.287), channel_id=1, source_target_pairs={{0,16},{8,24},{16,0},{24,8},{1,17},{9,25},{17,1},{25,9},{2,18},{10... | collective-permute-start | bytes 2359304 | tf_op jit(solution)/shard_map/ppermute | solution.py:55
  51.8 57.6 %collective-permute-start.3 = (bf16[192,2048]{1,0:T(8,128)(2,1)}, bf16[192,2048]{1,0:T(8,128)(2,1)}, u32[]{:S(2)}, u32[]{:S(2)}) collective-permute-start(bf16[192,2048]{1,0:T(8,128)(2,1)} %get-tuple-element.285), channel_id=1, source_target_pairs={{0,8},{8,0},{16,24},{24,16},{1,9},{9,1},{17,25},{25,17},{2,10},{10... | collective-permute-start | bytes 2359304 | tf_op jit(solution)/shard_map/ppermute | solution.py:51
  52.3 35.4 %collective-permute-start.4 = (bf16[192,2048]{1,0:T(8,128)(2,1)}, bf16[192,2048]{1,0:T(8,128)(2,1)S(1)}, u32[]{:S(2)}, u32[]{:S(2)}) collective-permute-start(bf16[192,2048]{1,0:T(8,128)(2,1)} %get-tuple-element.285), channel_id=1, source_target_pairs={{0,16},{8,24},{16,0},{24,8},{1,17},{9,25},{17,1},{25,9},{2,18},{10... | collective-permute-start | bytes 2359304 | tf_op jit(solution)/shard_map/ppermute | solution.py:55
  69.5 34.1 %collective-permute-start.2 = (bf16[192,2048]{1,0:T(8,128)(2,1)}, bf16[192,2048]{1,0:T(8,128)(2,1)S(1)}, u32[]{:S(2)}, u32[]{:S(2)}) collective-permute-start(bf16[192,2048]{1,0:T(8,128)(2,1)} %collective-permute-done), channel_id=1, source_target_pairs={{0,16},{8,24},{16,0},{24,8},{1,17},{9,25},{17,1},{25,9},{2,18},{10... | collective-permute-start | bytes 2359304 | tf_op jit(solution)/shard_map/ppermute | solution.py:55
  87.8 17.6 %collective-permute-start.5 = (bf16[192,2048]{1,0:T(8,128)(2,1)S(1)}, bf16[192,2048]{1,0:T(8,128)(2,1)S(1)}, u32[]{:S(2)}, u32[]{:S(2)}) collective-permute-start(bf16[192,2048]{1,0:T(8,128)(2,1)S(1)} %collective-permute-done.4), channel_id=1, source_target_pairs={{0,8},{8,0},{16,24},{24,16},{1,9},{9,1},{17,25},{25,17},{2,10},{10... | collective-permute-start | bytes 2359304 | tf_op jit(solution)/shard_map/ppermute | solution.py:51
  105.4 34.6 %collective-permute-start.9 = (bf16[768,1024]{1,0:T(8,128)(2,1)}, bf16[768,1024]{1,0:T(8,128)(2,1)}, u32[]{:S(2)}, u32[]{:S(2)}) collective-permute-start(bf16[768,1024]{1,0:T(8,128)(2,1)} %get-tuple-element.99.refs_0_), channel_id=1, source_target_pairs={{0,8},{8,0},{16,24},{24,16},{1,9},{9,1},{17,25},{25,17},{2,10},{10... | collective-permute-start | bytes 4718600 | tf_op jit(solution)/shard_map/ppermute | solution.py:51
  106.0 34.1 %collective-permute-start.10 = (bf16[768,1024]{1,0:T(8,128)(2,1)S(1)}, bf16[768,1024]{1,0:T(8,128)(2,1)S(1)}, u32[]{:S(2)}, u32[]{:S(2)}) collective-permute-start(bf16[768,1024]{1,0:T(8,128)(2,1)S(1)} %get-tuple-element.98.refs_0_.refs_4_), channel_id=1, source_target_pairs={{0,16},{8,24},{16,0},{24,8},{1,17},{9,25},{17,1},{25,9},{2,18},{10... | collective-permute-start | bytes 4718600 | tf_op jit(solution)/shard_map/ppermute | solution.py:55
  151.8 33.4 %collective-permute-start.13 = (bf16[768,1024]{1,0:T(8,128)(2,1)S(1)}, bf16[768,1024]{1,0:T(8,128)(2,1)S(1)}, u32[]{:S(2)}, u32[]{:S(2)}) collective-permute-start(bf16[768,1024]{1,0:T(8,128)(2,1)S(1)} %copy-done.5), channel_id=1, source_target_pairs={{0,8},{8,0},{16,24},{24,16},{1,9},{9,1},{17,25},{25,17},{2,10},{10... | collective-permute-start | bytes 4718600 | tf_op jit(solution)/shard_map/ppermute | solution.py:51
  152.6 32.5 %collective-permute-start.14 = (bf16[768,1024]{1,0:T(8,128)(2,1)}, bf16[768,1024]{1,0:T(8,128)(2,1)S(1)}, u32[]{:S(2)}, u32[]{:S(2)}) collective-permute-start(bf16[768,1024]{1,0:T(8,128)(2,1)} %get-tuple-element.99.refs_0_), channel_id=1, source_target_pairs={{0,16},{8,24},{16,0},{24,8},{1,17},{9,25},{17,1},{25,9},{2,18},{10... | collective-permute-start | bytes 4718600 | tf_op jit(solution)/shard_map/ppermute | solution.py:55
  186.8 20.5 %collective-permute-start.16 = (bf16[192,2048]{1,0:T(8,128)(2,1)S(1)}, bf16[192,2048]{1,0:T(8,128)(2,1)S(1)}, u32[]{:S(2)}, u32[]{:S(2)}) collective-permute-start(bf16[192,2048]{1,0:T(8,128)(2,1)S(1)} %get-tuple-element.205), channel_id=1, source_target_pairs={{0,8},{8,0},{16,24},{24,16},{1,9},{9,1},{17,25},{25,17},{2,10},{10... | collective-permute-start | bytes 2359304 | tf_op jit(solution)/shard_map/ppermute | solution.py:51
  187.9 32.6 %collective-permute-start.15 = (bf16[192,2048]{1,0:T(8,128)(2,1)S(1)}, bf16[192,2048]{1,0:T(8,128)(2,1)S(1)}, u32[]{:S(2)}, u32[]{:S(2)}) collective-permute-start(bf16[192,2048]{1,0:T(8,128)(2,1)S(1)} %get-tuple-element.202), channel_id=1, source_target_pairs={{0,8},{8,0},{16,24},{24,16},{1,9},{9,1},{17,25},{25,17},{2,10},{10... | collective-permute-start | bytes 2359304 | tf_op jit(solution)/shard_map/ppermute | solution.py:51
  188.8 31.7 %collective-permute-start.19 = (bf16[192,2048]{1,0:T(8,128)(2,1)S(1)}, bf16[192,2048]{1,0:T(8,128)(2,1)S(1)}, u32[]{:S(2)}, u32[]{:S(2)}) collective-permute-start(bf16[192,2048]{1,0:T(8,128)(2,1)S(1)} %get-tuple-element.203), channel_id=1, source_target_pairs={{0,16},{8,24},{16,0},{24,8},{1,17},{9,25},{17,1},{25,9},{2,18},{10... | collective-permute-start | bytes 2359304 | tf_op jit(solution)/shard_map/ppermute | solution.py:55
  207.5 19.8 %collective-permute-start.17 = (bf16[192,2048]{1,0:T(8,128)(2,1)S(1)}, bf16[192,2048]{1,0:T(8,128)(2,1)S(1)}, u32[]{:S(2)}, u32[]{:S(2)}) collective-permute-start(bf16[192,2048]{1,0:T(8,128)(2,1)S(1)} %add_convert_fusion.4), channel_id=1, source_target_pairs={{0,16},{8,24},{16,0},{24,8},{1,17},{9,25},{17,1},{25,9},{2,18},{10... | collective-permute-start | bytes 2359304 | tf_op jit(solution)/shard_map/ppermute | solution.py:55
  208.6 28.3 %collective-permute-start.18 = (bf16[192,2048]{1,0:T(8,128)(2,1)S(1)}, bf16[192,2048]{1,0:T(8,128)(2,1)S(1)}, u32[]{:S(2)}, u32[]{:S(2)}) collective-permute-start(bf16[192,2048]{1,0:T(8,128)(2,1)S(1)} %get-tuple-element.204), channel_id=1, source_target_pairs={{0,16},{8,24},{16,0},{24,8},{1,17},{9,25},{17,1},{25,9},{2,18},{10... | collective-permute-start | bytes 2359304 | tf_op jit(solution)/shard_map/ppermute | solution.py:55
  227.9 16.1 %collective-permute-start.20 = (bf16[192,2048]{1,0:T(8,128)(2,1)S(1)}, bf16[192,2048]{1,0:T(8,128)(2,1)S(1)}, u32[]{:S(2)}, u32[]{:S(2)}) collective-permute-start(bf16[192,2048]{1,0:T(8,128)(2,1)S(1)} %get-tuple-element.201), channel_id=1, source_target_pairs={{0,8},{8,0},{16,24},{24,16},{1,9},{9,1},{17,25},{25,17},{2,10},{10... | collective-permute-start | bytes 2359304 | tf_op jit(solution)/shard_map/ppermute | solution.py:51
  248.9 21.1 %collective-permute-start.21 = (bf16[768,1024]{1,0:T(8,128)(2,1)}, bf16[768,1024]{1,0:T(8,128)(2,1)}, u32[]{:S(2)}, u32[]{:S(2)}) collective-permute-start(bf16[768,1024]{1,0:T(8,128)(2,1)} %collective-permute-done.9.refs_1_), channel_id=1, source_target_pairs={{0,16},{8,24},{16,0},{24,8},{1,17},{9,25},{17,1},{25,9},{2,18},{10... | collective-permute-start | bytes 4718600 | tf_op jit(solution)/shard_map/ppermute | solution.py:55
  251.3 22.5 %collective-permute-start.22 = (bf16[768,1024]{1,0:T(8,128)(2,1)}, bf16[768,1024]{1,0:T(8,128)(2,1)}, u32[]{:S(2)}, u32[]{:S(2)}) collective-permute-start(bf16[768,1024]{1,0:T(8,128)(2,1)} %copy-done.18), channel_id=1, source_target_pairs={{0,8},{8,0},{16,24},{24,16},{1,9},{9,1},{17,25},{25,17},{2,10},{10... | collective-permute-start | bytes 4718600 | tf_op jit(solution)/shard_map/ppermute | solution.py:51
  252.8 10.3 all-to-all-start
  256.2 463.1 %reduce-scatter.7.cloned.1.call-start = ((), (), s32[]{:S(2)}) async-start(), calls=%async_computation.12 | async-start | bytes 14155776 | tf_op jit(solution)/shard_map/reduce_scatter | solution.py:898
  294.2 34.6 %collective-permute-start.23 = (bf16[768,1024]{1,0:T(8,128)(2,1)}, bf16[768,1024]{1,0:T(8,128)(2,1)}, u32[]{:S(2)}, u32[]{:S(2)}) collective-permute-start(bf16[768,1024]{1,0:T(8,128)(2,1)} %pad_maximum_fusion.10.refs_0_), channel_id=1, source_target_pairs={{0,8},{8,0},{16,24},{24,16},{1,9},{9,1},{17,25},{25,17},{2,10},{10... | collective-permute-start | bytes 4718600 | tf_op jit(solution)/shard_map/ppermute | solution.py:51
  295.7 33.3 %collective-permute-start.24 = (bf16[768,1024]{1,0:T(8,128)(2,1)}, bf16[768,1024]{1,0:T(8,128)(2,1)}, u32[]{:S(2)}, u32[]{:S(2)}) collective-permute-start(bf16[768,1024]{1,0:T(8,128)(2,1)} %pad_maximum_fusion.11.refs_0_.refs_4_), channel_id=1, source_target_pairs={{0,16},{8,24},{16,0},{24,8},{1,17},{9,25},{17,1},{25,9},{2,18},{10... | collective-permute-start | bytes 4718600 | tf_op jit(solution)/shard_map/ppermute | solution.py:55
  329.0 90.6 %collective-permute-start.25 = (bf16[768,1024]{1,0:T(8,128)(2,1)}, bf16[768,1024]{1,0:T(8,128)(2,1)}, u32[]{:S(2)}, u32[]{:S(2)}) collective-permute-start(bf16[768,1024]{1,0:T(8,128)(2,1)} %pad_maximum_fusion.11.refs_0_.refs_4_), channel_id=1, source_target_pairs={{0,8},{8,0},{16,24},{24,16},{1,9},{9,1},{17,25},{25,17},{2,10},{10... | collective-permute-start | bytes 4718600 | tf_op jit(solution)/shard_map/ppermute | solution.py:51
  330.6 122.0 %collective-permute-start.27 = (bf16[768,1024]{1,0:T(8,128)(2,1)}, bf16[768,1024]{1,0:T(8,128)(2,1)}, u32[]{:S(2)}, u32[]{:S(2)}) collective-permute-start(bf16[768,1024]{1,0:T(8,128)(2,1)} %pad_maximum_fusion.10.refs_0_), channel_id=1, source_target_pairs={{0,16},{8,24},{16,0},{24,8},{1,17},{9,25},{17,1},{25,9},{2,18},{10... | collective-permute-start | bytes 4718600 | tf_op jit(solution)/shard_map/ppermute | solution.py:55
  330.9 88.7 %collective-permute-start.26 = (bf16[768,1024]{1,0:T(8,128)(2,1)}, bf16[768,1024]{1,0:T(8,128)(2,1)}, u32[]{:S(2)}, u32[]{:S(2)}) collective-permute-start(bf16[768,1024]{1,0:T(8,128)(2,1)} %collective-permute-done.24.refs_2_.refs_6_), channel_id=1, source_target_pairs={{0,8},{8,0},{16,24},{24,16},{1,9},{9,1},{17,25},{25,17},{2,10},{10... | collective-permute-start | bytes 4718600 | tf_op jit(solution)/shard_map/ppermute | solution.py:51
  331.8 120.8 %collective-permute-start.28 = (bf16[768,1024]{1,0:T(8,128)(2,1)}, bf16[768,1024]{1,0:T(8,128)(2,1)}, u32[]{:S(2)}, u32[]{:S(2)}) collective-permute-start(bf16[768,1024]{1,0:T(8,128)(2,1)} %collective-permute-done.23.refs_1_), channel_id=1, source_target_pairs={{0,16},{8,24},{16,0},{24,8},{1,17},{9,25},{17,1},{25,9},{2,18},{10... | collective-permute-start | bytes 4718600 | tf_op jit(solution)/shard_map/ppermute | solution.py:55
  540.0 363.0 %reduce-scatter.5.cloned.1.call-start = ((), (), s32[]{:S(2)}) async-start(), calls=%async_computation.11 | async-start | bytes 14155776 | tf_op jit(solution)/shard_map/reduce_scatter | solution.py:936
  579.9 66.9 %collective-permute-start.29 = (bf16[2,768,1024]{2,1,0:T(8,128)(2,1)S(1)}, bf16[2,768,1024]{2,1,0:T(8,128)(2,1)S(1)}, u32[]{:S(2)}, u32[]{:S(2)}) collective-permute-start(bf16[2,768,1024]{2,1,0:T(8,128)(2,1)S(1)} %pad_maximum_fusion.4), channel_id=1, source_target_pairs={{0,8},{8,0},{16,24},{24,16},{1,9},{9,1},{17,25},{25,17},{2,10},{10... | collective-permute-start | bytes 9437192 | tf_op jit(solution)/shard_map/ppermute | solution.py:51
  580.6 68.5 %collective-permute-start.30 = (bf16[2,768,1024]{2,1,0:T(8,128)(2,1)S(1)}, bf16[2,768,1024]{2,1,0:T(8,128)(2,1)S(1)}, u32[]{:S(2)}, u32[]{:S(2)}) collective-permute-start(bf16[2,768,1024]{2,1,0:T(8,128)(2,1)S(1)} %pad_maximum_fusion.5), channel_id=1, source_target_pairs={{0,16},{8,24},{16,0},{24,8},{1,17},{9,25},{17,1},{25,9},{2,18},{10... | collective-permute-start | bytes 9437192 | tf_op jit(solution)/shard_map/ppermute | solution.py:55
  672.1 35.1 %collective-permute-start.31 = (bf16[768,1024]{1,0:T(8,128)(2,1)}, bf16[768,1024]{1,0:T(8,128)(2,1)}, u32[]{:S(2)}, u32[]{:S(2)}) collective-permute-start(bf16[768,1024]{1,0:T(8,128)(2,1)} %fusion.16), channel_id=1, source_target_pairs={{0,16},{8,24},{16,0},{24,8},{1,17},{9,25},{17,1},{25,9},{2,18},{10... | collective-permute-start | bytes 4718600 | tf_op jit(solution)/shard_map/ppermute | solution.py:55
  672.4 37.9 %collective-permute-start.32 = (bf16[768,1024]{1,0:T(8,128)(2,1)}, bf16[768,1024]{1,0:T(8,128)(2,1)}, u32[]{:S(2)}, u32[]{:S(2)}) collective-permute-start(bf16[768,1024]{1,0:T(8,128)(2,1)} %fusion.15), channel_id=1, source_target_pairs={{0,8},{8,0},{16,24},{24,16},{1,9},{9,1},{17,25},{25,17},{2,10},{10... | collective-permute-start | bytes 4718600 | tf_op jit(solution)/shard_map/ppermute | solution.py:51
  678.5 12.5 %all-to-all-start.1 = ((f32[8,384,2]{1,2,0:T(2,128)}), f32[8,384,2]{1,2,0:T(2,128)S(1)}, u32[]{:S(2)}, u32[]{:S(2)}) async-start(f32[8,384,2]{1,2,0:T(2,128)} %copy.294), calls=%async_computation.3 | async-start | bytes 49152 | tf_op jit(solution)/shard_map/all_to_all | solution.py:918
  685.1 292.7 %reduce-scatter.11.cloned.1.call-start = ((), (), s32[]{:S(2)}) async-start(), calls=%async_computation.14 | async-start | bytes 2359296 | tf_op jit(solution)/shard_map/reduce_scatter | solution.py:1008
  726.9 39.5 %collective-permute-start.33 = (bf16[192,2048]{1,0:T(8,128)(2,1)S(1)}, bf16[192,2048]{1,0:T(8,128)(2,1)S(1)}, u32[]{:S(2)}, u32[]{:S(2)}) collective-permute-start(bf16[192,2048]{1,0:T(8,128)(2,1)S(1)} %get-tuple-element.284), channel_id=1, source_target_pairs={{0,8},{8,0},{16,24},{24,16},{1,9},{9,1},{17,25},{25,17},{2,10},{10... | collective-permute-start | bytes 2359304 | tf_op jit(solution)/shard_map/ppermute | solution.py:51
  728.0 44.6 %collective-permute-start.34 = (bf16[192,2048]{1,0:T(8,128)(2,1)S(1)}, bf16[192,2048]{1,0:T(8,128)(2,1)S(1)}, u32[]{:S(2)}, u32[]{:S(2)}) collective-permute-start(bf16[192,2048]{1,0:T(8,128)(2,1)S(1)} %get-tuple-element.284), channel_id=1, source_target_pairs={{0,16},{8,24},{16,0},{24,8},{1,17},{9,25},{17,1},{25,9},{2,18},{10... | collective-permute-start | bytes 2359304 | tf_op jit(solution)/shard_map/ppermute | solution.py:55
  729.8 63.1 %collective-permute-start.36 = (bf16[192,2048]{1,0:T(8,128)(2,1)}, bf16[192,2048]{1,0:T(8,128)(2,1)S(1)}, u32[]{:S(2)}, u32[]{:S(2)}) collective-permute-start(bf16[192,2048]{1,0:T(8,128)(2,1)} %get-tuple-element.282), channel_id=1, source_target_pairs={{0,8},{8,0},{16,24},{24,16},{1,9},{9,1},{17,25},{25,17},{2,10},{10... | collective-permute-start | bytes 2359304 | tf_op jit(solution)/shard_map/ppermute | solution.py:51
  730.7 37.5 %collective-permute-start.37 = (bf16[192,2048]{1,0:T(8,128)(2,1)}, bf16[192,2048]{1,0:T(8,128)(2,1)S(1)}, u32[]{:S(2)}, u32[]{:S(2)}) collective-permute-start(bf16[192,2048]{1,0:T(8,128)(2,1)} %get-tuple-element.282), channel_id=1, source_target_pairs={{0,16},{8,24},{16,0},{24,8},{1,17},{9,25},{17,1},{25,9},{2,18},{10... | collective-permute-start | bytes 2359304 | tf_op jit(solution)/shard_map/ppermute | solution.py:55
  766.4 17.7 %collective-permute-start.35 = (bf16[192,2048]{1,0:T(8,128)(2,1)S(1)}, bf16[192,2048]{1,0:T(8,128)(2,1)S(1)}, u32[]{:S(2)}, u32[]{:S(2)}) collective-permute-start(bf16[192,2048]{1,0:T(8,128)(2,1)S(1)} %collective-permute-done.33), channel_id=1, source_target_pairs={{0,16},{8,24},{16,0},{24,8},{1,17},{9,25},{17,1},{25,9},{2,18},{10... | collective-permute-start | bytes 2359304 | tf_op jit(solution)/shard_map/ppermute | solution.py:55
  768.2 17.3 %collective-permute-start.38 = (bf16[192,2048]{1,0:T(8,128)(2,1)S(1)}, bf16[192,2048]{1,0:T(8,128)(2,1)S(1)}, u32[]{:S(2)}, u32[]{:S(2)}) collective-permute-start(bf16[192,2048]{1,0:T(8,128)(2,1)S(1)} %collective-permute-done.37), channel_id=1, source_target_pairs={{0,8},{8,0},{16,24},{24,16},{1,9},{9,1},{17,25},{25,17},{2,10},{10... | collective-permute-start | bytes 2359304 | tf_op jit(solution)/shard_map/ppermute | solution.py:51
  788.4 68.0 %collective-permute-start.39 = (bf16[2,768,1024]{2,1,0:T(8,128)(2,1)}, bf16[2,768,1024]{2,1,0:T(8,128)(2,1)}, u32[]{:S(2)}, u32[]{:S(2)}) collective-permute-start(bf16[2,768,1024]{2,1,0:T(8,128)(2,1)} %pad_maximum_fusion.6), channel_id=1, source_target_pairs={{0,8},{8,0},{16,24},{24,16},{1,9},{9,1},{17,25},{25,17},{2,10},{10... | collective-permute-start | bytes 9437192 | tf_op jit(solution)/shard_map/ppermute | solution.py:51
  792.4 67.7 %collective-permute-start.40 = (bf16[2,768,1024]{2,1,0:T(8,128)(2,1)}, bf16[2,768,1024]{2,1,0:T(8,128)(2,1)}, u32[]{:S(2)}, u32[]{:S(2)}) collective-permute-start(bf16[2,768,1024]{2,1,0:T(8,128)(2,1)} %pad_maximum_fusion.7), channel_id=1, source_target_pairs={{0,16},{8,24},{16,0},{24,8},{1,17},{9,25},{17,1},{25,9},{2,18},{10... | collective-permute-start | bytes 9437192 | tf_op jit(solution)/shard_map/ppermute | solution.py:55
  842.6 176.4 %reduce-scatter.9.cloned.1.call-start = ((), (), s32[]{:S(2)}) async-start(), calls=%async_computation.13 | async-start | bytes 7077888 | tf_op jit(solution)/shard_map/reduce_scatter | solution.py:1011
  860.1 5.4 collective-permute-start.41
  870.5 4.5 collective-permute-start.42
  903.0 32.9 %collective-permute-start.43 = (bf16[768,1024]{1,0:T(8,128)(2,1)}, bf16[768,1024]{1,0:T(8,128)(2,1)}, u32[]{:S(2)}, u32[]{:S(2)}) collective-permute-start(bf16[768,1024]{1,0:T(8,128)(2,1)} %add_convert_fusion.1), channel_id=1, source_target_pairs={{0,16},{8,24},{16,0},{24,8},{1,17},{9,25},{17,1},{25,9},{2,18},{10... | collective-permute-start | bytes 4718600 | tf_op jit(solution)/shard_map/ppermute | solution.py:55
  904.5 34.1 %collective-permute-start.44 = (bf16[768,1024]{1,0:T(8,128)(2,1)}, bf16[768,1024]{1,0:T(8,128)(2,1)}, u32[]{:S(2)}, u32[]{:S(2)}) collective-permute-start(bf16[768,1024]{1,0:T(8,128)(2,1)} %add_convert_fusion), channel_id=1, source_target_pairs={{0,8},{8,0},{16,24},{24,16},{1,9},{9,1},{17,25},{25,17},{2,10},{10... | collective-permute-start | bytes 4718600 | tf_op jit(solution)/shard_map/ppermute | solution.py:51
  939.3 31.2 %collective-permute-start.45 = (bf16[2,192,2048]{2,1,0:T(8,128)(2,1)S(1)}, bf16[2,192,2048]{2,1,0:T(8,128)(2,1)S(1)}, u32[]{:S(2)}, u32[]{:S(2)}) collective-permute-start(bf16[2,192,2048]{2,1,0:T(8,128)(2,1)S(1)} %pad_maximum_fusion.12), channel_id=1, source_target_pairs={{0,8},{8,0},{16,24},{24,16},{1,9},{9,1},{17,25},{25,17},{2,10},{10... | collective-permute-start | bytes 4718600 | tf_op jit(solution)/shard_map/ppermute | solution.py:51
  942.3 44.3 %collective-permute-start.47 = (bf16[2,192,2048]{2,1,0:T(8,128)(2,1)}, bf16[2,192,2048]{2,1,0:T(8,128)(2,1)}, u32[]{:S(2)}, u32[]{:S(2)}) collective-permute-start(bf16[2,192,2048]{2,1,0:T(8,128)(2,1)} %pad_maximum_fusion.13), channel_id=1, source_target_pairs={{0,16},{8,24},{16,0},{24,8},{1,17},{9,25},{17,1},{25,9},{2,18},{10... | collective-permute-start | bytes 4718600 | tf_op jit(solution)/shard_map/ppermute | solution.py:55
  971.7 16.8 %collective-permute-start.46 = (bf16[192,2048]{1,0:T(8,128)(2,1)}, bf16[192,2048]{1,0:T(8,128)(2,1)}, u32[]{:S(2)}, u32[]{:S(2)}) collective-permute-start(bf16[192,2048]{1,0:T(8,128)(2,1)} %fusion.19), channel_id=1, source_target_pairs={{0,16},{8,24},{16,0},{24,8},{1,17},{9,25},{17,1},{25,9},{2,18},{10... | collective-permute-start | bytes 2359304 | tf_op jit(solution)/shard_map/ppermute | solution.py:55
  974.1 10.7 %all-to-all-start.2 = ((f32[8,1,5120]{2,1,0:T(1,128)}), f32[8,1,5120]{2,1,0:T(1,128)S(1)}, u32[]{:S(2)}, u32[]{:S(2)}) async-start(f32[8,1,5120]{2,1,0:T(1,128)} %reshape.276), calls=%async_computation.6 | async-start | bytes 327680 | tf_op jit(solution)/shard_map/all_to_all | solution.py:135
  993.1 22.6 %collective-permute-start.48 = (bf16[192,2048]{1,0:T(8,128)(2,1)}, bf16[192,2048]{1,0:T(8,128)(2,1)}, u32[]{:S(2)}, u32[]{:S(2)}) collective-permute-start(bf16[192,2048]{1,0:T(8,128)(2,1)} %get-tuple-element.195), channel_id=1, source_target_pairs={{0,8},{8,0},{16,24},{24,16},{1,9},{9,1},{17,25},{25,17},{2,10},{10... | collective-permute-start | bytes 2359304 | tf_op jit(solution)/shard_map/ppermute | solution.py:51
  993.7 20.8 %collective-permute-start.52 = (f32[20,64]{1,0:T(8,128)S(1)}, f32[20,64]{1,0:T(8,128)S(1)}, u32[]{:S(2)}, u32[]{:S(2)}) collective-permute-start(f32[20,64]{1,0:T(8,128)S(1)} %bitcast.389), channel_id=1, source_target_pairs={{0,24},{8,16},{16,8},{24,0},{1,25},{9,17},{17,9},{25,1},{2,26},{10... | collective-permute-start | bytes 15368 | tf_op jit(solution)/shard_map/ppermute | solution.py:59
  995.8 18.7 %collective-permute-start.53 = (f32[20,64]{1,0:T(8,128)S(1)}, f32[20,64]{1,0:T(8,128)S(1)}, u32[]{:S(2)}, u32[]{:S(2)}) collective-permute-start(f32[20,64]{1,0:T(8,128)S(1)} %bitcast.390), channel_id=1, source_target_pairs={{0,16},{8,24},{16,0},{24,8},{1,17},{9,25},{17,1},{25,9},{2,18},{10... | collective-permute-start | bytes 15368 | tf_op jit(solution)/shard_map/ppermute | solution.py:55
  996.8 17.7 %collective-permute-start.54 = (f32[20,64]{1,0:T(8,128)S(1)}, f32[20,64]{1,0:T(8,128)S(1)}, u32[]{:S(2)}, u32[]{:S(2)}) collective-permute-start(f32[20,64]{1,0:T(8,128)S(1)} %bitcast.391), channel_id=1, source_target_pairs={{0,8},{8,0},{16,24},{24,16},{1,9},{9,1},{17,25},{25,17},{2,10},{10... | collective-permute-start | bytes 15368 | tf_op jit(solution)/shard_map/ppermute | solution.py:51
  1020.5 10.1 collective-permute-start.49
  1022.6 8.0 collective-permute-start.50
  1023.6 7.1 collective-permute-start.51
  (106 other events, 1255.5 us)
Sparse Core Ops, SparseCore 0:
  9.6 31.7 all-gather.4
  43.6 68.5 all-gather.6
  113.9 115.3 all-gather.10
  249.0 117.0 all-gather.8
  540.1 136.2 reduce-scatter.6
  678.5 127.9 reduce-scatter.4
  842.7 33.1 reduce-scatter.10
  903.1 68.2 reduce-scatter.8

commit v9 on v8

--- a/solution.py
+++ b/solution.py
@@ -132,8 +132,14 @@
     count, width = values.shape
     parts = values.reshape(count, ctx_size, exp_size, width // (ctx_size * exp_size))
     parts = jnp.transpose(parts, (2, 1, 0, 3))
-    parts = lax.all_to_all(parts, "exp", split_axis=0, concat_axis=0, tiled=True)
-    parts = jnp.sum(after(parts, *others), axis=0)
+    exp_index, step = lax.axis_index("exp"), exp_size // 2
+    while step:
+        upper = (exp_index // step) % 2
+        kept = lax.dynamic_slice_in_dim(parts, upper * step, step, 0)
+        sent = lax.dynamic_slice_in_dim(parts, (1 - upper) * step, step, 0)
+        parts = kept + lax.ppermute(sent, "exp", [(i, i ^ step) for i in range(exp_size)])
+        step //= 2
+    parts = after(parts[0], *others)
     return jnp.sum(exchange(parts, me), axis=0)
 
 
@@ -256,6 +262,8 @@
     else:
         ahead, direct = scatter_ahead(take, me), scatter_direct(take, me)
     sent = scatter_last_payload(take, me, ahead)
+    if joined:
+        sent = after_all(sent)
     last = send_y(sent[0]), send_x(sent[1])
     return jnp.concatenate(scatter_end(take, me, direct, last), axis=0), first, sent, last
 
@@ -645,13 +653,12 @@
     )(*tables[:3], ids, tables[3], hidden, router, raw, *parts)
 
 
-def combine_kernel(experts, start_ref, more_ref, wide_ref, pos_ref, *refs):
-    rows_refs, share_refs = refs[:experts], refs[experts : 2 * experts]
-    out_ref, own_ref, acc_ref = refs[2 * experts :]
+def combine_kernel(experts, shared, start_ref, more_ref, wide_ref, id_ref, pos_ref, *refs):
+    rows_refs, share_refs = refs[:experts], refs[experts:-2]
+    out_ref, acc_ref = refs[-2:]
     i = pl.program_id(0)
     span = lax.broadcasted_iota(jnp.int32, (TILE, TILE), 1)
-    wide_span = lax.broadcasted_iota(jnp.int32, (TILE, 384), 1)
-    last = rows_refs[0].shape[0] - TILE
+    last, width = rows_refs[0].shape[0] - TILE, rows_refs[0].shape[1]
 
     def window(e, j):
         base = start_ref[e, i] + j * TILE
@@ -662,36 +669,44 @@
 
     acc_ref[...] = sum(window(e, 0) for e in range(experts))
     for e in range(experts):
-        wide = pl.multiple_of(wide_ref[e, i], 128)
-        match = pos_ref[:, e : e + 1] - wide == wide_span
-        share = share_refs[e][:, pl.ds(wide, 384)]
-        own_ref[:, e : e + 1] = jnp.sum(jnp.where(match, share, 0.0), axis=1, keepdims=True)
 
         @pl.when(more_ref[e, i] > 0)
         def _():
             acc_ref[...] += window(e, 1)
 
-    out_ref[...] = acc_ref[...].astype(BF)
-
-
-def combine_rows(tables, rows, shares):
+    out_ref[:, :width] = acc_ref[...].astype(BF)
+    if shared:
+        wide_span = lax.broadcasted_iota(jnp.int32, (TILE, 384), 1)
+        column = lax.broadcasted_iota(jnp.int32, (TILE, shared), 1)
+        extra = jnp.zeros((TILE, shared), F32)
+        for e in range(experts):
+            wide = pl.multiple_of(wide_ref[e, i], 128)
+            match = pos_ref[:, e : e + 1] - wide == wide_span
+            share = share_refs[e][:, pl.ds(wide, 384)]
+            own = jnp.sum(jnp.where(match, share, 0.0), axis=1, keepdims=True)
+            head = own.astype(BF).astype(F32)
+            first = 2 * (id_ref[0] + e)
+            extra += jnp.where(column == first, head, 0.0)
+            extra += jnp.where(column == first + 1, own - head, 0.0)
+        out_ref[:, width:] = extra.astype(BF)
+
+
+def combine_rows(tables, ids, rows, shares=()):
     experts, (capacity, width) = len(rows), rows[0].shape
     total = tables[3].shape[0]
+    shared = 128 if shares else 0
     once = lambda shape: pl.BlockSpec(shape, lambda i, *_: (0, 0), pipeline_mode=pl.Buffered(1))
     tile = lambda n: pl.BlockSpec((TILE, n), lambda i, *_: (i, 0))
     return pl.pallas_call(
-        functools.partial(combine_kernel, experts),
-        out_shape=[
-            jax.ShapeDtypeStruct((total, width), BF),
-            jax.ShapeDtypeStruct((total, experts), F32),
-        ],
+        functools.partial(combine_kernel, experts, shared),
+        out_shape=jax.ShapeDtypeStruct((total, width + shared), BF),
         grid_spec=pltpu.PrefetchScalarGridSpec(
-            num_scalar_prefetch=3,
+            num_scalar_prefetch=4,
             grid=(total // TILE,),
             in_specs=[tile(experts)]
             + [once((capacity, width))] * experts
-            + [once((1, capacity))] * experts,
-            out_specs=[tile(width), tile(experts)],
+            + [once((1, capacity))] * len(shares),
+            out_specs=tile(width + shared),
             scratch_shapes=[pltpu.VMEM((TILE, width), F32)],
         ),
         compiler_params=pltpu.CompilerParams(vmem_limit_bytes=48 << 20),
@@ -700,7 +715,7 @@
             bytes_accessed=2 * (experts * capacity + total) * width,
             transcendentals=0,
         ),
-    )(*tables, *rows, *shares)
+    )(*tables[:3], ids, tables[3], *rows, *shares)
 
 
 def local(
@@ -894,7 +909,7 @@
             expert_rows(row_tables[e], e, ids, hidden_all, router_full, parts, backs[e][1])
         )
     shares = [m[4].reshape(1, capacity) for m in made]
-    grad_two_part, share_token = combine_rows(token_tables, [m[3] for m in made], shares)
+    grad_two_part = combine_rows(token_tables, ids, [m[3] for m in made], shares)
     grad_two = lax.psum_scatter(grad_two_part, "exp", scatter_dimension=0, tiled=True)
     def weight_grads(e, *others):
         rows, hidden, grad_hidden = after_all(made[e][:3], *others)
@@ -915,14 +930,6 @@
         ).astype(BF)
         for e in every
     ]
-    share_back = lax.all_to_all(
-        after(share_token, *results).reshape(exp_size, tok_rows, own_experts),
-        "exp",
-        split_axis=0,
-        concat_axis=0,
-        tiled=True,
-    )
-    grad_prob = jnp.swapaxes(share_back, 0, 1).reshape(tok_rows, experts)
     if ctx_size == 4:
         ahead, direct = split_sums((send_x(payload[0]), send_y(payload[1])))
         last = scatter_last_payload(take, me, ahead)
@@ -930,12 +937,16 @@
         last = send_y(last[0]), send_x(last[1])
     else:
         direct, last = scatter_expert_first(expert_grads[0], me), ()
-    mixture_part, unused = combine_rows(token_tables, results, shares)
+    mixture_part = combine_rows(token_tables, ids, results)
     directs, lasts = [direct], [last]
 
     mixture = lax.psum_scatter(mixture_part, "exp", scatter_dimension=0, tiled=True)
     output = (middle + mixture.astype(F32)).astype(BF)
     grad_two = after(grad_two, mixture_part).astype(F32)
+    grad_prob = jnp.sum(
+        grad_two[:, D : D + 2 * experts].reshape(tok_rows, experts, 2), axis=2
+    )
+    grad_two = grad_two[:, :D]
     grad_logits = (
         router_prob * (grad_prob - jnp.sum(router_prob * grad_prob, axis=-1, keepdims=True))
     ).astype(BF)

time: 1040 us -> 1030 us (level)
  starting transfers between devices: 72.5 us -> 86.3 us
    ppermute x26, waiting for transfers between devices: 156 us -> 128 us  [send_x(): return lax.ppermute(value, 'ctx', X_PAIRS)]
    ppermute x26, waiting for transfers between devices: 96.7 us -> 113 us  [send_y(): return lax.ppermute(value, 'ctx', Y_PAIRS)]
    ppermute x0 -> x3, waiting for transfers between devices: none -> 15.1 us  [sum_to_rows(): lax.ppermute(sent, 'exp', [(i, i ^ step) for i in range(exp_size)])]
    ppermute x0 -> x3, starting transfers between devices: none -> 15 us  [sum_to_rows(): lax.ppermute(sent, 'exp', [(i, i ^ step) for i in range(exp_size)])]
    all_to_all x2 -> x0, waiting for transfers between devices: 11.2 us -> none  [the longest x1 5.87 us: local(): lax.all_to_all(after(share_token, *results).reshape(exp_size, tok_rows, o...]
    unnamed x211 -> x223, local copies, waits for them, and re-layouts: 31.6 us -> 28.3 us
  transfers between devices with their start and end apart: 66 -> 67, of which waited for: 31 -> 29; matrix products, arithmetic and copies ran while one was open for 34% -> 34% of each run, Pallas kernels for 18% -> 19%
where the time goes in v9:
time: 1030 us
  waiting for transfers between devices  274 us (27%)
  Pallas kernels  261 us (25%)
  matrix products  160 us (16%)
  other arithmetic  123 us (12%)
  local copies, waits for them, and re-layouts  103 us (10%)
  starting transfers between devices  86.3 us (8%)
  between operations  21.8 us (2%)
    ppermute x26, waiting for transfers between devices, send_x(): return lax.ppermute(value, 'ctx', X_PAIRS)  128 us
    ppermute x26, waiting for transfers between devices, send_y(): return lax.ppermute(value, 'ctx', Y_PAIRS)  113 us
    pallas_call x2, Pallas kernels, expert_rows(): pl.pallas_call(functools.partial(expert_kernel, own), out_shape=[made(wid...  110 us
    pallas_call x2, Pallas kernels, back_rows(): pl.pallas_call(back_rows_kernel, out_shape=[jax.ShapeDtypeStruct((capacit...  54.3 us
    dot_general x2, matrix products, weight_grads(): lax.dot_general(rows, grad_hidden, TN, preferred_element_type=F32)  45 us
    pallas_call x2, Pallas kernels, combine_rows(): pl.pallas_call(functools.partial(combine_kernel, experts, shared), out_sh...  40 us
    ppermute x26, starting transfers between devices, send_x(): return lax.ppermute(value, 'ctx', X_PAIRS)  31.2 us
    pallas_call x1, Pallas kernels, attend_back(): pl.pallas_call(functools.partial(attend_back_kernel, tiles, 1.0 / math.sq...  30 us
  transfers between devices with their start and end apart: 67, of which 29 were waited for; matrix products, arithmetic and copies ran while one was open for 34% of the time, Pallas kernels for 19%

profile of v9, /device:TPU:0, one launch (start us, length us, event | category | flops | bytes accessed | tf_op | source)
XLA Modules:
  0.0 1028.5 jit_solution(6023518586865367502)
XLA Ops:
  17.2 4.0 collective-permute-start.6
  21.8 5.5 collective-permute-done.6
  27.3 3.7 collective-permute-done.7
  32.7 8.8 all-gather.5.cloned.1.call-done
  44.1 3.5 broadcast.182.clone
  63.1 6.8 collective-permute-done
  71.4 16.8 %collective-permute-done.4 = bf16[192,2048]{1,0:T(8,128)(2,1)S(1)} collective-permute-done((bf16[192,2048]{1,0:T(8,128)(2,1)}, bf16[192,2048]{1,0:T(8,128)(2,1)S(1)}, u32[]{:S(2)}, u32[]{:S(2)}) %collective-permute-start.4) | collective-permute-done | bytes 786464 | tf_op jit(solution)/shard_map/ppermute | solution.py:55
  90.2 2.7 constant_dynamic-update-slice_fusion.15
  95.1 8.9 collective-permute-done.2
  113.9 4.1 fusion.5
  121.2 6.1 fusion.3
  127.4 12.2 %fusion.101.qp_ref.kp_ref.vp_ref = f32[1536,1664]{1,0:T(8,128)S(1)} fusion(bf16[1536,2048]{1,0:T(8,128)(2,1)S(1)} %fusion.3, bf16[2048,1664]{1,0:T(8,128)(2,1)S(1)} %bitcast.363), kind=kOutput, calls=%fused_computation.389 | convolution fusion | flops 10468982784 | bytes 23330816 | tf_op jit(solution)/shard_map/dot_general | solution.py:805
  141.8 2.8 fusion.27
  154.0 25.9 %shard_map.272 = (bf16[1536,512]{1,0:T(8,128)(2,1)S(1)}, bf16[1536,512]{1,0:T(8,128)(2,1)}, bf16[1536,512]{1,0:T(8,128)(2,1)}, bf16[1536,512]{1,0:T(8,128)(2,1)}) custom-call(f32[1536,1664]{1,0:T(8,128)} %copy-done.24, f32[1536,1664]{1,0:T(8,128)} %copy-done.24, f32[1536,1664]{1,0:T(8,128)} %copy-done.24, f32[1536,2]{1,0:T(8,128)S(1)} %fusion.86.root_ref.key_root_ref, ...), custom_call_target="tpu_custom_call" | custom-call | flops 3221225472 | bytes 15728640 | tf_op jit(solution)/shard_map/pallas_call | solution.py:355
  180.0 5.6 fusion.102
  190.2 17.5 %collective-permute-done.16 = bf16[192,2048]{1,0:T(8,128)(2,1)S(1)} collective-permute-done((bf16[192,2048]{1,0:T(8,128)(2,1)S(1)}, bf16[192,2048]{1,0:T(8,128)(2,1)S(1)}, u32[]{:S(2)}, u32[]{:S(2)}) %collective-permute-start.16) | collective-permute-done | bytes 786464 | tf_op jit(solution)/shard_map/ppermute | solution.py:51
  210.0 11.0 %collective-permute-done.15 = bf16[192,2048]{1,0:T(8,128)(2,1)S(1)} collective-permute-done((bf16[192,2048]{1,0:T(8,128)(2,1)S(1)}, bf16[192,2048]{1,0:T(8,128)(2,1)S(1)}, u32[]{:S(2)}, u32[]{:S(2)}) %collective-permute-start.15) | collective-permute-done | bytes 786464 | tf_op jit(solution)/shard_map/ppermute | solution.py:51
  221.0 7.0 collective-permute-done.17
  230.1 7.2 collective-permute-done.18
  237.3 7.3 collective-permute-done.20
  253.3 3.7 all-to-all-start
  257.6 2.6 pad_maximum_fusion.10.refs_0_
  264.0 6.7 collective-permute-done.21.refs_3_
  270.7 3.9 collective-permute-done.22.refs_3_.refs_7_
  276.3 14.7 %select_reduce_fusion = s32[2,2048]{1,0:T(2,128)S(1)} fusion(s32[2,3072]{1,0:T(2,128)S(1)} %copy.272, pred[2,3072]{1,0:T(4,128)(4,1)S(1)} %bitcast.370), kind=kLoop, calls=%fused_computation | loop fusion | flops 50327552 | bytes 47104 | tf_op jit(solution)/shard_map/reduce_max | solution.py:868
  300.1 25.5 %collective-permute-done.23.refs_1_ = bf16[768,1024]{1,0:T(8,128)(2,1)} collective-permute-done((bf16[768,1024]{1,0:T(8,128)(2,1)}, bf16[768,1024]{1,0:T(8,128)(2,1)}, u32[]{:S(2)}, u32[]{:S(2)}) %collective-permute-start.23) | collective-permute-done | bytes 1572896 | tf_op jit(solution)/shard_map/ppermute | solution.py:51
  335.2 29.1 %shard_map.273 = (bf16[2048,2048]{1,0:T(8,128)(2,1)}, f32[2048,1024]{1,0:T(8,128)}, bf16[1024,2048]{1,0:T(8,128)(2,1)}) custom-call(s32[1]{0:T(128)} %get-tuple-element.323.tiles_ref, s32[8]{0:T(128)S(1)} %get-tuple-element.321.low_ref, s32[8]{0:T(128)S(1)} %get-tuple-element.319.windows_ref, s32[1]{0:T(128)} %bitcast.34.me_ref, s32[2048,1]{1,0:T(8,128)S(1)} %copy-done.8, ...), custom_call_target="tpu_custom_call" | custom-call | flops 11274289152 | bytes 37748736 | tf_op jit(solution)/shard_map/pallas_call | solution.py:532
  366.9 62.7 %shard_map.274 = (bf16[2048,2048]{1,0:T(8,128)(2,1)}, bf16[2048,1024]{1,0:T(8,128)(2,1)}, bf16[2048,2048]{1,0:T(8,128)(2,1)}, bf16[2048,2048]{1,0:T(8,128)(2,1)}, f32[2048,1]{1,0:T(8,128)}) custom-call(s32[1]{0:T(128)} %get-tuple-element.323.tiles_ref, s32[8]{0:T(128)} %copy-done.14, s32[8]{0:T(128)} %copy-done.15, s32[2]{0:T(128)} %pad_add_fusion.ids_ref.id_ref, ...), custom_call_target="tpu_custom_call" | custom-call | flops 30601641984 | bytes 58720256 | tf_op jit(solution)/shard_map/pallas_call | solution.py:632
  431.2 25.2 %shard_map.275 = (bf16[2048,2048]{1,0:T(8,128)(2,1)}, f32[2048,1024]{1,0:T(8,128)}, bf16[1024,2048]{1,0:T(8,128)(2,1)}) custom-call(s32[1]{0:T(128)} %get-tuple-element.322.tiles_ref, s32[8]{0:T(128)S(1)} %get-tuple-element.320.low_ref, s32[8]{0:T(128)S(1)} %get-tuple-element.318.windows_ref, s32[1]{0:T(128)} %bitcast.34.me_ref, ...), custom_call_target="tpu_custom_call" | custom-call | flops 11274289152 | bytes 37748736 | tf_op jit(solution)/shard_map/pallas_call | solution.py:532
  456.4 47.8 %shard_map.276 = (bf16[2048,2048]{1,0:T(8,128)(2,1)}, bf16[2048,1024]{1,0:T(8,128)(2,1)}, bf16[2048,2048]{1,0:T(8,128)(2,1)}, bf16[2048,2048]{1,0:T(8,128)(2,1)}, f32[2048,1]{1,0:T(8,128)}) custom-call(s32[1]{0:T(128)} %get-tuple-element.322.tiles_ref, s32[8]{0:T(128)} %copy-done.12, s32[8]{0:T(128)} %copy-done.13, s32[2]{0:T(128)} %pad_add_fusion.ids_ref.id_ref, ...), custom_call_target="tpu_custom_call" | custom-call | flops 30601641984 | bytes 58720256 | tf_op jit(solution)/shard_map/pallas_call | solution.py:632
  505.8 21.4 %shard_map.277 = bf16[3072,2176]{1,0:T(8,128)(2,1)} custom-call(s32[2,12]{1,0:T(2,128)S(1)} %copy.280.start_ref, s32[2,12]{1,0:T(2,128)S(1)} %copy.281.more_ref, s32[2,12]{1,0:T(2,128)S(1)} %copy.282.wide_ref, s32[2]{0:T(128)S(1)} %copy-done.11, s32[3072,2]{1,0:T(8,128)S(1)} %broadcast_select_fusion.pos_ref, bf16[2048,2048]{1,0:T(8,128)(2,1)} %get-tuple-element.109.refs_0_, ...), custom_call_target="tpu_custom_call" | custom-call | flops 6442450944 | bytes 29360128 | tf_op jit(solution)/shard_map/pallas_call | solution.py:700
  527.4 12.9 %convolution_convert_fusion.6 = bf16[1024,2048]{1,0:T(8,128)(2,1)S(1)} fusion(bf16[2048,1024]{1,0:T(8,128)(2,1)} %get-tuple-element.125, bf16[2048,2048]{1,0:T(8,128)(2,1)} %get-tuple-element.124), kind=kOutput, calls=%fused_computation.25 | convolution fusion | flops 8592031744 | bytes 16777216 | tf_op jit(solution)/shard_map/dot_general | solution.py:918
  541.5 22.4 %convolution_convert_fusion.4 = bf16[2048,2048]{1,0:T(8,128)(2,1)S(1)} fusion(bf16[2048,2048]{1,0:T(8,128)(2,1)} %get-tuple-element.121, bf16[2048,2048]{1,0:T(8,128)(2,1)} %get-tuple-element.122), kind=kOutput, calls=%fused_computation.14 | convolution fusion | flops 17184063488 | bytes 25165824 | tf_op jit(solution)/shard_map/dot_general | solution.py:917
  571.8 13.7 %convolution_convert_fusion.3.refs_0_ = bf16[2048,2048]{1,0:T(8,128)(2,1)} fusion(bf16[2048,1024]{1,0:T(8,128)(2,1)S(1)} %copy-done.104, bf16[1024,2048]{1,0:T(8,128)(2,1)} %get-tuple-element.126), kind=kOutput, calls=%fused_computation.13 | convolution fusion | flops 8594128896 | bytes 16777216 | tf_op jit(solution)/shard_map/dot_general | solution.py:928
  585.5 13.0 %convolution_convert_fusion.2.refs_1_ = bf16[2048,2048]{1,0:T(8,128)(2,1)} fusion(bf16[2048,1024]{1,0:T(8,128)(2,1)S(1)} %copy-done.103, bf16[1024,2048]{1,0:T(8,128)(2,1)} %get-tuple-element.129), kind=kOutput, calls=%fused_computation.12 | convolution fusion | flops 8594128896 | bytes 16777216 | tf_op jit(solution)/shard_map/dot_general | solution.py:928
  598.5 38.7 %collective-permute-done.29 = bf16[2,768,1024]{2,1,0:T(8,128)(2,1)S(1)} collective-permute-done((bf16[2,768,1024]{2,1,0:T(8,128)(2,1)S(1)}, bf16[2,768,1024]{2,1,0:T(8,128)(2,1)S(1)}, u32[]{:S(2)}, u32[]{:S(2)}) %collective-permute-start.29) | collective-permute-done | bytes 3145760 | tf_op jit(solution)/shard_map/ppermute | solution.py:51
  642.9 18.6 %shard_map.278 = bf16[3072,2048]{1,0:T(8,128)(2,1)} custom-call(s32[2,12]{1,0:T(2,128)S(1)} %copy.280.start_ref, s32[2,12]{1,0:T(2,128)S(1)} %copy.281.more_ref, s32[2,12]{1,0:T(2,128)S(1)} %copy.282.wide_ref, s32[2]{0:T(128)S(1)} %copy-done.11, s32[3072,2]{1,0:T(8,128)S(1)} %broadcast_select_fusion.pos_ref, ...), custom_call_target="tpu_custom_call" | custom-call | flops 6442450944 | bytes 29360128 | tf_op jit(solution)/shard_map/pallas_call | solution.py:700
  666.6 31.0 %collective-permute-done.31 = bf16[768,1024]{1,0:T(8,128)(2,1)S(1)} collective-permute-done((bf16[768,1024]{1,0:T(8,128)(2,1)}, bf16[768,1024]{1,0:T(8,128)(2,1)S(1)}, u32[]{:S(2)}, u32[]{:S(2)}) %collective-permute-start.31) | collective-permute-done | bytes 1572896 | tf_op jit(solution)/shard_map/ppermute | solution.py:55
  708.7 3.4 convert_element_type.313
  712.4 4.5 multiply_reduce_fusion.2
  720.4 3.8 collective-permute-start.33
  726.2 22.6 %convolution_convert_fusion.1 = bf16[2048,2048]{1,0:T(8,128)(2,1)S(1)} fusion(bf16[2048,2048]{1,0:T(8,128)(2,1)} %get-tuple-element.141, bf16[2048,2048]{1,0:T(8,128)(2,1)} %get-tuple-element.142), kind=kOutput, calls=%fused_computation.11 | convolution fusion | flops 17184063488 | bytes 25165824 | tf_op jit(solution)/shard_map/dot_general | solution.py:917
  748.9 12.7 %convolution_convert_fusion.5 = bf16[1024,2048]{1,0:T(8,128)(2,1)S(1)} fusion(bf16[2048,1024]{1,0:T(8,128)(2,1)} %get-tuple-element.143, bf16[2048,2048]{1,0:T(8,128)(2,1)} %get-tuple-element.144), kind=kOutput, calls=%fused_computation.24 | convolution fusion | flops 8592031744 | bytes 16777216 | tf_op jit(solution)/shard_map/dot_general | solution.py:918
  767.0 13.5 %collective-permute-done.35 = bf16[192,2048]{1,0:T(8,128)(2,1)S(1)} collective-permute-done((bf16[192,2048]{1,0:T(8,128)(2,1)S(1)}, bf16[192,2048]{1,0:T(8,128)(2,1)S(1)}, u32[]{:S(2)}, u32[]{:S(2)}) %collective-permute-start.35) | collective-permute-done | bytes 786464 | tf_op jit(solution)/shard_map/ppermute | solution.py:55
  790.8 5.0 convolution_convert_fusion.8.d_ref
  795.8 30.0 %shard_map.279 = (f32[1536,512]{1,0:T(8,128)}, f32[1536,512]{1,0:T(8,128)}, f32[1536,512]{1,0:T(8,128)}) custom-call(bf16[1536,512]{1,0:T(8,128)(2,1)S(1)} %copy-done.17, bf16[1536,512]{1,0:T(8,128)(2,1)S(1)} %copy-done.18, bf16[1536,512]{1,0:T(8,128)(2,1)} %get-tuple-element.135.v_ref, bf16[1536,512]{1,0:T(8,128)(2,1)} %convolution_convert_fusion.8.d_ref, ...), custom_call_target="tpu_custom_call" | custom-call | flops 8053063680 | bytes 15728640 | tf_op jit(solution)/shard_map/pallas_call | solution.py:444
  825.9 3.4 convert.34
  829.3 4.9 multiply_reduce_fusion.1
  834.2 4.6 convolution_convert_fusion.7
  839.3 13.3 %collective-permute-done.39 = bf16[2,768,1024]{2,1,0:T(8,128)(2,1)} collective-permute-done((bf16[2,768,1024]{2,1,0:T(8,128)(2,1)}, bf16[2,768,1024]{2,1,0:T(8,128)(2,1)}, u32[]{:S(2)}, u32[]{:S(2)}) %collective-permute-start.39) | collective-permute-done | bytes 3145760 | tf_op jit(solution)/shard_map/ppermute | solution.py:51
  852.6 3.4 collective-permute-done.40
  856.5 4.0 slice_bitcast_fusion.3
  865.7 4.0 slice_bitcast_fusion.2
  872.5 3.4 add_convert_fusion.1
  879.4 4.0 multiply_convert_fusion.1
  885.9 11.8 %convolution_convert_fusion = bf16[2048,1536]{1,0:T(8,128)(2,1)} fusion(bf16[1536,2048]{1,0:T(8,128)(2,1)S(1)} %bitcast.354, bf16[1536,1536]{1,0:T(8,128)(2,1)S(1)} %pad_maximum_fusion), kind=kOutput, calls=%fused_computation.10 | convolution fusion | flops 9666822144 | bytes 17301504 | tf_op jit(solution)/shard_map/dot_general | solution.py:1008
  900.7 16.6 %fusion.4 = (f32[2048]{0:T(1024)S(1)}, f32[1536,2048]{1,0:T(8,128)S(1)}) fusion(bf16[1536,2048]{1,0:T(8,128)(2,1)} %constant_dynamic-update-slice_fusion.9, f32[1536]{0:T(1024)S(1)} %copy-done.88, bf16[2048,1664]{1,0:T(8,128)(2,1)} %bitcast.360, bf16[1536,1536]{1,0:T(8,128)(2,1)} %copy-done.53), kind=kOutput, calls=%fused_computation.8 | convolution fusion | flops 10481563648 | bytes 30423040 | tf_op jit(solution)/shard_map/dot_general | solution.py:1005
  917.3 14.1 %collective-permute-done.43 = bf16[768,1024]{1,0:T(8,128)(2,1)} collective-permute-done((bf16[768,1024]{1,0:T(8,128)(2,1)}, bf16[768,1024]{1,0:T(8,128)(2,1)}, u32[]{:S(2)}, u32[]{:S(2)}) %collective-permute-start.43) | collective-permute-done | bytes 1572896 | tf_op jit(solution)/shard_map/ppermute | solution.py:55
  938.1 14.8 %collective-permute-start.52 = (f32[4,4,20,64]{3,0,1,2:T(4,128)}, f32[4,4,20,64]{3,0,1,2:T(4,128)}, u32[]{:S(2)}, u32[]{:S(2)}) collective-permute-start(f32[4,4,20,64]{3,0,1,2:T(4,128)} %dynamic-slice_bitcast_fusion.3), channel_id=1, source_target_pairs={{0,4},{1,5},{2,6},{3,7},{4,0},{5,1},{6,2},{7,3},{8,12},{9,13},{10,... | collective-permute-start | bytes 245768 | tf_op jit(solution)/shard_map/ppermute | solution.py:140
  953.0 8.3 collective-permute-done.52
  963.1 6.8 collective-permute-done.53
  972.9 3.0 fusion.18
  1000.1 3.2 fusion.20
  1010.2 6.5 fusion.13
  (539 shorter events, 220.4 us)
Async XLA Ops:
  7.2 34.3 %all-gather.5.cloned.1.call-start = ((), (), s32[]{:S(2)}) async-start(), calls=%async_computation.5 | async-start | bytes 2359296 | tf_op jit(solution)/shard_map/all_gather | solution.py:767
  7.9 110.1 %all-gather.7.cloned.1.call-start = ((), (), s32[]{:S(2)}) async-start(), calls=%async_computation.6 | async-start | bytes 7667712 | tf_op jit(solution)/shard_map/all_gather | solution.py:769
  17.2 10.1 collective-permute-start.6
  21.2 9.8 collective-permute-start.7
  21.7 9.6 collective-permute-start.8
  41.5 258.6 %all-gather.11.cloned.1.call-start = ((), (), s32[]{:S(2)}) async-start(), calls=%async_computation.8 | async-start | bytes 14155776 | tf_op jit(solution)/shard_map/all_gather | solution.py:783
  42.2 324.7 %all-gather.9.cloned.1.call-start = ((), (), s32[]{:S(2)}) async-start(), calls=%async_computation.7 | async-start | bytes 14155776 | tf_op jit(solution)/shard_map/all_gather | solution.py:896
  49.2 20.7 %collective-permute-start = (bf16[192,2048]{1,0:T(8,128)(2,1)}, bf16[192,2048]{1,0:T(8,128)(2,1)}, u32[]{:S(2)}, u32[]{:S(2)}) collective-permute-start(bf16[192,2048]{1,0:T(8,128)(2,1)} %get-tuple-element.285), channel_id=1, source_target_pairs={{0,8},{8,0},{16,24},{24,16},{1,9},{9,1},{17,25},{25,17},{2,10},{10... | collective-permute-start | bytes 2359304 | tf_op jit(solution)/shard_map/ppermute | solution.py:51
  50.7 42.2 %collective-permute-start.1 = (bf16[192,2048]{1,0:T(8,128)(2,1)}, bf16[192,2048]{1,0:T(8,128)(2,1)}, u32[]{:S(2)}, u32[]{:S(2)}) collective-permute-start(bf16[192,2048]{1,0:T(8,128)(2,1)} %get-tuple-element.285), channel_id=1, source_target_pairs={{0,16},{8,24},{16,0},{24,8},{1,17},{9,25},{17,1},{25,9},{2,18},{10... | collective-permute-start | bytes 2359304 | tf_op jit(solution)/shard_map/ppermute | solution.py:55
  52.1 57.6 %collective-permute-start.3 = (bf16[192,2048]{1,0:T(8,128)(2,1)}, bf16[192,2048]{1,0:T(8,128)(2,1)}, u32[]{:S(2)}, u32[]{:S(2)}) collective-permute-start(bf16[192,2048]{1,0:T(8,128)(2,1)} %get-tuple-element.283), channel_id=1, source_target_pairs={{0,8},{8,0},{16,24},{24,16},{1,9},{9,1},{17,25},{25,17},{2,10},{10... | collective-permute-start | bytes 2359304 | tf_op jit(solution)/shard_map/ppermute | solution.py:51
  52.7 35.4 %collective-permute-start.4 = (bf16[192,2048]{1,0:T(8,128)(2,1)}, bf16[192,2048]{1,0:T(8,128)(2,1)S(1)}, u32[]{:S(2)}, u32[]{:S(2)}) collective-permute-start(bf16[192,2048]{1,0:T(8,128)(2,1)} %get-tuple-element.283), channel_id=1, source_target_pairs={{0,16},{8,24},{16,0},{24,8},{1,17},{9,25},{17,1},{25,9},{2,18},{10... | collective-permute-start | bytes 2359304 | tf_op jit(solution)/shard_map/ppermute | solution.py:55
  69.9 34.1 %collective-permute-start.2 = (bf16[192,2048]{1,0:T(8,128)(2,1)}, bf16[192,2048]{1,0:T(8,128)(2,1)S(1)}, u32[]{:S(2)}, u32[]{:S(2)}) collective-permute-start(bf16[192,2048]{1,0:T(8,128)(2,1)} %collective-permute-done), channel_id=1, source_target_pairs={{0,16},{8,24},{16,0},{24,8},{1,17},{9,25},{17,1},{25,9},{2,18},{10... | collective-permute-start | bytes 2359304 | tf_op jit(solution)/shard_map/ppermute | solution.py:55
  88.1 17.6 %collective-permute-start.5 = (bf16[192,2048]{1,0:T(8,128)(2,1)S(1)}, bf16[192,2048]{1,0:T(8,128)(2,1)S(1)}, u32[]{:S(2)}, u32[]{:S(2)}) collective-permute-start(bf16[192,2048]{1,0:T(8,128)(2,1)S(1)} %collective-permute-done.4), channel_id=1, source_target_pairs={{0,8},{8,0},{16,24},{24,16},{1,9},{9,1},{17,25},{25,17},{2,10},{10... | collective-permute-start | bytes 2359304 | tf_op jit(solution)/shard_map/ppermute | solution.py:51
  105.8 34.4 %collective-permute-start.9 = (bf16[768,1024]{1,0:T(8,128)(2,1)}, bf16[768,1024]{1,0:T(8,128)(2,1)}, u32[]{:S(2)}, u32[]{:S(2)}) collective-permute-start(bf16[768,1024]{1,0:T(8,128)(2,1)} %get-tuple-element.97.refs_0_), channel_id=1, source_target_pairs={{0,8},{8,0},{16,24},{24,16},{1,9},{9,1},{17,25},{25,17},{2,10},{10... | collective-permute-start | bytes 4718600 | tf_op jit(solution)/shard_map/ppermute | solution.py:51
  106.3 33.9 %collective-permute-start.10 = (bf16[768,1024]{1,0:T(8,128)(2,1)S(1)}, bf16[768,1024]{1,0:T(8,128)(2,1)S(1)}, u32[]{:S(2)}, u32[]{:S(2)}) collective-permute-start(bf16[768,1024]{1,0:T(8,128)(2,1)S(1)} %get-tuple-element.96.refs_0_.refs_4_), channel_id=1, source_target_pairs={{0,16},{8,24},{16,0},{24,8},{1,17},{9,25},{17,1},{25,9},{2,18},{10... | collective-permute-start | bytes 4718600 | tf_op jit(solution)/shard_map/ppermute | solution.py:55
  151.9 33.7 %collective-permute-start.13 = (bf16[768,1024]{1,0:T(8,128)(2,1)S(1)}, bf16[768,1024]{1,0:T(8,128)(2,1)S(1)}, u32[]{:S(2)}, u32[]{:S(2)}) collective-permute-start(bf16[768,1024]{1,0:T(8,128)(2,1)S(1)} %copy-done.5), channel_id=1, source_target_pairs={{0,8},{8,0},{16,24},{24,16},{1,9},{9,1},{17,25},{25,17},{2,10},{10... | collective-permute-start | bytes 4718600 | tf_op jit(solution)/shard_map/ppermute | solution.py:51
  152.8 32.8 %collective-permute-start.14 = (bf16[768,1024]{1,0:T(8,128)(2,1)}, bf16[768,1024]{1,0:T(8,128)(2,1)S(1)}, u32[]{:S(2)}, u32[]{:S(2)}) collective-permute-start(bf16[768,1024]{1,0:T(8,128)(2,1)} %get-tuple-element.97.refs_0_), channel_id=1, source_target_pairs={{0,16},{8,24},{16,0},{24,8},{1,17},{9,25},{17,1},{25,9},{2,18},{10... | collective-permute-start | bytes 4718600 | tf_op jit(solution)/shard_map/ppermute | solution.py:55
  187.3 20.5 %collective-permute-start.16 = (bf16[192,2048]{1,0:T(8,128)(2,1)S(1)}, bf16[192,2048]{1,0:T(8,128)(2,1)S(1)}, u32[]{:S(2)}, u32[]{:S(2)}) collective-permute-start(bf16[192,2048]{1,0:T(8,128)(2,1)S(1)} %get-tuple-element.203), channel_id=1, source_target_pairs={{0,8},{8,0},{16,24},{24,16},{1,9},{9,1},{17,25},{25,17},{2,10},{10... | collective-permute-start | bytes 2359304 | tf_op jit(solution)/shard_map/ppermute | solution.py:51
  188.4 32.5 %collective-permute-start.15 = (bf16[192,2048]{1,0:T(8,128)(2,1)S(1)}, bf16[192,2048]{1,0:T(8,128)(2,1)S(1)}, u32[]{:S(2)}, u32[]{:S(2)}) collective-permute-start(bf16[192,2048]{1,0:T(8,128)(2,1)S(1)} %get-tuple-element.200), channel_id=1, source_target_pairs={{0,8},{8,0},{16,24},{24,16},{1,9},{9,1},{17,25},{25,17},{2,10},{10... | collective-permute-start | bytes 2359304 | tf_op jit(solution)/shard_map/ppermute | solution.py:51
  189.3 31.7 %collective-permute-start.19 = (bf16[192,2048]{1,0:T(8,128)(2,1)S(1)}, bf16[192,2048]{1,0:T(8,128)(2,1)S(1)}, u32[]{:S(2)}, u32[]{:S(2)}) collective-permute-start(bf16[192,2048]{1,0:T(8,128)(2,1)S(1)} %get-tuple-element.201), channel_id=1, source_target_pairs={{0,16},{8,24},{16,0},{24,8},{1,17},{9,25},{17,1},{25,9},{2,18},{10... | collective-permute-start | bytes 2359304 | tf_op jit(solution)/shard_map/ppermute | solution.py:55
  207.9 20.1 %collective-permute-start.17 = (bf16[192,2048]{1,0:T(8,128)(2,1)S(1)}, bf16[192,2048]{1,0:T(8,128)(2,1)S(1)}, u32[]{:S(2)}, u32[]{:S(2)}) collective-permute-start(bf16[192,2048]{1,0:T(8,128)(2,1)S(1)} %add_convert_fusion.4), channel_id=1, source_target_pairs={{0,16},{8,24},{16,0},{24,8},{1,17},{9,25},{17,1},{25,9},{2,18},{10... | collective-permute-start | bytes 2359304 | tf_op jit(solution)/shard_map/ppermute | solution.py:55
  208.9 28.4 %collective-permute-start.18 = (bf16[192,2048]{1,0:T(8,128)(2,1)S(1)}, bf16[192,2048]{1,0:T(8,128)(2,1)S(1)}, u32[]{:S(2)}, u32[]{:S(2)}) collective-permute-start(bf16[192,2048]{1,0:T(8,128)(2,1)S(1)} %get-tuple-element.202), channel_id=1, source_target_pairs={{0,16},{8,24},{16,0},{24,8},{1,17},{9,25},{17,1},{25,9},{2,18},{10... | collective-permute-start | bytes 2359304 | tf_op jit(solution)/shard_map/ppermute | solution.py:55
  228.6 15.9 %collective-permute-start.20 = (bf16[192,2048]{1,0:T(8,128)(2,1)S(1)}, bf16[192,2048]{1,0:T(8,128)(2,1)S(1)}, u32[]{:S(2)}, u32[]{:S(2)}) collective-permute-start(bf16[192,2048]{1,0:T(8,128)(2,1)S(1)} %get-tuple-element.199), channel_id=1, source_target_pairs={{0,8},{8,0},{16,24},{24,16},{1,9},{9,1},{17,25},{25,17},{2,10},{10... | collective-permute-start | bytes 2359304 | tf_op jit(solution)/shard_map/ppermute | solution.py:51
  249.5 21.2 %collective-permute-start.21 = (bf16[768,1024]{1,0:T(8,128)(2,1)}, bf16[768,1024]{1,0:T(8,128)(2,1)}, u32[]{:S(2)}, u32[]{:S(2)}) collective-permute-start(bf16[768,1024]{1,0:T(8,128)(2,1)} %collective-permute-done.9.refs_1_), channel_id=1, source_target_pairs={{0,16},{8,24},{16,0},{24,8},{1,17},{9,25},{17,1},{25,9},{2,18},{10... | collective-permute-start | bytes 4718600 | tf_op jit(solution)/shard_map/ppermute | solution.py:55
  251.9 22.6 %collective-permute-start.22 = (bf16[768,1024]{1,0:T(8,128)(2,1)S(1)}, bf16[768,1024]{1,0:T(8,128)(2,1)}, u32[]{:S(2)}, u32[]{:S(2)}) collective-permute-start(bf16[768,1024]{1,0:T(8,128)(2,1)S(1)} %copy-done.20), channel_id=1, source_target_pairs={{0,8},{8,0},{16,24},{24,16},{1,9},{9,1},{17,25},{25,17},{2,10},{10... | collective-permute-start | bytes 4718600 | tf_op jit(solution)/shard_map/ppermute | solution.py:51
  253.3 10.7 %all-to-all-start = ((s32[8,384,8]{1,2,0:T(8,128)}), s32[8,384,8]{1,2,0:T(8,128)S(1)}, u32[]{:S(2)}, u32[]{:S(2)}) async-start(s32[8,384,8]{1,2,0:T(8,128)} %broadcast_in_dim.55), calls=%async_computation | async-start | bytes 196608 | tf_op jit(solution)/shard_map/all_to_all | solution.py:776
  257.0 450.8 %reduce-scatter.7.cloned.1.call-start = ((), (), s32[]{:S(2)}) async-start(), calls=%async_computation.10 | async-start | bytes 15040512 | tf_op jit(solution)/shard_map/reduce_scatter | solution.py:913
  291.0 34.6 %collective-permute-start.23 = (bf16[768,1024]{1,0:T(8,128)(2,1)}, bf16[768,1024]{1,0:T(8,128)(2,1)}, u32[]{:S(2)}, u32[]{:S(2)}) collective-permute-start(bf16[768,1024]{1,0:T(8,128)(2,1)} %pad_maximum_fusion.10.refs_0_), channel_id=1, source_target_pairs={{0,8},{8,0},{16,24},{24,16},{1,9},{9,1},{17,25},{25,17},{2,10},{10... | collective-permute-start | bytes 4718600 | tf_op jit(solution)/shard_map/ppermute | solution.py:51
  292.5 33.2 %collective-permute-start.24 = (bf16[768,1024]{1,0:T(8,128)(2,1)}, bf16[768,1024]{1,0:T(8,128)(2,1)}, u32[]{:S(2)}, u32[]{:S(2)}) collective-permute-start(bf16[768,1024]{1,0:T(8,128)(2,1)} %pad_maximum_fusion.11.refs_0_.refs_4_), channel_id=1, source_target_pairs={{0,16},{8,24},{16,0},{24,8},{1,17},{9,25},{17,1},{25,9},{2,18},{10... | collective-permute-start | bytes 4718600 | tf_op jit(solution)/shard_map/ppermute | solution.py:55
  325.7 103.9 %collective-permute-start.25 = (bf16[768,1024]{1,0:T(8,128)(2,1)}, bf16[768,1024]{1,0:T(8,128)(2,1)}, u32[]{:S(2)}, u32[]{:S(2)}) collective-permute-start(bf16[768,1024]{1,0:T(8,128)(2,1)} %pad_maximum_fusion.11.refs_0_.refs_4_), channel_id=1, source_target_pairs={{0,8},{8,0},{16,24},{24,16},{1,9},{9,1},{17,25},{25,17},{2,10},{10... | collective-permute-start | bytes 4718600 | tf_op jit(solution)/shard_map/ppermute | solution.py:51
  327.4 129.0 %collective-permute-start.27 = (bf16[768,1024]{1,0:T(8,128)(2,1)}, bf16[768,1024]{1,0:T(8,128)(2,1)}, u32[]{:S(2)}, u32[]{:S(2)}) collective-permute-start(bf16[768,1024]{1,0:T(8,128)(2,1)} %pad_maximum_fusion.10.refs_0_), channel_id=1, source_target_pairs={{0,16},{8,24},{16,0},{24,8},{1,17},{9,25},{17,1},{25,9},{2,18},{10... | collective-permute-start | bytes 4718600 | tf_op jit(solution)/shard_map/ppermute | solution.py:55
  327.7 101.9 %collective-permute-start.26 = (bf16[768,1024]{1,0:T(8,128)(2,1)}, bf16[768,1024]{1,0:T(8,128)(2,1)}, u32[]{:S(2)}, u32[]{:S(2)}) collective-permute-start(bf16[768,1024]{1,0:T(8,128)(2,1)} %collective-permute-done.24.refs_2_.refs_6_), channel_id=1, source_target_pairs={{0,8},{8,0},{16,24},{24,16},{1,9},{9,1},{17,25},{25,17},{2,10},{10... | collective-permute-start | bytes 4718600 | tf_op jit(solution)/shard_map/ppermute | solution.py:51
  328.6 127.8 %collective-permute-start.28 = (bf16[768,1024]{1,0:T(8,128)(2,1)}, bf16[768,1024]{1,0:T(8,128)(2,1)}, u32[]{:S(2)}, u32[]{:S(2)}) collective-permute-start(bf16[768,1024]{1,0:T(8,128)(2,1)} %collective-permute-done.23.refs_1_), channel_id=1, source_target_pairs={{0,16},{8,24},{16,0},{24,8},{1,17},{9,25},{17,1},{25,9},{2,18},{10... | collective-permute-start | bytes 4718600 | tf_op jit(solution)/shard_map/ppermute | solution.py:55
  527.2 370.5 %reduce-scatter.5.cloned.1.call-start = ((), (), s32[]{:S(2)}) async-start(), calls=%async_computation.9 | async-start | bytes 14155776 | tf_op jit(solution)/shard_map/reduce_scatter | solution.py:943
  567.0 70.2 %collective-permute-start.29 = (bf16[2,768,1024]{2,1,0:T(8,128)(2,1)S(1)}, bf16[2,768,1024]{2,1,0:T(8,128)(2,1)S(1)}, u32[]{:S(2)}, u32[]{:S(2)}) collective-permute-start(bf16[2,768,1024]{2,1,0:T(8,128)(2,1)S(1)} %pad_maximum_fusion.4), channel_id=1, source_target_pairs={{0,8},{8,0},{16,24},{24,16},{1,9},{9,1},{17,25},{25,17},{2,10},{10... | collective-permute-start | bytes 9437192 | tf_op jit(solution)/shard_map/ppermute | solution.py:51
  569.8 69.5 %collective-permute-start.30 = (bf16[2,768,1024]{2,1,0:T(8,128)(2,1)S(1)}, bf16[2,768,1024]{2,1,0:T(8,128)(2,1)S(1)}, u32[]{:S(2)}, u32[]{:S(2)}) collective-permute-start(bf16[2,768,1024]{2,1,0:T(8,128)(2,1)S(1)} %pad_maximum_fusion.5), channel_id=1, source_target_pairs={{0,16},{8,24},{16,0},{24,8},{1,17},{9,25},{17,1},{25,9},{2,18},{10... | collective-permute-start | bytes 9437192 | tf_op jit(solution)/shard_map/ppermute | solution.py:55
  661.5 309.5 %reduce-scatter.11.cloned.1.call-start = ((), (), s32[]{:S(2)}) async-start(), calls=%async_computation.12 | async-start | bytes 2359296 | tf_op jit(solution)/shard_map/reduce_scatter | solution.py:1019
  661.6 36.0 %collective-permute-start.31 = (bf16[768,1024]{1,0:T(8,128)(2,1)}, bf16[768,1024]{1,0:T(8,128)(2,1)S(1)}, u32[]{:S(2)}, u32[]{:S(2)}) collective-permute-start(bf16[768,1024]{1,0:T(8,128)(2,1)} %fusion.16), channel_id=1, source_target_pairs={{0,16},{8,24},{16,0},{24,8},{1,17},{9,25},{17,1},{25,9},{2,18},{10... | collective-permute-start | bytes 4718600 | tf_op jit(solution)/shard_map/ppermute | solution.py:55
  662.1 38.1 %collective-permute-start.32 = (bf16[768,1024]{1,0:T(8,128)(2,1)}, bf16[768,1024]{1,0:T(8,128)(2,1)S(1)}, u32[]{:S(2)}, u32[]{:S(2)}) collective-permute-start(bf16[768,1024]{1,0:T(8,128)(2,1)} %fusion.15), channel_id=1, source_target_pairs={{0,8},{8,0},{16,24},{24,16},{1,9},{9,1},{17,25},{25,17},{2,10},{10... | collective-permute-start | bytes 4718600 | tf_op jit(solution)/shard_map/ppermute | solution.py:51
  720.4 41.2 %collective-permute-start.33 = (bf16[192,2048]{1,0:T(8,128)(2,1)S(1)}, bf16[192,2048]{1,0:T(8,128)(2,1)S(1)}, u32[]{:S(2)}, u32[]{:S(2)}) collective-permute-start(bf16[192,2048]{1,0:T(8,128)(2,1)S(1)} %get-tuple-element.282), channel_id=1, source_target_pairs={{0,8},{8,0},{16,24},{24,16},{1,9},{9,1},{17,25},{25,17},{2,10},{10... | collective-permute-start | bytes 2359304 | tf_op jit(solution)/shard_map/ppermute | solution.py:51
  724.2 42.7 %collective-permute-start.34 = (bf16[192,2048]{1,0:T(8,128)(2,1)S(1)}, bf16[192,2048]{1,0:T(8,128)(2,1)S(1)}, u32[]{:S(2)}, u32[]{:S(2)}) collective-permute-start(bf16[192,2048]{1,0:T(8,128)(2,1)S(1)} %get-tuple-element.282), channel_id=1, source_target_pairs={{0,16},{8,24},{16,0},{24,8},{1,17},{9,25},{17,1},{25,9},{2,18},{10... | collective-permute-start | bytes 2359304 | tf_op jit(solution)/shard_map/ppermute | solution.py:55
  724.2 65.1 %collective-permute-start.36 = (bf16[192,2048]{1,0:T(8,128)(2,1)}, bf16[192,2048]{1,0:T(8,128)(2,1)S(1)}, u32[]{:S(2)}, u32[]{:S(2)}) collective-permute-start(bf16[192,2048]{1,0:T(8,128)(2,1)} %get-tuple-element.280), channel_id=1, source_target_pairs={{0,8},{8,0},{16,24},{24,16},{1,9},{9,1},{17,25},{25,17},{2,10},{10... | collective-permute-start | bytes 2359304 | tf_op jit(solution)/shard_map/ppermute | solution.py:51
  724.2 37.6 %collective-permute-start.37 = (bf16[192,2048]{1,0:T(8,128)(2,1)}, bf16[192,2048]{1,0:T(8,128)(2,1)S(1)}, u32[]{:S(2)}, u32[]{:S(2)}) collective-permute-start(bf16[192,2048]{1,0:T(8,128)(2,1)} %get-tuple-element.280), channel_id=1, source_target_pairs={{0,16},{8,24},{16,0},{24,8},{1,17},{9,25},{17,1},{25,9},{2,18},{10... | collective-permute-start | bytes 2359304 | tf_op jit(solution)/shard_map/ppermute | solution.py:55
  761.6 18.8 %collective-permute-start.35 = (bf16[192,2048]{1,0:T(8,128)(2,1)S(1)}, bf16[192,2048]{1,0:T(8,128)(2,1)S(1)}, u32[]{:S(2)}, u32[]{:S(2)}) collective-permute-start(bf16[192,2048]{1,0:T(8,128)(2,1)S(1)} %collective-permute-done.33), channel_id=1, source_target_pairs={{0,16},{8,24},{16,0},{24,8},{1,17},{9,25},{17,1},{25,9},{2,18},{10... | collective-permute-start | bytes 2359304 | tf_op jit(solution)/shard_map/ppermute | solution.py:55
  761.9 18.9 %collective-permute-start.38 = (bf16[192,2048]{1,0:T(8,128)(2,1)S(1)}, bf16[192,2048]{1,0:T(8,128)(2,1)S(1)}, u32[]{:S(2)}, u32[]{:S(2)}) collective-permute-start(bf16[192,2048]{1,0:T(8,128)(2,1)S(1)} %collective-permute-done.37), channel_id=1, source_target_pairs={{0,8},{8,0},{16,24},{24,16},{1,9},{9,1},{17,25},{25,17},{2,10},{10... | collective-permute-start | bytes 2359304 | tf_op jit(solution)/shard_map/ppermute | solution.py:51
  783.7 68.9 %collective-permute-start.39 = (bf16[2,768,1024]{2,1,0:T(8,128)(2,1)}, bf16[2,768,1024]{2,1,0:T(8,128)(2,1)}, u32[]{:S(2)}, u32[]{:S(2)}) collective-permute-start(bf16[2,768,1024]{2,1,0:T(8,128)(2,1)} %pad_maximum_fusion.6), channel_id=1, source_target_pairs={{0,8},{8,0},{16,24},{24,16},{1,9},{9,1},{17,25},{25,17},{2,10},{10... | collective-permute-start | bytes 9437192 | tf_op jit(solution)/shard_map/ppermute | solution.py:51
  787.6 68.4 %collective-permute-start.40 = (bf16[2,768,1024]{2,1,0:T(8,128)(2,1)}, bf16[2,768,1024]{2,1,0:T(8,128)(2,1)}, u32[]{:S(2)}, u32[]{:S(2)}) collective-permute-start(bf16[2,768,1024]{2,1,0:T(8,128)(2,1)} %pad_maximum_fusion.7), channel_id=1, source_target_pairs={{0,16},{8,24},{16,0},{24,8},{1,17},{9,25},{17,1},{25,9},{2,18},{10... | collective-permute-start | bytes 9437192 | tf_op jit(solution)/shard_map/ppermute | solution.py:55
  838.9 166.1 %reduce-scatter.9.cloned.1.call-start = ((), (), s32[]{:S(2)}) async-start(), calls=%async_computation.11 | async-start | bytes 7077888 | tf_op jit(solution)/shard_map/reduce_scatter | solution.py:1022
  856.0 5.7 collective-permute-start.41
  864.7 5.0 collective-permute-start.42
  898.2 33.2 %collective-permute-start.43 = (bf16[768,1024]{1,0:T(8,128)(2,1)}, bf16[768,1024]{1,0:T(8,128)(2,1)}, u32[]{:S(2)}, u32[]{:S(2)}) collective-permute-start(bf16[768,1024]{1,0:T(8,128)(2,1)} %add_convert_fusion.1), channel_id=1, source_target_pairs={{0,16},{8,24},{16,0},{24,8},{1,17},{9,25},{17,1},{25,9},{2,18},{10... | collective-permute-start | bytes 4718600 | tf_op jit(solution)/shard_map/ppermute | solution.py:55
  899.2 33.5 %collective-permute-start.44 = (bf16[768,1024]{1,0:T(8,128)(2,1)}, bf16[768,1024]{1,0:T(8,128)(2,1)}, u32[]{:S(2)}, u32[]{:S(2)}) collective-permute-start(bf16[768,1024]{1,0:T(8,128)(2,1)} %add_convert_fusion), channel_id=1, source_target_pairs={{0,8},{8,0},{16,24},{24,16},{1,9},{9,1},{17,25},{25,17},{2,10},{10... | collective-permute-start | bytes 4718600 | tf_op jit(solution)/shard_map/ppermute | solution.py:51
  933.4 39.5 %collective-permute-start.46 = (bf16[2,192,2048]{2,1,0:T(8,128)(2,1)S(1)}, bf16[2,192,2048]{2,1,0:T(8,128)(2,1)}, u32[]{:S(2)}, u32[]{:S(2)}) collective-permute-start(bf16[2,192,2048]{2,1,0:T(8,128)(2,1)S(1)} %pad_maximum_fusion.13), channel_id=1, source_target_pairs={{0,16},{8,24},{16,0},{24,8},{1,17},{9,25},{17,1},{25,9},{2,18},{10... | collective-permute-start | bytes 4718600 | tf_op jit(solution)/shard_map/ppermute | solution.py:55
  934.1 38.8 %collective-permute-start.45 = (bf16[2,192,2048]{2,1,0:T(8,128)(2,1)S(1)}, bf16[2,192,2048]{2,1,0:T(8,128)(2,1)}, u32[]{:S(2)}, u32[]{:S(2)}) collective-permute-start(bf16[2,192,2048]{2,1,0:T(8,128)(2,1)S(1)} %pad_maximum_fusion.12), channel_id=1, source_target_pairs={{0,8},{8,0},{16,24},{24,16},{1,9},{9,1},{17,25},{25,17},{2,10},{10... | collective-permute-start | bytes 4718600 | tf_op jit(solution)/shard_map/ppermute | solution.py:51
  938.1 23.1 %collective-permute-start.52 = (f32[4,4,20,64]{3,0,1,2:T(4,128)}, f32[4,4,20,64]{3,0,1,2:T(4,128)}, u32[]{:S(2)}, u32[]{:S(2)}) collective-permute-start(f32[4,4,20,64]{3,0,1,2:T(4,128)} %dynamic-slice_bitcast_fusion.3), channel_id=1, source_target_pairs={{0,4},{1,5},{2,6},{3,7},{4,0},{5,1},{6,2},{7,3},{8,12},{9,13},{10,... | collective-permute-start | bytes 245768 | tf_op jit(solution)/shard_map/ppermute | solution.py:140
  963.0 6.9 collective-permute-start.53
  976.0 24.1 %collective-permute-start.47 = (bf16[192,2048]{1,0:T(8,128)(2,1)S(1)}, bf16[192,2048]{1,0:T(8,128)(2,1)S(1)}, u32[]{:S(2)}, u32[]{:S(2)}) collective-permute-start(bf16[192,2048]{1,0:T(8,128)(2,1)S(1)} %get-tuple-element.152), channel_id=1, source_target_pairs={{0,16},{8,24},{16,0},{24,8},{1,17},{9,25},{17,1},{25,9},{2,18},{10... | collective-permute-start | bytes 2359304 | tf_op jit(solution)/shard_map/ppermute | solution.py:55
  977.5 22.6 %collective-permute-start.48 = (bf16[192,2048]{1,0:T(8,128)(2,1)S(1)}, bf16[192,2048]{1,0:T(8,128)(2,1)S(1)}, u32[]{:S(2)}, u32[]{:S(2)}) collective-permute-start(bf16[192,2048]{1,0:T(8,128)(2,1)S(1)} %get-tuple-element.153), channel_id=1, source_target_pairs={{0,8},{8,0},{16,24},{24,16},{1,9},{9,1},{17,25},{25,17},{2,10},{10... | collective-permute-start | bytes 2359304 | tf_op jit(solution)/shard_map/ppermute | solution.py:51
  978.2 20.8 %collective-permute-start.55 = (f32[20,64]{1,0:T(8,128)S(1)}, f32[20,64]{1,0:T(8,128)S(1)}, u32[]{:S(2)}, u32[]{:S(2)}) collective-permute-start(f32[20,64]{1,0:T(8,128)S(1)} %bitcast.378), channel_id=1, source_target_pairs={{0,24},{8,16},{16,8},{24,0},{1,25},{9,17},{17,9},{25,1},{2,26},{10... | collective-permute-start | bytes 15368 | tf_op jit(solution)/shard_map/ppermute | solution.py:59
  979.7 19.3 %collective-permute-start.56 = (f32[20,64]{1,0:T(8,128)S(1)}, f32[20,64]{1,0:T(8,128)S(1)}, u32[]{:S(2)}, u32[]{:S(2)}) collective-permute-start(f32[20,64]{1,0:T(8,128)S(1)} %bitcast.379), channel_id=1, source_target_pairs={{0,16},{8,24},{16,0},{24,8},{1,17},{9,25},{17,1},{25,9},{2,18},{10... | collective-permute-start | bytes 15368 | tf_op jit(solution)/shard_map/ppermute | solution.py:55
  981.1 17.8 %collective-permute-start.57 = (f32[20,64]{1,0:T(8,128)S(1)}, f32[20,64]{1,0:T(8,128)S(1)}, u32[]{:S(2)}, u32[]{:S(2)}) collective-permute-start(f32[20,64]{1,0:T(8,128)S(1)} %bitcast.380), channel_id=1, source_target_pairs={{0,8},{8,0},{16,24},{24,16},{1,9},{9,1},{17,25},{25,17},{2,10},{10... | collective-permute-start | bytes 15368 | tf_op jit(solution)/shard_map/ppermute | solution.py:51
  1006.6 10.1 collective-permute-start.49
  1008.1 9.5 collective-permute-start.50
  1009.6 8.0 collective-permute-start.51
  (114 other events, 1407.8 us)
Sparse Core Ops, SparseCore 0:
  9.6 31.7 all-gather.4
  43.6 68.5 all-gather.6
  113.9 115.3 all-gather.10
  249.6 117.2 all-gather.8
  527.4 154.5 reduce-scatter.6
  684.1 127.5 reduce-scatter.4
  839.0 48.6 reduce-scatter.10
  897.9 87.0 reduce-scatter.8
